TPU v7x, 128 devices: a whole 4x4x4 slice. The times are simulated.
128 devices in a mesh: tgt: 32 (over z_hi, y, x), grp: 4 (over z_lo, core).
Axes of the slice: x: 4, y: 4, z: 4 (z_hi: 2, z_lo: 2; z = z_hi * 2 + z_lo), core: 2. Of those that a mesh axis runs over, the one named last changes fastest.
Arguments:
- targets: bfloat16 [32, 64, 64, 128], P('tgt', 'grp'), may hold values from -6 to 6
- partners: bfloat16 [32, 64, 64, 128], P('tgt'), may hold values from -6 to 6
- occupations: float32 [32], replicated, may hold values from 0.2 to 2
- slot_partner: int32 [32], replicated, may hold values from 0 to 31, each once
- screening: float32 [1], replicated, may hold values from 0.3 to 0.6
Outputs:
- exchange: float32 [32, 64, 64, 128], P('tgt', 'grp')
Inputs may be any that keep to these rules, and one draw needn't show every extreme that they name: `slot_partner`: every partner id appears in exactly one slot.
All inputs are finite; a program needn't handle non-finite values.
Results may differ from a plain program's by a relative error of at most 0.011.
Values may be sent and summed in bfloat16 or wider, within the bound.
No kernel may reach another device: no remote copies, remote signals or barrier semaphores. Data moves between devices by JAX's collectives and lax.ppermute only.
A program may use at most 64 MiB of HBM per device.

v0:
```python
import functools
import math

import jax
import jax.numpy as jnp
import numpy as np
from jax import lax
from jax.experimental import pallas as pl
from jax.experimental.pallas import tpu as pltpu
from jax.sharding import PartitionSpec as P


coulomb_scale = 0.1
points = 64
lanes = 2 * points
quarter = 16
pitch = 72
axes = ("tgt", "grp")
f32 = jnp.float32
bf16 = jnp.bfloat16


devices = [
    (zh, y, x, zl, c)
    for zh in range(2)
    for y in range(4)
    for x in range(4)
    for zl in range(2)
    for c in range(2)
]
number = {device: i for i, device in enumerate(devices)}


def outer(i):
    return (i + 3) % 4 if i % 2 == 0 else (i + 1) % 4


def first_source(zh, y, x, zl, c):
    return {
        (0, 0): (zh, y, x, 0, 1),
        (0, 1): (zh ^ 1, y, x, 1, 0),
        (1, 0): (zh, outer(y), x, 1, 1),
        (1, 1): (zh ^ 1, y, outer(x), 0, 0),
    }[zl, c]


def second_source(zh, y, x, zl, c):
    return {
        (0, 0): (zh, outer(y), outer(x), 0, 1),
        (0, 1): (zh ^ 1, outer(y), outer(x), 1, 0),
        (1, 0): (zh, y, outer(x), 1, 1),
        (1, 1): (zh ^ 1, outer(y), x, 0, 0),
    }[zl, c]


def offset_source(dy, dx, dz, dc):
    return lambda zh, y, x, zl, c: (zh, y ^ dy, x ^ dx, zl ^ dz, c ^ dc)


def receive(value, source):
    pairs = [(number[source(*device)], number[device]) for device in devices]
    return lax.ppermute(value, axes, pairs)


def slot_table():
    slot = lambda d: (d[0] * 4 + d[1]) * 4 + d[2]
    return np.array(
        [[slot(first_source(*d)), slot(second_source(*d))] for d in devices], np.int32
    )


def tables():
    indices = np.arange(points)
    phases = indices[:, None] * indices[None, :] % points
    angles = phases.astype(np.float32) * np.float32(2.0 * math.pi / points)
    scale = np.float32(1.0 / math.sqrt(points))
    rounded = lambda t: (t * scale).astype(bf16).astype(np.float32)
    return rounded(np.cos(angles)), rounded(np.sin(angles))


def section_matrices():
    cosine, sine = tables()
    both = lambda t: np.kron(np.eye(2, dtype=np.float32), t)
    left_forward = np.block([[cosine, sine], [-sine, cosine]])
    left_inverse = np.block([[cosine, -sine], [sine, cosine]])
    right_forward = np.block([[both(cosine), both(-sine)], [both(sine), both(cosine)]])
    right_inverse = np.block([[both(cosine), both(sine)], [both(-sine), both(cosine)]])
    return [
        jnp.asarray(m, bf16) for m in (left_forward, left_inverse, right_forward, right_inverse)
    ]


def coulomb_kernel(screening):
    indices = jnp.arange(points, dtype=jnp.int32)
    signed = jnp.where(indices < points // 2, indices, indices - points).astype(f32) * (
        2.0 * math.pi / points
    )
    squares = signed * signed
    wave_sq = squares[:, None, None] + squares[None, :, None] + jnp.tile(squares, 2)[None, None, :]
    screen_wave = screening[0] * (2.0 * math.pi / points)
    return coulomb_scale / (wave_sq + screen_wave * screen_wave)


def pair_kernel(
    place_ref, occupations_ref, slot_partner_ref,
    t0, t1, t2, t3, pa, pb, coulomb, lf_ref, li_ref, rf_ref, ri_ref,
    out,
    t_v, a_v, b_v, k_v, s_ref, o_v, in_sem, k_sem, out_sem,
):
    dot = functools.partial(jnp.dot, preferred_element_type=f32)
    place = place_ref[0]
    rows = quarter * points
    low = lax.broadcasted_iota(jnp.int32, (rows, lanes), 1) < points

    def block_of(step):
        return place ^ (2 * (step // 2) + step % 2)

    def fetches(step, t_ref):
        planes = pl.ds(block_of(step) * quarter, quarter)
        return [
            pltpu.make_async_copy(t_ref, t_v.at[step], in_sem.at[step, 0]),
            pltpu.make_async_copy(pa.at[planes], a_v.at[step], in_sem.at[step, 1]),
            pltpu.make_async_copy(pb.at[planes], b_v.at[step], in_sem.at[step, 2]),
        ]

    for step, t_ref in enumerate((t0, t1, t2, t3)):
        for copy in fetches(step, t_ref):
            copy.start()
    k_copy = pltpu.make_async_copy(coulomb, k_v, k_sem)
    k_copy.start()
    lf = lf_ref[...]
    li = li_ref[...]

    def load(ref, step):
        return ref[step].reshape(rows, lanes).astype(f32)

    def partner_parts(step):
        a = load(a_v, step)
        b = load(b_v, step)
        real = jnp.where(low, a, pltpu.roll(b, points, 1))
        imag = jnp.where(low, pltpu.roll(a, points, 1), b)
        return real, imag

    def forward(step, carry):
        for copy in fetches(step, t0):
            copy.wait()
        plane = block_of(step) * quarter
        t = load(t_v, step)
        swapped = pltpu.roll(t, points, 1)
        t_real = jnp.where(low, t, swapped)
        t_imag = jnp.where(low, swapped, t)
        p_real, p_imag = partner_parts(step)
        density = jnp.concatenate(
            [
                (p_real * t_real + p_imag * t_imag).astype(bf16),
                (p_real * t_imag - p_imag * t_real).astype(bf16),
            ],
            axis=1,
        )
        along_z = dot(density, rf_ref[...]).astype(bf16)
        columns = []
        for j in range(quarter):
            part = along_z[j * points : (j + 1) * points]
            columns.append(jnp.concatenate([part[:, :lanes], part[:, lanes:]], axis=0))
        along_y = dot(lf, jnp.concatenate(columns, axis=1))
        for j in range(quarter):
            s_ref[pl.ds(plane + j, lanes, stride=pitch), :] = along_y[:, j * lanes : (j + 1) * lanes]
        return carry

    lax.fori_loop(0, 4, forward, 0)
    k_copy.wait()

    def line(k, part):
        return pl.ds(pl.multiple_of((part * points + k) * pitch, 8), points)

    def middle(i, carry):
        first = i * quarter
        columns = []
        for j in range(quarter):
            parts = [s_ref[line(first + j, part), :].astype(bf16) for part in range(2)]
            columns.append(jnp.concatenate(parts, axis=0))
        spectrum = dot(lf, jnp.concatenate(columns, axis=1))
        weights = jnp.concatenate([k_v[first + j] for j in range(quarter)], axis=1)
        scaled = (spectrum * jnp.concatenate([weights, weights], axis=0)).astype(bf16)
        along_x = dot(li, scaled)
        for j in range(quarter):
            for part in range(2):
                s_ref[line(first + j, part), :] = along_x[
                    part * points : (part + 1) * points, j * lanes : (j + 1) * lanes
                ]
        return carry

    lax.fori_loop(0, 4, middle, 0)
    weight = [occupations_ref[slot_partner_ref[place_ref[1 + i]]] for i in range(2)]
    weight = jnp.where(low, weight[0], weight[1])

    def put(step):
        return pltpu.make_async_copy(o_v.at[step], out.at[step], out_sem.at[step])

    def inverse(step, carry):
        plane = block_of(step) * quarter
        columns = [
            s_ref[pl.ds(plane + j, lanes, stride=pitch), :].astype(bf16) for j in range(quarter)
        ]
        along_y = dot(li, jnp.concatenate(columns, axis=1)).astype(bf16)
        field = []
        for j in range(quarter):
            part = along_y[:, j * lanes : (j + 1) * lanes]
            field.append(jnp.concatenate([part[:points], part[points:]], axis=1))
        potential = dot(jnp.concatenate(field, axis=0), ri_ref[...])
        v_real = potential[:, :lanes] * weight
        v_imag = potential[:, lanes:] * weight
        p_real, p_imag = partner_parts(step)
        real = v_real * p_real - v_imag * p_imag
        imag = v_real * p_imag + v_imag * p_real
        total = jnp.where(low, real, imag) + pltpu.roll(jnp.where(low, imag, real), points, 1)
        o_v[step] = total.astype(bf16).reshape(quarter, points, lanes)
        put(step).start()
        return carry

    lax.fori_loop(0, 4, inverse, 0)
    for step in range(4):
        put(step).wait()


def exchange_part(place, occupations, slot_partner, pieces, first, second, coulomb, matrices):
    anywhere = pl.BlockSpec(memory_space=pl.ANY)
    scalar = pl.BlockSpec(memory_space=pltpu.SMEM)
    near = pl.BlockSpec(memory_space=pltpu.VMEM)
    planes = (4, quarter, points, lanes)
    return pl.pallas_call(
        pair_kernel,
        out_shape=jax.ShapeDtypeStruct(planes, bf16),
        in_specs=[scalar] * 3 + [anywhere] * 7 + [near] * 4,
        out_specs=anywhere,
        scratch_shapes=[
            pltpu.VMEM(planes, bf16),
            pltpu.VMEM(planes, bf16),
            pltpu.VMEM(planes, bf16),
            pltpu.VMEM((points, points, lanes), f32),
            pltpu.VMEM((2 * points * pitch, lanes), f32),
            pltpu.VMEM(planes, bf16),
            pltpu.SemaphoreType.DMA((4, 3)),
            pltpu.SemaphoreType.DMA,
            pltpu.SemaphoreType.DMA((4,)),
        ],
        compiler_params=pltpu.CompilerParams(vmem_limit_bytes=40 << 20),
        cost_estimate=pl.CostEstimate(
            flops=5 * 10**9, bytes_accessed=24 * 2**20, transcendentals=0
        ),
    )(place, occupations, slot_partner, *pieces, first, second, coulomb, *matrices)


def body(targets, partners, occupations, slot_partner, screening):
    own = targets[0]
    partner = partners[0]
    first = receive(partner, first_source)
    second = receive(partner, second_source)
    orders = [(0, 1), (1, 1), (1, 0), (0, 0)]
    halves = []
    for dy, dx in orders:
        same = own if (dy, dx) == (0, 0) else receive(own, offset_source(dy, dx, 0, 0))
        halves.append((same, receive(own, offset_source(dy, dx, 1, 0))))
    coulomb = coulomb_kernel(screening)
    matrices = section_matrices()
    device = lax.axis_index("tgt") * 4 + lax.axis_index("grp")
    slots = lax.dynamic_slice_in_dim(jnp.asarray(slot_table()), device, 1)[0]
    place = jnp.concatenate([lax.axis_index("grp")[None].astype(jnp.int32), slots])
    sibling = offset_source(0, 0, 0, 1)
    sums = []
    for n, ((dy, dx), (same, other)) in enumerate(zip(orders, halves)):
        pieces = [same, receive(same, sibling), other, receive(other, sibling)]
        if n >= 2:
            place, *sums[n - 2] = lax.optimization_barrier((place, *sums[n - 2]))
        part = exchange_part(
            place, occupations, slot_partner, pieces, first, second, coulomb, matrices
        )
        place, part = lax.optimization_barrier((place, part))
        both = []
        for dz in range(2):
            crossed = receive(part[2 * dz + 1], sibling)
            summed = part[2 * dz].astype(f32) + crossed.astype(f32)
            both.append(summed if (dy, dx, dz) == (0, 0, 0) else summed.astype(bf16))
        sums.append(both)
    terms = []
    for (dy, dx), both in zip(orders, sums):
        for dz in range(2):
            if (dy, dx, dz) == (0, 0, 0):
                terms.append(both[dz])
            else:
                arrived = receive(both[dz], offset_source(dy, dx, dz, 0))
                terms.append(arrived.astype(f32))
    return -sum(terms[1:], terms[0])[None]


def solution(mesh):
    in_specs = (P("tgt", "grp", None, None), P("tgt", None, None, None), P(), P(), P())
    out_specs = P("tgt", "grp", None, None)

    return jax.shard_map(body, mesh=mesh, in_specs=in_specs, out_specs=out_specs, check_vma=False)
```

profile of v0, /device:TPU:0, one launch (start us, length us, event | category | flops | bytes accessed | tf_op | source)
XLA Modules:
  0.0 118.6 jit_solution(12653746267113430339)
XLA Ops:
  0.0 5.9 %collective-permute-start.4 = (bf16[64,64,128]{2,1,0:T(8,128)(2,1)}, bf16[64,64,128]{2,1,0:T(8,128)(2,1)S(1)}, u32[]{:S(2)}, u32[]{:S(2)}) collective-permute-start(bf16[64,64,128]{2,1,0:T(8,128)(2,1)} %bitcast.57), channel_id=1, source_target_pairs={{1,0},{66,1},{51,2},{76,3},{5,4},{70,5},{55,6},{72,7},{9,8},{74,9}... | collective-permute-start | bytes 3145736 | tf_op jit(solution)/shard_map/ppermute | solution.py:62
  5.9 0.8 collective-permute-start.5
  6.6 1.5 %collective-permute-start = (bf16[16,64,128]{2,1,0:T(8,128)(2,1)}, bf16[16,64,128]{2,1,0:T(8,128)(2,1)S(1)}, u32[]{:S(2)}, u32[]{:S(2)}) collective-permute-start(bf16[16,64,128]{2,1,0:T(8,128)(2,1)} %bitcast.48), channel_id=1, source_target_pairs={{4,0},{5,1},{6,2},{7,3},{0,4},{1,5},{2,6},{3,7},{12,8},{13,9},{14,... | collective-permute-start | bytes 786440 | tf_op jit(solution)/shard_map/ppermute | solution.py:62
  8.1 2.1 %collective-permute-start.2 = (bf16[16,64,128]{2,1,0:T(8,128)(2,1)}, bf16[16,64,128]{2,1,0:T(8,128)(2,1)S(1)}, u32[]{:S(2)}, u32[]{:S(2)}) collective-permute-start(bf16[16,64,128]{2,1,0:T(8,128)(2,1)} %bitcast.49), channel_id=1, source_target_pairs={{6,0},{7,1},{4,2},{5,3},{2,4},{3,5},{0,6},{1,7},{14,8},{15,9},{12,... | collective-permute-start | bytes 786440 | tf_op jit(solution)/shard_map/ppermute | solution.py:62
  10.3 0.0 collective-permute-start.6
  10.3 0.7 dynamic-slice_bitcast_fusion
  11.0 4.1 %collective-permute-done.t0 = bf16[16,64,128]{2,1,0:T(8,128)(2,1)S(1)} collective-permute-done((bf16[16,64,128]{2,1,0:T(8,128)(2,1)}, bf16[16,64,128]{2,1,0:T(8,128)(2,1)S(1)}, u32[]{:S(2)}, u32[]{:S(2)}) %collective-permute-start) | collective-permute-done | bytes 262176 | tf_op jit(solution)/shard_map/ppermute | solution.py:62
  15.0 2.0 %collective-permute-start.8 = (bf16[16,64,128]{2,1,0:T(8,128)(2,1)}, bf16[16,64,128]{2,1,0:T(8,128)(2,1)}, u32[]{:S(2)}, u32[]{:S(2)}) collective-permute-start(bf16[16,64,128]{2,1,0:T(8,128)(2,1)} %bitcast.51), channel_id=1, source_target_pairs={{22,0},{23,1},{20,2},{21,3},{18,4},{19,5},{16,6},{17,7},{30,8},{31... | collective-permute-start | bytes 786440 | tf_op jit(solution)/shard_map/ppermute | solution.py:62
  17.1 5.6 %collective-permute-done.2.t2 = bf16[16,64,128]{2,1,0:T(8,128)(2,1)S(1)} collective-permute-done((bf16[16,64,128]{2,1,0:T(8,128)(2,1)}, bf16[16,64,128]{2,1,0:T(8,128)(2,1)S(1)}, u32[]{:S(2)}, u32[]{:S(2)}) %collective-permute-start.2) | collective-permute-done | bytes 262176 | tf_op jit(solution)/shard_map/ppermute | solution.py:62
  22.6 0.8 collective-permute-start.14
  23.4 0.1 pad_add_fusion.place_ref
  23.5 0.6 tile.2
  24.0 1.3 %add.109 = f32[128]{0:T(128)} reshape(f32[2,64]{1,0:T(2,128)} %tile.2) | data formatting | bytes 1024 | tf_op jit(solution)/shard_map/add | solution.py:99
  26.0 0.1 broadcast_add_fusion
  26.1 0.9 collective-permute-done.6.t0
  27.0 2.8 %collective-permute-start.16 = (bf16[16,64,128]{2,1,0:T(8,128)(2,1)}, bf16[16,64,128]{2,1,0:T(8,128)(2,1)S(1)}, u32[]{:S(2)}, u32[]{:S(2)}) collective-permute-start(bf16[16,64,128]{2,1,0:T(8,128)(2,1)} %bitcast.53), channel_id=1, source_target_pairs={{18,0},{19,1},{16,2},{17,3},{22,4},{23,5},{20,6},{21,7},{26,8},{27... | collective-permute-start | bytes 786440 | tf_op jit(solution)/shard_map/ppermute | solution.py:62
  29.8 2.5 %collective-permute-done.8.t2 = bf16[16,64,128]{2,1,0:T(8,128)(2,1)} collective-permute-done((bf16[16,64,128]{2,1,0:T(8,128)(2,1)}, bf16[16,64,128]{2,1,0:T(8,128)(2,1)}, u32[]{:S(2)}, u32[]{:S(2)}) %collective-permute-start.8) | collective-permute-done | bytes 262176 | tf_op jit(solution)/shard_map/ppermute | solution.py:62
  32.3 0.0 collective-permute-start.1
  32.3 6.6 %collective-permute-done.14.t0 = bf16[16,64,128]{2,1,0:T(8,128)(2,1)S(1)} collective-permute-done((bf16[16,64,128]{2,1,0:T(8,128)(2,1)}, bf16[16,64,128]{2,1,0:T(8,128)(2,1)S(1)}, u32[]{:S(2)}, u32[]{:S(2)}) %collective-permute-start.14) | collective-permute-done | bytes 262176 | tf_op jit(solution)/shard_map/ppermute | solution.py:62
  38.8 0.0 collective-permute-start.3
  38.8 1.2 %add_divide_fusion.coulomb = f32[64,64,128]{2,1,0:T(8,128)S(1)} fusion(f32[]{:T(128)} %bitcast.4, f32[128]{0:T(128)} %add.109, f32[64,64]{1,0:T(8,128)S(1)} %broadcast_add_fusion), kind=kLoop, calls=%fused_computation | loop fusion | flops 1572864 | bytes 2114052 | tf_op jit(solution)/shard_map/div | solution.py:101
  40.1 3.1 %collective-permute-done.16.t2 = bf16[16,64,128]{2,1,0:T(8,128)(2,1)S(1)} collective-permute-done((bf16[16,64,128]{2,1,0:T(8,128)(2,1)}, bf16[16,64,128]{2,1,0:T(8,128)(2,1)S(1)}, u32[]{:S(2)}, u32[]{:S(2)}) %collective-permute-start.16) | collective-permute-done | bytes 262176 | tf_op jit(solution)/shard_map/ppermute | solution.py:62
  43.2 2.6 %collective-permute-start.27 = (bf16[16,64,128]{2,1,0:T(8,128)(2,1)S(1)}, bf16[16,64,128]{2,1,0:T(8,128)(2,1)S(1)}, u32[]{:S(2)}, u32[]{:S(2)}) collective-permute-start(bf16[16,64,128]{2,1,0:T(8,128)(2,1)S(1)} %bitcast.54), channel_id=1, source_target_pairs={{2,0},{3,1},{0,2},{1,3},{6,4},{7,5},{4,6},{5,7},{10,8},{11,9},{8,1... | collective-permute-start | bytes 786440 | tf_op jit(solution)/shard_map/ppermute | solution.py:62
  45.8 0.0 collective-permute-done.1.t1
  45.8 0.5 collective-permute-start.9
  46.4 0.0 collective-permute-done.4.pa
  46.4 0.1 collective-permute-start.15
  46.4 0.4 collective-permute-start.17
  46.9 8.4 %shard_map.100 = bf16[4,16,64,128]{3,2,1,0:T(8,128)(2,1)S(1)} custom-call(s32[3]{0:T(128)S(1)} %pad_add_fusion.place_ref, f32[32]{0:T(128)S(1)} %copy-done.1, s32[32]{0:T(128)S(1)} %copy-done.2, bf16[16,64,128]{2,1,0:T(8,128)(2,1)S(1)} %collective-permute-done.t0, bf16[16,64,128]{2,1,0:T(8,128)(2,1)S(1)} %collective-permute-done.1.t1, ...), custom_call_target="tpu_custom_call" | custom-call | flops 5000000000 | bytes 25165824 | tf_op jit(solution)/shard_map/pallas_call | solution.py:231
  55.3 0.2 collective-permute-start.10
  55.5 0.0 collective-permute-done.9.t3
  55.5 0.4 collective-permute-start.11
  55.9 8.3 %shard_map.101 = bf16[4,16,64,128]{3,2,1,0:T(8,128)(2,1)S(1)} custom-call(s32[3]{0:T(128)S(1)} %pad_add_fusion.place_ref, f32[32]{0:T(128)S(1)} %copy-done.1, s32[32]{0:T(128)S(1)} %copy-done.2, bf16[16,64,128]{2,1,0:T(8,128)(2,1)S(1)} %collective-permute-done.6.t0, bf16[16,64,128]{2,1,0:T(8,128)(2,1)S(1)} %collective-permute-done.7.t1, ...), custom_call_target="tpu_custom_call" | custom-call | flops 5000000000 | bytes 25165824 | tf_op jit(solution)/shard_map/pallas_call | solution.py:231
  64.3 0.0 collective-permute-done.27.t2
  64.3 0.2 collective-permute-start.26
  64.5 0.4 collective-permute-start.28
  64.9 0.1 collective-permute-start.18
  65.0 0.2 fusion.9
  65.2 0.0 collective-permute-done.15.t1
  65.2 0.7 collective-permute-start.19
  65.9 0.0 collective-permute-done.17.t3
  65.9 8.4 %shard_map.102 = bf16[4,16,64,128]{3,2,1,0:T(8,128)(2,1)S(1)} custom-call(s32[3]{0:T(128)S(1)} %pad_add_fusion.place_ref, f32[32]{0:T(128)S(1)} %copy-done.1, s32[32]{0:T(128)S(1)} %copy-done.2, bf16[16,64,128]{2,1,0:T(8,128)(2,1)S(1)} %collective-permute-done.14.t0, bf16[16,64,128]{2,1,0:T(8,128)(2,1)S(1)} %collective-permute-done.15.t1, ...), custom_call_target="tpu_custom_call" | custom-call | flops 5000000000 | bytes 25165824 | tf_op jit(solution)/shard_map/pallas_call | solution.py:231
  74.3 0.2 fusion.7
  74.5 8.4 %shard_map.103 = bf16[4,16,64,128]{3,2,1,0:T(8,128)(2,1)S(1)} custom-call(s32[3]{0:T(128)S(1)} %pad_add_fusion.place_ref, f32[32]{0:T(128)S(1)} %copy-done.1, s32[32]{0:T(128)S(1)} %copy-done.2, bf16[16,64,128]{2,1,0:T(8,128)(2,1)S(1)} %bitcast.56, bf16[16,64,128]{2,1,0:T(8,128)(2,1)S(1)} %collective-permute-done.26.t1, ...), custom_call_target="tpu_custom_call" | custom-call | flops 5000000000 | bytes 25165824 | tf_op jit(solution)/shard_map/pallas_call | solution.py:231
  82.9 0.2 collective-permute-start.30
  83.1 0.5 collective-permute-start.22
  83.6 0.1 collective-permute-start.24
  83.7 0.4 collective-permute-start.29
  84.1 2.1 %collective-permute-start.20 = (bf16[16,64,128]{2,1,0:T(8,128)(2,1)S(1)}, bf16[16,64,128]{2,1,0:T(8,128)(2,1)S(1)}, u32[]{:S(2)}, u32[]{:S(2)}) collective-permute-start(bf16[16,64,128]{2,1,0:T(8,128)(2,1)S(1)} %get-tuple-element.26), channel_id=1, source_target_pairs={{20,0},{21,1},{22,2},{23,3},{16,4},{17,5},{18,6},{19,7},{28,8},{29... | collective-permute-start | bytes 786440 | tf_op jit(solution)/shard_map/ppermute | solution.py:62
  86.2 0.3 collective-permute-start.21
  86.5 0.1 fusion
  86.6 1.0 collective-permute-start.12
  87.6 2.5 %collective-permute-start.13 = (bf16[16,64,128]{2,1,0:T(8,128)(2,1)S(1)}, bf16[16,64,128]{2,1,0:T(8,128)(2,1)S(1)}, u32[]{:S(2)}, u32[]{:S(2)}) collective-permute-start(bf16[16,64,128]{2,1,0:T(8,128)(2,1)S(1)} %get-tuple-element.22), channel_id=1, source_target_pairs={{6,0},{7,1},{4,2},{5,3},{2,4},{3,5},{0,6},{1,7},{14,8},{15,9},{12,... | collective-permute-start | bytes 786440 | tf_op jit(solution)/shard_map/ppermute | solution.py:62
  90.1 0.2 fusion.6
  90.3 1.1 collective-permute-start.23
  91.4 2.8 %collective-permute-done.20 = bf16[16,64,128]{2,1,0:T(8,128)(2,1)S(1)} collective-permute-done((bf16[16,64,128]{2,1,0:T(8,128)(2,1)S(1)}, bf16[16,64,128]{2,1,0:T(8,128)(2,1)S(1)}, u32[]{:S(2)}, u32[]{:S(2)}) %collective-permute-start.20) | collective-permute-done | bytes 262176 | tf_op jit(solution)/shard_map/ppermute | solution.py:62
  94.3 0.5 collective-permute-start.25
  94.8 4.5 %collective-permute-done.21 = bf16[16,64,128]{2,1,0:T(8,128)(2,1)S(1)} collective-permute-done((bf16[16,64,128]{2,1,0:T(8,128)(2,1)S(1)}, bf16[16,64,128]{2,1,0:T(8,128)(2,1)S(1)}, u32[]{:S(2)}, u32[]{:S(2)}) %collective-permute-start.21) | collective-permute-done | bytes 262176 | tf_op jit(solution)/shard_map/ppermute | solution.py:62
  99.4 1.9 %collective-permute-start.31 = (bf16[16,64,128]{2,1,0:T(8,128)(2,1)S(1)}, bf16[16,64,128]{2,1,0:T(8,128)(2,1)S(1)}, u32[]{:S(2)}, u32[]{:S(2)}) collective-permute-start(bf16[16,64,128]{2,1,0:T(8,128)(2,1)S(1)} %fusion), channel_id=1, source_target_pairs={{2,0},{3,1},{0,2},{1,3},{6,4},{7,5},{4,6},{5,7},{10,8},{11,9},{8,1... | collective-permute-start | bytes 786440 | tf_op jit(solution)/shard_map/ppermute | solution.py:62
  101.3 3.7 %collective-permute-done.12 = bf16[16,64,128]{2,1,0:T(8,128)(2,1)S(1)} collective-permute-done((bf16[16,64,128]{2,1,0:T(8,128)(2,1)S(1)}, bf16[16,64,128]{2,1,0:T(8,128)(2,1)S(1)}, u32[]{:S(2)}, u32[]{:S(2)}) %collective-permute-start.12) | collective-permute-done | bytes 262176 | tf_op jit(solution)/shard_map/ppermute | solution.py:62
  105.0 9.3 %collective-permute-done.13 = bf16[16,64,128]{2,1,0:T(8,128)(2,1)S(1)} collective-permute-done((bf16[16,64,128]{2,1,0:T(8,128)(2,1)S(1)}, bf16[16,64,128]{2,1,0:T(8,128)(2,1)S(1)}, u32[]{:S(2)}, u32[]{:S(2)}) %collective-permute-start.13) | collective-permute-done | bytes 262176 | tf_op jit(solution)/shard_map/ppermute | solution.py:62
  114.3 0.4 collective-permute-done.25
  114.7 2.7 %collective-permute-done.31 = bf16[16,64,128]{2,1,0:T(8,128)(2,1)S(1)} collective-permute-done((bf16[16,64,128]{2,1,0:T(8,128)(2,1)S(1)}, bf16[16,64,128]{2,1,0:T(8,128)(2,1)S(1)}, u32[]{:S(2)}, u32[]{:S(2)}) %collective-permute-start.31) | collective-permute-done | bytes 262176 | tf_op jit(solution)/shard_map/ppermute | solution.py:62
  117.4 1.2 fusion.4
  (34 shorter events, 0.2 us)
Async XLA Ops:
  0.0 46.9 %copy-start.3 = (bf16[256,256]{1,0:T(8,128)(2,1)S(1)}, bf16[256,256]{1,0:T(8,128)(2,1)}, u32[]{:S(2)}) copy-start(bf16[256,256]{1,0:T(8,128)(2,1)} %constant.40.clone.rf_ref) | copy-start | bytes 393220
  0.0 43.2 %copy-start = (bf16[1,16,64,128]{3,2,1,0:T(8,128)(2,1)S(1)}, bf16[1,16,64,128]{3,2,1,0:T(8,128)(2,1)}, u32[]{:S(2)}) copy-start(bf16[1,16,64,128]{3,2,1,0:T(8,128)(2,1)} %param.10) | copy-start | bytes 786436
  0.0 46.9 %copy-start.1 = (f32[32]{0:T(128)S(1)}, f32[32]{0:T(128)}, u32[]{:S(2)}) copy-start(f32[32]{0:T(128)} %occupations_ref.7) | copy-start | bytes 388
  0.0 46.9 %copy-start.2 = (s32[32]{0:T(128)S(1)}, s32[32]{0:T(128)}, u32[]{:S(2)}) copy-start(s32[32]{0:T(128)} %slot_partner_ref.7) | copy-start | bytes 388
  0.0 46.3 %collective-permute-start.4 = (bf16[64,64,128]{2,1,0:T(8,128)(2,1)}, bf16[64,64,128]{2,1,0:T(8,128)(2,1)S(1)}, u32[]{:S(2)}, u32[]{:S(2)}) collective-permute-start(bf16[64,64,128]{2,1,0:T(8,128)(2,1)} %bitcast.57), channel_id=1, source_target_pairs={{1,0},{66,1},{51,2},{76,3},{5,4},{70,5},{55,6},{72,7},{9,8},{74,9}... | collective-permute-start | bytes 3145736 | tf_op jit(solution)/shard_map/ppermute | solution.py:62
  5.9 40.6 %collective-permute-start.5 = (bf16[64,64,128]{2,1,0:T(8,128)(2,1)}, bf16[64,64,128]{2,1,0:T(8,128)(2,1)S(1)}, u32[]{:S(2)}, u32[]{:S(2)}) collective-permute-start(bf16[64,64,128]{2,1,0:T(8,128)(2,1)} %bitcast.58), channel_id=1, source_target_pairs={{61,0},{126,1},{15,2},{112,3},{57,4},{122,5},{11,6},{116,7},{53,8}... | collective-permute-start | bytes 3145736 | tf_op jit(solution)/shard_map/ppermute | solution.py:62
  6.6 8.4 %collective-permute-start = (bf16[16,64,128]{2,1,0:T(8,128)(2,1)}, bf16[16,64,128]{2,1,0:T(8,128)(2,1)S(1)}, u32[]{:S(2)}, u32[]{:S(2)}) collective-permute-start(bf16[16,64,128]{2,1,0:T(8,128)(2,1)} %bitcast.48), channel_id=1, source_target_pairs={{4,0},{5,1},{6,2},{7,3},{0,4},{1,5},{2,6},{3,7},{12,8},{13,9},{14,... | collective-permute-start | bytes 786440 | tf_op jit(solution)/shard_map/ppermute | solution.py:62
  8.1 14.5 %collective-permute-start.2 = (bf16[16,64,128]{2,1,0:T(8,128)(2,1)}, bf16[16,64,128]{2,1,0:T(8,128)(2,1)S(1)}, u32[]{:S(2)}, u32[]{:S(2)}) collective-permute-start(bf16[16,64,128]{2,1,0:T(8,128)(2,1)} %bitcast.49), channel_id=1, source_target_pairs={{6,0},{7,1},{4,2},{5,3},{2,4},{3,5},{0,6},{1,7},{14,8},{15,9},{12,... | collective-permute-start | bytes 786440 | tf_op jit(solution)/shard_map/ppermute | solution.py:62
  10.3 16.7 %collective-permute-start.6 = (bf16[16,64,128]{2,1,0:T(8,128)(2,1)}, bf16[16,64,128]{2,1,0:T(8,128)(2,1)S(1)}, u32[]{:S(2)}, u32[]{:S(2)}) collective-permute-start(bf16[16,64,128]{2,1,0:T(8,128)(2,1)} %bitcast.50), channel_id=1, source_target_pairs={{20,0},{21,1},{22,2},{23,3},{16,4},{17,5},{18,6},{19,7},{28,8},{29... | collective-permute-start | bytes 786440 | tf_op jit(solution)/shard_map/ppermute | solution.py:62
  15.0 17.2 %collective-permute-start.8 = (bf16[16,64,128]{2,1,0:T(8,128)(2,1)}, bf16[16,64,128]{2,1,0:T(8,128)(2,1)}, u32[]{:S(2)}, u32[]{:S(2)}) collective-permute-start(bf16[16,64,128]{2,1,0:T(8,128)(2,1)} %bitcast.51), channel_id=1, source_target_pairs={{22,0},{23,1},{20,2},{21,3},{18,4},{19,5},{16,6},{17,7},{30,8},{31... | collective-permute-start | bytes 786440 | tf_op jit(solution)/shard_map/ppermute | solution.py:62
  22.6 16.2 %collective-permute-start.14 = (bf16[16,64,128]{2,1,0:T(8,128)(2,1)}, bf16[16,64,128]{2,1,0:T(8,128)(2,1)S(1)}, u32[]{:S(2)}, u32[]{:S(2)}) collective-permute-start(bf16[16,64,128]{2,1,0:T(8,128)(2,1)} %bitcast.52), channel_id=1, source_target_pairs={{16,0},{17,1},{18,2},{19,3},{20,4},{21,5},{22,6},{23,7},{24,8},{25... | collective-permute-start | bytes 786440 | tf_op jit(solution)/shard_map/ppermute | solution.py:62
  25.3 21.6 %copy-start.4 = (bf16[256,256]{1,0:T(8,128)(2,1)S(1)}, bf16[256,256]{1,0:T(8,128)(2,1)}, u32[]{:S(2)}) copy-start(bf16[256,256]{1,0:T(8,128)(2,1)} %constant.41.clone.ri_ref) | copy-start | bytes 393220
  25.3 21.6 %copy-start.5 = (bf16[128,128]{1,0:T(8,128)(2,1)S(1)}, bf16[128,128]{1,0:T(8,128)(2,1)}, u32[]{:S(2)}) copy-start(bf16[128,128]{1,0:T(8,128)(2,1)} %constant.38.clone.lf_ref) | copy-start | bytes 98308
  25.3 21.6 %copy-start.6 = (bf16[128,128]{1,0:T(8,128)(2,1)S(1)}, bf16[128,128]{1,0:T(8,128)(2,1)}, u32[]{:S(2)}) copy-start(bf16[128,128]{1,0:T(8,128)(2,1)} %constant.39.clone.li_ref) | copy-start | bytes 98308
  27.0 16.2 %collective-permute-start.16 = (bf16[16,64,128]{2,1,0:T(8,128)(2,1)}, bf16[16,64,128]{2,1,0:T(8,128)(2,1)S(1)}, u32[]{:S(2)}, u32[]{:S(2)}) collective-permute-start(bf16[16,64,128]{2,1,0:T(8,128)(2,1)} %bitcast.53), channel_id=1, source_target_pairs={{18,0},{19,1},{16,2},{17,3},{22,4},{23,5},{20,6},{21,7},{26,8},{27... | collective-permute-start | bytes 786440 | tf_op jit(solution)/shard_map/ppermute | solution.py:62
  32.3 13.6 %collective-permute-start.1 = (bf16[16,64,128]{2,1,0:T(8,128)(2,1)S(1)}, bf16[16,64,128]{2,1,0:T(8,128)(2,1)S(1)}, u32[]{:S(2)}, u32[]{:S(2)}) collective-permute-start(bf16[16,64,128]{2,1,0:T(8,128)(2,1)S(1)} %collective-permute-done.t0), channel_id=1, source_target_pairs={{1,0},{0,1},{3,2},{2,3},{5,4},{4,5},{7,6},{6,7},{9,8},{8,9},{11,10... | collective-permute-start | bytes 786440 | tf_op jit(solution)/shard_map/ppermute | solution.py:62
  38.8 7.0 %collective-permute-start.3 = (bf16[16,64,128]{2,1,0:T(8,128)(2,1)S(1)}, bf16[16,64,128]{2,1,0:T(8,128)(2,1)S(1)}, u32[]{:S(2)}, u32[]{:S(2)}) collective-permute-start(bf16[16,64,128]{2,1,0:T(8,128)(2,1)S(1)} %collective-permute-done.2.t2), channel_id=1, source_target_pairs={{1,0},{0,1},{3,2},{2,3},{5,4},{4,5},{7,6},{6,7},{9,8},{8,9},{11,10... | collective-permute-start | bytes 786440 | tf_op jit(solution)/shard_map/ppermute | solution.py:62
  43.2 21.1 %collective-permute-start.27 = (bf16[16,64,128]{2,1,0:T(8,128)(2,1)S(1)}, bf16[16,64,128]{2,1,0:T(8,128)(2,1)S(1)}, u32[]{:S(2)}, u32[]{:S(2)}) collective-permute-start(bf16[16,64,128]{2,1,0:T(8,128)(2,1)S(1)} %bitcast.54), channel_id=1, source_target_pairs={{2,0},{3,1},{0,2},{1,3},{6,4},{7,5},{4,6},{5,7},{10,8},{11,9},{8,1... | collective-permute-start | bytes 786440 | tf_op jit(solution)/shard_map/ppermute | solution.py:62
  45.8 9.5 %collective-permute-start.7 = (bf16[16,64,128]{2,1,0:T(8,128)(2,1)S(1)}, bf16[16,64,128]{2,1,0:T(8,128)(2,1)S(1)}, u32[]{:S(2)}, u32[]{:S(2)}) collective-permute-start(bf16[16,64,128]{2,1,0:T(8,128)(2,1)S(1)} %collective-permute-done.6.t0), channel_id=1, source_target_pairs={{1,0},{0,1},{3,2},{2,3},{5,4},{4,5},{7,6},{6,7},{9,8},{8,9},{11,10... | collective-permute-start | bytes 786440 | tf_op jit(solution)/shard_map/ppermute | solution.py:62
  45.8 9.6 %collective-permute-start.9 = (bf16[16,64,128]{2,1,0:T(8,128)(2,1)}, bf16[16,64,128]{2,1,0:T(8,128)(2,1)S(1)}, u32[]{:S(2)}, u32[]{:S(2)}) collective-permute-start(bf16[16,64,128]{2,1,0:T(8,128)(2,1)} %collective-permute-done.8.t2), channel_id=1, source_target_pairs={{1,0},{0,1},{3,2},{2,3},{5,4},{4,5},{7,6},{6,7},{9,8},{8,9},{11,10... | collective-permute-start | bytes 786440 | tf_op jit(solution)/shard_map/ppermute | solution.py:62
  46.4 18.8 %collective-permute-start.15 = (bf16[16,64,128]{2,1,0:T(8,128)(2,1)S(1)}, bf16[16,64,128]{2,1,0:T(8,128)(2,1)S(1)}, u32[]{:S(2)}, u32[]{:S(2)}) collective-permute-start(bf16[16,64,128]{2,1,0:T(8,128)(2,1)S(1)} %collective-permute-done.14.t0), channel_id=1, source_target_pairs={{1,0},{0,1},{3,2},{2,3},{5,4},{4,5},{7,6},{6,7},{9,8},{8,9},{11,10... | collective-permute-start | bytes 786440 | tf_op jit(solution)/shard_map/ppermute | solution.py:62
  46.4 19.4 %collective-permute-start.17 = (bf16[16,64,128]{2,1,0:T(8,128)(2,1)S(1)}, bf16[16,64,128]{2,1,0:T(8,128)(2,1)S(1)}, u32[]{:S(2)}, u32[]{:S(2)}) collective-permute-start(bf16[16,64,128]{2,1,0:T(8,128)(2,1)S(1)} %collective-permute-done.16.t2), channel_id=1, source_target_pairs={{1,0},{0,1},{3,2},{2,3},{5,4},{4,5},{7,6},{6,7},{9,8},{8,9},{11,10... | collective-permute-start | bytes 786440 | tf_op jit(solution)/shard_map/ppermute | solution.py:62
  55.3 9.2 %collective-permute-start.10 = (bf16[16,64,128]{2,1,0:T(8,128)(2,1)S(1)}, bf16[16,64,128]{2,1,0:T(8,128)(2,1)S(1)}, u32[]{:S(2)}, u32[]{:S(2)}) collective-permute-start(bf16[16,64,128]{2,1,0:T(8,128)(2,1)S(1)} %get-tuple-element.44), channel_id=1, source_target_pairs={{1,0},{0,1},{3,2},{2,3},{5,4},{4,5},{7,6},{6,7},{9,8},{8,9},{11,10... | collective-permute-start | bytes 786440 | tf_op jit(solution)/shard_map/ppermute | solution.py:62
  55.5 9.4 %collective-permute-start.11 = (bf16[16,64,128]{2,1,0:T(8,128)(2,1)S(1)}, bf16[16,64,128]{2,1,0:T(8,128)(2,1)S(1)}, u32[]{:S(2)}, u32[]{:S(2)}) collective-permute-start(bf16[16,64,128]{2,1,0:T(8,128)(2,1)S(1)} %get-tuple-element.43), channel_id=1, source_target_pairs={{1,0},{0,1},{3,2},{2,3},{5,4},{4,5},{7,6},{6,7},{9,8},{8,9},{11,10... | collective-permute-start | bytes 786440 | tf_op jit(solution)/shard_map/ppermute | solution.py:62
  64.3 10.1 %collective-permute-start.26 = (bf16[16,64,128]{2,1,0:T(8,128)(2,1)S(1)}, bf16[16,64,128]{2,1,0:T(8,128)(2,1)S(1)}, u32[]{:S(2)}, u32[]{:S(2)}) collective-permute-start(bf16[16,64,128]{2,1,0:T(8,128)(2,1)S(1)} %bitcast.55), channel_id=1, source_target_pairs={{1,0},{0,1},{3,2},{2,3},{5,4},{4,5},{7,6},{6,7},{9,8},{8,9},{11,10... | collective-permute-start | bytes 786440 | tf_op jit(solution)/shard_map/ppermute | solution.py:62
  64.5 10.0 %collective-permute-start.28 = (bf16[16,64,128]{2,1,0:T(8,128)(2,1)S(1)}, bf16[16,64,128]{2,1,0:T(8,128)(2,1)S(1)}, u32[]{:S(2)}, u32[]{:S(2)}) collective-permute-start(bf16[16,64,128]{2,1,0:T(8,128)(2,1)S(1)} %collective-permute-done.27.t2), channel_id=1, source_target_pairs={{1,0},{0,1},{3,2},{2,3},{5,4},{4,5},{7,6},{6,7},{9,8},{8,9},{11,10... | collective-permute-start | bytes 786440 | tf_op jit(solution)/shard_map/ppermute | solution.py:62
  64.9 9.3 %collective-permute-start.18 = (bf16[16,64,128]{2,1,0:T(8,128)(2,1)S(1)}, bf16[16,64,128]{2,1,0:T(8,128)(2,1)S(1)}, u32[]{:S(2)}, u32[]{:S(2)}) collective-permute-start(bf16[16,64,128]{2,1,0:T(8,128)(2,1)S(1)} %get-tuple-element.40), channel_id=1, source_target_pairs={{1,0},{0,1},{3,2},{2,3},{5,4},{4,5},{7,6},{6,7},{9,8},{8,9},{11,10... | collective-permute-start | bytes 786440 | tf_op jit(solution)/shard_map/ppermute | solution.py:62
  65.2 9.0 %collective-permute-start.19 = (bf16[16,64,128]{2,1,0:T(8,128)(2,1)S(1)}, bf16[16,64,128]{2,1,0:T(8,128)(2,1)S(1)}, u32[]{:S(2)}, u32[]{:S(2)}) collective-permute-start(bf16[16,64,128]{2,1,0:T(8,128)(2,1)S(1)} %get-tuple-element.39), channel_id=1, source_target_pairs={{1,0},{0,1},{3,2},{2,3},{5,4},{4,5},{7,6},{6,7},{9,8},{8,9},{11,10... | collective-permute-start | bytes 786440 | tf_op jit(solution)/shard_map/ppermute | solution.py:62
  82.9 3.4 %collective-permute-start.30 = (bf16[16,64,128]{2,1,0:T(8,128)(2,1)S(1)}, bf16[16,64,128]{2,1,0:T(8,128)(2,1)S(1)}, u32[]{:S(2)}, u32[]{:S(2)}) collective-permute-start(bf16[16,64,128]{2,1,0:T(8,128)(2,1)S(1)} %get-tuple-element.36), channel_id=1, source_target_pairs={{1,0},{0,1},{3,2},{2,3},{5,4},{4,5},{7,6},{6,7},{9,8},{8,9},{11,10... | collective-permute-start | bytes 786440 | tf_op jit(solution)/shard_map/ppermute | solution.py:62
  83.1 3.5 %collective-permute-start.22 = (bf16[16,64,128]{2,1,0:T(8,128)(2,1)S(1)}, bf16[16,64,128]{2,1,0:T(8,128)(2,1)S(1)}, u32[]{:S(2)}, u32[]{:S(2)}) collective-permute-start(bf16[16,64,128]{2,1,0:T(8,128)(2,1)S(1)} %get-tuple-element.33), channel_id=1, source_target_pairs={{1,0},{0,1},{3,2},{2,3},{5,4},{4,5},{7,6},{6,7},{9,8},{8,9},{11,10... | collective-permute-start | bytes 786440 | tf_op jit(solution)/shard_map/ppermute | solution.py:62
  83.6 4.0 %collective-permute-start.24 = (bf16[16,64,128]{2,1,0:T(8,128)(2,1)S(1)}, bf16[16,64,128]{2,1,0:T(8,128)(2,1)S(1)}, u32[]{:S(2)}, u32[]{:S(2)}) collective-permute-start(bf16[16,64,128]{2,1,0:T(8,128)(2,1)S(1)} %get-tuple-element.34), channel_id=1, source_target_pairs={{1,0},{0,1},{3,2},{2,3},{5,4},{4,5},{7,6},{6,7},{9,8},{8,9},{11,10... | collective-permute-start | bytes 786440 | tf_op jit(solution)/shard_map/ppermute | solution.py:62
  83.7 6.6 %collective-permute-start.29 = (bf16[16,64,128]{2,1,0:T(8,128)(2,1)S(1)}, bf16[16,64,128]{2,1,0:T(8,128)(2,1)S(1)}, u32[]{:S(2)}, u32[]{:S(2)}) collective-permute-start(bf16[16,64,128]{2,1,0:T(8,128)(2,1)S(1)} %get-tuple-element.35), channel_id=1, source_target_pairs={{1,0},{0,1},{3,2},{2,3},{5,4},{4,5},{7,6},{6,7},{9,8},{8,9},{11,10... | collective-permute-start | bytes 786440 | tf_op jit(solution)/shard_map/ppermute | solution.py:62
  84.1 10.2 %collective-permute-start.20 = (bf16[16,64,128]{2,1,0:T(8,128)(2,1)S(1)}, bf16[16,64,128]{2,1,0:T(8,128)(2,1)S(1)}, u32[]{:S(2)}, u32[]{:S(2)}) collective-permute-start(bf16[16,64,128]{2,1,0:T(8,128)(2,1)S(1)} %get-tuple-element.26), channel_id=1, source_target_pairs={{20,0},{21,1},{22,2},{23,3},{16,4},{17,5},{18,6},{19,7},{28,8},{29... | collective-permute-start | bytes 786440 | tf_op jit(solution)/shard_map/ppermute | solution.py:62
  86.2 13.1 %collective-permute-start.21 = (bf16[16,64,128]{2,1,0:T(8,128)(2,1)S(1)}, bf16[16,64,128]{2,1,0:T(8,128)(2,1)S(1)}, u32[]{:S(2)}, u32[]{:S(2)}) collective-permute-start(bf16[16,64,128]{2,1,0:T(8,128)(2,1)S(1)} %get-tuple-element.27), channel_id=1, source_target_pairs={{22,0},{23,1},{20,2},{21,3},{18,4},{19,5},{16,6},{17,7},{30,8},{31... | collective-permute-start | bytes 786440 | tf_op jit(solution)/shard_map/ppermute | solution.py:62
  86.6 18.4 %collective-permute-start.12 = (bf16[16,64,128]{2,1,0:T(8,128)(2,1)S(1)}, bf16[16,64,128]{2,1,0:T(8,128)(2,1)S(1)}, u32[]{:S(2)}, u32[]{:S(2)}) collective-permute-start(bf16[16,64,128]{2,1,0:T(8,128)(2,1)S(1)} %get-tuple-element.21), channel_id=1, source_target_pairs={{4,0},{5,1},{6,2},{7,3},{0,4},{1,5},{2,6},{3,7},{12,8},{13,9},{14,... | collective-permute-start | bytes 786440 | tf_op jit(solution)/shard_map/ppermute | solution.py:62
  87.6 26.7 %collective-permute-start.13 = (bf16[16,64,128]{2,1,0:T(8,128)(2,1)S(1)}, bf16[16,64,128]{2,1,0:T(8,128)(2,1)S(1)}, u32[]{:S(2)}, u32[]{:S(2)}) collective-permute-start(bf16[16,64,128]{2,1,0:T(8,128)(2,1)S(1)} %get-tuple-element.22), channel_id=1, source_target_pairs={{6,0},{7,1},{4,2},{5,3},{2,4},{3,5},{0,6},{1,7},{14,8},{15,9},{12,... | collective-permute-start | bytes 786440 | tf_op jit(solution)/shard_map/ppermute | solution.py:62
  90.3 24.0 %collective-permute-start.23 = (bf16[16,64,128]{2,1,0:T(8,128)(2,1)S(1)}, bf16[16,64,128]{2,1,0:T(8,128)(2,1)S(1)}, u32[]{:S(2)}, u32[]{:S(2)}) collective-permute-start(bf16[16,64,128]{2,1,0:T(8,128)(2,1)S(1)} %get-tuple-element.31), channel_id=1, source_target_pairs={{16,0},{17,1},{18,2},{19,3},{20,4},{21,5},{22,6},{23,7},{24,8},{25... | collective-permute-start | bytes 786440 | tf_op jit(solution)/shard_map/ppermute | solution.py:62
  94.3 20.5 %collective-permute-start.25 = (bf16[16,64,128]{2,1,0:T(8,128)(2,1)S(1)}, bf16[16,64,128]{2,1,0:T(8,128)(2,1)S(1)}, u32[]{:S(2)}, u32[]{:S(2)}) collective-permute-start(bf16[16,64,128]{2,1,0:T(8,128)(2,1)S(1)} %get-tuple-element.32), channel_id=1, source_target_pairs={{18,0},{19,1},{16,2},{17,3},{22,4},{23,5},{20,6},{21,7},{26,8},{27... | collective-permute-start | bytes 786440 | tf_op jit(solution)/shard_map/ppermute | solution.py:62
  99.4 18.1 %collective-permute-start.31 = (bf16[16,64,128]{2,1,0:T(8,128)(2,1)S(1)}, bf16[16,64,128]{2,1,0:T(8,128)(2,1)S(1)}, u32[]{:S(2)}, u32[]{:S(2)}) collective-permute-start(bf16[16,64,128]{2,1,0:T(8,128)(2,1)S(1)} %fusion), channel_id=1, source_target_pairs={{2,0},{3,1},{0,2},{1,3},{6,4},{7,5},{4,6},{5,7},{10,8},{11,9},{8,1... | collective-permute-start | bytes 786440 | tf_op jit(solution)/shard_map/ppermute | solution.py:62
where the time goes:
time: 119 us
  waiting for transfers between devices  46.3 us (39%)
  Pallas kernels  33.4 us (28%)
  starting transfers between devices  32.2 us (27%)
  other arithmetic  3.14 us (3%)
  local copies, waits for them, and re-layouts  2.69 us (2%)
    ppermute x32, waiting for transfers between devices, receive(): return lax.ppermute(value, axes, pairs)  46.3 us
    pallas_call x4, Pallas kernels, exchange_part(): pl.pallas_call(pair_kernel, out_shape=jax.ShapeDtypeStruct(planes, bf16),...  33.4 us
    ppermute x32, starting transfers between devices, receive(): return lax.ppermute(value, axes, pairs)  32.2 us
  transfers between devices with their start and end apart: 32, of which 12 were waited for; matrix products, arithmetic and copies ran while one was open for 4% of the time, Pallas kernels for 21%

commit v1 on v0

--- a/solution.py
+++ b/solution.py
@@ -14,6 +14,7 @@
 points = 64
 lanes = 2 * points
 quarter = 16
+splits = 4
 pitch = 72
 axes = ("tgt", "grp")
 f32 = jnp.float32
@@ -90,7 +91,14 @@
     ]
 
 
-def coulomb_kernel(screening):
+def pair_weights(occupations, slot_partner, slots):
+    ids = jnp.arange(occupations.shape[0], dtype=jnp.int32)
+    match = slot_partner[:, None] == ids[None, :]
+    by_slot = jnp.sum(jnp.where(match, occupations[None, :], 0.0), axis=1)
+    return jnp.sum(jnp.where(slots[:, None] == ids[None, :], by_slot[None, :], 0.0), axis=1)
+
+
+def coulomb_kernel(screening, weights):
     indices = jnp.arange(points, dtype=jnp.int32)
     signed = jnp.where(indices < points // 2, indices, indices - points).astype(f32) * (
         2.0 * math.pi / points
@@ -98,22 +106,23 @@
     squares = signed * signed
     wave_sq = squares[:, None, None] + squares[None, :, None] + jnp.tile(squares, 2)[None, None, :]
     screen_wave = screening[0] * (2.0 * math.pi / points)
-    return coulomb_scale / (wave_sq + screen_wave * screen_wave)
+    lane = jnp.arange(lanes, dtype=jnp.int32)
+    weight = jnp.where(lane < points, weights[0], weights[1])
+    return (coulomb_scale / (wave_sq + screen_wave * screen_wave)) * weight[None, None, :]
 
 
 def pair_kernel(
-    place_ref, occupations_ref, slot_partner_ref,
-    t0, t1, t2, t3, pa, pb, coulomb, lf_ref, li_ref, rf_ref, ri_ref,
+    place_ref, t0, t1, t2, t3, pa, pb, coulomb, lf_ref, li_ref, rf_ref, ri_ref,
     out,
-    t_v, a_v, b_v, k_v, s_ref, o_v, in_sem, k_sem, out_sem,
+    t_v, a_v, b_v, k_v, s_ref, z_ref, y_ref, o_v, in_sem, k_sem, out_sem,
 ):
     dot = functools.partial(jnp.dot, preferred_element_type=f32)
     place = place_ref[0]
     rows = quarter * points
-    low = lax.broadcasted_iota(jnp.int32, (rows, lanes), 1) < points
+    low = lax.broadcasted_iota(jnp.int16, (rows, lanes), 1) < points
 
     def block_of(step):
-        return place ^ (2 * (step // 2) + step % 2)
+        return place ^ step
 
     def fetches(step, t_ref):
         planes = pl.ds(block_of(step) * quarter, quarter)
@@ -132,42 +141,59 @@
     li = li_ref[...]
 
     def load(ref, step):
-        return ref[step].reshape(rows, lanes).astype(f32)
-
-    def partner_parts(step):
+        return ref[step].reshape(rows, lanes)
+
+    def swap(v):
+        return pltpu.roll(v, points, 1)
+
+    def last_section(field, matrix):
+        part = rows // splits
+        parts = [dot(field[n * part : (n + 1) * part], matrix).astype(bf16) for n in range(splits)]
+        return jnp.concatenate(parts, axis=0)
+
+    def arrive(step):
+        for copy in fetches(step, t0):
+            copy.wait()
+
+    def forward_z(step):
+        t = load(t_v, step)
+        swapped = swap(t)
+        t_real = jnp.where(low, t, swapped)
+        t_imag = jnp.where(low, swapped, t)
         a = load(a_v, step)
         b = load(b_v, step)
-        real = jnp.where(low, a, pltpu.roll(b, points, 1))
-        imag = jnp.where(low, pltpu.roll(a, points, 1), b)
-        return real, imag
+        p_real = jnp.where(low, a, swap(b))
+        p_imag = jnp.where(low, swap(a), b)
+        a_v[step] = p_real.reshape(quarter, points, lanes)
+        b_v[step] = p_imag.reshape(quarter, points, lanes)
+        density = jnp.concatenate(
+            [p_real * t_real + p_imag * t_imag, p_real * t_imag - p_imag * t_real], axis=1
+        )
+        along_z = last_section(density, rf_ref[...])
+        slot = step % 2
+        for j in range(quarter):
+            for c in range(2):
+                z_ref[slot, j, c * points : (c + 1) * points] = along_z[
+                    j * points : (j + 1) * points, c * lanes : (c + 1) * lanes
+                ]
+
+    def forward_y(step):
+        slot = step % 2
+        plane = block_of(step) * quarter
+        along_y = dot(lf, jnp.concatenate([z_ref[slot, j] for j in range(quarter)], axis=1))
+        for j in range(quarter):
+            s_ref[pl.ds(plane + j, lanes, stride=pitch), :] = along_y[:, j * lanes : (j + 1) * lanes]
 
     def forward(step, carry):
-        for copy in fetches(step, t0):
-            copy.wait()
-        plane = block_of(step) * quarter
-        t = load(t_v, step)
-        swapped = pltpu.roll(t, points, 1)
-        t_real = jnp.where(low, t, swapped)
-        t_imag = jnp.where(low, swapped, t)
-        p_real, p_imag = partner_parts(step)
-        density = jnp.concatenate(
-            [
-                (p_real * t_real + p_imag * t_imag).astype(bf16),
-                (p_real * t_imag - p_imag * t_real).astype(bf16),
-            ],
-            axis=1,
-        )
-        along_z = dot(density, rf_ref[...]).astype(bf16)
-        columns = []
-        for j in range(quarter):
-            part = along_z[j * points : (j + 1) * points]
-            columns.append(jnp.concatenate([part[:, :lanes], part[:, lanes:]], axis=0))
-        along_y = dot(lf, jnp.concatenate(columns, axis=1))
-        for j in range(quarter):
-            s_ref[pl.ds(plane + j, lanes, stride=pitch), :] = along_y[:, j * lanes : (j + 1) * lanes]
+        arrive(step + 1)
+        forward_y(step)
+        forward_z(step + 1)
         return carry
 
-    lax.fori_loop(0, 4, forward, 0)
+    arrive(0)
+    forward_z(0)
+    lax.fori_loop(0, 3, forward, 0)
+    forward_y(3)
     k_copy.wait()
 
     def line(k, part):
@@ -191,39 +217,49 @@
         return carry
 
     lax.fori_loop(0, 4, middle, 0)
-    weight = [occupations_ref[slot_partner_ref[place_ref[1 + i]]] for i in range(2)]
-    weight = jnp.where(low, weight[0], weight[1])
 
     def put(step):
         return pltpu.make_async_copy(o_v.at[step], out.at[step], out_sem.at[step])
 
-    def inverse(step, carry):
+    def inverse_y(step):
+        slot = step % 2
         plane = block_of(step) * quarter
         columns = [
             s_ref[pl.ds(plane + j, lanes, stride=pitch), :].astype(bf16) for j in range(quarter)
         ]
         along_y = dot(li, jnp.concatenate(columns, axis=1)).astype(bf16)
-        field = []
-        for j in range(quarter):
-            part = along_y[:, j * lanes : (j + 1) * lanes]
-            field.append(jnp.concatenate([part[:points], part[points:]], axis=1))
-        potential = dot(jnp.concatenate(field, axis=0), ri_ref[...])
-        v_real = potential[:, :lanes] * weight
-        v_imag = potential[:, lanes:] * weight
-        p_real, p_imag = partner_parts(step)
+        for j in range(quarter):
+            for c in range(2):
+                y_ref[slot, j * points : (j + 1) * points, c * lanes : (c + 1) * lanes] = along_y[
+                    c * points : (c + 1) * points, j * lanes : (j + 1) * lanes
+                ]
+
+    def inverse_z(step):
+        potential = last_section(y_ref[step % 2], ri_ref[...])
+        v_real = potential[:, :lanes]
+        v_imag = potential[:, lanes:]
+        p_real = load(a_v, step)
+        p_imag = load(b_v, step)
         real = v_real * p_real - v_imag * p_imag
         imag = v_real * p_imag + v_imag * p_real
-        total = jnp.where(low, real, imag) + pltpu.roll(jnp.where(low, imag, real), points, 1)
-        o_v[step] = total.astype(bf16).reshape(quarter, points, lanes)
+        total = jnp.where(low, real, imag) + swap(jnp.where(low, imag, real))
+        o_v[step] = total.reshape(quarter, points, lanes)
+
+    def inverse(step, carry):
+        inverse_z(step)
+        inverse_y(step + 1)
         put(step).start()
         return carry
 
-    lax.fori_loop(0, 4, inverse, 0)
+    inverse_y(0)
+    lax.fori_loop(0, 3, inverse, 0)
+    inverse_z(3)
+    put(3).start()
     for step in range(4):
         put(step).wait()
 
 
-def exchange_part(place, occupations, slot_partner, pieces, first, second, coulomb, matrices):
+def exchange_part(place, pieces, first, second, coulomb, matrices):
     anywhere = pl.BlockSpec(memory_space=pl.ANY)
     scalar = pl.BlockSpec(memory_space=pltpu.SMEM)
     near = pl.BlockSpec(memory_space=pltpu.VMEM)
@@ -231,7 +267,7 @@
     return pl.pallas_call(
         pair_kernel,
         out_shape=jax.ShapeDtypeStruct(planes, bf16),
-        in_specs=[scalar] * 3 + [anywhere] * 7 + [near] * 4,
+        in_specs=[scalar] + [anywhere] * 7 + [near] * 4,
         out_specs=anywhere,
         scratch_shapes=[
             pltpu.VMEM(planes, bf16),
@@ -239,6 +275,8 @@
             pltpu.VMEM(planes, bf16),
             pltpu.VMEM((points, points, lanes), f32),
             pltpu.VMEM((2 * points * pitch, lanes), f32),
+            pltpu.VMEM((2, quarter, lanes, lanes), bf16),
+            pltpu.VMEM((2, quarter * points, 2 * lanes), bf16),
             pltpu.VMEM(planes, bf16),
             pltpu.SemaphoreType.DMA((4, 3)),
             pltpu.SemaphoreType.DMA,
@@ -248,7 +286,7 @@
         cost_estimate=pl.CostEstimate(
             flops=5 * 10**9, bytes_accessed=24 * 2**20, transcendentals=0
         ),
-    )(place, occupations, slot_partner, *pieces, first, second, coulomb, *matrices)
+    )(place, *pieces, first, second, coulomb, *matrices)
 
 
 def body(targets, partners, occupations, slot_partner, screening):
@@ -256,26 +294,28 @@
     partner = partners[0]
     first = receive(partner, first_source)
     second = receive(partner, second_source)
-    orders = [(0, 1), (1, 1), (1, 0), (0, 0)]
+    orders = [(0, 1), (1, 0), (1, 1), (0, 0)]
     halves = []
     for dy, dx in orders:
         same = own if (dy, dx) == (0, 0) else receive(own, offset_source(dy, dx, 0, 0))
         halves.append((same, receive(own, offset_source(dy, dx, 1, 0))))
-    coulomb = coulomb_kernel(screening)
     matrices = section_matrices()
     device = lax.axis_index("tgt") * 4 + lax.axis_index("grp")
     slots = lax.dynamic_slice_in_dim(jnp.asarray(slot_table()), device, 1)[0]
-    place = jnp.concatenate([lax.axis_index("grp")[None].astype(jnp.int32), slots])
+    place = lax.axis_index("grp")[None].astype(jnp.int32)
+    coulomb = coulomb_kernel(screening, pair_weights(occupations, slot_partner, slots))
     sibling = offset_source(0, 0, 0, 1)
     sums = []
+    marks = []
     for n, ((dy, dx), (same, other)) in enumerate(zip(orders, halves)):
+        if n >= 2:
+            _, same, other = lax.optimization_barrier((marks[n - 2], same, other))
         pieces = [same, receive(same, sibling), other, receive(other, sibling)]
-        if n >= 2:
-            place, *sums[n - 2] = lax.optimization_barrier((place, *sums[n - 2]))
-        part = exchange_part(
-            place, occupations, slot_partner, pieces, first, second, coulomb, matrices
-        )
+        for m in {2: [0], 3: [1, 2]}.get(n, []):
+            place, *sums[m] = lax.optimization_barrier((place, *sums[m]))
+        part = exchange_part(place, pieces, first, second, coulomb, matrices)
         place, part = lax.optimization_barrier((place, part))
+        marks.append(place)
         both = []
         for dz in range(2):
             crossed = receive(part[2 * dz + 1], sibling)

time: 119 us -> 101 us (0.85)
  the two profiles are of different devices: /device:TPU:0 before, /device:TPU:26 now
where the time goes in v1:
time: 101 us; the launch traced here: 99 us
  waiting for transfers between devices  32.6 us (32%)
  starting transfers between devices  31.1 us (31%)
  Pallas kernels  28 us (28%)
  other arithmetic  4.76 us (5%)
  local copies, waits for them, and re-layouts  1.59 us (2%)
    ppermute x32, waiting for transfers between devices, receive(): return lax.ppermute(value, axes, pairs)  32.6 us
    ppermute x32, starting transfers between devices, receive(): return lax.ppermute(value, axes, pairs)  31.1 us
    pallas_call x4, Pallas kernels, exchange_part(): pl.pallas_call(pair_kernel, out_shape=jax.ShapeDtypeStruct(planes, bf16),...  28 us
  transfers between devices with their start and end apart: 32, of which 14 were waited for; matrix products, arithmetic and copies ran while one was open for 5% of the time, Pallas kernels for 21%

profile of v1, /device:TPU:26, one launch (start us, length us, event | category | flops | bytes accessed | tf_op | source)
XLA Modules:
  0.0 99.0 jit_solution(3907867475236431760)
XLA Ops:
  0.0 0.0 copy-start.2
  0.0 0.0 copy-start
  0.0 0.6 collective-permute-start
  0.6 2.8 %collective-permute-start.2 = (bf16[16,64,128]{2,1,0:T(8,128)(2,1)}, bf16[16,64,128]{2,1,0:T(8,128)(2,1)S(1)}, u32[]{:S(2)}, u32[]{:S(2)}) collective-permute-start(bf16[16,64,128]{2,1,0:T(8,128)(2,1)} %bitcast.51), channel_id=1, source_target_pairs={{6,0},{7,1},{4,2},{5,3},{2,4},{3,5},{0,6},{1,7},{14,8},{15,9},{12,... | collective-permute-start | bytes 786440 | tf_op jit(solution)/shard_map/ppermute | solution.py:63
  3.5 2.3 %collective-permute-start.4 = (bf16[64,64,128]{2,1,0:T(8,128)(2,1)}, bf16[64,64,128]{2,1,0:T(8,128)(2,1)S(1)}, u32[]{:S(2)}, u32[]{:S(2)}) collective-permute-start(bf16[64,64,128]{2,1,0:T(8,128)(2,1)} %bitcast.59), channel_id=1, source_target_pairs={{1,0},{66,1},{51,2},{76,3},{5,4},{70,5},{55,6},{72,7},{9,8},{74,9}... | collective-permute-start | bytes 3145736 | tf_op jit(solution)/shard_map/ppermute | solution.py:63
  5.8 2.6 %collective-permute-start.5 = (bf16[64,64,128]{2,1,0:T(8,128)(2,1)}, bf16[64,64,128]{2,1,0:T(8,128)(2,1)S(1)}, u32[]{:S(2)}, u32[]{:S(2)}) collective-permute-start(bf16[64,64,128]{2,1,0:T(8,128)(2,1)} %bitcast.60), channel_id=1, source_target_pairs={{61,0},{126,1},{15,2},{112,3},{57,4},{122,5},{11,6},{116,7},{53,8}... | collective-permute-start | bytes 3145736 | tf_op jit(solution)/shard_map/ppermute | solution.py:63
  8.4 0.7 dynamic-slice_bitcast_fusion
  9.1 0.8 select_reduce_fusion
  10.0 0.2 fusion.11
  10.1 0.6 fusion.15
  10.8 1.2 %compare_select_fusion.2 = f32[128]{0:T(128)S(1)} fusion(f32[]{:T(128)} %bitcast.6, f32[]{:T(128)} %bitcast.5), kind=kLoop, calls=%fused_computation.33 | loop fusion | flops 256 | bytes 520 | tf_op jit(solution)/shard_map/jit(_where)/select_n | solution.py:110
  12.7 0.1 add.107
  12.8 0.1 broadcast_add_fusion
  12.9 0.0 collective-permute-done.t0
  12.9 0.9 collective-permute-start.8
  13.7 1.8 %collective-permute-done.2.t2 = bf16[16,64,128]{2,1,0:T(8,128)(2,1)S(1)} collective-permute-done((bf16[16,64,128]{2,1,0:T(8,128)(2,1)}, bf16[16,64,128]{2,1,0:T(8,128)(2,1)S(1)}, u32[]{:S(2)}, u32[]{:S(2)}) %collective-permute-start.2) | collective-permute-done | bytes 262176 | tf_op jit(solution)/shard_map/ppermute | solution.py:63
  15.5 0.0 collective-permute-start.1
  15.5 0.0 collective-permute-done.6.t0
  15.5 0.5 collective-permute-start.3
  16.0 0.6 divide_multiply_fusion.coulomb
  16.6 4.4 %collective-permute-done.8.t2 = bf16[16,64,128]{2,1,0:T(8,128)(2,1)S(1)} collective-permute-done((bf16[16,64,128]{2,1,0:T(8,128)(2,1)}, bf16[16,64,128]{2,1,0:T(8,128)(2,1)S(1)}, u32[]{:S(2)}, u32[]{:S(2)}) %collective-permute-start.8) | collective-permute-done | bytes 262176 | tf_op jit(solution)/shard_map/ppermute | solution.py:63
  21.0 2.0 %collective-permute-start.14 = (bf16[16,64,128]{2,1,0:T(8,128)(2,1)S(1)}, bf16[16,64,128]{2,1,0:T(8,128)(2,1)S(1)}, u32[]{:S(2)}, u32[]{:S(2)}) collective-permute-start(bf16[16,64,128]{2,1,0:T(8,128)(2,1)S(1)} %bitcast.54), channel_id=1, source_target_pairs={{20,0},{21,1},{22,2},{23,3},{16,4},{17,5},{18,6},{19,7},{28,8},{29... | collective-permute-start | bytes 786440 | tf_op jit(solution)/shard_map/ppermute | solution.py:63
  23.0 1.5 %collective-permute-start.15 = (bf16[16,64,128]{2,1,0:T(8,128)(2,1)S(1)}, bf16[16,64,128]{2,1,0:T(8,128)(2,1)S(1)}, u32[]{:S(2)}, u32[]{:S(2)}) collective-permute-start(bf16[16,64,128]{2,1,0:T(8,128)(2,1)S(1)} %bitcast.55), channel_id=1, source_target_pairs={{22,0},{23,1},{20,2},{21,3},{18,4},{19,5},{16,6},{17,7},{30,8},{31... | collective-permute-start | bytes 786440 | tf_op jit(solution)/shard_map/ppermute | solution.py:63
  24.4 0.9 collective-permute-start.26
  25.4 3.9 %collective-permute-done.4.pa = bf16[64,64,128]{2,1,0:T(8,128)(2,1)S(1)} collective-permute-done((bf16[64,64,128]{2,1,0:T(8,128)(2,1)}, bf16[64,64,128]{2,1,0:T(8,128)(2,1)S(1)}, u32[]{:S(2)}, u32[]{:S(2)}) %collective-permute-start.4) | collective-permute-done | bytes 1048608 | tf_op jit(solution)/shard_map/ppermute | solution.py:63
  29.3 1.9 %collective-permute-done.5.pb = bf16[64,64,128]{2,1,0:T(8,128)(2,1)S(1)} collective-permute-done((bf16[64,64,128]{2,1,0:T(8,128)(2,1)}, bf16[64,64,128]{2,1,0:T(8,128)(2,1)S(1)}, u32[]{:S(2)}, u32[]{:S(2)}) %collective-permute-start.5) | collective-permute-done | bytes 1048608 | tf_op jit(solution)/shard_map/ppermute | solution.py:63
  31.3 1.9 %collective-permute-start.9 = (bf16[16,64,128]{2,1,0:T(8,128)(2,1)S(1)}, bf16[16,64,128]{2,1,0:T(8,128)(2,1)S(1)}, u32[]{:S(2)}, u32[]{:S(2)}) collective-permute-start(bf16[16,64,128]{2,1,0:T(8,128)(2,1)S(1)} %collective-permute-done.8.t2), channel_id=1, source_target_pairs={{1,0},{0,1},{3,2},{2,3},{5,4},{4,5},{7,6},{6,7},{9,8},{8,9},{11,10... | collective-permute-start | bytes 786440 | tf_op jit(solution)/shard_map/ppermute | solution.py:63
  33.1 7.0 %shard_map.100 = bf16[4,16,64,128]{3,2,1,0:T(8,128)(2,1)S(1)} custom-call(s32[1]{0:T(128)} %bitcast.place_ref, bf16[16,64,128]{2,1,0:T(8,128)(2,1)S(1)} %collective-permute-done.t0, bf16[16,64,128]{2,1,0:T(8,128)(2,1)S(1)} %collective-permute-done.1.t1, bf16[16,64,128]{2,1,0:T(8,128)(2,1)S(1)} %collective-permute-done.2.t2, ...), custom_call_target="tpu_custom_call" | custom-call | flops 5000000000 | bytes 25165824 | tf_op jit(solution)/shard_map/pallas_call | solution.py:267
  40.2 0.0 collective-permute-done.7.t1
  40.2 0.1 collective-permute-start.11
  40.3 0.5 collective-permute-start.10
  40.8 7.0 %shard_map.101 = bf16[4,16,64,128]{3,2,1,0:T(8,128)(2,1)S(1)} custom-call(s32[1]{0:T(128)} %bitcast.place_ref, bf16[16,64,128]{2,1,0:T(8,128)(2,1)S(1)} %collective-permute-done.6.t0, bf16[16,64,128]{2,1,0:T(8,128)(2,1)S(1)} %collective-permute-done.7.t1, bf16[16,64,128]{2,1,0:T(8,128)(2,1)S(1)} %collective-permute-done.8.t2, ...), custom_call_target="tpu_custom_call" | custom-call | flops 5000000000 | bytes 25165824 | tf_op jit(solution)/shard_map/pallas_call | solution.py:267
  47.8 0.2 collective-permute-start.16
  48.0 0.4 collective-permute-start.17
  48.5 0.2 collective-permute-start.19
  48.7 0.4 collective-permute-start.18
  49.1 0.2 fusion.9
  49.3 0.2 collective-permute-done.16.t1
  49.5 0.4 collective-permute-done.17.t3
  49.8 7.0 %shard_map.102 = bf16[4,16,64,128]{3,2,1,0:T(8,128)(2,1)S(1)} custom-call(s32[1]{0:T(128)} %bitcast.place_ref, bf16[16,64,128]{2,1,0:T(8,128)(2,1)S(1)} %collective-permute-done.14.t0, bf16[16,64,128]{2,1,0:T(8,128)(2,1)S(1)} %collective-permute-done.16.t1, bf16[16,64,128]{2,1,0:T(8,128)(2,1)S(1)} %collective-permute-done.15.t2, ...), custom_call_target="tpu_custom_call" | custom-call | flops 5000000000 | bytes 25165824 | tf_op jit(solution)/shard_map/pallas_call | solution.py:267
  56.9 0.2 collective-permute-start.23
  57.1 0.4 collective-permute-start.22
  57.5 0.1 collective-permute-start.27
  57.6 0.4 collective-permute-start.28
  58.0 0.2 fusion.7
  58.2 0.3 collective-permute-done.23
  58.5 0.4 collective-permute-done.22
  58.9 0.2 fusion.5
  59.1 0.2 collective-permute-done.27.t1
  59.3 0.4 collective-permute-done.28.t3
  59.6 7.0 %shard_map.103 = bf16[4,16,64,128]{3,2,1,0:T(8,128)(2,1)S(1)} custom-call(s32[1]{0:T(128)} %bitcast.place_ref, bf16[16,64,128]{2,1,0:T(8,128)(2,1)S(1)} %bitcast.58, bf16[16,64,128]{2,1,0:T(8,128)(2,1)S(1)} %collective-permute-done.27.t1, bf16[16,64,128]{2,1,0:T(8,128)(2,1)S(1)} %collective-permute-done.26.t2, ...), custom_call_target="tpu_custom_call" | custom-call | flops 5000000000 | bytes 25165824 | tf_op jit(solution)/shard_map/pallas_call | solution.py:267
  66.7 0.2 collective-permute-start.30
  66.9 0.9 collective-permute-start.20
  67.8 3.8 %collective-permute-start.13 = (bf16[16,64,128]{2,1,0:T(8,128)(2,1)S(1)}, bf16[16,64,128]{2,1,0:T(8,128)(2,1)S(1)}, u32[]{:S(2)}, u32[]{:S(2)}) collective-permute-start(bf16[16,64,128]{2,1,0:T(8,128)(2,1)S(1)} %get-tuple-element.29), channel_id=1, source_target_pairs={{6,0},{7,1},{4,2},{5,3},{2,4},{3,5},{0,6},{1,7},{14,8},{15,9},{12,... | collective-permute-start | bytes 786440 | tf_op jit(solution)/shard_map/ppermute | solution.py:63
  71.6 0.2 collective-permute-start.12
  71.9 0.1 fusion
  71.9 8.5 %collective-permute-done.21 = bf16[16,64,128]{2,1,0:T(8,128)(2,1)S(1)} collective-permute-done((bf16[16,64,128]{2,1,0:T(8,128)(2,1)S(1)}, bf16[16,64,128]{2,1,0:T(8,128)(2,1)S(1)}, u32[]{:S(2)}, u32[]{:S(2)}) %collective-permute-start.21) | collective-permute-done | bytes 262176 | tf_op jit(solution)/shard_map/ppermute | solution.py:63
  80.5 1.3 %collective-permute-start.25 = (bf16[16,64,128]{2,1,0:T(8,128)(2,1)S(1)}, bf16[16,64,128]{2,1,0:T(8,128)(2,1)S(1)}, u32[]{:S(2)}, u32[]{:S(2)}) collective-permute-start(bf16[16,64,128]{2,1,0:T(8,128)(2,1)S(1)} %get-tuple-element.40), channel_id=1, source_target_pairs={{22,0},{23,1},{20,2},{21,3},{18,4},{19,5},{16,6},{17,7},{30,8},{31... | collective-permute-start | bytes 786440 | tf_op jit(solution)/shard_map/ppermute | solution.py:63
  81.8 2.8 %collective-permute-start.24 = (bf16[16,64,128]{2,1,0:T(8,128)(2,1)S(1)}, bf16[16,64,128]{2,1,0:T(8,128)(2,1)S(1)}, u32[]{:S(2)}, u32[]{:S(2)}) collective-permute-start(bf16[16,64,128]{2,1,0:T(8,128)(2,1)S(1)} %get-tuple-element.39), channel_id=1, source_target_pairs={{20,0},{21,1},{22,2},{23,3},{16,4},{17,5},{18,6},{19,7},{28,8},{29... | collective-permute-start | bytes 786440 | tf_op jit(solution)/shard_map/ppermute | solution.py:63
  84.5 3.1 %collective-permute-start.31 = (bf16[16,64,128]{2,1,0:T(8,128)(2,1)S(1)}, bf16[16,64,128]{2,1,0:T(8,128)(2,1)S(1)}, u32[]{:S(2)}, u32[]{:S(2)}) collective-permute-start(bf16[16,64,128]{2,1,0:T(8,128)(2,1)S(1)} %fusion), channel_id=1, source_target_pairs={{2,0},{3,1},{0,2},{1,3},{6,4},{7,5},{4,6},{5,7},{10,8},{11,9},{8,1... | collective-permute-start | bytes 786440 | tf_op jit(solution)/shard_map/ppermute | solution.py:63
  87.6 5.5 %collective-permute-done.25 = bf16[16,64,128]{2,1,0:T(8,128)(2,1)S(1)} collective-permute-done((bf16[16,64,128]{2,1,0:T(8,128)(2,1)S(1)}, bf16[16,64,128]{2,1,0:T(8,128)(2,1)S(1)}, u32[]{:S(2)}, u32[]{:S(2)}) %collective-permute-start.25) | collective-permute-done | bytes 262176 | tf_op jit(solution)/shard_map/ppermute | solution.py:63
  93.1 4.6 %collective-permute-done.24 = bf16[16,64,128]{2,1,0:T(8,128)(2,1)S(1)} collective-permute-done((bf16[16,64,128]{2,1,0:T(8,128)(2,1)S(1)}, bf16[16,64,128]{2,1,0:T(8,128)(2,1)S(1)}, u32[]{:S(2)}, u32[]{:S(2)}) %collective-permute-start.24) | collective-permute-done | bytes 262176 | tf_op jit(solution)/shard_map/ppermute | solution.py:63
  97.7 0.1 collective-permute-done.31
  97.8 1.2 %fusion.4 = f32[1,16,64,128]{3,2,1,0:T(8,128)} fusion(bf16[16,64,128]{2,1,0:T(8,128)(2,1)S(1)} %collective-permute-done.31, bf16[16,64,128]{2,1,0:T(8,128)(2,1)S(1)} %collective-permute-done.29, bf16[16,64,128]{2,1,0:T(8,128)(2,1)S(1)} %collective-permute-done.25, bf16[16,64,128]{2,1,0:T(8,128)(2,1)S(1)} %collective-permute-done.24, ...), kind=kLoop, calls=%fused_computation.7 | loop fusion | flops 2359296 | bytes 2883584 | tf_op jit(solution)/shard_map/neg | solution.py:333
  (33 shorter events, 0.2 us)
Async XLA Ops:
  0.0 33.1 %copy-start.3 = (bf16[128,128]{1,0:T(8,128)(2,1)S(1)}, bf16[128,128]{1,0:T(8,128)(2,1)}, u32[]{:S(2)}) copy-start(bf16[128,128]{1,0:T(8,128)(2,1)} %constant.42.clone.lf_ref) | copy-start | bytes 98308
  0.0 33.1 %copy-start.4 = (bf16[128,128]{1,0:T(8,128)(2,1)S(1)}, bf16[128,128]{1,0:T(8,128)(2,1)}, u32[]{:S(2)}) copy-start(bf16[128,128]{1,0:T(8,128)(2,1)} %constant.43.clone.li_ref) | copy-start | bytes 98308
  0.0 33.1 %copy-start.1 = (bf16[256,256]{1,0:T(8,128)(2,1)S(1)}, bf16[256,256]{1,0:T(8,128)(2,1)}, u32[]{:S(2)}) copy-start(bf16[256,256]{1,0:T(8,128)(2,1)} %constant.44.clone.rf_ref) | copy-start | bytes 393220
  0.0 33.1 %copy-start.2 = (bf16[256,256]{1,0:T(8,128)(2,1)S(1)}, bf16[256,256]{1,0:T(8,128)(2,1)}, u32[]{:S(2)}) copy-start(bf16[256,256]{1,0:T(8,128)(2,1)} %constant.45.clone.ri_ref) | copy-start | bytes 393220
  0.0 21.0 %copy-start = (bf16[1,16,64,128]{3,2,1,0:T(8,128)(2,1)S(1)}, bf16[1,16,64,128]{3,2,1,0:T(8,128)(2,1)}, u32[]{:S(2)}) copy-start(bf16[1,16,64,128]{3,2,1,0:T(8,128)(2,1)} %param.10) | copy-start | bytes 786436
  0.0 12.8 %collective-permute-start = (bf16[16,64,128]{2,1,0:T(8,128)(2,1)}, bf16[16,64,128]{2,1,0:T(8,128)(2,1)S(1)}, u32[]{:S(2)}, u32[]{:S(2)}) collective-permute-start(bf16[16,64,128]{2,1,0:T(8,128)(2,1)} %bitcast.50), channel_id=1, source_target_pairs={{4,0},{5,1},{6,2},{7,3},{0,4},{1,5},{2,6},{3,7},{12,8},{13,9},{14,... | collective-permute-start | bytes 786440 | tf_op jit(solution)/shard_map/ppermute | solution.py:63
  0.6 14.8 %collective-permute-start.2 = (bf16[16,64,128]{2,1,0:T(8,128)(2,1)}, bf16[16,64,128]{2,1,0:T(8,128)(2,1)S(1)}, u32[]{:S(2)}, u32[]{:S(2)}) collective-permute-start(bf16[16,64,128]{2,1,0:T(8,128)(2,1)} %bitcast.51), channel_id=1, source_target_pairs={{6,0},{7,1},{4,2},{5,3},{2,4},{3,5},{0,6},{1,7},{14,8},{15,9},{12,... | collective-permute-start | bytes 786440 | tf_op jit(solution)/shard_map/ppermute | solution.py:63
  3.5 25.8 %collective-permute-start.4 = (bf16[64,64,128]{2,1,0:T(8,128)(2,1)}, bf16[64,64,128]{2,1,0:T(8,128)(2,1)S(1)}, u32[]{:S(2)}, u32[]{:S(2)}) collective-permute-start(bf16[64,64,128]{2,1,0:T(8,128)(2,1)} %bitcast.59), channel_id=1, source_target_pairs={{1,0},{66,1},{51,2},{76,3},{5,4},{70,5},{55,6},{72,7},{9,8},{74,9}... | collective-permute-start | bytes 3145736 | tf_op jit(solution)/shard_map/ppermute | solution.py:63
  5.8 25.4 %collective-permute-start.5 = (bf16[64,64,128]{2,1,0:T(8,128)(2,1)}, bf16[64,64,128]{2,1,0:T(8,128)(2,1)S(1)}, u32[]{:S(2)}, u32[]{:S(2)}) collective-permute-start(bf16[64,64,128]{2,1,0:T(8,128)(2,1)} %bitcast.60), channel_id=1, source_target_pairs={{61,0},{126,1},{15,2},{112,3},{57,4},{122,5},{11,6},{116,7},{53,8}... | collective-permute-start | bytes 3145736 | tf_op jit(solution)/shard_map/ppermute | solution.py:63
  8.4 7.1 %collective-permute-start.6 = (bf16[16,64,128]{2,1,0:T(8,128)(2,1)}, bf16[16,64,128]{2,1,0:T(8,128)(2,1)S(1)}, u32[]{:S(2)}, u32[]{:S(2)}) collective-permute-start(bf16[16,64,128]{2,1,0:T(8,128)(2,1)} %bitcast.52), channel_id=1, source_target_pairs={{16,0},{17,1},{18,2},{19,3},{20,4},{21,5},{22,6},{23,7},{24,8},{25... | collective-permute-start | bytes 786440 | tf_op jit(solution)/shard_map/ppermute | solution.py:63
  12.9 8.1 %collective-permute-start.8 = (bf16[16,64,128]{2,1,0:T(8,128)(2,1)}, bf16[16,64,128]{2,1,0:T(8,128)(2,1)S(1)}, u32[]{:S(2)}, u32[]{:S(2)}) collective-permute-start(bf16[16,64,128]{2,1,0:T(8,128)(2,1)} %bitcast.53), channel_id=1, source_target_pairs={{18,0},{19,1},{16,2},{17,3},{22,4},{23,5},{20,6},{21,7},{26,8},{27... | collective-permute-start | bytes 786440 | tf_op jit(solution)/shard_map/ppermute | solution.py:63
  15.5 7.5 %collective-permute-start.1 = (bf16[16,64,128]{2,1,0:T(8,128)(2,1)S(1)}, bf16[16,64,128]{2,1,0:T(8,128)(2,1)S(1)}, u32[]{:S(2)}, u32[]{:S(2)}) collective-permute-start(bf16[16,64,128]{2,1,0:T(8,128)(2,1)S(1)} %collective-permute-done.t0), channel_id=1, source_target_pairs={{1,0},{0,1},{3,2},{2,3},{5,4},{4,5},{7,6},{6,7},{9,8},{8,9},{11,10... | collective-permute-start | bytes 786440 | tf_op jit(solution)/shard_map/ppermute | solution.py:63
  15.5 9.0 %collective-permute-start.3 = (bf16[16,64,128]{2,1,0:T(8,128)(2,1)S(1)}, bf16[16,64,128]{2,1,0:T(8,128)(2,1)S(1)}, u32[]{:S(2)}, u32[]{:S(2)}) collective-permute-start(bf16[16,64,128]{2,1,0:T(8,128)(2,1)S(1)} %collective-permute-done.2.t2), channel_id=1, source_target_pairs={{1,0},{0,1},{3,2},{2,3},{5,4},{4,5},{7,6},{6,7},{9,8},{8,9},{11,10... | collective-permute-start | bytes 786440 | tf_op jit(solution)/shard_map/ppermute | solution.py:63
  21.0 26.8 %collective-permute-start.14 = (bf16[16,64,128]{2,1,0:T(8,128)(2,1)S(1)}, bf16[16,64,128]{2,1,0:T(8,128)(2,1)S(1)}, u32[]{:S(2)}, u32[]{:S(2)}) collective-permute-start(bf16[16,64,128]{2,1,0:T(8,128)(2,1)S(1)} %bitcast.54), channel_id=1, source_target_pairs={{20,0},{21,1},{22,2},{23,3},{16,4},{17,5},{18,6},{19,7},{28,8},{29... | collective-permute-start | bytes 786440 | tf_op jit(solution)/shard_map/ppermute | solution.py:63
  23.0 24.8 %collective-permute-start.15 = (bf16[16,64,128]{2,1,0:T(8,128)(2,1)S(1)}, bf16[16,64,128]{2,1,0:T(8,128)(2,1)S(1)}, u32[]{:S(2)}, u32[]{:S(2)}) collective-permute-start(bf16[16,64,128]{2,1,0:T(8,128)(2,1)S(1)} %bitcast.55), channel_id=1, source_target_pairs={{22,0},{23,1},{20,2},{21,3},{18,4},{19,5},{16,6},{17,7},{30,8},{31... | collective-permute-start | bytes 786440 | tf_op jit(solution)/shard_map/ppermute | solution.py:63
  24.4 33.0 %collective-permute-start.26 = (bf16[16,64,128]{2,1,0:T(8,128)(2,1)S(1)}, bf16[16,64,128]{2,1,0:T(8,128)(2,1)S(1)}, u32[]{:S(2)}, u32[]{:S(2)}) collective-permute-start(bf16[16,64,128]{2,1,0:T(8,128)(2,1)S(1)} %bitcast.56), channel_id=1, source_target_pairs={{2,0},{3,1},{0,2},{1,3},{6,4},{7,5},{4,6},{5,7},{10,8},{11,9},{8,1... | collective-permute-start | bytes 786440 | tf_op jit(solution)/shard_map/ppermute | solution.py:63
  29.3 10.9 %collective-permute-start.7 = (bf16[16,64,128]{2,1,0:T(8,128)(2,1)S(1)}, bf16[16,64,128]{2,1,0:T(8,128)(2,1)S(1)}, u32[]{:S(2)}, u32[]{:S(2)}) collective-permute-start(bf16[16,64,128]{2,1,0:T(8,128)(2,1)S(1)} %collective-permute-done.6.t0), channel_id=1, source_target_pairs={{1,0},{0,1},{3,2},{2,3},{5,4},{4,5},{7,6},{6,7},{9,8},{8,9},{11,10... | collective-permute-start | bytes 786440 | tf_op jit(solution)/shard_map/ppermute | solution.py:63
  31.3 9.0 %collective-permute-start.9 = (bf16[16,64,128]{2,1,0:T(8,128)(2,1)S(1)}, bf16[16,64,128]{2,1,0:T(8,128)(2,1)S(1)}, u32[]{:S(2)}, u32[]{:S(2)}) collective-permute-start(bf16[16,64,128]{2,1,0:T(8,128)(2,1)S(1)} %collective-permute-done.8.t2), channel_id=1, source_target_pairs={{1,0},{0,1},{3,2},{2,3},{5,4},{4,5},{7,6},{6,7},{9,8},{8,9},{11,10... | collective-permute-start | bytes 786440 | tf_op jit(solution)/shard_map/ppermute | solution.py:63
  40.2 8.3 %collective-permute-start.11 = (bf16[16,64,128]{2,1,0:T(8,128)(2,1)S(1)}, bf16[16,64,128]{2,1,0:T(8,128)(2,1)S(1)}, u32[]{:S(2)}, u32[]{:S(2)}) collective-permute-start(bf16[16,64,128]{2,1,0:T(8,128)(2,1)S(1)} %get-tuple-element.57), channel_id=1, source_target_pairs={{1,0},{0,1},{3,2},{2,3},{5,4},{4,5},{7,6},{6,7},{9,8},{8,9},{11,10... | collective-permute-start | bytes 786440 | tf_op jit(solution)/shard_map/ppermute | solution.py:63
  40.3 8.3 %collective-permute-start.10 = (bf16[16,64,128]{2,1,0:T(8,128)(2,1)S(1)}, bf16[16,64,128]{2,1,0:T(8,128)(2,1)S(1)}, u32[]{:S(2)}, u32[]{:S(2)}) collective-permute-start(bf16[16,64,128]{2,1,0:T(8,128)(2,1)S(1)} %get-tuple-element.58), channel_id=1, source_target_pairs={{1,0},{0,1},{3,2},{2,3},{5,4},{4,5},{7,6},{6,7},{9,8},{8,9},{11,10... | collective-permute-start | bytes 786440 | tf_op jit(solution)/shard_map/ppermute | solution.py:63
  47.8 1.6 %collective-permute-start.16 = (bf16[16,64,128]{2,1,0:T(8,128)(2,1)S(1)}, bf16[16,64,128]{2,1,0:T(8,128)(2,1)S(1)}, u32[]{:S(2)}, u32[]{:S(2)}) collective-permute-start(bf16[16,64,128]{2,1,0:T(8,128)(2,1)S(1)} %collective-permute-done.14.t0), channel_id=1, source_target_pairs={{1,0},{0,1},{3,2},{2,3},{5,4},{4,5},{7,6},{6,7},{9,8},{8,9},{11,10... | collective-permute-start | bytes 786440 | tf_op jit(solution)/shard_map/ppermute | solution.py:63
  48.0 1.8 %collective-permute-start.17 = (bf16[16,64,128]{2,1,0:T(8,128)(2,1)S(1)}, bf16[16,64,128]{2,1,0:T(8,128)(2,1)S(1)}, u32[]{:S(2)}, u32[]{:S(2)}) collective-permute-start(bf16[16,64,128]{2,1,0:T(8,128)(2,1)S(1)} %collective-permute-done.15.t2), channel_id=1, source_target_pairs={{1,0},{0,1},{3,2},{2,3},{5,4},{4,5},{7,6},{6,7},{9,8},{8,9},{11,10... | collective-permute-start | bytes 786440 | tf_op jit(solution)/shard_map/ppermute | solution.py:63
  48.5 9.1 %collective-permute-start.19 = (bf16[16,64,128]{2,1,0:T(8,128)(2,1)S(1)}, bf16[16,64,128]{2,1,0:T(8,128)(2,1)S(1)}, u32[]{:S(2)}, u32[]{:S(2)}) collective-permute-start(bf16[16,64,128]{2,1,0:T(8,128)(2,1)S(1)} %get-tuple-element.53), channel_id=1, source_target_pairs={{1,0},{0,1},{3,2},{2,3},{5,4},{4,5},{7,6},{6,7},{9,8},{8,9},{11,10... | collective-permute-start | bytes 786440 | tf_op jit(solution)/shard_map/ppermute | solution.py:63
  48.7 9.3 %collective-permute-start.18 = (bf16[16,64,128]{2,1,0:T(8,128)(2,1)S(1)}, bf16[16,64,128]{2,1,0:T(8,128)(2,1)S(1)}, u32[]{:S(2)}, u32[]{:S(2)}) collective-permute-start(bf16[16,64,128]{2,1,0:T(8,128)(2,1)S(1)} %get-tuple-element.54), channel_id=1, source_target_pairs={{1,0},{0,1},{3,2},{2,3},{5,4},{4,5},{7,6},{6,7},{9,8},{8,9},{11,10... | collective-permute-start | bytes 786440 | tf_op jit(solution)/shard_map/ppermute | solution.py:63
  56.9 1.6 %collective-permute-start.23 = (bf16[16,64,128]{2,1,0:T(8,128)(2,1)S(1)}, bf16[16,64,128]{2,1,0:T(8,128)(2,1)S(1)}, u32[]{:S(2)}, u32[]{:S(2)}) collective-permute-start(bf16[16,64,128]{2,1,0:T(8,128)(2,1)S(1)} %get-tuple-element.49), channel_id=1, source_target_pairs={{1,0},{0,1},{3,2},{2,3},{5,4},{4,5},{7,6},{6,7},{9,8},{8,9},{11,10... | collective-permute-start | bytes 786440 | tf_op jit(solution)/shard_map/ppermute | solution.py:63
  57.1 1.8 %collective-permute-start.22 = (bf16[16,64,128]{2,1,0:T(8,128)(2,1)S(1)}, bf16[16,64,128]{2,1,0:T(8,128)(2,1)S(1)}, u32[]{:S(2)}, u32[]{:S(2)}) collective-permute-start(bf16[16,64,128]{2,1,0:T(8,128)(2,1)S(1)} %get-tuple-element.50), channel_id=1, source_target_pairs={{1,0},{0,1},{3,2},{2,3},{5,4},{4,5},{7,6},{6,7},{9,8},{8,9},{11,10... | collective-permute-start | bytes 786440 | tf_op jit(solution)/shard_map/ppermute | solution.py:63
  57.5 1.8 %collective-permute-start.27 = (bf16[16,64,128]{2,1,0:T(8,128)(2,1)S(1)}, bf16[16,64,128]{2,1,0:T(8,128)(2,1)S(1)}, u32[]{:S(2)}, u32[]{:S(2)}) collective-permute-start(bf16[16,64,128]{2,1,0:T(8,128)(2,1)S(1)} %bitcast.57), channel_id=1, source_target_pairs={{1,0},{0,1},{3,2},{2,3},{5,4},{4,5},{7,6},{6,7},{9,8},{8,9},{11,10... | collective-permute-start | bytes 786440 | tf_op jit(solution)/shard_map/ppermute | solution.py:63
  57.6 2.0 %collective-permute-start.28 = (bf16[16,64,128]{2,1,0:T(8,128)(2,1)S(1)}, bf16[16,64,128]{2,1,0:T(8,128)(2,1)S(1)}, u32[]{:S(2)}, u32[]{:S(2)}) collective-permute-start(bf16[16,64,128]{2,1,0:T(8,128)(2,1)S(1)} %collective-permute-done.26.t2), channel_id=1, source_target_pairs={{1,0},{0,1},{3,2},{2,3},{5,4},{4,5},{7,6},{6,7},{9,8},{8,9},{11,10... | collective-permute-start | bytes 786440 | tf_op jit(solution)/shard_map/ppermute | solution.py:63
  66.7 5.2 %collective-permute-start.30 = (bf16[16,64,128]{2,1,0:T(8,128)(2,1)S(1)}, bf16[16,64,128]{2,1,0:T(8,128)(2,1)S(1)}, u32[]{:S(2)}, u32[]{:S(2)}) collective-permute-start(bf16[16,64,128]{2,1,0:T(8,128)(2,1)S(1)} %get-tuple-element.46), channel_id=1, source_target_pairs={{1,0},{0,1},{3,2},{2,3},{5,4},{4,5},{7,6},{6,7},{9,8},{8,9},{11,10... | collective-permute-start | bytes 786440 | tf_op jit(solution)/shard_map/ppermute | solution.py:63
  66.9 13.6 %collective-permute-start.21 = (bf16[16,64,128]{2,1,0:T(8,128)(2,1)S(1)}, bf16[16,64,128]{2,1,0:T(8,128)(2,1)S(1)}, u32[]{:S(2)}, u32[]{:S(2)}) collective-permute-start(bf16[16,64,128]{2,1,0:T(8,128)(2,1)S(1)} %get-tuple-element.36), channel_id=1, source_target_pairs={{18,0},{19,1},{16,2},{17,3},{22,4},{23,5},{20,6},{21,7},{26,8},{27... | collective-permute-start | bytes 786440 | tf_op jit(solution)/shard_map/ppermute | solution.py:63
  66.9 14.9 %collective-permute-start.20 = (bf16[16,64,128]{2,1,0:T(8,128)(2,1)S(1)}, bf16[16,64,128]{2,1,0:T(8,128)(2,1)S(1)}, u32[]{:S(2)}, u32[]{:S(2)}) collective-permute-start(bf16[16,64,128]{2,1,0:T(8,128)(2,1)S(1)} %get-tuple-element.35), channel_id=1, source_target_pairs={{16,0},{17,1},{18,2},{19,3},{20,4},{21,5},{22,6},{23,7},{24,8},{25... | collective-permute-start | bytes 786440 | tf_op jit(solution)/shard_map/ppermute | solution.py:63
  67.8 16.7 %collective-permute-start.13 = (bf16[16,64,128]{2,1,0:T(8,128)(2,1)S(1)}, bf16[16,64,128]{2,1,0:T(8,128)(2,1)S(1)}, u32[]{:S(2)}, u32[]{:S(2)}) collective-permute-start(bf16[16,64,128]{2,1,0:T(8,128)(2,1)S(1)} %get-tuple-element.29), channel_id=1, source_target_pairs={{6,0},{7,1},{4,2},{5,3},{2,4},{3,5},{0,6},{1,7},{14,8},{15,9},{12,... | collective-permute-start | bytes 786440 | tf_op jit(solution)/shard_map/ppermute | solution.py:63
  71.6 16.0 %collective-permute-start.12 = (bf16[16,64,128]{2,1,0:T(8,128)(2,1)S(1)}, bf16[16,64,128]{2,1,0:T(8,128)(2,1)S(1)}, u32[]{:S(2)}, u32[]{:S(2)}) collective-permute-start(bf16[16,64,128]{2,1,0:T(8,128)(2,1)S(1)} %get-tuple-element.28), channel_id=1, source_target_pairs={{4,0},{5,1},{6,2},{7,3},{0,4},{1,5},{2,6},{3,7},{12,8},{13,9},{14,... | collective-permute-start | bytes 786440 | tf_op jit(solution)/shard_map/ppermute | solution.py:63
  71.9 15.7 %collective-permute-start.29 = (bf16[16,64,128]{2,1,0:T(8,128)(2,1)S(1)}, bf16[16,64,128]{2,1,0:T(8,128)(2,1)S(1)}, u32[]{:S(2)}, u32[]{:S(2)}) collective-permute-start(bf16[16,64,128]{2,1,0:T(8,128)(2,1)S(1)} %get-tuple-element.45), channel_id=1, source_target_pairs={{1,0},{0,1},{3,2},{2,3},{5,4},{4,5},{7,6},{6,7},{9,8},{8,9},{11,10... | collective-permute-start | bytes 786440 | tf_op jit(solution)/shard_map/ppermute | solution.py:63
  80.5 12.6 %collective-permute-start.25 = (bf16[16,64,128]{2,1,0:T(8,128)(2,1)S(1)}, bf16[16,64,128]{2,1,0:T(8,128)(2,1)S(1)}, u32[]{:S(2)}, u32[]{:S(2)}) collective-permute-start(bf16[16,64,128]{2,1,0:T(8,128)(2,1)S(1)} %get-tuple-element.40), channel_id=1, source_target_pairs={{22,0},{23,1},{20,2},{21,3},{18,4},{19,5},{16,6},{17,7},{30,8},{31... | collective-permute-start | bytes 786440 | tf_op jit(solution)/shard_map/ppermute | solution.py:63
  81.8 15.9 %collective-permute-start.24 = (bf16[16,64,128]{2,1,0:T(8,128)(2,1)S(1)}, bf16[16,64,128]{2,1,0:T(8,128)(2,1)S(1)}, u32[]{:S(2)}, u32[]{:S(2)}) collective-permute-start(bf16[16,64,128]{2,1,0:T(8,128)(2,1)S(1)} %get-tuple-element.39), channel_id=1, source_target_pairs={{20,0},{21,1},{22,2},{23,3},{16,4},{17,5},{18,6},{19,7},{28,8},{29... | collective-permute-start | bytes 786440 | tf_op jit(solution)/shard_map/ppermute | solution.py:63
  84.5 13.2 %collective-permute-start.31 = (bf16[16,64,128]{2,1,0:T(8,128)(2,1)S(1)}, bf16[16,64,128]{2,1,0:T(8,128)(2,1)S(1)}, u32[]{:S(2)}, u32[]{:S(2)}) collective-permute-start(bf16[16,64,128]{2,1,0:T(8,128)(2,1)S(1)} %fusion), channel_id=1, source_target_pairs={{2,0},{3,1},{0,2},{1,3},{6,4},{7,5},{4,6},{5,7},{10,8},{11,9},{8,1... | collective-permute-start | bytes 786440 | tf_op jit(solution)/shard_map/ppermute | solution.py:63

commit v2 on v1

--- a/solution.py
+++ b/solution.py
@@ -111,11 +111,21 @@
     return (coulomb_scale / (wave_sq + screen_wave * screen_wave)) * weight[None, None, :]
 
 
-def pair_kernel(
-    place_ref, t0, t1, t2, t3, pa, pb, coulomb, lf_ref, li_ref, rf_ref, ri_ref,
-    out,
-    t_v, a_v, b_v, k_v, s_ref, z_ref, y_ref, o_v, in_sem, k_sem, out_sem,
-):
+def pair_kernel(two_targets, stage, *refs):
+    refs = list(refs)
+    take = lambda count: [refs.pop(0) for _ in range(count)]
+    (place_ref,) = take(1)
+    if two_targets:
+        targets = [take(4), take(4)]
+        (shared,) = take(1)
+    else:
+        shared = take(4)
+        partners = take(2)
+    coulomb, lf_ref, li_ref, rf_ref, ri_ref = take(5)
+    earlier = take(2) if stage == "last" else []
+    outs = take(2 if two_targets else 1)
+    x_v, a_v, b_v, k_v, s_ref, z_ref, y_ref, o_v, e_v, in_sem, k_sem, e_sem, out_sem = refs
+
     dot = functools.partial(jnp.dot, preferred_element_type=f32)
     place = place_ref[0]
     rows = quarter * points
@@ -124,19 +134,27 @@
     def block_of(step):
         return place ^ step
 
-    def fetches(step, t_ref):
+    def fetches(step, n):
         planes = pl.ds(block_of(step) * quarter, quarter)
+        if two_targets:
+            sources = [shared.at[planes], targets[0][n], targets[1][n]]
+        else:
+            sources = [shared[n], partners[0].at[planes], partners[1].at[planes]]
         return [
-            pltpu.make_async_copy(t_ref, t_v.at[step], in_sem.at[step, 0]),
-            pltpu.make_async_copy(pa.at[planes], a_v.at[step], in_sem.at[step, 1]),
-            pltpu.make_async_copy(pb.at[planes], b_v.at[step], in_sem.at[step, 2]),
+            pltpu.make_async_copy(source, v.at[step], in_sem.at[step, i])
+            for i, (source, v) in enumerate(zip(sources, (x_v, a_v, b_v)))
         ]
 
-    for step, t_ref in enumerate((t0, t1, t2, t3)):
-        for copy in fetches(step, t_ref):
+    for step in range(4):
+        for copy in fetches(step, step):
             copy.start()
     k_copy = pltpu.make_async_copy(coulomb, k_v, k_sem)
     k_copy.start()
+    e_copies = [
+        pltpu.make_async_copy(source, e_v.at[i], e_sem.at[i]) for i, source in enumerate(earlier)
+    ]
+    for copy in e_copies:
+        copy.start()
     lf = lf_ref[...]
     li = li_ref[...]
 
@@ -145,6 +163,9 @@
 
     def swap(v):
         return pltpu.roll(v, points, 1)
+
+    def planes_of(v):
+        return v.reshape(quarter, points, lanes)
 
     def last_section(field, matrix):
         part = rows // splits
@@ -152,20 +173,22 @@
         return jnp.concatenate(parts, axis=0)
 
     def arrive(step):
-        for copy in fetches(step, t0):
+        for copy in fetches(step, 0):
             copy.wait()
 
     def forward_z(step):
-        t = load(t_v, step)
-        swapped = swap(t)
-        t_real = jnp.where(low, t, swapped)
-        t_imag = jnp.where(low, swapped, t)
+        x = load(x_v, step)
+        swapped = swap(x)
+        x_real = jnp.where(low, x, swapped)
+        x_imag = jnp.where(low, swapped, x)
         a = load(a_v, step)
         b = load(b_v, step)
-        p_real = jnp.where(low, a, swap(b))
-        p_imag = jnp.where(low, swap(a), b)
-        a_v[step] = p_real.reshape(quarter, points, lanes)
-        b_v[step] = p_imag.reshape(quarter, points, lanes)
+        q_real = jnp.where(low, a, swap(b))
+        q_imag = jnp.where(low, swap(a), b)
+        p_real, p_imag = (x_real, x_imag) if two_targets else (q_real, q_imag)
+        t_real, t_imag = (q_real, q_imag) if two_targets else (x_real, x_imag)
+        a_v[step] = planes_of(p_real)
+        b_v[step] = planes_of(p_imag)
         density = jnp.concatenate(
             [p_real * t_real + p_imag * t_imag, p_real * t_imag - p_imag * t_real], axis=1
         )
@@ -217,9 +240,14 @@
         return carry
 
     lax.fori_loop(0, 4, middle, 0)
+    for copy in e_copies:
+        copy.wait()
 
     def put(step):
-        return pltpu.make_async_copy(o_v.at[step], out.at[step], out_sem.at[step])
+        return [
+            pltpu.make_async_copy(o_v.at[i, step], out.at[step], out_sem.at[i, step])
+            for i, out in enumerate(outs)
+        ]
 
     def inverse_y(step):
         slot = step % 2
@@ -242,33 +270,49 @@
         p_imag = load(b_v, step)
         real = v_real * p_real - v_imag * p_imag
         imag = v_real * p_imag + v_imag * p_real
-        total = jnp.where(low, real, imag) + swap(jnp.where(low, imag, real))
-        o_v[step] = total.reshape(quarter, points, lanes)
+        if stage == "first":
+            results = [real, imag]
+        elif stage == "last":
+            real = real + e_v[0, step].reshape(rows, lanes)
+            imag = imag + e_v[1, step].reshape(rows, lanes)
+            results = [jnp.where(low, real, swap(imag)), jnp.where(low, swap(real), imag)]
+        else:
+            results = [jnp.where(low, real, imag) + swap(jnp.where(low, imag, real))]
+        for i, result in enumerate(results):
+            o_v[i, step] = planes_of(result)
 
     def inverse(step, carry):
         inverse_z(step)
         inverse_y(step + 1)
-        put(step).start()
+        for copy in put(step):
+            copy.start()
         return carry
 
     inverse_y(0)
     lax.fori_loop(0, 3, inverse, 0)
     inverse_z(3)
-    put(3).start()
+    for copy in put(3):
+        copy.start()
     for step in range(4):
-        put(step).wait()
-
-
-def exchange_part(place, pieces, first, second, coulomb, matrices):
+        for copy in put(step):
+            copy.wait()
+
+
+def exchange_part(place, sides, coulomb, matrices, two_targets=False, stage="only", earlier=()):
     anywhere = pl.BlockSpec(memory_space=pl.ANY)
     scalar = pl.BlockSpec(memory_space=pltpu.SMEM)
     near = pl.BlockSpec(memory_space=pltpu.VMEM)
     planes = (4, quarter, points, lanes)
+    both = (2, *planes)
+    outs = 2 if two_targets else 1
     return pl.pallas_call(
-        pair_kernel,
-        out_shape=jax.ShapeDtypeStruct(planes, bf16),
-        in_specs=[scalar] + [anywhere] * 7 + [near] * 4,
-        out_specs=anywhere,
+        functools.partial(pair_kernel, two_targets, stage),
+        out_shape=[jax.ShapeDtypeStruct(planes, bf16)] * outs,
+        in_specs=[scalar]
+        + [anywhere] * (len(sides) + 1)
+        + [near] * 4
+        + [anywhere] * len(earlier),
+        out_specs=[anywhere] * outs,
         scratch_shapes=[
             pltpu.VMEM(planes, bf16),
             pltpu.VMEM(planes, bf16),
@@ -277,51 +321,75 @@
             pltpu.VMEM((2 * points * pitch, lanes), f32),
             pltpu.VMEM((2, quarter, lanes, lanes), bf16),
             pltpu.VMEM((2, quarter * points, 2 * lanes), bf16),
-            pltpu.VMEM(planes, bf16),
+            pltpu.VMEM(both, bf16),
+            pltpu.VMEM(both, bf16),
             pltpu.SemaphoreType.DMA((4, 3)),
             pltpu.SemaphoreType.DMA,
-            pltpu.SemaphoreType.DMA((4,)),
+            pltpu.SemaphoreType.DMA((2,)),
+            pltpu.SemaphoreType.DMA((2, 4)),
         ],
         compiler_params=pltpu.CompilerParams(vmem_limit_bytes=40 << 20),
         cost_estimate=pl.CostEstimate(
             flops=5 * 10**9, bytes_accessed=24 * 2**20, transcendentals=0
         ),
-    )(place, *pieces, first, second, coulomb, *matrices)
+    )(place, *sides, coulomb, *matrices, *earlier)
 
 
 def body(targets, partners, occupations, slot_partner, screening):
     own = targets[0]
     partner = partners[0]
     first = receive(partner, first_source)
-    second = receive(partner, second_source)
     orders = [(0, 1), (1, 0), (1, 1), (0, 0)]
     halves = []
     for dy, dx in orders:
-        same = own if (dy, dx) == (0, 0) else receive(own, offset_source(dy, dx, 0, 0))
-        halves.append((same, receive(own, offset_source(dy, dx, 1, 0))))
+        half = []
+        for dz in range(2):
+            source = offset_source(dy, dx, dz, 0)
+            half.append(own if (dy, dx, dz) == (0, 0, 0) else receive(own, source))
+        halves.append(half)
+    second = receive(partner, second_source)
     matrices = section_matrices()
     device = lax.axis_index("tgt") * 4 + lax.axis_index("grp")
     slots = lax.dynamic_slice_in_dim(jnp.asarray(slot_table()), device, 1)[0]
     place = lax.axis_index("grp")[None].astype(jnp.int32)
-    coulomb = coulomb_kernel(screening, pair_weights(occupations, slot_partner, slots))
+    weights = pair_weights(occupations, slot_partner, slots)
     sibling = offset_source(0, 0, 0, 1)
-    sums = []
-    marks = []
-    for n, ((dy, dx), (same, other)) in enumerate(zip(orders, halves)):
-        if n >= 2:
-            _, same, other = lax.optimization_barrier((marks[n - 2], same, other))
-        pieces = [same, receive(same, sibling), other, receive(other, sibling)]
-        for m in {2: [0], 3: [1, 2]}.get(n, []):
-            place, *sums[m] = lax.optimization_barrier((place, *sums[m]))
-        part = exchange_part(place, pieces, first, second, coulomb, matrices)
-        place, part = lax.optimization_barrier((place, part))
-        marks.append(place)
+
+    def pieces(n, mark=None):
+        same, other = halves[n]
+        if mark is not None:
+            _, same, other = lax.optimization_barrier((mark, same, other))
+        return [same, receive(same, sibling), other, receive(other, sibling)]
+
+    def core_sum(part, rounded):
         both = []
         for dz in range(2):
             crossed = receive(part[2 * dz + 1], sibling)
             summed = part[2 * dz].astype(f32) + crossed.astype(f32)
-            both.append(summed if (dy, dx, dz) == (0, 0, 0) else summed.astype(bf16))
-        sums.append(both)
+            both.append(summed.astype(bf16) if rounded[dz] else summed)
+        return both
+
+    def call(place, *args, **kwargs):
+        parts = exchange_part(place, *args, **kwargs)
+        return lax.optimization_barrier((place, *parts))
+
+    two = pieces(0) + pieces(1)
+    coulombs = [
+        coulomb_kernel(screening, (weights[a], weights[b])) for a, b in ((0, 0), (1, 1), (0, 1))
+    ]
+    place, *earlier = call(
+        place, two + [first], coulombs[0], matrices, two_targets=True, stage="first"
+    )
+    mark = place
+    place, *parts = call(place, two + [second], coulombs[1], matrices, True, "last", earlier)
+    sums = [core_sum(part, (True, True)) for part in parts]
+    place, *flat = lax.optimization_barrier((place, *sums[0], *sums[1]))
+    sums = [flat[:2], flat[2:]]
+    place, part = call(place, pieces(2, mark) + [first, second], coulombs[2], matrices)
+    sums.append(core_sum(part, (True, True)))
+    place, *sums[2] = lax.optimization_barrier((place, *sums[2]))
+    place, part = call(place, pieces(3, mark) + [first, second], coulombs[2], matrices)
+    sums.append(core_sum(part, (False, True)))
     terms = []
     for (dy, dx), both in zip(orders, sums):
         for dz in range(2):

time: 101 us -> 113 us (1.12)
  the two profiles are of different devices: /device:TPU:26 before, /device:TPU:32 now
where the time goes in v2:
time: 113 us
  waiting for transfers between devices  40.8 us (36%)
  starting transfers between devices  34.5 us (31%)
  Pallas kernels  28.8 us (25%)
  other arithmetic  6.26 us (6%)
  local copies, waits for them, and re-layouts  1.53 us (1%)
    ppermute x32, waiting for transfers between devices, receive(): return lax.ppermute(value, axes, pairs)  40.8 us
    ppermute x32, starting transfers between devices, receive(): return lax.ppermute(value, axes, pairs)  34.5 us
    pallas_call x4, Pallas kernels, exchange_part(): pl.pallas_call(functools.partial(pair_kernel, two_targets, stage), out_sh...  28.8 us
  transfers between devices with their start and end apart: 32, of which 13 were waited for; matrix products, arithmetic and copies ran while one was open for 6% of the time, Pallas kernels for 19%

profile of v2, /device:TPU:32, one launch (start us, length us, event | category | flops | bytes accessed | tf_op | source)
XLA Modules:
  0.0 112.8 jit_solution(9996662400927456821)
XLA Ops:
  0.0 1.5 %collective-permute-start = (bf16[16,64,128]{2,1,0:T(8,128)(2,1)}, bf16[16,64,128]{2,1,0:T(8,128)(2,1)S(1)}, u32[]{:S(2)}, u32[]{:S(2)}) collective-permute-start(bf16[16,64,128]{2,1,0:T(8,128)(2,1)} %bitcast.50), channel_id=1, source_target_pairs={{4,0},{5,1},{6,2},{7,3},{0,4},{1,5},{2,6},{3,7},{12,8},{13,9},{14,... | collective-permute-start | bytes 786440 | tf_op jit(solution)/shard_map/ppermute | solution.py:63
  1.5 0.0 collective-permute-start.2
  1.5 1.7 %collective-permute-start.4 = (bf16[16,64,128]{2,1,0:T(8,128)(2,1)}, bf16[16,64,128]{2,1,0:T(8,128)(2,1)S(1)}, u32[]{:S(2)}, u32[]{:S(2)}) collective-permute-start(bf16[16,64,128]{2,1,0:T(8,128)(2,1)} %bitcast.52), channel_id=1, source_target_pairs={{16,0},{17,1},{18,2},{19,3},{20,4},{21,5},{22,6},{23,7},{24,8},{25... | collective-permute-start | bytes 786440 | tf_op jit(solution)/shard_map/ppermute | solution.py:63
  3.1 1.8 %collective-permute-start.6 = (bf16[16,64,128]{2,1,0:T(8,128)(2,1)}, bf16[16,64,128]{2,1,0:T(8,128)(2,1)S(1)}, u32[]{:S(2)}, u32[]{:S(2)}) collective-permute-start(bf16[16,64,128]{2,1,0:T(8,128)(2,1)} %bitcast.53), channel_id=1, source_target_pairs={{18,0},{19,1},{16,2},{17,3},{22,4},{23,5},{20,6},{21,7},{26,8},{27... | collective-permute-start | bytes 786440 | tf_op jit(solution)/shard_map/ppermute | solution.py:63
  5.0 0.2 collective-permute-start.8
  5.2 0.7 dynamic-slice_bitcast_fusion
  5.9 0.8 select_reduce_fusion
  6.7 0.2 fusion.14
  6.9 0.6 fusion.18
  7.5 1.9 %collective-permute-done.refs_1_ = bf16[16,64,128]{2,1,0:T(8,128)(2,1)S(1)} collective-permute-done((bf16[16,64,128]{2,1,0:T(8,128)(2,1)}, bf16[16,64,128]{2,1,0:T(8,128)(2,1)S(1)}, u32[]{:S(2)}, u32[]{:S(2)}) %collective-permute-start) | collective-permute-done | bytes 262176 | tf_op jit(solution)/shard_map/ppermute | solution.py:63
  9.4 1.0 collective-permute-start.1
  10.4 1.2 %compare_select_fusion.1 = f32[128]{0:T(128)S(1)} fusion(f32[]{:T(128)} %bitcast.6, f32[]{:T(128)} %bitcast.5), kind=kLoop, calls=%fused_computation.35 | loop fusion | flops 256 | bytes 520 | tf_op jit(solution)/shard_map/jit(_where)/select_n | solution.py:110
  11.6 0.1 add.139
  12.4 4.2 %collective-permute-done.2.refs_3_ = bf16[16,64,128]{2,1,0:T(8,128)(2,1)S(1)} collective-permute-done((bf16[16,64,128]{2,1,0:T(8,128)(2,1)}, bf16[16,64,128]{2,1,0:T(8,128)(2,1)S(1)}, u32[]{:S(2)}, u32[]{:S(2)}) %collective-permute-start.2) | collective-permute-done | bytes 262176 | tf_op jit(solution)/shard_map/ppermute | solution.py:63
  16.6 5.9 %collective-permute-start.9 = (bf16[64,64,128]{2,1,0:T(8,128)(2,1)}, bf16[64,64,128]{2,1,0:T(8,128)(2,1)S(1)}, u32[]{:S(2)}, u32[]{:S(2)}) collective-permute-start(bf16[64,64,128]{2,1,0:T(8,128)(2,1)} %bitcast.60), channel_id=1, source_target_pairs={{61,0},{126,1},{15,2},{112,3},{57,4},{122,5},{11,6},{116,7},{53,8}... | collective-permute-start | bytes 3145736 | tf_op jit(solution)/shard_map/ppermute | solution.py:63
  22.5 0.1 broadcast_add_fusion
  22.6 0.0 collective-permute-done.4.refs_5_
  22.6 0.1 collective-permute-start.3
  22.7 0.5 collective-permute-start.5
  23.2 0.0 collective-permute-done.1.refs_2_
  23.2 0.1 collective-permute-start.7
  23.3 0.0 copy-start.4
  23.3 2.1 %fusion = (f32[64,64,128]{2,1,0:T(8,128)S(1)}, f32[64,64,128]{2,1,0:T(8,128)S(1)}, f32[64,64,128]{2,1,0:T(8,128)S(1)}) fusion(f32[128]{0:T(128)S(1)} %compare_select_fusion.1, f32[]{:T(128)} %bitcast.3, f32[128]{0:T(128)S(1)} %add.139, f32[64,64]{1,0:T(8,128)S(1)} %broadcast_add_fusion, f32[]{:T(128)} %bitcast.6, f32[]{:T(128)} %bitcast.5), kind=kLoop, calls=%fused_computation.1 | loop fusion | flops 3145728 | bytes 6308876 | tf_op jit(solution)/shard_map/mul | solution.py:111
  25.4 0.0 collective-permute-done.3.refs_4_
  25.5 0.1 collective-permute-start.18
  25.6 4.4 %collective-permute-start.19 = (bf16[16,64,128]{2,1,0:T(8,128)(2,1)S(1)}, bf16[16,64,128]{2,1,0:T(8,128)(2,1)S(1)}, u32[]{:S(2)}, u32[]{:S(2)}) collective-permute-start(bf16[16,64,128]{2,1,0:T(8,128)(2,1)S(1)} %bitcast.55), channel_id=1, source_target_pairs={{22,0},{23,1},{20,2},{21,3},{18,4},{19,5},{16,6},{17,7},{30,8},{31... | collective-permute-start | bytes 786440 | tf_op jit(solution)/shard_map/ppermute | solution.py:63
  30.0 7.1 %shard_map.100 = (bf16[4,16,64,128]{3,2,1,0:T(8,128)(2,1)S(1)}, bf16[4,16,64,128]{3,2,1,0:T(8,128)(2,1)S(1)}) custom-call(s32[1]{0:T(128)} %bitcast.refs_0_, bf16[16,64,128]{2,1,0:T(8,128)(2,1)S(1)} %collective-permute-done.refs_1_, bf16[16,64,128]{2,1,0:T(8,128)(2,1)S(1)} %collective-permute-done.1.refs_2_, ...), custom_call_target="tpu_custom_call" | custom-call | flops 5000000000 | bytes 25165824 | tf_op jit(solution)/shard_map/pallas_call | solution.py:308
  37.1 6.0 %collective-permute-done.9.refs_9_.refs_6_ = bf16[64,64,128]{2,1,0:T(8,128)(2,1)S(1)} collective-permute-done((bf16[64,64,128]{2,1,0:T(8,128)(2,1)}, bf16[64,64,128]{2,1,0:T(8,128)(2,1)S(1)}, u32[]{:S(2)}, u32[]{:S(2)}) %collective-permute-start.9) | collective-permute-done | bytes 1048608 | tf_op jit(solution)/shard_map/ppermute | solution.py:63
  43.1 7.5 %shard_map.101 = (bf16[4,16,64,128]{3,2,1,0:T(8,128)(2,1)S(1)}, bf16[4,16,64,128]{3,2,1,0:T(8,128)(2,1)S(1)}) custom-call(s32[1]{0:T(128)} %bitcast.refs_0_, bf16[16,64,128]{2,1,0:T(8,128)(2,1)S(1)} %collective-permute-done.refs_1_, bf16[16,64,128]{2,1,0:T(8,128)(2,1)S(1)} %collective-permute-done.1.refs_2_, ...), custom_call_target="tpu_custom_call" | custom-call | flops 5000000000 | bytes 25165824 | tf_op jit(solution)/shard_map/pallas_call | solution.py:308
  50.7 4.1 %collective-permute-start.12 = (bf16[16,64,128]{2,1,0:T(8,128)(2,1)S(1)}, bf16[16,64,128]{2,1,0:T(8,128)(2,1)S(1)}, u32[]{:S(2)}, u32[]{:S(2)}) collective-permute-start(bf16[16,64,128]{2,1,0:T(8,128)(2,1)S(1)} %get-tuple-element.64), channel_id=1, source_target_pairs={{1,0},{0,1},{3,2},{2,3},{5,4},{4,5},{7,6},{6,7},{9,8},{8,9},{11,10... | collective-permute-start | bytes 786440 | tf_op jit(solution)/shard_map/ppermute | solution.py:63
  54.8 0.1 collective-permute-start.13
  55.0 0.5 collective-permute-start.10
  55.5 0.1 collective-permute-start.11
  55.6 3.1 %collective-permute-start.26 = (bf16[16,64,128]{2,1,0:T(8,128)(2,1)S(1)}, bf16[16,64,128]{2,1,0:T(8,128)(2,1)S(1)}, u32[]{:S(2)}, u32[]{:S(2)}) collective-permute-start(bf16[16,64,128]{2,1,0:T(8,128)(2,1)S(1)} %bitcast.56), channel_id=1, source_target_pairs={{2,0},{3,1},{0,2},{1,3},{6,4},{7,5},{4,6},{5,7},{10,8},{11,9},{8,1... | collective-permute-start | bytes 786440 | tf_op jit(solution)/shard_map/ppermute | solution.py:63
  58.7 0.1 collective-permute-start.20
  58.8 0.4 collective-permute-start.21
  59.2 0.2 fusion.10
  59.4 0.2 fusion.12
  59.6 0.6 collective-permute-done.20.refs_2_
  60.2 0.4 collective-permute-done.21.refs_4_
  60.6 7.1 %shard_map.102 = bf16[4,16,64,128]{3,2,1,0:T(8,128)(2,1)S(1)} custom-call(s32[1]{0:T(128)} %bitcast.refs_0_, bf16[16,64,128]{2,1,0:T(8,128)(2,1)S(1)} %collective-permute-done.18.refs_1_, bf16[16,64,128]{2,1,0:T(8,128)(2,1)S(1)} %collective-permute-done.20.refs_2_, bf16[16,64,128]{2,1,0:T(8,128)(2,1)S(1)} %collective-permute-done.19.refs_3_, ...), custom_call_target="tpu_custom_call" | custom-call | flops 5000000000 | bytes 25165824 | tf_op jit(solution)/shard_map/pallas_call | solution.py:308
  67.7 0.2 collective-permute-start.22
  67.9 0.4 collective-permute-start.23
  68.3 0.1 collective-permute-start.27
  68.5 0.4 collective-permute-start.28
  68.8 0.5 collective-permute-done.22
  69.3 0.4 collective-permute-done.23
  69.7 0.2 fusion.8
  69.9 0.2 collective-permute-done.27.refs_2_
  70.1 0.4 collective-permute-done.28.refs_4_
  70.5 7.1 %shard_map.103 = bf16[4,16,64,128]{3,2,1,0:T(8,128)(2,1)S(1)} custom-call(s32[1]{0:T(128)} %bitcast.refs_0_, bf16[16,64,128]{2,1,0:T(8,128)(2,1)S(1)} %bitcast.58, bf16[16,64,128]{2,1,0:T(8,128)(2,1)S(1)} %collective-permute-done.27.refs_2_, bf16[16,64,128]{2,1,0:T(8,128)(2,1)S(1)} %collective-permute-done.26.refs_3_, ...), custom_call_target="tpu_custom_call" | custom-call | flops 5000000000 | bytes 25165824 | tf_op jit(solution)/shard_map/pallas_call | solution.py:308
  77.6 0.2 collective-permute-start.30
  77.8 0.3 collective-permute-start.14
  78.1 1.8 %collective-permute-start.15 = (bf16[16,64,128]{2,1,0:T(8,128)(2,1)S(1)}, bf16[16,64,128]{2,1,0:T(8,128)(2,1)S(1)}, u32[]{:S(2)}, u32[]{:S(2)}) collective-permute-start(bf16[16,64,128]{2,1,0:T(8,128)(2,1)S(1)} %get-tuple-element.41), channel_id=1, source_target_pairs={{6,0},{7,1},{4,2},{5,3},{2,4},{3,5},{0,6},{1,7},{14,8},{15,9},{12,... | collective-permute-start | bytes 786440 | tf_op jit(solution)/shard_map/ppermute | solution.py:63
  79.9 0.1 collective-permute-start.16
  80.1 2.7 %collective-permute-start.17 = (bf16[16,64,128]{2,1,0:T(8,128)(2,1)S(1)}, bf16[16,64,128]{2,1,0:T(8,128)(2,1)S(1)}, u32[]{:S(2)}, u32[]{:S(2)}) collective-permute-start(bf16[16,64,128]{2,1,0:T(8,128)(2,1)S(1)} %get-tuple-element.43), channel_id=1, source_target_pairs={{18,0},{19,1},{16,2},{17,3},{22,4},{23,5},{20,6},{21,7},{26,8},{27... | collective-permute-start | bytes 786440 | tf_op jit(solution)/shard_map/ppermute | solution.py:63
  82.8 0.1 fusion.3
  82.9 4.1 %collective-permute-done.14 = bf16[16,64,128]{2,1,0:T(8,128)(2,1)S(1)} collective-permute-done((bf16[16,64,128]{2,1,0:T(8,128)(2,1)S(1)}, bf16[16,64,128]{2,1,0:T(8,128)(2,1)S(1)}, u32[]{:S(2)}, u32[]{:S(2)}) %collective-permute-start.14) | collective-permute-done | bytes 262176 | tf_op jit(solution)/shard_map/ppermute | solution.py:63
  87.0 8.2 %collective-permute-done.15 = bf16[16,64,128]{2,1,0:T(8,128)(2,1)S(1)} collective-permute-done((bf16[16,64,128]{2,1,0:T(8,128)(2,1)S(1)}, bf16[16,64,128]{2,1,0:T(8,128)(2,1)S(1)}, u32[]{:S(2)}, u32[]{:S(2)}) %collective-permute-start.15) | collective-permute-done | bytes 262176 | tf_op jit(solution)/shard_map/ppermute | solution.py:63
  95.2 2.1 %collective-permute-start.25 = (bf16[16,64,128]{2,1,0:T(8,128)(2,1)S(1)}, bf16[16,64,128]{2,1,0:T(8,128)(2,1)S(1)}, u32[]{:S(2)}, u32[]{:S(2)}) collective-permute-start(bf16[16,64,128]{2,1,0:T(8,128)(2,1)S(1)} %get-tuple-element.50), channel_id=1, source_target_pairs={{22,0},{23,1},{20,2},{21,3},{18,4},{19,5},{16,6},{17,7},{30,8},{31... | collective-permute-start | bytes 786440 | tf_op jit(solution)/shard_map/ppermute | solution.py:63
  97.2 0.5 collective-permute-start.31
  97.7 9.0 %collective-permute-done.17 = bf16[16,64,128]{2,1,0:T(8,128)(2,1)S(1)} collective-permute-done((bf16[16,64,128]{2,1,0:T(8,128)(2,1)S(1)}, bf16[16,64,128]{2,1,0:T(8,128)(2,1)S(1)}, u32[]{:S(2)}, u32[]{:S(2)}) %collective-permute-start.17) | collective-permute-done | bytes 262176 | tf_op jit(solution)/shard_map/ppermute | solution.py:63
  106.7 4.9 %collective-permute-done.31 = bf16[16,64,128]{2,1,0:T(8,128)(2,1)S(1)} collective-permute-done((bf16[16,64,128]{2,1,0:T(8,128)(2,1)S(1)}, bf16[16,64,128]{2,1,0:T(8,128)(2,1)S(1)}, u32[]{:S(2)}, u32[]{:S(2)}) %collective-permute-start.31) | collective-permute-done | bytes 262176 | tf_op jit(solution)/shard_map/ppermute | solution.py:63
  111.6 1.2 %fusion.7 = f32[1,16,64,128]{3,2,1,0:T(8,128)} fusion(bf16[16,64,128]{2,1,0:T(8,128)(2,1)S(1)} %collective-permute-done.31, bf16[16,64,128]{2,1,0:T(8,128)(2,1)S(1)} %collective-permute-done.29, bf16[16,64,128]{2,1,0:T(8,128)(2,1)S(1)} %collective-permute-done.25, bf16[16,64,128]{2,1,0:T(8,128)(2,1)S(1)} %collective-permute-done.24, ...), kind=kLoop, calls=%fused_computation.10 | loop fusion | flops 2359296 | bytes 2883584 | tf_op jit(solution)/shard_map/neg | solution.py:401
  (33 shorter events, 0.2 us)
Async XLA Ops:
  0.0 9.4 %collective-permute-start = (bf16[16,64,128]{2,1,0:T(8,128)(2,1)}, bf16[16,64,128]{2,1,0:T(8,128)(2,1)S(1)}, u32[]{:S(2)}, u32[]{:S(2)}) collective-permute-start(bf16[16,64,128]{2,1,0:T(8,128)(2,1)} %bitcast.50), channel_id=1, source_target_pairs={{4,0},{5,1},{6,2},{7,3},{0,4},{1,5},{2,6},{3,7},{12,8},{13,9},{14,... | collective-permute-start | bytes 786440 | tf_op jit(solution)/shard_map/ppermute | solution.py:63
  1.5 15.1 %collective-permute-start.2 = (bf16[16,64,128]{2,1,0:T(8,128)(2,1)}, bf16[16,64,128]{2,1,0:T(8,128)(2,1)S(1)}, u32[]{:S(2)}, u32[]{:S(2)}) collective-permute-start(bf16[16,64,128]{2,1,0:T(8,128)(2,1)} %bitcast.51), channel_id=1, source_target_pairs={{6,0},{7,1},{4,2},{5,3},{2,4},{3,5},{0,6},{1,7},{14,8},{15,9},{12,... | collective-permute-start | bytes 786440 | tf_op jit(solution)/shard_map/ppermute | solution.py:63
  1.5 21.1 %collective-permute-start.4 = (bf16[16,64,128]{2,1,0:T(8,128)(2,1)}, bf16[16,64,128]{2,1,0:T(8,128)(2,1)S(1)}, u32[]{:S(2)}, u32[]{:S(2)}) collective-permute-start(bf16[16,64,128]{2,1,0:T(8,128)(2,1)} %bitcast.52), channel_id=1, source_target_pairs={{16,0},{17,1},{18,2},{19,3},{20,4},{21,5},{22,6},{23,7},{24,8},{25... | collective-permute-start | bytes 786440 | tf_op jit(solution)/shard_map/ppermute | solution.py:63
  3.1 19.5 %collective-permute-start.6 = (bf16[16,64,128]{2,1,0:T(8,128)(2,1)}, bf16[16,64,128]{2,1,0:T(8,128)(2,1)S(1)}, u32[]{:S(2)}, u32[]{:S(2)}) collective-permute-start(bf16[16,64,128]{2,1,0:T(8,128)(2,1)} %bitcast.53), channel_id=1, source_target_pairs={{18,0},{19,1},{16,2},{17,3},{22,4},{23,5},{20,6},{21,7},{26,8},{27... | collective-permute-start | bytes 786440 | tf_op jit(solution)/shard_map/ppermute | solution.py:63
  5.0 25.0 %collective-permute-start.8 = (bf16[64,64,128]{2,1,0:T(8,128)(2,1)}, bf16[64,64,128]{2,1,0:T(8,128)(2,1)S(1)}, u32[]{:S(2)}, u32[]{:S(2)}) collective-permute-start(bf16[64,64,128]{2,1,0:T(8,128)(2,1)} %bitcast.59), channel_id=1, source_target_pairs={{1,0},{66,1},{51,2},{76,3},{5,4},{70,5},{55,6},{72,7},{9,8},{74,9}... | collective-permute-start | bytes 3145736 | tf_op jit(solution)/shard_map/ppermute | solution.py:63
  9.4 13.8 %collective-permute-start.1 = (bf16[16,64,128]{2,1,0:T(8,128)(2,1)S(1)}, bf16[16,64,128]{2,1,0:T(8,128)(2,1)S(1)}, u32[]{:S(2)}, u32[]{:S(2)}) collective-permute-start(bf16[16,64,128]{2,1,0:T(8,128)(2,1)S(1)} %collective-permute-done.refs_1_), channel_id=1, source_target_pairs={{1,0},{0,1},{3,2},{2,3},{5,4},{4,5},{7,6},{6,7},{9,8},{8,9},{11,10... | collective-permute-start | bytes 786440 | tf_op jit(solution)/shard_map/ppermute | solution.py:63
  16.6 26.6 %collective-permute-start.9 = (bf16[64,64,128]{2,1,0:T(8,128)(2,1)}, bf16[64,64,128]{2,1,0:T(8,128)(2,1)S(1)}, u32[]{:S(2)}, u32[]{:S(2)}) collective-permute-start(bf16[64,64,128]{2,1,0:T(8,128)(2,1)} %bitcast.60), channel_id=1, source_target_pairs={{61,0},{126,1},{15,2},{112,3},{57,4},{122,5},{11,6},{116,7},{53,8}... | collective-permute-start | bytes 3145736 | tf_op jit(solution)/shard_map/ppermute | solution.py:63
  22.6 2.9 %collective-permute-start.3 = (bf16[16,64,128]{2,1,0:T(8,128)(2,1)S(1)}, bf16[16,64,128]{2,1,0:T(8,128)(2,1)S(1)}, u32[]{:S(2)}, u32[]{:S(2)}) collective-permute-start(bf16[16,64,128]{2,1,0:T(8,128)(2,1)S(1)} %collective-permute-done.2.refs_3_), channel_id=1, source_target_pairs={{1,0},{0,1},{3,2},{2,3},{5,4},{4,5},{7,6},{6,7},{9,8},{8,9},{11,10... | collective-permute-start | bytes 786440 | tf_op jit(solution)/shard_map/ppermute | solution.py:63
  22.7 2.9 %collective-permute-start.5 = (bf16[16,64,128]{2,1,0:T(8,128)(2,1)S(1)}, bf16[16,64,128]{2,1,0:T(8,128)(2,1)S(1)}, u32[]{:S(2)}, u32[]{:S(2)}) collective-permute-start(bf16[16,64,128]{2,1,0:T(8,128)(2,1)S(1)} %collective-permute-done.4.refs_5_), channel_id=1, source_target_pairs={{1,0},{0,1},{3,2},{2,3},{5,4},{4,5},{7,6},{6,7},{9,8},{8,9},{11,10... | collective-permute-start | bytes 786440 | tf_op jit(solution)/shard_map/ppermute | solution.py:63
  23.2 6.8 %collective-permute-start.7 = (bf16[16,64,128]{2,1,0:T(8,128)(2,1)S(1)}, bf16[16,64,128]{2,1,0:T(8,128)(2,1)S(1)}, u32[]{:S(2)}, u32[]{:S(2)}) collective-permute-start(bf16[16,64,128]{2,1,0:T(8,128)(2,1)S(1)} %collective-permute-done.6.refs_7_), channel_id=1, source_target_pairs={{1,0},{0,1},{3,2},{2,3},{5,4},{4,5},{7,6},{6,7},{9,8},{8,9},{11,10... | collective-permute-start | bytes 786440 | tf_op jit(solution)/shard_map/ppermute | solution.py:63
  23.3 2.2 %copy-start = (bf16[1,16,64,128]{3,2,1,0:T(8,128)(2,1)S(1)}, bf16[1,16,64,128]{3,2,1,0:T(8,128)(2,1)}, u32[]{:S(2)}) copy-start(bf16[1,16,64,128]{3,2,1,0:T(8,128)(2,1)} %param.10) | copy-start | bytes 786436
  23.3 6.7 %copy-start.1 = (bf16[256,256]{1,0:T(8,128)(2,1)S(1)}, bf16[256,256]{1,0:T(8,128)(2,1)}, u32[]{:S(2)}) copy-start(bf16[256,256]{1,0:T(8,128)(2,1)} %constant.44.clone.refs_13_.refs_10_) | copy-start | bytes 393220
  23.3 6.7 %copy-start.2 = (bf16[256,256]{1,0:T(8,128)(2,1)S(1)}, bf16[256,256]{1,0:T(8,128)(2,1)}, u32[]{:S(2)}) copy-start(bf16[256,256]{1,0:T(8,128)(2,1)} %constant.45.clone.refs_14_.refs_11_) | copy-start | bytes 393220
  23.3 6.7 %copy-start.3 = (bf16[128,128]{1,0:T(8,128)(2,1)S(1)}, bf16[128,128]{1,0:T(8,128)(2,1)}, u32[]{:S(2)}) copy-start(bf16[128,128]{1,0:T(8,128)(2,1)} %constant.42.clone.refs_11_.refs_8_) | copy-start | bytes 98308
  23.3 6.7 %copy-start.4 = (bf16[128,128]{1,0:T(8,128)(2,1)S(1)}, bf16[128,128]{1,0:T(8,128)(2,1)}, u32[]{:S(2)}) copy-start(bf16[128,128]{1,0:T(8,128)(2,1)} %constant.43.clone.refs_12_.refs_9_) | copy-start | bytes 98308
  25.5 30.0 %collective-permute-start.18 = (bf16[16,64,128]{2,1,0:T(8,128)(2,1)S(1)}, bf16[16,64,128]{2,1,0:T(8,128)(2,1)S(1)}, u32[]{:S(2)}, u32[]{:S(2)}) collective-permute-start(bf16[16,64,128]{2,1,0:T(8,128)(2,1)S(1)} %bitcast.54), channel_id=1, source_target_pairs={{20,0},{21,1},{22,2},{23,3},{16,4},{17,5},{18,6},{19,7},{28,8},{29... | collective-permute-start | bytes 786440 | tf_op jit(solution)/shard_map/ppermute | solution.py:63
  25.6 30.0 %collective-permute-start.19 = (bf16[16,64,128]{2,1,0:T(8,128)(2,1)S(1)}, bf16[16,64,128]{2,1,0:T(8,128)(2,1)S(1)}, u32[]{:S(2)}, u32[]{:S(2)}) collective-permute-start(bf16[16,64,128]{2,1,0:T(8,128)(2,1)S(1)} %bitcast.55), channel_id=1, source_target_pairs={{22,0},{23,1},{20,2},{21,3},{18,4},{19,5},{16,6},{17,7},{30,8},{31... | collective-permute-start | bytes 786440 | tf_op jit(solution)/shard_map/ppermute | solution.py:63
  50.7 7.9 %collective-permute-start.12 = (bf16[16,64,128]{2,1,0:T(8,128)(2,1)S(1)}, bf16[16,64,128]{2,1,0:T(8,128)(2,1)S(1)}, u32[]{:S(2)}, u32[]{:S(2)}) collective-permute-start(bf16[16,64,128]{2,1,0:T(8,128)(2,1)S(1)} %get-tuple-element.64), channel_id=1, source_target_pairs={{1,0},{0,1},{3,2},{2,3},{5,4},{4,5},{7,6},{6,7},{9,8},{8,9},{11,10... | collective-permute-start | bytes 786440 | tf_op jit(solution)/shard_map/ppermute | solution.py:63
  54.8 4.0 %collective-permute-start.13 = (bf16[16,64,128]{2,1,0:T(8,128)(2,1)S(1)}, bf16[16,64,128]{2,1,0:T(8,128)(2,1)S(1)}, u32[]{:S(2)}, u32[]{:S(2)}) collective-permute-start(bf16[16,64,128]{2,1,0:T(8,128)(2,1)S(1)} %get-tuple-element.63), channel_id=1, source_target_pairs={{1,0},{0,1},{3,2},{2,3},{5,4},{4,5},{7,6},{6,7},{9,8},{8,9},{11,10... | collective-permute-start | bytes 786440 | tf_op jit(solution)/shard_map/ppermute | solution.py:63
  55.0 4.4 %collective-permute-start.10 = (bf16[16,64,128]{2,1,0:T(8,128)(2,1)S(1)}, bf16[16,64,128]{2,1,0:T(8,128)(2,1)S(1)}, u32[]{:S(2)}, u32[]{:S(2)}) collective-permute-start(bf16[16,64,128]{2,1,0:T(8,128)(2,1)S(1)} %get-tuple-element.68), channel_id=1, source_target_pairs={{1,0},{0,1},{3,2},{2,3},{5,4},{4,5},{7,6},{6,7},{9,8},{8,9},{11,10... | collective-permute-start | bytes 786440 | tf_op jit(solution)/shard_map/ppermute | solution.py:63
  55.5 3.9 %collective-permute-start.11 = (bf16[16,64,128]{2,1,0:T(8,128)(2,1)S(1)}, bf16[16,64,128]{2,1,0:T(8,128)(2,1)S(1)}, u32[]{:S(2)}, u32[]{:S(2)}) collective-permute-start(bf16[16,64,128]{2,1,0:T(8,128)(2,1)S(1)} %get-tuple-element.67), channel_id=1, source_target_pairs={{1,0},{0,1},{3,2},{2,3},{5,4},{4,5},{7,6},{6,7},{9,8},{8,9},{11,10... | collective-permute-start | bytes 786440 | tf_op jit(solution)/shard_map/ppermute | solution.py:63
  55.6 12.7 %collective-permute-start.26 = (bf16[16,64,128]{2,1,0:T(8,128)(2,1)S(1)}, bf16[16,64,128]{2,1,0:T(8,128)(2,1)S(1)}, u32[]{:S(2)}, u32[]{:S(2)}) collective-permute-start(bf16[16,64,128]{2,1,0:T(8,128)(2,1)S(1)} %bitcast.56), channel_id=1, source_target_pairs={{2,0},{3,1},{0,2},{1,3},{6,4},{7,5},{4,6},{5,7},{10,8},{11,9},{8,1... | collective-permute-start | bytes 786440 | tf_op jit(solution)/shard_map/ppermute | solution.py:63
  58.7 1.5 %collective-permute-start.20 = (bf16[16,64,128]{2,1,0:T(8,128)(2,1)S(1)}, bf16[16,64,128]{2,1,0:T(8,128)(2,1)S(1)}, u32[]{:S(2)}, u32[]{:S(2)}) collective-permute-start(bf16[16,64,128]{2,1,0:T(8,128)(2,1)S(1)} %collective-permute-done.18.refs_1_), channel_id=1, source_target_pairs={{1,0},{0,1},{3,2},{2,3},{5,4},{4,5},{7,6},{6,7},{9,8},{8,9},{11,10... | collective-permute-start | bytes 786440 | tf_op jit(solution)/shard_map/ppermute | solution.py:63
  58.8 1.8 %collective-permute-start.21 = (bf16[16,64,128]{2,1,0:T(8,128)(2,1)S(1)}, bf16[16,64,128]{2,1,0:T(8,128)(2,1)S(1)}, u32[]{:S(2)}, u32[]{:S(2)}) collective-permute-start(bf16[16,64,128]{2,1,0:T(8,128)(2,1)S(1)} %collective-permute-done.19.refs_3_), channel_id=1, source_target_pairs={{1,0},{0,1},{3,2},{2,3},{5,4},{4,5},{7,6},{6,7},{9,8},{8,9},{11,10... | collective-permute-start | bytes 786440 | tf_op jit(solution)/shard_map/ppermute | solution.py:63
  67.7 1.6 %collective-permute-start.22 = (bf16[16,64,128]{2,1,0:T(8,128)(2,1)S(1)}, bf16[16,64,128]{2,1,0:T(8,128)(2,1)S(1)}, u32[]{:S(2)}, u32[]{:S(2)}) collective-permute-start(bf16[16,64,128]{2,1,0:T(8,128)(2,1)S(1)} %get-tuple-element.60), channel_id=1, source_target_pairs={{1,0},{0,1},{3,2},{2,3},{5,4},{4,5},{7,6},{6,7},{9,8},{8,9},{11,10... | collective-permute-start | bytes 786440 | tf_op jit(solution)/shard_map/ppermute | solution.py:63
  67.9 1.8 %collective-permute-start.23 = (bf16[16,64,128]{2,1,0:T(8,128)(2,1)S(1)}, bf16[16,64,128]{2,1,0:T(8,128)(2,1)S(1)}, u32[]{:S(2)}, u32[]{:S(2)}) collective-permute-start(bf16[16,64,128]{2,1,0:T(8,128)(2,1)S(1)} %get-tuple-element.59), channel_id=1, source_target_pairs={{1,0},{0,1},{3,2},{2,3},{5,4},{4,5},{7,6},{6,7},{9,8},{8,9},{11,10... | collective-permute-start | bytes 786440 | tf_op jit(solution)/shard_map/ppermute | solution.py:63
  68.3 1.8 %collective-permute-start.27 = (bf16[16,64,128]{2,1,0:T(8,128)(2,1)S(1)}, bf16[16,64,128]{2,1,0:T(8,128)(2,1)S(1)}, u32[]{:S(2)}, u32[]{:S(2)}) collective-permute-start(bf16[16,64,128]{2,1,0:T(8,128)(2,1)S(1)} %bitcast.57), channel_id=1, source_target_pairs={{1,0},{0,1},{3,2},{2,3},{5,4},{4,5},{7,6},{6,7},{9,8},{8,9},{11,10... | collective-permute-start | bytes 786440 | tf_op jit(solution)/shard_map/ppermute | solution.py:63
  68.5 2.0 %collective-permute-start.28 = (bf16[16,64,128]{2,1,0:T(8,128)(2,1)S(1)}, bf16[16,64,128]{2,1,0:T(8,128)(2,1)S(1)}, u32[]{:S(2)}, u32[]{:S(2)}) collective-permute-start(bf16[16,64,128]{2,1,0:T(8,128)(2,1)S(1)} %collective-permute-done.26.refs_3_), channel_id=1, source_target_pairs={{1,0},{0,1},{3,2},{2,3},{5,4},{4,5},{7,6},{6,7},{9,8},{8,9},{11,10... | collective-permute-start | bytes 786440 | tf_op jit(solution)/shard_map/ppermute | solution.py:63
  77.6 5.2 %collective-permute-start.30 = (bf16[16,64,128]{2,1,0:T(8,128)(2,1)S(1)}, bf16[16,64,128]{2,1,0:T(8,128)(2,1)S(1)}, u32[]{:S(2)}, u32[]{:S(2)}) collective-permute-start(bf16[16,64,128]{2,1,0:T(8,128)(2,1)S(1)} %get-tuple-element.56), channel_id=1, source_target_pairs={{1,0},{0,1},{3,2},{2,3},{5,4},{4,5},{7,6},{6,7},{9,8},{8,9},{11,10... | collective-permute-start | bytes 786440 | tf_op jit(solution)/shard_map/ppermute | solution.py:63
  77.8 9.2 %collective-permute-start.14 = (bf16[16,64,128]{2,1,0:T(8,128)(2,1)S(1)}, bf16[16,64,128]{2,1,0:T(8,128)(2,1)S(1)}, u32[]{:S(2)}, u32[]{:S(2)}) collective-permute-start(bf16[16,64,128]{2,1,0:T(8,128)(2,1)S(1)} %get-tuple-element.40), channel_id=1, source_target_pairs={{4,0},{5,1},{6,2},{7,3},{0,4},{1,5},{2,6},{3,7},{12,8},{13,9},{14,... | collective-permute-start | bytes 786440 | tf_op jit(solution)/shard_map/ppermute | solution.py:63
  78.1 17.1 %collective-permute-start.15 = (bf16[16,64,128]{2,1,0:T(8,128)(2,1)S(1)}, bf16[16,64,128]{2,1,0:T(8,128)(2,1)S(1)}, u32[]{:S(2)}, u32[]{:S(2)}) collective-permute-start(bf16[16,64,128]{2,1,0:T(8,128)(2,1)S(1)} %get-tuple-element.41), channel_id=1, source_target_pairs={{6,0},{7,1},{4,2},{5,3},{2,4},{3,5},{0,6},{1,7},{14,8},{15,9},{12,... | collective-permute-start | bytes 786440 | tf_op jit(solution)/shard_map/ppermute | solution.py:63
  79.9 17.3 %collective-permute-start.16 = (bf16[16,64,128]{2,1,0:T(8,128)(2,1)S(1)}, bf16[16,64,128]{2,1,0:T(8,128)(2,1)S(1)}, u32[]{:S(2)}, u32[]{:S(2)}) collective-permute-start(bf16[16,64,128]{2,1,0:T(8,128)(2,1)S(1)} %get-tuple-element.42), channel_id=1, source_target_pairs={{16,0},{17,1},{18,2},{19,3},{20,4},{21,5},{22,6},{23,7},{24,8},{25... | collective-permute-start | bytes 786440 | tf_op jit(solution)/shard_map/ppermute | solution.py:63
  80.1 26.6 %collective-permute-start.17 = (bf16[16,64,128]{2,1,0:T(8,128)(2,1)S(1)}, bf16[16,64,128]{2,1,0:T(8,128)(2,1)S(1)}, u32[]{:S(2)}, u32[]{:S(2)}) collective-permute-start(bf16[16,64,128]{2,1,0:T(8,128)(2,1)S(1)} %get-tuple-element.43), channel_id=1, source_target_pairs={{18,0},{19,1},{16,2},{17,3},{22,4},{23,5},{20,6},{21,7},{26,8},{27... | collective-permute-start | bytes 786440 | tf_op jit(solution)/shard_map/ppermute | solution.py:63
  82.8 23.9 %collective-permute-start.29 = (bf16[16,64,128]{2,1,0:T(8,128)(2,1)S(1)}, bf16[16,64,128]{2,1,0:T(8,128)(2,1)S(1)}, u32[]{:S(2)}, u32[]{:S(2)}) collective-permute-start(bf16[16,64,128]{2,1,0:T(8,128)(2,1)S(1)} %get-tuple-element.55), channel_id=1, source_target_pairs={{1,0},{0,1},{3,2},{2,3},{5,4},{4,5},{7,6},{6,7},{9,8},{8,9},{11,10... | collective-permute-start | bytes 786440 | tf_op jit(solution)/shard_map/ppermute | solution.py:63
  87.0 19.7 %collective-permute-start.24 = (bf16[16,64,128]{2,1,0:T(8,128)(2,1)S(1)}, bf16[16,64,128]{2,1,0:T(8,128)(2,1)S(1)}, u32[]{:S(2)}, u32[]{:S(2)}) collective-permute-start(bf16[16,64,128]{2,1,0:T(8,128)(2,1)S(1)} %get-tuple-element.49), channel_id=1, source_target_pairs={{20,0},{21,1},{22,2},{23,3},{16,4},{17,5},{18,6},{19,7},{28,8},{29... | collective-permute-start | bytes 786440 | tf_op jit(solution)/shard_map/ppermute | solution.py:63
  95.2 11.6 %collective-permute-start.25 = (bf16[16,64,128]{2,1,0:T(8,128)(2,1)S(1)}, bf16[16,64,128]{2,1,0:T(8,128)(2,1)S(1)}, u32[]{:S(2)}, u32[]{:S(2)}) collective-permute-start(bf16[16,64,128]{2,1,0:T(8,128)(2,1)S(1)} %get-tuple-element.50), channel_id=1, source_target_pairs={{22,0},{23,1},{20,2},{21,3},{18,4},{19,5},{16,6},{17,7},{30,8},{31... | collective-permute-start | bytes 786440 | tf_op jit(solution)/shard_map/ppermute | solution.py:63
  97.2 14.4 %collective-permute-start.31 = (bf16[16,64,128]{2,1,0:T(8,128)(2,1)S(1)}, bf16[16,64,128]{2,1,0:T(8,128)(2,1)S(1)}, u32[]{:S(2)}, u32[]{:S(2)}) collective-permute-start(bf16[16,64,128]{2,1,0:T(8,128)(2,1)S(1)} %fusion.3), channel_id=1, source_target_pairs={{2,0},{3,1},{0,2},{1,3},{6,4},{7,5},{4,6},{5,7},{10,8},{11,9},{8,1... | collective-permute-start | bytes 786440 | tf_op jit(solution)/shard_map/ppermute | solution.py:63

commit v3 on v2

--- a/solution.py
+++ b/solution.py
@@ -341,11 +341,14 @@
     first = receive(partner, first_source)
     orders = [(0, 1), (1, 0), (1, 1), (0, 0)]
     halves = []
-    for dy, dx in orders:
+    sent = own
+    for n, (dy, dx) in enumerate(orders):
+        if n == 2:
+            sent, *halves[1] = lax.optimization_barrier((own, *halves[1]))
         half = []
         for dz in range(2):
             source = offset_source(dy, dx, dz, 0)
-            half.append(own if (dy, dx, dz) == (0, 0, 0) else receive(own, source))
+            half.append(own if (dy, dx, dz) == (0, 0, 0) else receive(sent, source))
         halves.append(half)
     second = receive(partner, second_source)
     matrices = section_matrices()
@@ -359,7 +362,10 @@
         same, other = halves[n]
         if mark is not None:
             _, same, other = lax.optimization_barrier((mark, same, other))
-        return [same, receive(same, sibling), other, receive(other, sibling)]
+        crossed = []
+        for piece in (same, other):
+            crossed.append(receive(piece, sibling))
+        return [same, crossed[0], other, crossed[1]]
 
     def core_sum(part, rounded):
         both = []
@@ -373,10 +379,13 @@
         parts = exchange_part(place, *args, **kwargs)
         return lax.optimization_barrier((place, *parts))
 
-    two = pieces(0) + pieces(1)
     coulombs = [
         coulomb_kernel(screening, (weights[a], weights[b])) for a, b in ((0, 0), (1, 1), (0, 1))
     ]
+    *coulombs, halves[0][1], halves[1][1] = lax.optimization_barrier(
+        (*coulombs, halves[0][1], halves[1][1])
+    )
+    two = pieces(0) + pieces(1)
     place, *earlier = call(
         place, two + [first], coulombs[0], matrices, two_targets=True, stage="first"
     )

time: 113 us -> 104 us (0.920)
  the two profiles are of different devices: /device:TPU:32 before, /device:TPU:26 now
where the time goes in v3:
time: 104 us; the launch traced here: 103 us
  waiting for transfers between devices  36.2 us (35%)
  starting transfers between devices  29.5 us (28%)
  Pallas kernels  28.8 us (28%)
  other arithmetic  6.25 us (6%)
  local copies, waits for them, and re-layouts  1.56 us (2%)
    ppermute x32, waiting for transfers between devices, receive(): return lax.ppermute(value, axes, pairs)  36.2 us
    ppermute x32, starting transfers between devices, receive(): return lax.ppermute(value, axes, pairs)  29.5 us
    pallas_call x4, Pallas kernels, exchange_part(): pl.pallas_call(functools.partial(pair_kernel, two_targets, stage), out_sh...  28.8 us
    mul x1, other arithmetic, coulomb_kernel(): coulomb_scale / (wave_sq + screen_wave * screen_wave) * weight[None, None...  2.12 us
  transfers between devices with their start and end apart: 32, of which 12 were waited for; matrix products, arithmetic and copies ran while one was open for 6% of the time, Pallas kernels for 21%

profile of v3, /device:TPU:26, one launch (start us, length us, event | category | flops | bytes accessed | tf_op | source)
XLA Modules:
  0.0 103.2 jit_solution(11571747530302441611)
XLA Ops:
  0.0 0.7 collective-permute-start.3
  0.7 2.6 %collective-permute-start.4 = (bf16[16,64,128]{2,1,0:T(8,128)(2,1)}, bf16[16,64,128]{2,1,0:T(8,128)(2,1)S(1)}, u32[]{:S(2)}, u32[]{:S(2)}) collective-permute-start(bf16[16,64,128]{2,1,0:T(8,128)(2,1)} %bitcast.51), channel_id=1, source_target_pairs={{18,0},{19,1},{16,2},{17,3},{22,4},{23,5},{20,6},{21,7},{26,8},{27... | collective-permute-start | bytes 786440 | tf_op jit(solution)/shard_map/ppermute | solution.py:63
  3.4 0.1 collective-permute-start.2
  3.5 4.2 %collective-permute-start.8 = (bf16[64,64,128]{2,1,0:T(8,128)(2,1)}, bf16[64,64,128]{2,1,0:T(8,128)(2,1)S(1)}, u32[]{:S(2)}, u32[]{:S(2)}) collective-permute-start(bf16[64,64,128]{2,1,0:T(8,128)(2,1)} %bitcast.59), channel_id=1, source_target_pairs={{1,0},{66,1},{51,2},{76,3},{5,4},{70,5},{55,6},{72,7},{9,8},{74,9}... | collective-permute-start | bytes 3145736 | tf_op jit(solution)/shard_map/ppermute | solution.py:63
  7.7 2.2 %collective-permute-start.9 = (bf16[64,64,128]{2,1,0:T(8,128)(2,1)}, bf16[64,64,128]{2,1,0:T(8,128)(2,1)S(1)}, u32[]{:S(2)}, u32[]{:S(2)}) collective-permute-start(bf16[64,64,128]{2,1,0:T(8,128)(2,1)} %bitcast.60), channel_id=1, source_target_pairs={{61,0},{126,1},{15,2},{112,3},{57,4},{122,5},{11,6},{116,7},{53,8}... | collective-permute-start | bytes 3145736 | tf_op jit(solution)/shard_map/ppermute | solution.py:63
  9.9 0.1 broadcast_add_fusion
  10.0 0.7 dynamic-slice_bitcast_fusion
  10.7 0.8 select_reduce_fusion
  11.5 0.2 fusion.14
  11.7 0.6 fusion.18
  12.3 0.1 add.139
  13.1 1.2 %compare_select_fusion.1 = f32[128]{0:T(128)S(1)} fusion(f32[]{:T(128)} %bitcast.5, f32[]{:T(128)} %bitcast.4), kind=kLoop, calls=%fused_computation.35 | loop fusion | flops 256 | bytes 520 | tf_op jit(solution)/shard_map/jit(_where)/select_n | solution.py:110
  14.3 0.0 copy-start
  14.3 0.0 copy-start.1
  14.3 0.0 copy-start.2
  14.3 0.0 copy-start.3
  14.3 0.0 copy-start.4
  14.3 2.1 %fusion = (f32[64,64,128]{2,1,0:T(8,128)S(1)}, f32[64,64,128]{2,1,0:T(8,128)S(1)}, f32[64,64,128]{2,1,0:T(8,128)S(1)}) fusion(f32[128]{0:T(128)S(1)} %compare_select_fusion.1, f32[]{:T(128)} %bitcast.2, f32[128]{0:T(128)S(1)} %add.139, f32[64,64]{1,0:T(8,128)S(1)} %broadcast_add_fusion, f32[]{:T(128)} %bitcast.5, f32[]{:T(128)} %bitcast.4), kind=kLoop, calls=%fused_computation.1 | loop fusion | flops 3145728 | bytes 6308876 | tf_op jit(solution)/shard_map/mul | solution.py:111
  16.5 0.0 collective-permute-done.3.refs_5_
  16.5 1.6 %collective-permute-start = (bf16[16,64,128]{2,1,0:T(8,128)(2,1)S(1)}, bf16[16,64,128]{2,1,0:T(8,128)(2,1)S(1)}, u32[]{:S(2)}, u32[]{:S(2)}) collective-permute-start(bf16[16,64,128]{2,1,0:T(8,128)(2,1)S(1)} %bitcast.53), channel_id=1, source_target_pairs={{4,0},{5,1},{6,2},{7,3},{0,4},{1,5},{2,6},{3,7},{12,8},{13,9},{14,... | collective-permute-start | bytes 786440 | tf_op jit(solution)/shard_map/ppermute | solution.py:63
  18.1 0.5 collective-permute-start.7
  18.6 4.6 %collective-permute-done.refs_1_ = bf16[16,64,128]{2,1,0:T(8,128)(2,1)S(1)} collective-permute-done((bf16[16,64,128]{2,1,0:T(8,128)(2,1)S(1)}, bf16[16,64,128]{2,1,0:T(8,128)(2,1)S(1)}, u32[]{:S(2)}, u32[]{:S(2)}) %collective-permute-start) | collective-permute-done | bytes 262176 | tf_op jit(solution)/shard_map/ppermute | solution.py:63
  23.2 0.5 collective-permute-start.1
  23.7 2.1 %collective-permute-start.18 = (bf16[16,64,128]{2,1,0:T(8,128)(2,1)S(1)}, bf16[16,64,128]{2,1,0:T(8,128)(2,1)S(1)}, u32[]{:S(2)}, u32[]{:S(2)}) collective-permute-start(bf16[16,64,128]{2,1,0:T(8,128)(2,1)S(1)} %bitcast.54), channel_id=1, source_target_pairs={{20,0},{21,1},{22,2},{23,3},{16,4},{17,5},{18,6},{19,7},{28,8},{29... | collective-permute-start | bytes 786440 | tf_op jit(solution)/shard_map/ppermute | solution.py:63
  25.8 0.1 collective-permute-start.19
  25.9 4.6 %collective-permute-done.8.refs_9_.refs_5_ = bf16[64,64,128]{2,1,0:T(8,128)(2,1)S(1)} collective-permute-done((bf16[64,64,128]{2,1,0:T(8,128)(2,1)}, bf16[64,64,128]{2,1,0:T(8,128)(2,1)S(1)}, u32[]{:S(2)}, u32[]{:S(2)}) %collective-permute-start.8) | collective-permute-done | bytes 1048608 | tf_op jit(solution)/shard_map/ppermute | solution.py:63
  30.6 7.1 %shard_map.100 = (bf16[4,16,64,128]{3,2,1,0:T(8,128)(2,1)S(1)}, bf16[4,16,64,128]{3,2,1,0:T(8,128)(2,1)S(1)}) custom-call(s32[1]{0:T(128)} %bitcast.refs_0_, bf16[16,64,128]{2,1,0:T(8,128)(2,1)S(1)} %collective-permute-done.refs_1_, bf16[16,64,128]{2,1,0:T(8,128)(2,1)S(1)} %collective-permute-done.1.refs_2_, ...), custom_call_target="tpu_custom_call" | custom-call | flops 5000000000 | bytes 25165824 | tf_op jit(solution)/shard_map/pallas_call | solution.py:308
  37.7 7.6 %shard_map.101 = (bf16[4,16,64,128]{3,2,1,0:T(8,128)(2,1)S(1)}, bf16[4,16,64,128]{3,2,1,0:T(8,128)(2,1)S(1)}) custom-call(s32[1]{0:T(128)} %bitcast.refs_0_, bf16[16,64,128]{2,1,0:T(8,128)(2,1)S(1)} %collective-permute-done.refs_1_, bf16[16,64,128]{2,1,0:T(8,128)(2,1)S(1)} %collective-permute-done.1.refs_2_, ...), custom_call_target="tpu_custom_call" | custom-call | flops 5000000000 | bytes 25165824 | tf_op jit(solution)/shard_map/pallas_call | solution.py:308
  45.3 0.4 collective-permute-start.12
  45.7 0.2 collective-permute-start.13
  45.9 0.4 collective-permute-start.10
  46.3 0.2 collective-permute-start.11
  46.5 2.1 %collective-permute-start.26 = (bf16[16,64,128]{2,1,0:T(8,128)(2,1)S(1)}, bf16[16,64,128]{2,1,0:T(8,128)(2,1)S(1)}, u32[]{:S(2)}, u32[]{:S(2)}) collective-permute-start(bf16[16,64,128]{2,1,0:T(8,128)(2,1)S(1)} %bitcast.56), channel_id=1, source_target_pairs={{2,0},{3,1},{0,2},{1,3},{6,4},{7,5},{4,6},{5,7},{10,8},{11,9},{8,1... | collective-permute-start | bytes 786440 | tf_op jit(solution)/shard_map/ppermute | solution.py:63
  48.6 0.1 collective-permute-start.20
  48.8 0.4 collective-permute-start.21
  49.2 0.2 fusion.10
  49.4 0.2 fusion.12
  49.6 0.6 collective-permute-done.20.refs_2_
  50.2 0.4 collective-permute-done.21.refs_4_
  50.6 7.1 %shard_map.102 = bf16[4,16,64,128]{3,2,1,0:T(8,128)(2,1)S(1)} custom-call(s32[1]{0:T(128)} %bitcast.refs_0_, bf16[16,64,128]{2,1,0:T(8,128)(2,1)S(1)} %collective-permute-done.18.refs_1_, bf16[16,64,128]{2,1,0:T(8,128)(2,1)S(1)} %collective-permute-done.20.refs_2_, bf16[16,64,128]{2,1,0:T(8,128)(2,1)S(1)} %collective-permute-done.19.refs_3_, ...), custom_call_target="tpu_custom_call" | custom-call | flops 5000000000 | bytes 25165824 | tf_op jit(solution)/shard_map/pallas_call | solution.py:308
  57.7 0.2 collective-permute-start.22
  57.9 0.4 collective-permute-start.23
  58.3 0.1 collective-permute-start.27
  58.4 0.4 collective-permute-start.28
  58.8 0.5 collective-permute-done.22
  59.3 0.4 collective-permute-done.23
  59.7 0.2 fusion.8
  59.9 0.2 collective-permute-done.27.refs_2_
  60.1 0.4 collective-permute-done.28.refs_4_
  60.4 7.1 %shard_map.103 = bf16[4,16,64,128]{3,2,1,0:T(8,128)(2,1)S(1)} custom-call(s32[1]{0:T(128)} %bitcast.refs_0_, bf16[16,64,128]{2,1,0:T(8,128)(2,1)S(1)} %bitcast.58, bf16[16,64,128]{2,1,0:T(8,128)(2,1)S(1)} %collective-permute-done.27.refs_2_, bf16[16,64,128]{2,1,0:T(8,128)(2,1)S(1)} %collective-permute-done.26.refs_3_, ...), custom_call_target="tpu_custom_call" | custom-call | flops 5000000000 | bytes 25165824 | tf_op jit(solution)/shard_map/pallas_call | solution.py:308
  67.6 0.2 collective-permute-start.30
  67.8 0.9 collective-permute-start.14
  68.7 1.2 %collective-permute-start.15 = (bf16[16,64,128]{2,1,0:T(8,128)(2,1)S(1)}, bf16[16,64,128]{2,1,0:T(8,128)(2,1)S(1)}, u32[]{:S(2)}, u32[]{:S(2)}) collective-permute-start(bf16[16,64,128]{2,1,0:T(8,128)(2,1)S(1)} %get-tuple-element.55), channel_id=1, source_target_pairs={{6,0},{7,1},{4,2},{5,3},{2,4},{3,5},{0,6},{1,7},{14,8},{15,9},{12,... | collective-permute-start | bytes 786440 | tf_op jit(solution)/shard_map/ppermute | solution.py:63
  69.9 0.7 collective-permute-start.16
  70.7 2.1 %collective-permute-start.17 = (bf16[16,64,128]{2,1,0:T(8,128)(2,1)S(1)}, bf16[16,64,128]{2,1,0:T(8,128)(2,1)S(1)}, u32[]{:S(2)}, u32[]{:S(2)}) collective-permute-start(bf16[16,64,128]{2,1,0:T(8,128)(2,1)S(1)} %get-tuple-element.57), channel_id=1, source_target_pairs={{18,0},{19,1},{16,2},{17,3},{22,4},{23,5},{20,6},{21,7},{26,8},{27... | collective-permute-start | bytes 786440 | tf_op jit(solution)/shard_map/ppermute | solution.py:63
  72.7 0.1 fusion.3
  72.8 4.1 %collective-permute-done.14 = bf16[16,64,128]{2,1,0:T(8,128)(2,1)S(1)} collective-permute-done((bf16[16,64,128]{2,1,0:T(8,128)(2,1)S(1)}, bf16[16,64,128]{2,1,0:T(8,128)(2,1)S(1)}, u32[]{:S(2)}, u32[]{:S(2)}) %collective-permute-start.14) | collective-permute-done | bytes 262176 | tf_op jit(solution)/shard_map/ppermute | solution.py:63
  77.0 1.1 %collective-permute-start.24 = (bf16[16,64,128]{2,1,0:T(8,128)(2,1)S(1)}, bf16[16,64,128]{2,1,0:T(8,128)(2,1)S(1)}, u32[]{:S(2)}, u32[]{:S(2)}) collective-permute-start(bf16[16,64,128]{2,1,0:T(8,128)(2,1)S(1)} %get-tuple-element.65), channel_id=1, source_target_pairs={{20,0},{21,1},{22,2},{23,3},{16,4},{17,5},{18,6},{19,7},{28,8},{29... | collective-permute-start | bytes 786440 | tf_op jit(solution)/shard_map/ppermute | solution.py:63
  78.1 7.4 %collective-permute-done.15 = bf16[16,64,128]{2,1,0:T(8,128)(2,1)S(1)} collective-permute-done((bf16[16,64,128]{2,1,0:T(8,128)(2,1)S(1)}, bf16[16,64,128]{2,1,0:T(8,128)(2,1)S(1)}, u32[]{:S(2)}, u32[]{:S(2)}) %collective-permute-start.15) | collective-permute-done | bytes 262176 | tf_op jit(solution)/shard_map/ppermute | solution.py:63
  85.5 2.7 %collective-permute-start.25 = (bf16[16,64,128]{2,1,0:T(8,128)(2,1)S(1)}, bf16[16,64,128]{2,1,0:T(8,128)(2,1)S(1)}, u32[]{:S(2)}, u32[]{:S(2)}) collective-permute-start(bf16[16,64,128]{2,1,0:T(8,128)(2,1)S(1)} %get-tuple-element.66), channel_id=1, source_target_pairs={{22,0},{23,1},{20,2},{21,3},{18,4},{19,5},{16,6},{17,7},{30,8},{31... | collective-permute-start | bytes 786440 | tf_op jit(solution)/shard_map/ppermute | solution.py:63
  88.2 0.9 collective-permute-start.31
  89.1 7.9 %collective-permute-done.17 = bf16[16,64,128]{2,1,0:T(8,128)(2,1)S(1)} collective-permute-done((bf16[16,64,128]{2,1,0:T(8,128)(2,1)S(1)}, bf16[16,64,128]{2,1,0:T(8,128)(2,1)S(1)}, u32[]{:S(2)}, u32[]{:S(2)}) %collective-permute-start.17) | collective-permute-done | bytes 262176 | tf_op jit(solution)/shard_map/ppermute | solution.py:63
  97.1 5.0 %collective-permute-done.31 = bf16[16,64,128]{2,1,0:T(8,128)(2,1)S(1)} collective-permute-done((bf16[16,64,128]{2,1,0:T(8,128)(2,1)S(1)}, bf16[16,64,128]{2,1,0:T(8,128)(2,1)S(1)}, u32[]{:S(2)}, u32[]{:S(2)}) %collective-permute-start.31) | collective-permute-done | bytes 262176 | tf_op jit(solution)/shard_map/ppermute | solution.py:63
  102.1 1.2 %fusion.7 = f32[1,16,64,128]{3,2,1,0:T(8,128)} fusion(bf16[16,64,128]{2,1,0:T(8,128)(2,1)S(1)} %collective-permute-done.31, bf16[16,64,128]{2,1,0:T(8,128)(2,1)S(1)} %collective-permute-done.29, bf16[16,64,128]{2,1,0:T(8,128)(2,1)S(1)} %collective-permute-done.25, bf16[16,64,128]{2,1,0:T(8,128)(2,1)S(1)} %collective-permute-done.24, ...), kind=kLoop, calls=%fused_computation.10 | loop fusion | flops 2359296 | bytes 2883584 | tf_op jit(solution)/shard_map/neg | solution.py:410
  (33 shorter events, 0.2 us)
Async XLA Ops:
  0.0 16.5 %collective-permute-start.3 = (bf16[16,64,128]{2,1,0:T(8,128)(2,1)}, bf16[16,64,128]{2,1,0:T(8,128)(2,1)S(1)}, u32[]{:S(2)}, u32[]{:S(2)}) collective-permute-start(bf16[16,64,128]{2,1,0:T(8,128)(2,1)} %bitcast.50), channel_id=1, source_target_pairs={{16,0},{17,1},{18,2},{19,3},{20,4},{21,5},{22,6},{23,7},{24,8},{25... | collective-permute-start | bytes 786440 | tf_op jit(solution)/shard_map/ppermute | solution.py:63
  0.7 17.3 %collective-permute-start.4 = (bf16[16,64,128]{2,1,0:T(8,128)(2,1)}, bf16[16,64,128]{2,1,0:T(8,128)(2,1)S(1)}, u32[]{:S(2)}, u32[]{:S(2)}) collective-permute-start(bf16[16,64,128]{2,1,0:T(8,128)(2,1)} %bitcast.51), channel_id=1, source_target_pairs={{18,0},{19,1},{16,2},{17,3},{22,4},{23,5},{20,6},{21,7},{26,8},{27... | collective-permute-start | bytes 786440 | tf_op jit(solution)/shard_map/ppermute | solution.py:63
  3.4 14.7 %collective-permute-start.2 = (bf16[16,64,128]{2,1,0:T(8,128)(2,1)}, bf16[16,64,128]{2,1,0:T(8,128)(2,1)S(1)}, u32[]{:S(2)}, u32[]{:S(2)}) collective-permute-start(bf16[16,64,128]{2,1,0:T(8,128)(2,1)} %bitcast.52), channel_id=1, source_target_pairs={{6,0},{7,1},{4,2},{5,3},{2,4},{3,5},{0,6},{1,7},{14,8},{15,9},{12,... | collective-permute-start | bytes 786440 | tf_op jit(solution)/shard_map/ppermute | solution.py:63
  3.5 27.1 %collective-permute-start.8 = (bf16[64,64,128]{2,1,0:T(8,128)(2,1)}, bf16[64,64,128]{2,1,0:T(8,128)(2,1)S(1)}, u32[]{:S(2)}, u32[]{:S(2)}) collective-permute-start(bf16[64,64,128]{2,1,0:T(8,128)(2,1)} %bitcast.59), channel_id=1, source_target_pairs={{1,0},{66,1},{51,2},{76,3},{5,4},{70,5},{55,6},{72,7},{9,8},{74,9}... | collective-permute-start | bytes 3145736 | tf_op jit(solution)/shard_map/ppermute | solution.py:63
  7.7 30.0 %collective-permute-start.9 = (bf16[64,64,128]{2,1,0:T(8,128)(2,1)}, bf16[64,64,128]{2,1,0:T(8,128)(2,1)S(1)}, u32[]{:S(2)}, u32[]{:S(2)}) collective-permute-start(bf16[64,64,128]{2,1,0:T(8,128)(2,1)} %bitcast.60), channel_id=1, source_target_pairs={{61,0},{126,1},{15,2},{112,3},{57,4},{122,5},{11,6},{116,7},{53,8}... | collective-permute-start | bytes 3145736 | tf_op jit(solution)/shard_map/ppermute | solution.py:63
  14.3 2.2 %copy-start = (bf16[1,16,64,128]{3,2,1,0:T(8,128)(2,1)S(1)}, bf16[1,16,64,128]{3,2,1,0:T(8,128)(2,1)}, u32[]{:S(2)}) copy-start(bf16[1,16,64,128]{3,2,1,0:T(8,128)(2,1)} %param.10) | copy-start | bytes 786436
  14.3 16.3 %copy-start.1 = (bf16[256,256]{1,0:T(8,128)(2,1)S(1)}, bf16[256,256]{1,0:T(8,128)(2,1)}, u32[]{:S(2)}) copy-start(bf16[256,256]{1,0:T(8,128)(2,1)} %constant.44.clone.refs_13_.refs_10_) | copy-start | bytes 393220
  14.3 16.3 %copy-start.2 = (bf16[256,256]{1,0:T(8,128)(2,1)S(1)}, bf16[256,256]{1,0:T(8,128)(2,1)}, u32[]{:S(2)}) copy-start(bf16[256,256]{1,0:T(8,128)(2,1)} %constant.45.clone.refs_14_.refs_11_) | copy-start | bytes 393220
  14.3 16.2 %copy-start.3 = (bf16[128,128]{1,0:T(8,128)(2,1)S(1)}, bf16[128,128]{1,0:T(8,128)(2,1)}, u32[]{:S(2)}) copy-start(bf16[128,128]{1,0:T(8,128)(2,1)} %constant.42.clone.refs_11_.refs_8_) | copy-start | bytes 98308
  14.3 16.2 %copy-start.4 = (bf16[128,128]{1,0:T(8,128)(2,1)S(1)}, bf16[128,128]{1,0:T(8,128)(2,1)}, u32[]{:S(2)}) copy-start(bf16[128,128]{1,0:T(8,128)(2,1)} %constant.43.clone.refs_12_.refs_9_) | copy-start | bytes 98308
  16.5 6.7 %collective-permute-start = (bf16[16,64,128]{2,1,0:T(8,128)(2,1)S(1)}, bf16[16,64,128]{2,1,0:T(8,128)(2,1)S(1)}, u32[]{:S(2)}, u32[]{:S(2)}) collective-permute-start(bf16[16,64,128]{2,1,0:T(8,128)(2,1)S(1)} %bitcast.53), channel_id=1, source_target_pairs={{4,0},{5,1},{6,2},{7,3},{0,4},{1,5},{2,6},{3,7},{12,8},{13,9},{14,... | collective-permute-start | bytes 786440 | tf_op jit(solution)/shard_map/ppermute | solution.py:63
  18.1 5.1 %collective-permute-start.5 = (bf16[16,64,128]{2,1,0:T(8,128)(2,1)S(1)}, bf16[16,64,128]{2,1,0:T(8,128)(2,1)S(1)}, u32[]{:S(2)}, u32[]{:S(2)}) collective-permute-start(bf16[16,64,128]{2,1,0:T(8,128)(2,1)S(1)} %collective-permute-done.2.refs_3_), channel_id=1, source_target_pairs={{1,0},{0,1},{3,2},{2,3},{5,4},{4,5},{7,6},{6,7},{9,8},{8,9},{11,10... | collective-permute-start | bytes 786440 | tf_op jit(solution)/shard_map/ppermute | solution.py:63
  18.1 5.6 %collective-permute-start.7 = (bf16[16,64,128]{2,1,0:T(8,128)(2,1)S(1)}, bf16[16,64,128]{2,1,0:T(8,128)(2,1)S(1)}, u32[]{:S(2)}, u32[]{:S(2)}) collective-permute-start(bf16[16,64,128]{2,1,0:T(8,128)(2,1)S(1)} %collective-permute-done.4.refs_7_), channel_id=1, source_target_pairs={{1,0},{0,1},{3,2},{2,3},{5,4},{4,5},{7,6},{6,7},{9,8},{8,9},{11,10... | collective-permute-start | bytes 786440 | tf_op jit(solution)/shard_map/ppermute | solution.py:63
  23.2 2.7 %collective-permute-start.6 = (bf16[16,64,128]{2,1,0:T(8,128)(2,1)S(1)}, bf16[16,64,128]{2,1,0:T(8,128)(2,1)S(1)}, u32[]{:S(2)}, u32[]{:S(2)}) collective-permute-start(bf16[16,64,128]{2,1,0:T(8,128)(2,1)S(1)} %collective-permute-done.3.refs_5_), channel_id=1, source_target_pairs={{1,0},{0,1},{3,2},{2,3},{5,4},{4,5},{7,6},{6,7},{9,8},{8,9},{11,10... | collective-permute-start | bytes 786440 | tf_op jit(solution)/shard_map/ppermute | solution.py:63
  23.2 2.8 %collective-permute-start.1 = (bf16[16,64,128]{2,1,0:T(8,128)(2,1)S(1)}, bf16[16,64,128]{2,1,0:T(8,128)(2,1)S(1)}, u32[]{:S(2)}, u32[]{:S(2)}) collective-permute-start(bf16[16,64,128]{2,1,0:T(8,128)(2,1)S(1)} %collective-permute-done.refs_1_), channel_id=1, source_target_pairs={{1,0},{0,1},{3,2},{2,3},{5,4},{4,5},{7,6},{6,7},{9,8},{8,9},{11,10... | collective-permute-start | bytes 786440 | tf_op jit(solution)/shard_map/ppermute | solution.py:63
  23.7 22.6 %collective-permute-start.18 = (bf16[16,64,128]{2,1,0:T(8,128)(2,1)S(1)}, bf16[16,64,128]{2,1,0:T(8,128)(2,1)S(1)}, u32[]{:S(2)}, u32[]{:S(2)}) collective-permute-start(bf16[16,64,128]{2,1,0:T(8,128)(2,1)S(1)} %bitcast.54), channel_id=1, source_target_pairs={{20,0},{21,1},{22,2},{23,3},{16,4},{17,5},{18,6},{19,7},{28,8},{29... | collective-permute-start | bytes 786440 | tf_op jit(solution)/shard_map/ppermute | solution.py:63
  25.8 20.7 %collective-permute-start.19 = (bf16[16,64,128]{2,1,0:T(8,128)(2,1)S(1)}, bf16[16,64,128]{2,1,0:T(8,128)(2,1)S(1)}, u32[]{:S(2)}, u32[]{:S(2)}) collective-permute-start(bf16[16,64,128]{2,1,0:T(8,128)(2,1)S(1)} %bitcast.55), channel_id=1, source_target_pairs={{22,0},{23,1},{20,2},{21,3},{18,4},{19,5},{16,6},{17,7},{30,8},{31... | collective-permute-start | bytes 786440 | tf_op jit(solution)/shard_map/ppermute | solution.py:63
  45.3 3.3 %collective-permute-start.12 = (bf16[16,64,128]{2,1,0:T(8,128)(2,1)S(1)}, bf16[16,64,128]{2,1,0:T(8,128)(2,1)S(1)}, u32[]{:S(2)}, u32[]{:S(2)}) collective-permute-start(bf16[16,64,128]{2,1,0:T(8,128)(2,1)S(1)} %get-tuple-element.80), channel_id=1, source_target_pairs={{1,0},{0,1},{3,2},{2,3},{5,4},{4,5},{7,6},{6,7},{9,8},{8,9},{11,10... | collective-permute-start | bytes 786440 | tf_op jit(solution)/shard_map/ppermute | solution.py:63
  45.7 3.1 %collective-permute-start.13 = (bf16[16,64,128]{2,1,0:T(8,128)(2,1)S(1)}, bf16[16,64,128]{2,1,0:T(8,128)(2,1)S(1)}, u32[]{:S(2)}, u32[]{:S(2)}) collective-permute-start(bf16[16,64,128]{2,1,0:T(8,128)(2,1)S(1)} %get-tuple-element.79), channel_id=1, source_target_pairs={{1,0},{0,1},{3,2},{2,3},{5,4},{4,5},{7,6},{6,7},{9,8},{8,9},{11,10... | collective-permute-start | bytes 786440 | tf_op jit(solution)/shard_map/ppermute | solution.py:63
  45.9 3.4 %collective-permute-start.10 = (bf16[16,64,128]{2,1,0:T(8,128)(2,1)S(1)}, bf16[16,64,128]{2,1,0:T(8,128)(2,1)S(1)}, u32[]{:S(2)}, u32[]{:S(2)}) collective-permute-start(bf16[16,64,128]{2,1,0:T(8,128)(2,1)S(1)} %get-tuple-element.84), channel_id=1, source_target_pairs={{1,0},{0,1},{3,2},{2,3},{5,4},{4,5},{7,6},{6,7},{9,8},{8,9},{11,10... | collective-permute-start | bytes 786440 | tf_op jit(solution)/shard_map/ppermute | solution.py:63
  46.3 3.0 %collective-permute-start.11 = (bf16[16,64,128]{2,1,0:T(8,128)(2,1)S(1)}, bf16[16,64,128]{2,1,0:T(8,128)(2,1)S(1)}, u32[]{:S(2)}, u32[]{:S(2)}) collective-permute-start(bf16[16,64,128]{2,1,0:T(8,128)(2,1)S(1)} %get-tuple-element.83), channel_id=1, source_target_pairs={{1,0},{0,1},{3,2},{2,3},{5,4},{4,5},{7,6},{6,7},{9,8},{8,9},{11,10... | collective-permute-start | bytes 786440 | tf_op jit(solution)/shard_map/ppermute | solution.py:63
  46.5 11.8 %collective-permute-start.26 = (bf16[16,64,128]{2,1,0:T(8,128)(2,1)S(1)}, bf16[16,64,128]{2,1,0:T(8,128)(2,1)S(1)}, u32[]{:S(2)}, u32[]{:S(2)}) collective-permute-start(bf16[16,64,128]{2,1,0:T(8,128)(2,1)S(1)} %bitcast.56), channel_id=1, source_target_pairs={{2,0},{3,1},{0,2},{1,3},{6,4},{7,5},{4,6},{5,7},{10,8},{11,9},{8,1... | collective-permute-start | bytes 786440 | tf_op jit(solution)/shard_map/ppermute | solution.py:63
  48.6 1.5 %collective-permute-start.20 = (bf16[16,64,128]{2,1,0:T(8,128)(2,1)S(1)}, bf16[16,64,128]{2,1,0:T(8,128)(2,1)S(1)}, u32[]{:S(2)}, u32[]{:S(2)}) collective-permute-start(bf16[16,64,128]{2,1,0:T(8,128)(2,1)S(1)} %collective-permute-done.18.refs_1_), channel_id=1, source_target_pairs={{1,0},{0,1},{3,2},{2,3},{5,4},{4,5},{7,6},{6,7},{9,8},{8,9},{11,10... | collective-permute-start | bytes 786440 | tf_op jit(solution)/shard_map/ppermute | solution.py:63
  48.8 1.8 %collective-permute-start.21 = (bf16[16,64,128]{2,1,0:T(8,128)(2,1)S(1)}, bf16[16,64,128]{2,1,0:T(8,128)(2,1)S(1)}, u32[]{:S(2)}, u32[]{:S(2)}) collective-permute-start(bf16[16,64,128]{2,1,0:T(8,128)(2,1)S(1)} %collective-permute-done.19.refs_3_), channel_id=1, source_target_pairs={{1,0},{0,1},{3,2},{2,3},{5,4},{4,5},{7,6},{6,7},{9,8},{8,9},{11,10... | collective-permute-start | bytes 786440 | tf_op jit(solution)/shard_map/ppermute | solution.py:63
  57.7 1.6 %collective-permute-start.22 = (bf16[16,64,128]{2,1,0:T(8,128)(2,1)S(1)}, bf16[16,64,128]{2,1,0:T(8,128)(2,1)S(1)}, u32[]{:S(2)}, u32[]{:S(2)}) collective-permute-start(bf16[16,64,128]{2,1,0:T(8,128)(2,1)S(1)} %get-tuple-element.76), channel_id=1, source_target_pairs={{1,0},{0,1},{3,2},{2,3},{5,4},{4,5},{7,6},{6,7},{9,8},{8,9},{11,10... | collective-permute-start | bytes 786440 | tf_op jit(solution)/shard_map/ppermute | solution.py:63
  57.9 1.8 %collective-permute-start.23 = (bf16[16,64,128]{2,1,0:T(8,128)(2,1)S(1)}, bf16[16,64,128]{2,1,0:T(8,128)(2,1)S(1)}, u32[]{:S(2)}, u32[]{:S(2)}) collective-permute-start(bf16[16,64,128]{2,1,0:T(8,128)(2,1)S(1)} %get-tuple-element.75), channel_id=1, source_target_pairs={{1,0},{0,1},{3,2},{2,3},{5,4},{4,5},{7,6},{6,7},{9,8},{8,9},{11,10... | collective-permute-start | bytes 786440 | tf_op jit(solution)/shard_map/ppermute | solution.py:63
  58.3 1.8 %collective-permute-start.27 = (bf16[16,64,128]{2,1,0:T(8,128)(2,1)S(1)}, bf16[16,64,128]{2,1,0:T(8,128)(2,1)S(1)}, u32[]{:S(2)}, u32[]{:S(2)}) collective-permute-start(bf16[16,64,128]{2,1,0:T(8,128)(2,1)S(1)} %bitcast.57), channel_id=1, source_target_pairs={{1,0},{0,1},{3,2},{2,3},{5,4},{4,5},{7,6},{6,7},{9,8},{8,9},{11,10... | collective-permute-start | bytes 786440 | tf_op jit(solution)/shard_map/ppermute | solution.py:63
  58.4 2.0 %collective-permute-start.28 = (bf16[16,64,128]{2,1,0:T(8,128)(2,1)S(1)}, bf16[16,64,128]{2,1,0:T(8,128)(2,1)S(1)}, u32[]{:S(2)}, u32[]{:S(2)}) collective-permute-start(bf16[16,64,128]{2,1,0:T(8,128)(2,1)S(1)} %collective-permute-done.26.refs_3_), channel_id=1, source_target_pairs={{1,0},{0,1},{3,2},{2,3},{5,4},{4,5},{7,6},{6,7},{9,8},{8,9},{11,10... | collective-permute-start | bytes 786440 | tf_op jit(solution)/shard_map/ppermute | solution.py:63
  67.6 5.2 %collective-permute-start.30 = (bf16[16,64,128]{2,1,0:T(8,128)(2,1)S(1)}, bf16[16,64,128]{2,1,0:T(8,128)(2,1)S(1)}, u32[]{:S(2)}, u32[]{:S(2)}) collective-permute-start(bf16[16,64,128]{2,1,0:T(8,128)(2,1)S(1)} %get-tuple-element.72), channel_id=1, source_target_pairs={{1,0},{0,1},{3,2},{2,3},{5,4},{4,5},{7,6},{6,7},{9,8},{8,9},{11,10... | collective-permute-start | bytes 786440 | tf_op jit(solution)/shard_map/ppermute | solution.py:63
  67.8 9.2 %collective-permute-start.14 = (bf16[16,64,128]{2,1,0:T(8,128)(2,1)S(1)}, bf16[16,64,128]{2,1,0:T(8,128)(2,1)S(1)}, u32[]{:S(2)}, u32[]{:S(2)}) collective-permute-start(bf16[16,64,128]{2,1,0:T(8,128)(2,1)S(1)} %get-tuple-element.54), channel_id=1, source_target_pairs={{4,0},{5,1},{6,2},{7,3},{0,4},{1,5},{2,6},{3,7},{12,8},{13,9},{14,... | collective-permute-start | bytes 786440 | tf_op jit(solution)/shard_map/ppermute | solution.py:63
  68.7 16.9 %collective-permute-start.15 = (bf16[16,64,128]{2,1,0:T(8,128)(2,1)S(1)}, bf16[16,64,128]{2,1,0:T(8,128)(2,1)S(1)}, u32[]{:S(2)}, u32[]{:S(2)}) collective-permute-start(bf16[16,64,128]{2,1,0:T(8,128)(2,1)S(1)} %get-tuple-element.55), channel_id=1, source_target_pairs={{6,0},{7,1},{4,2},{5,3},{2,4},{3,5},{0,6},{1,7},{14,8},{15,9},{12,... | collective-permute-start | bytes 786440 | tf_op jit(solution)/shard_map/ppermute | solution.py:63
  69.9 18.3 %collective-permute-start.16 = (bf16[16,64,128]{2,1,0:T(8,128)(2,1)S(1)}, bf16[16,64,128]{2,1,0:T(8,128)(2,1)S(1)}, u32[]{:S(2)}, u32[]{:S(2)}) collective-permute-start(bf16[16,64,128]{2,1,0:T(8,128)(2,1)S(1)} %get-tuple-element.56), channel_id=1, source_target_pairs={{16,0},{17,1},{18,2},{19,3},{20,4},{21,5},{22,6},{23,7},{24,8},{25... | collective-permute-start | bytes 786440 | tf_op jit(solution)/shard_map/ppermute | solution.py:63
  70.7 26.4 %collective-permute-start.17 = (bf16[16,64,128]{2,1,0:T(8,128)(2,1)S(1)}, bf16[16,64,128]{2,1,0:T(8,128)(2,1)S(1)}, u32[]{:S(2)}, u32[]{:S(2)}) collective-permute-start(bf16[16,64,128]{2,1,0:T(8,128)(2,1)S(1)} %get-tuple-element.57), channel_id=1, source_target_pairs={{18,0},{19,1},{16,2},{17,3},{22,4},{23,5},{20,6},{21,7},{26,8},{27... | collective-permute-start | bytes 786440 | tf_op jit(solution)/shard_map/ppermute | solution.py:63
  72.7 24.4 %collective-permute-start.29 = (bf16[16,64,128]{2,1,0:T(8,128)(2,1)S(1)}, bf16[16,64,128]{2,1,0:T(8,128)(2,1)S(1)}, u32[]{:S(2)}, u32[]{:S(2)}) collective-permute-start(bf16[16,64,128]{2,1,0:T(8,128)(2,1)S(1)} %get-tuple-element.71), channel_id=1, source_target_pairs={{1,0},{0,1},{3,2},{2,3},{5,4},{4,5},{7,6},{6,7},{9,8},{8,9},{11,10... | collective-permute-start | bytes 786440 | tf_op jit(solution)/shard_map/ppermute | solution.py:63
  77.0 20.1 %collective-permute-start.24 = (bf16[16,64,128]{2,1,0:T(8,128)(2,1)S(1)}, bf16[16,64,128]{2,1,0:T(8,128)(2,1)S(1)}, u32[]{:S(2)}, u32[]{:S(2)}) collective-permute-start(bf16[16,64,128]{2,1,0:T(8,128)(2,1)S(1)} %get-tuple-element.65), channel_id=1, source_target_pairs={{20,0},{21,1},{22,2},{23,3},{16,4},{17,5},{18,6},{19,7},{28,8},{29... | collective-permute-start | bytes 786440 | tf_op jit(solution)/shard_map/ppermute | solution.py:63
  85.5 11.6 %collective-permute-start.25 = (bf16[16,64,128]{2,1,0:T(8,128)(2,1)S(1)}, bf16[16,64,128]{2,1,0:T(8,128)(2,1)S(1)}, u32[]{:S(2)}, u32[]{:S(2)}) collective-permute-start(bf16[16,64,128]{2,1,0:T(8,128)(2,1)S(1)} %get-tuple-element.66), channel_id=1, source_target_pairs={{22,0},{23,1},{20,2},{21,3},{18,4},{19,5},{16,6},{17,7},{30,8},{31... | collective-permute-start | bytes 786440 | tf_op jit(solution)/shard_map/ppermute | solution.py:63
  88.2 13.8 %collective-permute-start.31 = (bf16[16,64,128]{2,1,0:T(8,128)(2,1)S(1)}, bf16[16,64,128]{2,1,0:T(8,128)(2,1)S(1)}, u32[]{:S(2)}, u32[]{:S(2)}) collective-permute-start(bf16[16,64,128]{2,1,0:T(8,128)(2,1)S(1)} %fusion.3), channel_id=1, source_target_pairs={{2,0},{3,1},{0,2},{1,3},{6,4},{7,5},{4,6},{5,7},{10,8},{11,9},{8,1... | collective-permute-start | bytes 786440 | tf_op jit(solution)/shard_map/ppermute | solution.py:63

commit v4 on v3

--- a/solution.py
+++ b/solution.py
@@ -123,7 +123,8 @@
         partners = take(2)
     coulomb, lf_ref, li_ref, rf_ref, ri_ref = take(5)
     earlier = take(2) if stage == "last" else []
-    outs = take(2 if two_targets else 1)
+    outs = take(2)
+    results_count = 2 if two_targets else 1
     x_v, a_v, b_v, k_v, s_ref, z_ref, y_ref, o_v, e_v, in_sem, k_sem, e_sem, out_sem = refs
 
     dot = functools.partial(jnp.dot, preferred_element_type=f32)
@@ -151,7 +152,7 @@
     k_copy = pltpu.make_async_copy(coulomb, k_v, k_sem)
     k_copy.start()
     e_copies = [
-        pltpu.make_async_copy(source, e_v.at[i], e_sem.at[i]) for i, source in enumerate(earlier)
+        pltpu.make_async_copy(source, e_v.at[dc], e_sem.at[dc]) for dc, source in enumerate(earlier)
     ]
     for copy in e_copies:
         copy.start()
@@ -243,10 +244,12 @@
     for copy in e_copies:
         copy.wait()
 
-    def put(step):
+    def put(step, dc):
         return [
-            pltpu.make_async_copy(o_v.at[i, step], out.at[step], out_sem.at[i, step])
-            for i, out in enumerate(outs)
+            pltpu.make_async_copy(
+                o_v.at[i, step], outs[dc].at[i, step // 2], out_sem.at[i, step]
+            )
+            for i in range(results_count)
         ]
 
     def inverse_y(step):
@@ -273,8 +276,8 @@
         if stage == "first":
             results = [real, imag]
         elif stage == "last":
-            real = real + e_v[0, step].reshape(rows, lanes)
-            imag = imag + e_v[1, step].reshape(rows, lanes)
+            real = real + e_v[step % 2, 0, step // 2].reshape(rows, lanes)
+            imag = imag + e_v[step % 2, 1, step // 2].reshape(rows, lanes)
             results = [jnp.where(low, real, swap(imag)), jnp.where(low, swap(real), imag)]
         else:
             results = [jnp.where(low, real, imag) + swap(jnp.where(low, imag, real))]
@@ -284,17 +287,22 @@
     def inverse(step, carry):
         inverse_z(step)
         inverse_y(step + 1)
-        for copy in put(step):
-            copy.start()
+        for dc in range(2):
+
+            @pl.when(step % 2 == dc)
+            def _():
+                for copy in put(step, dc):
+                    copy.start()
+
         return carry
 
     inverse_y(0)
     lax.fori_loop(0, 3, inverse, 0)
     inverse_z(3)
-    for copy in put(3):
+    for copy in put(3, 1):
         copy.start()
     for step in range(4):
-        for copy in put(step):
+        for copy in put(step, step % 2):
             copy.wait()
 
 
@@ -303,16 +311,16 @@
     scalar = pl.BlockSpec(memory_space=pltpu.SMEM)
     near = pl.BlockSpec(memory_space=pltpu.VMEM)
     planes = (4, quarter, points, lanes)
-    both = (2, *planes)
-    outs = 2 if two_targets else 1
+    results = 2 if two_targets else 1
+    halves = (results, 2, quarter, points, lanes)
     return pl.pallas_call(
         functools.partial(pair_kernel, two_targets, stage),
-        out_shape=[jax.ShapeDtypeStruct(planes, bf16)] * outs,
+        out_shape=[jax.ShapeDtypeStruct(halves, bf16)] * 2,
         in_specs=[scalar]
         + [anywhere] * (len(sides) + 1)
         + [near] * 4
         + [anywhere] * len(earlier),
-        out_specs=[anywhere] * outs,
+        out_specs=[anywhere] * 2,
         scratch_shapes=[
             pltpu.VMEM(planes, bf16),
             pltpu.VMEM(planes, bf16),
@@ -321,8 +329,8 @@
             pltpu.VMEM((2 * points * pitch, lanes), f32),
             pltpu.VMEM((2, quarter, lanes, lanes), bf16),
             pltpu.VMEM((2, quarter * points, 2 * lanes), bf16),
-            pltpu.VMEM(both, bf16),
-            pltpu.VMEM(both, bf16),
+            pltpu.VMEM((results, *planes), bf16),
+            pltpu.VMEM((2, *halves), bf16),
             pltpu.SemaphoreType.DMA((4, 3)),
             pltpu.SemaphoreType.DMA,
             pltpu.SemaphoreType.DMA((2,)),
@@ -348,7 +356,7 @@
         half = []
         for dz in range(2):
             source = offset_source(dy, dx, dz, 0)
-            half.append(own if (dy, dx, dz) == (0, 0, 0) else receive(sent, source))
+            half.append(own if (dy, dx) == (0, 0) else receive(sent, source))
         halves.append(half)
     second = receive(partner, second_source)
     matrices = section_matrices()
@@ -367,11 +375,11 @@
             crossed.append(receive(piece, sibling))
         return [same, crossed[0], other, crossed[1]]
 
-    def core_sum(part, rounded):
+    def core_sum(kept, given, rounded):
         both = []
         for dz in range(2):
-            crossed = receive(part[2 * dz + 1], sibling)
-            summed = part[2 * dz].astype(f32) + crossed.astype(f32)
+            crossed = receive(given[dz], sibling)
+            summed = kept[dz].astype(f32) + crossed.astype(f32)
             both.append(summed.astype(bf16) if rounded[dz] else summed)
         return both
 
@@ -390,15 +398,18 @@
         place, two + [first], coulombs[0], matrices, two_targets=True, stage="first"
     )
     mark = place
-    place, *parts = call(place, two + [second], coulombs[1], matrices, True, "last", earlier)
-    sums = [core_sum(part, (True, True)) for part in parts]
+    _, sent = lax.optimization_barrier((mark, own))
+    halves[3][1] = receive(sent, offset_source(0, 0, 1, 0))
+    place, kept, given = call(place, two + [second], coulombs[1], matrices, True, "last", earlier)
+    crossed = receive(given, sibling)
+    place, kept_2, given_2 = call(place, pieces(2, mark) + [first, second], coulombs[2], matrices)
+    summed = (kept.astype(f32) + crossed.astype(f32)).astype(bf16)
+    sums = [[summed[n, dz] for dz in range(2)] for n in range(2)]
+    sums.append(core_sum(kept_2[0], given_2[0], (True, True)))
     place, *flat = lax.optimization_barrier((place, *sums[0], *sums[1]))
-    sums = [flat[:2], flat[2:]]
-    place, part = call(place, pieces(2, mark) + [first, second], coulombs[2], matrices)
-    sums.append(core_sum(part, (True, True)))
-    place, *sums[2] = lax.optimization_barrier((place, *sums[2]))
-    place, part = call(place, pieces(3, mark) + [first, second], coulombs[2], matrices)
-    sums.append(core_sum(part, (False, True)))
+    sums[:2] = [flat[:2], flat[2:]]
+    place, kept, given = call(place, pieces(3, mark) + [first, second], coulombs[2], matrices)
+    sums.append(core_sum(kept[0], given[0], (False, True)))
     terms = []
     for (dy, dx), both in zip(orders, sums):
         for dz in range(2):

time: 104 us -> 105 us (level)
  the two profiles are of different devices: /device:TPU:26 before, /device:TPU:16 now
where the time goes in v4:
time: 105 us
  waiting for transfers between devices  41.4 us (39%)
  Pallas kernels  28.9 us (28%)
  starting transfers between devices  26.2 us (25%)
  other arithmetic  6.28 us (6%)
  local copies, waits for them, and re-layouts  1.54 us (1%)
    ppermute x29, waiting for transfers between devices, receive(): return lax.ppermute(value, axes, pairs)  41.4 us
    pallas_call x4, Pallas kernels, exchange_part(): pl.pallas_call(functools.partial(pair_kernel, two_targets, stage), out_sh...  28.9 us
    ppermute x29, starting transfers between devices, receive(): return lax.ppermute(value, axes, pairs)  26.2 us
    mul x1, other arithmetic, coulomb_kernel(): coulomb_scale / (wave_sq + screen_wave * screen_wave) * weight[None, None...  2.1 us
  transfers between devices with their start and end apart: 29, of which 14 were waited for; matrix products, arithmetic and copies ran while one was open for 6% of the time, Pallas kernels for 27%

profile of v4, /device:TPU:16, one launch (start us, length us, event | category | flops | bytes accessed | tf_op | source)
XLA Modules:
  0.0 105.2 jit_solution(11906675838746138418)
XLA Ops:
  0.0 1.3 %collective-permute-start.3 = (bf16[16,64,128]{2,1,0:T(8,128)(2,1)}, bf16[16,64,128]{2,1,0:T(8,128)(2,1)S(1)}, u32[]{:S(2)}, u32[]{:S(2)}) collective-permute-start(bf16[16,64,128]{2,1,0:T(8,128)(2,1)} %bitcast.38), channel_id=1, source_target_pairs={{16,0},{17,1},{18,2},{19,3},{20,4},{21,5},{22,6},{23,7},{24,8},{25... | collective-permute-start | bytes 786440 | tf_op jit(solution)/shard_map/ppermute | solution.py:63
  1.3 2.1 %collective-permute-start.4 = (bf16[16,64,128]{2,1,0:T(8,128)(2,1)}, bf16[16,64,128]{2,1,0:T(8,128)(2,1)S(1)}, u32[]{:S(2)}, u32[]{:S(2)}) collective-permute-start(bf16[16,64,128]{2,1,0:T(8,128)(2,1)} %bitcast.39), channel_id=1, source_target_pairs={{18,0},{19,1},{16,2},{17,3},{22,4},{23,5},{20,6},{21,7},{26,8},{27... | collective-permute-start | bytes 786440 | tf_op jit(solution)/shard_map/ppermute | solution.py:63
  3.4 1.0 collective-permute-start.2
  4.4 4.2 %collective-permute-start.8 = (bf16[64,64,128]{2,1,0:T(8,128)(2,1)}, bf16[64,64,128]{2,1,0:T(8,128)(2,1)S(1)}, u32[]{:S(2)}, u32[]{:S(2)}) collective-permute-start(bf16[64,64,128]{2,1,0:T(8,128)(2,1)} %bitcast.47), channel_id=1, source_target_pairs={{1,0},{66,1},{51,2},{76,3},{5,4},{70,5},{55,6},{72,7},{9,8},{74,9}... | collective-permute-start | bytes 3145736 | tf_op jit(solution)/shard_map/ppermute | solution.py:63
  8.6 1.1 collective-permute-start.9
  9.6 0.1 broadcast_add_fusion
  9.7 0.7 dynamic-slice_bitcast_fusion
  10.4 0.8 select_reduce_fusion
  11.3 0.2 fusion.10
  11.5 0.6 fusion.14
  12.0 0.1 add.130
  12.8 1.2 %compare_select_fusion.1 = f32[128]{0:T(128)S(1)} fusion(f32[]{:T(128)} %bitcast.5, f32[]{:T(128)} %bitcast.4), kind=kLoop, calls=%fused_computation.28 | loop fusion | flops 256 | bytes 520 | tf_op jit(solution)/shard_map/jit(_where)/select_n | solution.py:110
  14.0 0.0 copy-start
  14.0 0.0 copy-start.1
  14.0 0.0 copy-start.2
  14.0 0.0 copy-start.3
  14.0 0.0 copy-start.4
  14.0 2.1 %fusion = (f32[64,64,128]{2,1,0:T(8,128)S(1)}, f32[64,64,128]{2,1,0:T(8,128)S(1)}, f32[64,64,128]{2,1,0:T(8,128)S(1)}) fusion(f32[128]{0:T(128)S(1)} %compare_select_fusion.1, f32[]{:T(128)} %bitcast.2, f32[128]{0:T(128)S(1)} %add.130, f32[64,64]{1,0:T(8,128)S(1)} %broadcast_add_fusion, f32[]{:T(128)} %bitcast.5, f32[]{:T(128)} %bitcast.4), kind=kLoop, calls=%fused_computation.2 | loop fusion | flops 3145728 | bytes 6308876 | tf_op jit(solution)/shard_map/mul | solution.py:111
  16.1 0.0 collective-permute-done.3.refs_5_
  16.2 0.6 collective-permute-start
  16.8 0.8 collective-permute-done.4.refs_7_
  17.6 0.0 collective-permute-done.2.refs_3_
  17.6 0.5 collective-permute-start.7
  18.1 6.4 %collective-permute-done.refs_1_ = bf16[16,64,128]{2,1,0:T(8,128)(2,1)S(1)} collective-permute-done((bf16[16,64,128]{2,1,0:T(8,128)(2,1)S(1)}, bf16[16,64,128]{2,1,0:T(8,128)(2,1)S(1)}, u32[]{:S(2)}, u32[]{:S(2)}) %collective-permute-start) | collective-permute-done | bytes 262176 | tf_op jit(solution)/shard_map/ppermute | solution.py:63
  24.6 0.5 collective-permute-start.1
  25.1 0.8 collective-permute-start.10
  25.8 0.2 collective-permute-done.6.refs_6_
  26.1 0.7 collective-permute-start.11
  26.8 5.2 %collective-permute-done.8.refs_9_.refs_5_ = bf16[64,64,128]{2,1,0:T(8,128)(2,1)S(1)} collective-permute-done((bf16[64,64,128]{2,1,0:T(8,128)(2,1)}, bf16[64,64,128]{2,1,0:T(8,128)(2,1)S(1)}, u32[]{:S(2)}, u32[]{:S(2)}) %collective-permute-start.8) | collective-permute-done | bytes 1048608 | tf_op jit(solution)/shard_map/ppermute | solution.py:63
  32.0 7.2 %shard_map.100 = (bf16[2,2,16,64,128]{4,3,2,1,0:T(8,128)(2,1)S(1)}, bf16[2,2,16,64,128]{4,3,2,1,0:T(8,128)(2,1)S(1)}) custom-call(s32[1]{0:T(128)} %bitcast.refs_0_, bf16[16,64,128]{2,1,0:T(8,128)(2,1)S(1)} %collective-permute-done.refs_1_, bf16[16,64,128]{2,1,0:T(8,128)(2,1)S(1)} %collective-permute-done.1.refs_2_, ...), custom_call_target="tpu_custom_call" | custom-call | flops 5000000000 | bytes 25165824 | tf_op jit(solution)/shard_map/pallas_call | solution.py:316
  39.2 7.6 %shard_map.101 = (bf16[2,2,16,64,128]{4,3,2,1,0:T(8,128)(2,1)S(1)}, bf16[2,2,16,64,128]{4,3,2,1,0:T(8,128)(2,1)S(1)}) custom-call(s32[1]{0:T(128)} %bitcast.refs_0_, bf16[16,64,128]{2,1,0:T(8,128)(2,1)S(1)} %collective-permute-done.refs_1_, bf16[16,64,128]{2,1,0:T(8,128)(2,1)S(1)} %collective-permute-done.1.refs_2_, ...), custom_call_target="tpu_custom_call" | custom-call | flops 5000000000 | bytes 25165824 | tf_op jit(solution)/shard_map/pallas_call | solution.py:316
  46.8 0.1 collective-permute-start.14
  46.9 0.5 collective-permute-start.12
  47.4 0.1 collective-permute-start.13
  47.5 1.4 %collective-permute-start.23 = (bf16[16,64,128]{2,1,0:T(8,128)(2,1)S(1)}, bf16[16,64,128]{2,1,0:T(8,128)(2,1)S(1)}, u32[]{:S(2)}, u32[]{:S(2)}) collective-permute-start(bf16[16,64,128]{2,1,0:T(8,128)(2,1)S(1)} %bitcast.44), channel_id=1, source_target_pairs={{2,0},{3,1},{0,2},{1,3},{6,4},{7,5},{4,6},{5,7},{10,8},{11,9},{8,1... | collective-permute-start | bytes 786440 | tf_op jit(solution)/shard_map/ppermute | solution.py:63
  48.8 1.0 collective-permute-done.12.refs_2_
  49.9 0.4 collective-permute-done.13.refs_4_
  50.2 7.1 %shard_map.102 = (bf16[1,2,16,64,128]{4,3,2,1,0:T(8,128)(2,1)S(1)}, bf16[1,2,16,64,128]{4,3,2,1,0:T(8,128)(2,1)S(1)}) custom-call(s32[1]{0:T(128)} %bitcast.refs_0_, bf16[16,64,128]{2,1,0:T(8,128)(2,1)S(1)} %collective-permute-done.10.refs_1_, bf16[16,64,128]{2,1,0:T(8,128)(2,1)S(1)} %collective-permute-done.12.refs_2_, ...), custom_call_target="tpu_custom_call" | custom-call | flops 5000000000 | bytes 25165824 | tf_op jit(solution)/shard_map/pallas_call | solution.py:316
  57.4 0.2 collective-permute-start.19
  57.6 0.4 collective-permute-start.21
  58.0 0.1 collective-permute-start.24
  58.1 0.4 collective-permute-start.25
  58.5 0.4 add_convert_fusion
  58.9 0.1 slice_bitcast_fusion
  59.0 0.7 collective-permute-done.24.refs_2_
  59.8 0.4 collective-permute-done.25.refs_4_
  60.1 7.1 %shard_map.103 = (bf16[1,2,16,64,128]{4,3,2,1,0:T(8,128)(2,1)S(1)}, bf16[1,2,16,64,128]{4,3,2,1,0:T(8,128)(2,1)S(1)}) custom-call(s32[1]{0:T(128)} %bitcast.refs_0_, bf16[16,64,128]{2,1,0:T(8,128)(2,1)S(1)} %bitcast.46, bf16[16,64,128]{2,1,0:T(8,128)(2,1)S(1)} %collective-permute-done.24.refs_2_, bf16[16,64,128]{2,1,0:T(8,128)(2,1)S(1)} %collective-permute-done.23.refs_3_, ...), custom_call_target="tpu_custom_call" | custom-call | flops 5000000000 | bytes 25165824 | tf_op jit(solution)/shard_map/pallas_call | solution.py:316
  67.3 0.2 collective-permute-start.27
  67.5 0.2 fusion.9
  67.7 1.0 collective-permute-start.20
  68.7 2.8 %collective-permute-start.22 = (bf16[16,64,128]{2,1,0:T(8,128)(2,1)S(1)}, bf16[16,64,128]{2,1,0:T(8,128)(2,1)S(1)}, u32[]{:S(2)}, u32[]{:S(2)}) collective-permute-start(bf16[16,64,128]{2,1,0:T(8,128)(2,1)S(1)} %get-tuple-element.84), channel_id=1, source_target_pairs={{22,0},{23,1},{20,2},{21,3},{18,4},{19,5},{16,6},{17,7},{30,8},{31... | collective-permute-start | bytes 786440 | tf_op jit(solution)/shard_map/ppermute | solution.py:63
  71.5 1.1 %collective-permute-start.15 = (bf16[16,64,128]{2,1,0:T(8,128)(2,1)S(1)}, bf16[16,64,128]{2,1,0:T(8,128)(2,1)S(1)}, u32[]{:S(2)}, u32[]{:S(2)}) collective-permute-start(bf16[16,64,128]{2,1,0:T(8,128)(2,1)S(1)} %get-tuple-element.65), channel_id=1, source_target_pairs={{4,0},{5,1},{6,2},{7,3},{0,4},{1,5},{2,6},{3,7},{12,8},{13,9},{14,... | collective-permute-start | bytes 786440 | tf_op jit(solution)/shard_map/ppermute | solution.py:63
  72.5 1.1 %collective-permute-start.16 = (bf16[16,64,128]{2,1,0:T(8,128)(2,1)S(1)}, bf16[16,64,128]{2,1,0:T(8,128)(2,1)S(1)}, u32[]{:S(2)}, u32[]{:S(2)}) collective-permute-start(bf16[16,64,128]{2,1,0:T(8,128)(2,1)S(1)} %get-tuple-element.66), channel_id=1, source_target_pairs={{6,0},{7,1},{4,2},{5,3},{2,4},{3,5},{0,6},{1,7},{14,8},{15,9},{12,... | collective-permute-start | bytes 786440 | tf_op jit(solution)/shard_map/ppermute | solution.py:63
  73.6 0.1 fusion.3
  73.7 4.1 %collective-permute-done.20 = bf16[16,64,128]{2,1,0:T(8,128)(2,1)S(1)} collective-permute-done((bf16[16,64,128]{2,1,0:T(8,128)(2,1)S(1)}, bf16[16,64,128]{2,1,0:T(8,128)(2,1)S(1)}, u32[]{:S(2)}, u32[]{:S(2)}) %collective-permute-start.20) | collective-permute-done | bytes 262176 | tf_op jit(solution)/shard_map/ppermute | solution.py:63
  77.9 1.5 %collective-permute-start.17 = (bf16[16,64,128]{2,1,0:T(8,128)(2,1)S(1)}, bf16[16,64,128]{2,1,0:T(8,128)(2,1)S(1)}, u32[]{:S(2)}, u32[]{:S(2)}) collective-permute-start(bf16[16,64,128]{2,1,0:T(8,128)(2,1)S(1)} %get-tuple-element.67), channel_id=1, source_target_pairs={{16,0},{17,1},{18,2},{19,3},{20,4},{21,5},{22,6},{23,7},{24,8},{25... | collective-permute-start | bytes 786440 | tf_op jit(solution)/shard_map/ppermute | solution.py:63
  79.4 4.9 %collective-permute-done.22 = bf16[16,64,128]{2,1,0:T(8,128)(2,1)S(1)} collective-permute-done((bf16[16,64,128]{2,1,0:T(8,128)(2,1)S(1)}, bf16[16,64,128]{2,1,0:T(8,128)(2,1)S(1)}, u32[]{:S(2)}, u32[]{:S(2)}) %collective-permute-start.22) | collective-permute-done | bytes 262176 | tf_op jit(solution)/shard_map/ppermute | solution.py:63
  84.3 1.7 %collective-permute-start.18 = (bf16[16,64,128]{2,1,0:T(8,128)(2,1)S(1)}, bf16[16,64,128]{2,1,0:T(8,128)(2,1)S(1)}, u32[]{:S(2)}, u32[]{:S(2)}) collective-permute-start(bf16[16,64,128]{2,1,0:T(8,128)(2,1)S(1)} %get-tuple-element.68), channel_id=1, source_target_pairs={{18,0},{19,1},{16,2},{17,3},{22,4},{23,5},{20,6},{21,7},{26,8},{27... | collective-permute-start | bytes 786440 | tf_op jit(solution)/shard_map/ppermute | solution.py:63
  86.0 1.0 collective-permute-start.28
  87.0 2.3 %collective-permute-done.15 = bf16[16,64,128]{2,1,0:T(8,128)(2,1)S(1)} collective-permute-done((bf16[16,64,128]{2,1,0:T(8,128)(2,1)S(1)}, bf16[16,64,128]{2,1,0:T(8,128)(2,1)S(1)}, u32[]{:S(2)}, u32[]{:S(2)}) %collective-permute-start.15) | collective-permute-done | bytes 262176 | tf_op jit(solution)/shard_map/ppermute | solution.py:63
  89.2 10.4 %collective-permute-done.16 = bf16[16,64,128]{2,1,0:T(8,128)(2,1)S(1)} collective-permute-done((bf16[16,64,128]{2,1,0:T(8,128)(2,1)S(1)}, bf16[16,64,128]{2,1,0:T(8,128)(2,1)S(1)}, u32[]{:S(2)}, u32[]{:S(2)}) %collective-permute-start.16) | collective-permute-done | bytes 262176 | tf_op jit(solution)/shard_map/ppermute | solution.py:63
  99.6 0.2 collective-permute-done.18
  99.8 4.3 %collective-permute-done.28 = bf16[16,64,128]{2,1,0:T(8,128)(2,1)S(1)} collective-permute-done((bf16[16,64,128]{2,1,0:T(8,128)(2,1)S(1)}, bf16[16,64,128]{2,1,0:T(8,128)(2,1)S(1)}, u32[]{:S(2)}, u32[]{:S(2)}) %collective-permute-start.28) | collective-permute-done | bytes 262176 | tf_op jit(solution)/shard_map/ppermute | solution.py:63
  104.0 1.2 %fusion.7 = f32[1,16,64,128]{3,2,1,0:T(8,128)} fusion(bf16[16,64,128]{2,1,0:T(8,128)(2,1)S(1)} %collective-permute-done.28, bf16[16,64,128]{2,1,0:T(8,128)(2,1)S(1)} %collective-permute-done.26, bf16[16,64,128]{2,1,0:T(8,128)(2,1)S(1)} %collective-permute-done.22, bf16[16,64,128]{2,1,0:T(8,128)(2,1)S(1)} %collective-permute-done.20, ...), kind=kLoop, calls=%fused_computation.11 | loop fusion | flops 2359296 | bytes 2883584 | tf_op jit(solution)/shard_map/neg | solution.py:421
  (25 shorter events, 0.1 us)
Async XLA Ops:
  0.0 16.2 %collective-permute-start.3 = (bf16[16,64,128]{2,1,0:T(8,128)(2,1)}, bf16[16,64,128]{2,1,0:T(8,128)(2,1)S(1)}, u32[]{:S(2)}, u32[]{:S(2)}) collective-permute-start(bf16[16,64,128]{2,1,0:T(8,128)(2,1)} %bitcast.38), channel_id=1, source_target_pairs={{16,0},{17,1},{18,2},{19,3},{20,4},{21,5},{22,6},{23,7},{24,8},{25... | collective-permute-start | bytes 786440 | tf_op jit(solution)/shard_map/ppermute | solution.py:63
  1.3 16.3 %collective-permute-start.4 = (bf16[16,64,128]{2,1,0:T(8,128)(2,1)}, bf16[16,64,128]{2,1,0:T(8,128)(2,1)S(1)}, u32[]{:S(2)}, u32[]{:S(2)}) collective-permute-start(bf16[16,64,128]{2,1,0:T(8,128)(2,1)} %bitcast.39), channel_id=1, source_target_pairs={{18,0},{19,1},{16,2},{17,3},{22,4},{23,5},{20,6},{21,7},{26,8},{27... | collective-permute-start | bytes 786440 | tf_op jit(solution)/shard_map/ppermute | solution.py:63
  3.4 14.2 %collective-permute-start.2 = (bf16[16,64,128]{2,1,0:T(8,128)(2,1)}, bf16[16,64,128]{2,1,0:T(8,128)(2,1)S(1)}, u32[]{:S(2)}, u32[]{:S(2)}) collective-permute-start(bf16[16,64,128]{2,1,0:T(8,128)(2,1)} %bitcast.40), channel_id=1, source_target_pairs={{6,0},{7,1},{4,2},{5,3},{2,4},{3,5},{0,6},{1,7},{14,8},{15,9},{12,... | collective-permute-start | bytes 786440 | tf_op jit(solution)/shard_map/ppermute | solution.py:63
  4.4 27.6 %collective-permute-start.8 = (bf16[64,64,128]{2,1,0:T(8,128)(2,1)}, bf16[64,64,128]{2,1,0:T(8,128)(2,1)S(1)}, u32[]{:S(2)}, u32[]{:S(2)}) collective-permute-start(bf16[64,64,128]{2,1,0:T(8,128)(2,1)} %bitcast.47), channel_id=1, source_target_pairs={{1,0},{66,1},{51,2},{76,3},{5,4},{70,5},{55,6},{72,7},{9,8},{74,9}... | collective-permute-start | bytes 3145736 | tf_op jit(solution)/shard_map/ppermute | solution.py:63
  8.6 30.6 %collective-permute-start.9 = (bf16[64,64,128]{2,1,0:T(8,128)(2,1)}, bf16[64,64,128]{2,1,0:T(8,128)(2,1)S(1)}, u32[]{:S(2)}, u32[]{:S(2)}) collective-permute-start(bf16[64,64,128]{2,1,0:T(8,128)(2,1)} %bitcast.48), channel_id=1, source_target_pairs={{61,0},{126,1},{15,2},{112,3},{57,4},{122,5},{11,6},{116,7},{53,8}... | collective-permute-start | bytes 3145736 | tf_op jit(solution)/shard_map/ppermute | solution.py:63
  14.0 2.2 %copy-start = (bf16[1,16,64,128]{3,2,1,0:T(8,128)(2,1)S(1)}, bf16[1,16,64,128]{3,2,1,0:T(8,128)(2,1)}, u32[]{:S(2)}) copy-start(bf16[1,16,64,128]{3,2,1,0:T(8,128)(2,1)} %param.10) | copy-start | bytes 786436
  14.0 18.0 %copy-start.1 = (bf16[256,256]{1,0:T(8,128)(2,1)S(1)}, bf16[256,256]{1,0:T(8,128)(2,1)}, u32[]{:S(2)}) copy-start(bf16[256,256]{1,0:T(8,128)(2,1)} %constant.44.clone.refs_13_.refs_10_) | copy-start | bytes 393220
  14.0 18.0 %copy-start.2 = (bf16[256,256]{1,0:T(8,128)(2,1)S(1)}, bf16[256,256]{1,0:T(8,128)(2,1)}, u32[]{:S(2)}) copy-start(bf16[256,256]{1,0:T(8,128)(2,1)} %constant.45.clone.refs_14_.refs_11_) | copy-start | bytes 393220
  14.0 18.0 %copy-start.3 = (bf16[128,128]{1,0:T(8,128)(2,1)S(1)}, bf16[128,128]{1,0:T(8,128)(2,1)}, u32[]{:S(2)}) copy-start(bf16[128,128]{1,0:T(8,128)(2,1)} %constant.42.clone.refs_11_.refs_8_) | copy-start | bytes 98308
  14.0 18.0 %copy-start.4 = (bf16[128,128]{1,0:T(8,128)(2,1)S(1)}, bf16[128,128]{1,0:T(8,128)(2,1)}, u32[]{:S(2)}) copy-start(bf16[128,128]{1,0:T(8,128)(2,1)} %constant.43.clone.refs_12_.refs_9_) | copy-start | bytes 98308
  16.2 8.4 %collective-permute-start = (bf16[16,64,128]{2,1,0:T(8,128)(2,1)S(1)}, bf16[16,64,128]{2,1,0:T(8,128)(2,1)S(1)}, u32[]{:S(2)}, u32[]{:S(2)}) collective-permute-start(bf16[16,64,128]{2,1,0:T(8,128)(2,1)S(1)} %bitcast.41), channel_id=1, source_target_pairs={{4,0},{5,1},{6,2},{7,3},{0,4},{1,5},{2,6},{3,7},{12,8},{13,9},{14,... | collective-permute-start | bytes 786440 | tf_op jit(solution)/shard_map/ppermute | solution.py:63
  17.6 7.0 %collective-permute-start.5 = (bf16[16,64,128]{2,1,0:T(8,128)(2,1)S(1)}, bf16[16,64,128]{2,1,0:T(8,128)(2,1)S(1)}, u32[]{:S(2)}, u32[]{:S(2)}) collective-permute-start(bf16[16,64,128]{2,1,0:T(8,128)(2,1)S(1)} %collective-permute-done.2.refs_3_), channel_id=1, source_target_pairs={{1,0},{0,1},{3,2},{2,3},{5,4},{4,5},{7,6},{6,7},{9,8},{8,9},{11,10... | collective-permute-start | bytes 786440 | tf_op jit(solution)/shard_map/ppermute | solution.py:63
  17.6 7.5 %collective-permute-start.7 = (bf16[16,64,128]{2,1,0:T(8,128)(2,1)S(1)}, bf16[16,64,128]{2,1,0:T(8,128)(2,1)S(1)}, u32[]{:S(2)}, u32[]{:S(2)}) collective-permute-start(bf16[16,64,128]{2,1,0:T(8,128)(2,1)S(1)} %collective-permute-done.4.refs_7_), channel_id=1, source_target_pairs={{1,0},{0,1},{3,2},{2,3},{5,4},{4,5},{7,6},{6,7},{9,8},{8,9},{11,10... | collective-permute-start | bytes 786440 | tf_op jit(solution)/shard_map/ppermute | solution.py:63
  24.6 1.5 %collective-permute-start.6 = (bf16[16,64,128]{2,1,0:T(8,128)(2,1)S(1)}, bf16[16,64,128]{2,1,0:T(8,128)(2,1)S(1)}, u32[]{:S(2)}, u32[]{:S(2)}) collective-permute-start(bf16[16,64,128]{2,1,0:T(8,128)(2,1)S(1)} %collective-permute-done.3.refs_5_), channel_id=1, source_target_pairs={{1,0},{0,1},{3,2},{2,3},{5,4},{4,5},{7,6},{6,7},{9,8},{8,9},{11,10... | collective-permute-start | bytes 786440 | tf_op jit(solution)/shard_map/ppermute | solution.py:63
  24.6 2.2 %collective-permute-start.1 = (bf16[16,64,128]{2,1,0:T(8,128)(2,1)S(1)}, bf16[16,64,128]{2,1,0:T(8,128)(2,1)S(1)}, u32[]{:S(2)}, u32[]{:S(2)}) collective-permute-start(bf16[16,64,128]{2,1,0:T(8,128)(2,1)S(1)} %collective-permute-done.refs_1_), channel_id=1, source_target_pairs={{1,0},{0,1},{3,2},{2,3},{5,4},{4,5},{7,6},{6,7},{9,8},{8,9},{11,10... | collective-permute-start | bytes 786440 | tf_op jit(solution)/shard_map/ppermute | solution.py:63
  25.1 21.8 %collective-permute-start.10 = (bf16[16,64,128]{2,1,0:T(8,128)(2,1)S(1)}, bf16[16,64,128]{2,1,0:T(8,128)(2,1)S(1)}, u32[]{:S(2)}, u32[]{:S(2)}) collective-permute-start(bf16[16,64,128]{2,1,0:T(8,128)(2,1)S(1)} %bitcast.42), channel_id=1, source_target_pairs={{20,0},{21,1},{22,2},{23,3},{16,4},{17,5},{18,6},{19,7},{28,8},{29... | collective-permute-start | bytes 786440 | tf_op jit(solution)/shard_map/ppermute | solution.py:63
  26.1 20.8 %collective-permute-start.11 = (bf16[16,64,128]{2,1,0:T(8,128)(2,1)S(1)}, bf16[16,64,128]{2,1,0:T(8,128)(2,1)S(1)}, u32[]{:S(2)}, u32[]{:S(2)}) collective-permute-start(bf16[16,64,128]{2,1,0:T(8,128)(2,1)S(1)} %bitcast.43), channel_id=1, source_target_pairs={{22,0},{23,1},{20,2},{21,3},{18,4},{19,5},{16,6},{17,7},{30,8},{31... | collective-permute-start | bytes 786440 | tf_op jit(solution)/shard_map/ppermute | solution.py:63
  46.8 11.7 %collective-permute-start.14 = (bf16[2,2,16,64,128]{4,3,2,1,0:T(8,128)(2,1)S(1)}, bf16[2,2,16,64,128]{4,3,2,1,0:T(8,128)(2,1)S(1)}, u32[]{:S(2)}, u32[]{:S(2)}) collective-permute-start(bf16[2,2,16,64,128]{4,3,2,1,0:T(8,128)(2,1)S(1)} %get-tuple-element.64), channel_id=1, source_target_pairs={{1,0},{0,1},{3,2},{2,3},{5,4},{4,5},{7,6},{6,7},{9,8},{8,9},{11,10... | collective-permute-start | bytes 3145736 | tf_op jit(solution)/shard_map/ppermute | solution.py:63
  46.9 3.0 %collective-permute-start.12 = (bf16[16,64,128]{2,1,0:T(8,128)(2,1)S(1)}, bf16[16,64,128]{2,1,0:T(8,128)(2,1)S(1)}, u32[]{:S(2)}, u32[]{:S(2)}) collective-permute-start(bf16[16,64,128]{2,1,0:T(8,128)(2,1)S(1)} %collective-permute-done.10.refs_1_), channel_id=1, source_target_pairs={{1,0},{0,1},{3,2},{2,3},{5,4},{4,5},{7,6},{6,7},{9,8},{8,9},{11,10... | collective-permute-start | bytes 786440 | tf_op jit(solution)/shard_map/ppermute | solution.py:63
  47.4 2.9 %collective-permute-start.13 = (bf16[16,64,128]{2,1,0:T(8,128)(2,1)S(1)}, bf16[16,64,128]{2,1,0:T(8,128)(2,1)S(1)}, u32[]{:S(2)}, u32[]{:S(2)}) collective-permute-start(bf16[16,64,128]{2,1,0:T(8,128)(2,1)S(1)} %collective-permute-done.11.refs_3_), channel_id=1, source_target_pairs={{1,0},{0,1},{3,2},{2,3},{5,4},{4,5},{7,6},{6,7},{9,8},{8,9},{11,10... | collective-permute-start | bytes 786440 | tf_op jit(solution)/shard_map/ppermute | solution.py:63
  47.5 10.5 %collective-permute-start.23 = (bf16[16,64,128]{2,1,0:T(8,128)(2,1)S(1)}, bf16[16,64,128]{2,1,0:T(8,128)(2,1)S(1)}, u32[]{:S(2)}, u32[]{:S(2)}) collective-permute-start(bf16[16,64,128]{2,1,0:T(8,128)(2,1)S(1)} %bitcast.44), channel_id=1, source_target_pairs={{2,0},{3,1},{0,2},{1,3},{6,4},{7,5},{4,6},{5,7},{10,8},{11,9},{8,1... | collective-permute-start | bytes 786440 | tf_op jit(solution)/shard_map/ppermute | solution.py:63
  57.4 10.1 %collective-permute-start.19 = (bf16[16,64,128]{2,1,0:T(8,128)(2,1)S(1)}, bf16[16,64,128]{2,1,0:T(8,128)(2,1)S(1)}, u32[]{:S(2)}, u32[]{:S(2)}) collective-permute-start(bf16[16,64,128]{2,1,0:T(8,128)(2,1)S(1)} %get-tuple-element.85), channel_id=1, source_target_pairs={{1,0},{0,1},{3,2},{2,3},{5,4},{4,5},{7,6},{6,7},{9,8},{8,9},{11,10... | collective-permute-start | bytes 786440 | tf_op jit(solution)/shard_map/ppermute | solution.py:63
  57.6 9.9 %collective-permute-start.21 = (bf16[16,64,128]{2,1,0:T(8,128)(2,1)S(1)}, bf16[16,64,128]{2,1,0:T(8,128)(2,1)S(1)}, u32[]{:S(2)}, u32[]{:S(2)}) collective-permute-start(bf16[16,64,128]{2,1,0:T(8,128)(2,1)S(1)} %get-tuple-element.86), channel_id=1, source_target_pairs={{1,0},{0,1},{3,2},{2,3},{5,4},{4,5},{7,6},{6,7},{9,8},{8,9},{11,10... | collective-permute-start | bytes 786440 | tf_op jit(solution)/shard_map/ppermute | solution.py:63
  58.0 1.8 %collective-permute-start.24 = (bf16[16,64,128]{2,1,0:T(8,128)(2,1)S(1)}, bf16[16,64,128]{2,1,0:T(8,128)(2,1)S(1)}, u32[]{:S(2)}, u32[]{:S(2)}) collective-permute-start(bf16[16,64,128]{2,1,0:T(8,128)(2,1)S(1)} %bitcast.45), channel_id=1, source_target_pairs={{1,0},{0,1},{3,2},{2,3},{5,4},{4,5},{7,6},{6,7},{9,8},{8,9},{11,10... | collective-permute-start | bytes 786440 | tf_op jit(solution)/shard_map/ppermute | solution.py:63
  58.1 2.0 %collective-permute-start.25 = (bf16[16,64,128]{2,1,0:T(8,128)(2,1)S(1)}, bf16[16,64,128]{2,1,0:T(8,128)(2,1)S(1)}, u32[]{:S(2)}, u32[]{:S(2)}) collective-permute-start(bf16[16,64,128]{2,1,0:T(8,128)(2,1)S(1)} %collective-permute-done.23.refs_3_), channel_id=1, source_target_pairs={{1,0},{0,1},{3,2},{2,3},{5,4},{4,5},{7,6},{6,7},{9,8},{8,9},{11,10... | collective-permute-start | bytes 786440 | tf_op jit(solution)/shard_map/ppermute | solution.py:63
  67.3 5.3 %collective-permute-start.27 = (bf16[16,64,128]{2,1,0:T(8,128)(2,1)S(1)}, bf16[16,64,128]{2,1,0:T(8,128)(2,1)S(1)}, u32[]{:S(2)}, u32[]{:S(2)}) collective-permute-start(bf16[16,64,128]{2,1,0:T(8,128)(2,1)S(1)} %get-tuple-element.88), channel_id=1, source_target_pairs={{1,0},{0,1},{3,2},{2,3},{5,4},{4,5},{7,6},{6,7},{9,8},{8,9},{11,10... | collective-permute-start | bytes 786440 | tf_op jit(solution)/shard_map/ppermute | solution.py:63
  67.7 10.2 %collective-permute-start.20 = (bf16[16,64,128]{2,1,0:T(8,128)(2,1)S(1)}, bf16[16,64,128]{2,1,0:T(8,128)(2,1)S(1)}, u32[]{:S(2)}, u32[]{:S(2)}) collective-permute-start(bf16[16,64,128]{2,1,0:T(8,128)(2,1)S(1)} %get-tuple-element.83), channel_id=1, source_target_pairs={{20,0},{21,1},{22,2},{23,3},{16,4},{17,5},{18,6},{19,7},{28,8},{29... | collective-permute-start | bytes 786440 | tf_op jit(solution)/shard_map/ppermute | solution.py:63
  68.7 15.6 %collective-permute-start.22 = (bf16[16,64,128]{2,1,0:T(8,128)(2,1)S(1)}, bf16[16,64,128]{2,1,0:T(8,128)(2,1)S(1)}, u32[]{:S(2)}, u32[]{:S(2)}) collective-permute-start(bf16[16,64,128]{2,1,0:T(8,128)(2,1)S(1)} %get-tuple-element.84), channel_id=1, source_target_pairs={{22,0},{23,1},{20,2},{21,3},{18,4},{19,5},{16,6},{17,7},{30,8},{31... | collective-permute-start | bytes 786440 | tf_op jit(solution)/shard_map/ppermute | solution.py:63
  71.5 14.5 %collective-permute-start.26 = (bf16[16,64,128]{2,1,0:T(8,128)(2,1)S(1)}, bf16[16,64,128]{2,1,0:T(8,128)(2,1)S(1)}, u32[]{:S(2)}, u32[]{:S(2)}) collective-permute-start(bf16[16,64,128]{2,1,0:T(8,128)(2,1)S(1)} %get-tuple-element.87), channel_id=1, source_target_pairs={{1,0},{0,1},{3,2},{2,3},{5,4},{4,5},{7,6},{6,7},{9,8},{8,9},{11,10... | collective-permute-start | bytes 786440 | tf_op jit(solution)/shard_map/ppermute | solution.py:63
  71.5 17.7 %collective-permute-start.15 = (bf16[16,64,128]{2,1,0:T(8,128)(2,1)S(1)}, bf16[16,64,128]{2,1,0:T(8,128)(2,1)S(1)}, u32[]{:S(2)}, u32[]{:S(2)}) collective-permute-start(bf16[16,64,128]{2,1,0:T(8,128)(2,1)S(1)} %get-tuple-element.65), channel_id=1, source_target_pairs={{4,0},{5,1},{6,2},{7,3},{0,4},{1,5},{2,6},{3,7},{12,8},{13,9},{14,... | collective-permute-start | bytes 786440 | tf_op jit(solution)/shard_map/ppermute | solution.py:63
  72.5 27.0 %collective-permute-start.16 = (bf16[16,64,128]{2,1,0:T(8,128)(2,1)S(1)}, bf16[16,64,128]{2,1,0:T(8,128)(2,1)S(1)}, u32[]{:S(2)}, u32[]{:S(2)}) collective-permute-start(bf16[16,64,128]{2,1,0:T(8,128)(2,1)S(1)} %get-tuple-element.66), channel_id=1, source_target_pairs={{6,0},{7,1},{4,2},{5,3},{2,4},{3,5},{0,6},{1,7},{14,8},{15,9},{12,... | collective-permute-start | bytes 786440 | tf_op jit(solution)/shard_map/ppermute | solution.py:63
  77.9 21.7 %collective-permute-start.17 = (bf16[16,64,128]{2,1,0:T(8,128)(2,1)S(1)}, bf16[16,64,128]{2,1,0:T(8,128)(2,1)S(1)}, u32[]{:S(2)}, u32[]{:S(2)}) collective-permute-start(bf16[16,64,128]{2,1,0:T(8,128)(2,1)S(1)} %get-tuple-element.67), channel_id=1, source_target_pairs={{16,0},{17,1},{18,2},{19,3},{20,4},{21,5},{22,6},{23,7},{24,8},{25... | collective-permute-start | bytes 786440 | tf_op jit(solution)/shard_map/ppermute | solution.py:63
  84.3 15.5 %collective-permute-start.18 = (bf16[16,64,128]{2,1,0:T(8,128)(2,1)S(1)}, bf16[16,64,128]{2,1,0:T(8,128)(2,1)S(1)}, u32[]{:S(2)}, u32[]{:S(2)}) collective-permute-start(bf16[16,64,128]{2,1,0:T(8,128)(2,1)S(1)} %get-tuple-element.68), channel_id=1, source_target_pairs={{18,0},{19,1},{16,2},{17,3},{22,4},{23,5},{20,6},{21,7},{26,8},{27... | collective-permute-start | bytes 786440 | tf_op jit(solution)/shard_map/ppermute | solution.py:63
  86.0 18.1 %collective-permute-start.28 = (bf16[16,64,128]{2,1,0:T(8,128)(2,1)S(1)}, bf16[16,64,128]{2,1,0:T(8,128)(2,1)S(1)}, u32[]{:S(2)}, u32[]{:S(2)}) collective-permute-start(bf16[16,64,128]{2,1,0:T(8,128)(2,1)S(1)} %fusion.3), channel_id=1, source_target_pairs={{2,0},{3,1},{0,2},{1,3},{6,4},{7,5},{4,6},{5,7},{10,8},{11,9},{8,1... | collective-permute-start | bytes 786440 | tf_op jit(solution)/shard_map/ppermute | solution.py:63

commit v5 on v4

--- a/solution.py
+++ b/solution.py
@@ -402,23 +402,27 @@
     halves[3][1] = receive(sent, offset_source(0, 0, 1, 0))
     place, kept, given = call(place, two + [second], coulombs[1], matrices, True, "last", earlier)
     crossed = receive(given, sibling)
-    place, kept_2, given_2 = call(place, pieces(2, mark) + [first, second], coulombs[2], matrices)
     summed = (kept.astype(f32) + crossed.astype(f32)).astype(bf16)
     sums = [[summed[n, dz] for dz in range(2)] for n in range(2)]
-    sums.append(core_sum(kept_2[0], given_2[0], (True, True)))
     place, *flat = lax.optimization_barrier((place, *sums[0], *sums[1]))
     sums[:2] = [flat[:2], flat[2:]]
+    place, kept, given = call(place, pieces(2, mark) + [first, second], coulombs[2], matrices)
+    sums.append(core_sum(kept[0], given[0], (True, True)))
+    place, *sums[2] = lax.optimization_barrier((place, *sums[2]))
     place, kept, given = call(place, pieces(3, mark) + [first, second], coulombs[2], matrices)
-    sums.append(core_sum(kept[0], given[0], (False, True)))
-    terms = []
-    for (dy, dx), both in zip(orders, sums):
+    crossed = receive(given[0, 1], sibling)
+    crossed_0 = receive(given[0, 0], sibling)
+    leaving = (kept[0, 1].astype(f32) + crossed.astype(f32)).astype(bf16)
+    leaving, kept_0 = lax.optimization_barrier((leaving, kept[0, 0]))
+    sums.append([kept_0.astype(f32) + crossed_0.astype(f32), leaving])
+    arrived = {}
+    for n, ((dy, dx), both) in enumerate(zip(orders, sums)):
         for dz in range(2):
-            if (dy, dx, dz) == (0, 0, 0):
-                terms.append(both[dz])
-            else:
-                arrived = receive(both[dz], offset_source(dy, dx, dz, 0))
-                terms.append(arrived.astype(f32))
-    return -sum(terms[1:], terms[0])[None]
+            if (dy, dx, dz) != (0, 0, 0):
+                arrived[n, dz] = receive(both[dz], offset_source(dy, dx, dz, 0)).astype(f32)
+    early = sum((arrived[n, dz] for n in range(3) for dz in range(2)), sums[3][0])
+    early = lax.optimization_barrier(early)
+    return -(early + arrived[3, 1])[None]
 
 
 def solution(mesh):

time: 105 us -> 113 us (1.076)
  the two profiles are of different devices: /device:TPU:16 before, /device:TPU:1 now
where the time goes in v5:
time: 113 us
  waiting for transfers between devices  44.3 us (39%)
  starting transfers between devices  30.5 us (27%)
  Pallas kernels  28.9 us (26%)
  other arithmetic  6.3 us (6%)
  local copies, waits for them, and re-layouts  1.55 us (1%)
    ppermute x29, waiting for transfers between devices, receive(): return lax.ppermute(value, axes, pairs)  44.3 us
    ppermute x29, starting transfers between devices, receive(): return lax.ppermute(value, axes, pairs)  30.5 us
    pallas_call x4, Pallas kernels, exchange_part(): pl.pallas_call(functools.partial(pair_kernel, two_targets, stage), out_sh...  28.9 us
  transfers between devices with their start and end apart: 29, of which 13 were waited for; matrix products, arithmetic and copies ran while one was open for 6% of the time, Pallas kernels for 19%

profile of v5, /device:TPU:1, one launch (start us, length us, event | category | flops | bytes accessed | tf_op | source)
XLA Modules:
  0.0 112.6 jit_solution(6753165007545567983)
XLA Ops:
  0.0 2.0 %collective-permute-start = (bf16[16,64,128]{2,1,0:T(8,128)(2,1)}, bf16[16,64,128]{2,1,0:T(8,128)(2,1)S(1)}, u32[]{:S(2)}, u32[]{:S(2)}) collective-permute-start(bf16[16,64,128]{2,1,0:T(8,128)(2,1)} %bitcast.37), channel_id=1, source_target_pairs={{4,0},{5,1},{6,2},{7,3},{0,4},{1,5},{2,6},{3,7},{12,8},{13,9},{14,... | collective-permute-start | bytes 786440 | tf_op jit(solution)/shard_map/ppermute | solution.py:63
  2.0 1.6 %collective-permute-start.2 = (bf16[16,64,128]{2,1,0:T(8,128)(2,1)}, bf16[16,64,128]{2,1,0:T(8,128)(2,1)S(1)}, u32[]{:S(2)}, u32[]{:S(2)}) collective-permute-start(bf16[16,64,128]{2,1,0:T(8,128)(2,1)} %bitcast.38), channel_id=1, source_target_pairs={{6,0},{7,1},{4,2},{5,3},{2,4},{3,5},{0,6},{1,7},{14,8},{15,9},{12,... | collective-permute-start | bytes 786440 | tf_op jit(solution)/shard_map/ppermute | solution.py:63
  3.6 1.3 %collective-permute-start.3 = (bf16[16,64,128]{2,1,0:T(8,128)(2,1)}, bf16[16,64,128]{2,1,0:T(8,128)(2,1)S(1)}, u32[]{:S(2)}, u32[]{:S(2)}) collective-permute-start(bf16[16,64,128]{2,1,0:T(8,128)(2,1)} %bitcast.39), channel_id=1, source_target_pairs={{16,0},{17,1},{18,2},{19,3},{20,4},{21,5},{22,6},{23,7},{24,8},{25... | collective-permute-start | bytes 786440 | tf_op jit(solution)/shard_map/ppermute | solution.py:63
  4.9 0.0 collective-permute-start.4
  4.9 1.5 %collective-permute-start.8 = (bf16[64,64,128]{2,1,0:T(8,128)(2,1)}, bf16[64,64,128]{2,1,0:T(8,128)(2,1)S(1)}, u32[]{:S(2)}, u32[]{:S(2)}) collective-permute-start(bf16[64,64,128]{2,1,0:T(8,128)(2,1)} %bitcast.46), channel_id=1, source_target_pairs={{1,0},{66,1},{51,2},{76,3},{5,4},{70,5},{55,6},{72,7},{9,8},{74,9}... | collective-permute-start | bytes 3145736 | tf_op jit(solution)/shard_map/ppermute | solution.py:63
  6.5 0.8 select_reduce_fusion
  7.3 0.7 dynamic-slice_bitcast_fusion
  8.0 0.2 fusion.6
  8.2 0.6 fusion.10
  8.8 1.2 %compare_select_fusion.1 = f32[128]{0:T(128)S(1)} fusion(f32[]{:T(128)} %bitcast.5, f32[]{:T(128)} %bitcast.4), kind=kLoop, calls=%fused_computation.26 | loop fusion | flops 256 | bytes 520 | tf_op jit(solution)/shard_map/jit(_where)/select_n | solution.py:110
  10.6 0.1 add.130
  10.7 0.1 broadcast_add_fusion
  10.8 7.1 %collective-permute-start.9 = (bf16[64,64,128]{2,1,0:T(8,128)(2,1)}, bf16[64,64,128]{2,1,0:T(8,128)(2,1)S(1)}, u32[]{:S(2)}, u32[]{:S(2)}) collective-permute-start(bf16[64,64,128]{2,1,0:T(8,128)(2,1)} %bitcast.47), channel_id=1, source_target_pairs={{61,0},{126,1},{15,2},{112,3},{57,4},{122,5},{11,6},{116,7},{53,8}... | collective-permute-start | bytes 3145736 | tf_op jit(solution)/shard_map/ppermute | solution.py:63
  17.9 0.0 collective-permute-done.3.refs_5_
  17.9 0.0 copy-start.2
  18.0 0.0 copy-start.3
  18.0 0.0 copy-start.4
  18.0 2.1 %fusion = (f32[64,64,128]{2,1,0:T(8,128)S(1)}, f32[64,64,128]{2,1,0:T(8,128)S(1)}, f32[64,64,128]{2,1,0:T(8,128)S(1)}) fusion(f32[128]{0:T(128)S(1)} %compare_select_fusion.1, f32[]{:T(128)} %bitcast.2, f32[128]{0:T(128)S(1)} %add.130, f32[64,64]{1,0:T(8,128)S(1)} %broadcast_add_fusion, f32[]{:T(128)} %bitcast.5, f32[]{:T(128)} %bitcast.4), kind=kLoop, calls=%fused_computation.2 | loop fusion | flops 3145728 | bytes 6308876 | tf_op jit(solution)/shard_map/mul | solution.py:111
  20.1 1.6 %collective-permute-start.5 = (bf16[16,64,128]{2,1,0:T(8,128)(2,1)S(1)}, bf16[16,64,128]{2,1,0:T(8,128)(2,1)S(1)}, u32[]{:S(2)}, u32[]{:S(2)}) collective-permute-start(bf16[16,64,128]{2,1,0:T(8,128)(2,1)S(1)} %collective-permute-done.2.refs_3_), channel_id=1, source_target_pairs={{1,0},{0,1},{3,2},{2,3},{5,4},{4,5},{7,6},{6,7},{9,8},{8,9},{11,10... | collective-permute-start | bytes 786440 | tf_op jit(solution)/shard_map/ppermute | solution.py:63
  21.7 0.0 collective-permute-start.6
  21.7 0.5 collective-permute-start.7
  22.2 0.6 collective-permute-done.5.refs_4_
  22.8 0.4 collective-permute-done.6.refs_6_
  23.2 0.4 collective-permute-done.7.refs_8_
  23.6 1.6 %collective-permute-done.8.refs_9_.refs_5_ = bf16[64,64,128]{2,1,0:T(8,128)(2,1)S(1)} collective-permute-done((bf16[64,64,128]{2,1,0:T(8,128)(2,1)}, bf16[64,64,128]{2,1,0:T(8,128)(2,1)S(1)}, u32[]{:S(2)}, u32[]{:S(2)}) %collective-permute-start.8) | collective-permute-done | bytes 1048608 | tf_op jit(solution)/shard_map/ppermute | solution.py:63
  25.2 7.2 %shard_map.100 = (bf16[2,2,16,64,128]{4,3,2,1,0:T(8,128)(2,1)S(1)}, bf16[2,2,16,64,128]{4,3,2,1,0:T(8,128)(2,1)S(1)}) custom-call(s32[1]{0:T(128)} %bitcast.refs_0_, bf16[16,64,128]{2,1,0:T(8,128)(2,1)S(1)} %collective-permute-done.refs_1_, bf16[16,64,128]{2,1,0:T(8,128)(2,1)S(1)} %collective-permute-done.1.refs_2_, ...), custom_call_target="tpu_custom_call" | custom-call | flops 5000000000 | bytes 25165824 | tf_op jit(solution)/shard_map/pallas_call | solution.py:316
  32.4 0.0 copy-start
  32.4 10.6 %collective-permute-done.9.refs_9_.refs_6_ = bf16[64,64,128]{2,1,0:T(8,128)(2,1)S(1)} collective-permute-done((bf16[64,64,128]{2,1,0:T(8,128)(2,1)}, bf16[64,64,128]{2,1,0:T(8,128)(2,1)S(1)}, u32[]{:S(2)}, u32[]{:S(2)}) %collective-permute-start.9) | collective-permute-done | bytes 1048608 | tf_op jit(solution)/shard_map/ppermute | solution.py:63
  43.0 7.5 %shard_map.101 = (bf16[2,2,16,64,128]{4,3,2,1,0:T(8,128)(2,1)S(1)}, bf16[2,2,16,64,128]{4,3,2,1,0:T(8,128)(2,1)S(1)}) custom-call(s32[1]{0:T(128)} %bitcast.refs_0_, bf16[16,64,128]{2,1,0:T(8,128)(2,1)S(1)} %collective-permute-done.refs_1_, bf16[16,64,128]{2,1,0:T(8,128)(2,1)S(1)} %collective-permute-done.1.refs_2_, ...), custom_call_target="tpu_custom_call" | custom-call | flops 5000000000 | bytes 25165824 | tf_op jit(solution)/shard_map/pallas_call | solution.py:316
  50.6 0.1 collective-permute-start.10
  50.7 0.1 collective-permute-start.11
  50.7 1.9 %collective-permute-start.12 = (bf16[16,64,128]{2,1,0:T(8,128)(2,1)S(1)}, bf16[16,64,128]{2,1,0:T(8,128)(2,1)S(1)}, u32[]{:S(2)}, u32[]{:S(2)}) collective-permute-start(bf16[16,64,128]{2,1,0:T(8,128)(2,1)S(1)} %bitcast.42), channel_id=1, source_target_pairs={{22,0},{23,1},{20,2},{21,3},{18,4},{19,5},{16,6},{17,7},{30,8},{31... | collective-permute-start | bytes 786440 | tf_op jit(solution)/shard_map/ppermute | solution.py:63
  52.6 6.4 %collective-permute-done.11.refs_1_ = bf16[16,64,128]{2,1,0:T(8,128)(2,1)S(1)} collective-permute-done((bf16[16,64,128]{2,1,0:T(8,128)(2,1)S(1)}, bf16[16,64,128]{2,1,0:T(8,128)(2,1)S(1)}, u32[]{:S(2)}, u32[]{:S(2)}) %collective-permute-start.11) | collective-permute-done | bytes 262176 | tf_op jit(solution)/shard_map/ppermute | solution.py:63
  59.1 5.2 %collective-permute-done.12.refs_3_ = bf16[16,64,128]{2,1,0:T(8,128)(2,1)S(1)} collective-permute-done((bf16[16,64,128]{2,1,0:T(8,128)(2,1)S(1)}, bf16[16,64,128]{2,1,0:T(8,128)(2,1)S(1)}, u32[]{:S(2)}, u32[]{:S(2)}) %collective-permute-start.12) | collective-permute-done | bytes 262176 | tf_op jit(solution)/shard_map/ppermute | solution.py:63
  64.2 1.3 %collective-permute-start.13 = (bf16[16,64,128]{2,1,0:T(8,128)(2,1)S(1)}, bf16[16,64,128]{2,1,0:T(8,128)(2,1)S(1)}, u32[]{:S(2)}, u32[]{:S(2)}) collective-permute-start(bf16[16,64,128]{2,1,0:T(8,128)(2,1)S(1)} %collective-permute-done.11.refs_1_), channel_id=1, source_target_pairs={{1,0},{0,1},{3,2},{2,3},{5,4},{4,5},{7,6},{6,7},{9,8},{8,9},{11,10... | collective-permute-start | bytes 786440 | tf_op jit(solution)/shard_map/ppermute | solution.py:63
  65.5 0.0 collective-permute-start.14
  65.5 1.6 %collective-permute-start.17 = (bf16[16,64,128]{2,1,0:T(8,128)(2,1)S(1)}, bf16[16,64,128]{2,1,0:T(8,128)(2,1)S(1)}, u32[]{:S(2)}, u32[]{:S(2)}) collective-permute-start(bf16[16,64,128]{2,1,0:T(8,128)(2,1)S(1)} %bitcast.43), channel_id=1, source_target_pairs={{2,0},{3,1},{0,2},{1,3},{6,4},{7,5},{4,6},{5,7},{10,8},{11,9},{8,1... | collective-permute-start | bytes 786440 | tf_op jit(solution)/shard_map/ppermute | solution.py:63
  67.2 0.4 add_convert_fusion
  67.6 0.1 slice_bitcast_fusion
  67.7 7.1 %shard_map.102 = (bf16[1,2,16,64,128]{4,3,2,1,0:T(8,128)(2,1)S(1)}, bf16[1,2,16,64,128]{4,3,2,1,0:T(8,128)(2,1)S(1)}) custom-call(s32[1]{0:T(128)} %bitcast.refs_0_, bf16[16,64,128]{2,1,0:T(8,128)(2,1)S(1)} %collective-permute-done.11.refs_1_, bf16[16,64,128]{2,1,0:T(8,128)(2,1)S(1)} %collective-permute-done.13.refs_2_, ...), custom_call_target="tpu_custom_call" | custom-call | flops 5000000000 | bytes 25165824 | tf_op jit(solution)/shard_map/pallas_call | solution.py:316
  74.9 0.9 collective-permute-start.16
  75.7 0.1 collective-permute-start.15
  75.8 0.4 collective-permute-start.18
  76.2 0.1 collective-permute-start.19
  76.3 0.2 collective-permute-start.25
  76.5 0.4 collective-permute-done.16
  76.9 1.3 %collective-permute-start.24 = (bf16[16,64,128]{2,1,0:T(8,128)(2,1)S(1)}, bf16[16,64,128]{2,1,0:T(8,128)(2,1)S(1)}, u32[]{:S(2)}, u32[]{:S(2)}) collective-permute-start(bf16[16,64,128]{2,1,0:T(8,128)(2,1)S(1)} %get-tuple-element.84), channel_id=1, source_target_pairs={{16,0},{17,1},{18,2},{19,3},{20,4},{21,5},{22,6},{23,7},{24,8},{25... | collective-permute-start | bytes 786440 | tf_op jit(solution)/shard_map/ppermute | solution.py:63
  78.1 0.2 fusion.4
  78.4 7.1 %shard_map.103 = (bf16[1,2,16,64,128]{4,3,2,1,0:T(8,128)(2,1)S(1)}, bf16[1,2,16,64,128]{4,3,2,1,0:T(8,128)(2,1)S(1)}) custom-call(s32[1]{0:T(128)} %bitcast.refs_0_, bf16[16,64,128]{2,1,0:T(8,128)(2,1)S(1)} %bitcast.45, bf16[16,64,128]{2,1,0:T(8,128)(2,1)S(1)} %collective-permute-done.18.refs_2_, bf16[16,64,128]{2,1,0:T(8,128)(2,1)S(1)} %collective-permute-done.17.refs_3_, ...), custom_call_target="tpu_custom_call" | custom-call | flops 5000000000 | bytes 25165824 | tf_op jit(solution)/shard_map/pallas_call | solution.py:316
  85.5 1.0 collective-permute-start.20
  86.5 0.6 collective-permute-start.23
  87.1 1.5 %collective-permute-start.22 = (bf16[16,64,128]{2,1,0:T(8,128)(2,1)S(1)}, bf16[16,64,128]{2,1,0:T(8,128)(2,1)S(1)}, u32[]{:S(2)}, u32[]{:S(2)}) collective-permute-start(bf16[16,64,128]{2,1,0:T(8,128)(2,1)S(1)} %get-tuple-element.82), channel_id=1, source_target_pairs={{4,0},{5,1},{6,2},{7,3},{0,4},{1,5},{2,6},{3,7},{12,8},{13,9},{14,... | collective-permute-start | bytes 786440 | tf_op jit(solution)/shard_map/ppermute | solution.py:63
  88.6 0.3 collective-permute-start.27
  88.9 0.9 collective-permute-done.24
  89.8 1.5 %collective-permute-start.26 = (bf16[16,64,128]{2,1,0:T(8,128)(2,1)S(1)}, bf16[16,64,128]{2,1,0:T(8,128)(2,1)S(1)}, u32[]{:S(2)}, u32[]{:S(2)}) collective-permute-start(bf16[16,64,128]{2,1,0:T(8,128)(2,1)S(1)} %get-tuple-element.86), channel_id=1, source_target_pairs={{20,0},{21,1},{22,2},{23,3},{16,4},{17,5},{18,6},{19,7},{28,8},{29... | collective-permute-start | bytes 786440 | tf_op jit(solution)/shard_map/ppermute | solution.py:63
  91.3 1.2 %collective-permute-start.21 = (bf16[16,64,128]{2,1,0:T(8,128)(2,1)S(1)}, bf16[16,64,128]{2,1,0:T(8,128)(2,1)S(1)}, u32[]{:S(2)}, u32[]{:S(2)}) collective-permute-start(bf16[16,64,128]{2,1,0:T(8,128)(2,1)S(1)} %get-tuple-element.94), channel_id=1, source_target_pairs={{1,0},{0,1},{3,2},{2,3},{5,4},{4,5},{7,6},{6,7},{9,8},{8,9},{11,10... | collective-permute-start | bytes 786440 | tf_op jit(solution)/shard_map/ppermute | solution.py:63
  92.5 0.1 fusion.3
  92.6 2.6 %collective-permute-done.23 = bf16[16,64,128]{2,1,0:T(8,128)(2,1)S(1)} collective-permute-done((bf16[16,64,128]{2,1,0:T(8,128)(2,1)S(1)}, bf16[16,64,128]{2,1,0:T(8,128)(2,1)S(1)}, u32[]{:S(2)}, u32[]{:S(2)}) %collective-permute-start.23) | collective-permute-done | bytes 262176 | tf_op jit(solution)/shard_map/ppermute | solution.py:63
  95.2 0.9 collective-permute-start.28
  96.1 4.4 %collective-permute-done.22 = bf16[16,64,128]{2,1,0:T(8,128)(2,1)S(1)} collective-permute-done((bf16[16,64,128]{2,1,0:T(8,128)(2,1)S(1)}, bf16[16,64,128]{2,1,0:T(8,128)(2,1)S(1)}, u32[]{:S(2)}, u32[]{:S(2)}) %collective-permute-start.22) | collective-permute-done | bytes 262176 | tf_op jit(solution)/shard_map/ppermute | solution.py:63
  100.5 5.6 %collective-permute-done.27 = bf16[16,64,128]{2,1,0:T(8,128)(2,1)S(1)} collective-permute-done((bf16[16,64,128]{2,1,0:T(8,128)(2,1)S(1)}, bf16[16,64,128]{2,1,0:T(8,128)(2,1)S(1)}, u32[]{:S(2)}, u32[]{:S(2)}) %collective-permute-start.27) | collective-permute-done | bytes 262176 | tf_op jit(solution)/shard_map/ppermute | solution.py:63
  106.1 5.3 %collective-permute-done.26 = bf16[16,64,128]{2,1,0:T(8,128)(2,1)S(1)} collective-permute-done((bf16[16,64,128]{2,1,0:T(8,128)(2,1)S(1)}, bf16[16,64,128]{2,1,0:T(8,128)(2,1)S(1)}, u32[]{:S(2)}, u32[]{:S(2)}) %collective-permute-start.26) | collective-permute-done | bytes 262176 | tf_op jit(solution)/shard_map/ppermute | solution.py:63
  111.3 0.3 convert_add_fusion.3
  111.7 0.9 negate_bitcast_fusion
  (27 shorter events, 0.2 us)
Async XLA Ops:
  0.0 10.8 %collective-permute-start = (bf16[16,64,128]{2,1,0:T(8,128)(2,1)}, bf16[16,64,128]{2,1,0:T(8,128)(2,1)S(1)}, u32[]{:S(2)}, u32[]{:S(2)}) collective-permute-start(bf16[16,64,128]{2,1,0:T(8,128)(2,1)} %bitcast.37), channel_id=1, source_target_pairs={{4,0},{5,1},{6,2},{7,3},{0,4},{1,5},{2,6},{3,7},{12,8},{13,9},{14,... | collective-permute-start | bytes 786440 | tf_op jit(solution)/shard_map/ppermute | solution.py:63
  2.0 18.1 %collective-permute-start.2 = (bf16[16,64,128]{2,1,0:T(8,128)(2,1)}, bf16[16,64,128]{2,1,0:T(8,128)(2,1)S(1)}, u32[]{:S(2)}, u32[]{:S(2)}) collective-permute-start(bf16[16,64,128]{2,1,0:T(8,128)(2,1)} %bitcast.38), channel_id=1, source_target_pairs={{6,0},{7,1},{4,2},{5,3},{2,4},{3,5},{0,6},{1,7},{14,8},{15,9},{12,... | collective-permute-start | bytes 786440 | tf_op jit(solution)/shard_map/ppermute | solution.py:63
  3.6 14.3 %collective-permute-start.3 = (bf16[16,64,128]{2,1,0:T(8,128)(2,1)}, bf16[16,64,128]{2,1,0:T(8,128)(2,1)S(1)}, u32[]{:S(2)}, u32[]{:S(2)}) collective-permute-start(bf16[16,64,128]{2,1,0:T(8,128)(2,1)} %bitcast.39), channel_id=1, source_target_pairs={{16,0},{17,1},{18,2},{19,3},{20,4},{21,5},{22,6},{23,7},{24,8},{25... | collective-permute-start | bytes 786440 | tf_op jit(solution)/shard_map/ppermute | solution.py:63
  4.9 15.2 %collective-permute-start.4 = (bf16[16,64,128]{2,1,0:T(8,128)(2,1)}, bf16[16,64,128]{2,1,0:T(8,128)(2,1)S(1)}, u32[]{:S(2)}, u32[]{:S(2)}) collective-permute-start(bf16[16,64,128]{2,1,0:T(8,128)(2,1)} %bitcast.40), channel_id=1, source_target_pairs={{18,0},{19,1},{16,2},{17,3},{22,4},{23,5},{20,6},{21,7},{26,8},{27... | collective-permute-start | bytes 786440 | tf_op jit(solution)/shard_map/ppermute | solution.py:63
  4.9 20.3 %collective-permute-start.8 = (bf16[64,64,128]{2,1,0:T(8,128)(2,1)}, bf16[64,64,128]{2,1,0:T(8,128)(2,1)S(1)}, u32[]{:S(2)}, u32[]{:S(2)}) collective-permute-start(bf16[64,64,128]{2,1,0:T(8,128)(2,1)} %bitcast.46), channel_id=1, source_target_pairs={{1,0},{66,1},{51,2},{76,3},{5,4},{70,5},{55,6},{72,7},{9,8},{74,9}... | collective-permute-start | bytes 3145736 | tf_op jit(solution)/shard_map/ppermute | solution.py:63
  10.8 32.2 %collective-permute-start.9 = (bf16[64,64,128]{2,1,0:T(8,128)(2,1)}, bf16[64,64,128]{2,1,0:T(8,128)(2,1)S(1)}, u32[]{:S(2)}, u32[]{:S(2)}) collective-permute-start(bf16[64,64,128]{2,1,0:T(8,128)(2,1)} %bitcast.47), channel_id=1, source_target_pairs={{61,0},{126,1},{15,2},{112,3},{57,4},{122,5},{11,6},{116,7},{53,8}... | collective-permute-start | bytes 3145736 | tf_op jit(solution)/shard_map/ppermute | solution.py:63
  17.9 3.8 %collective-permute-start.1 = (bf16[16,64,128]{2,1,0:T(8,128)(2,1)S(1)}, bf16[16,64,128]{2,1,0:T(8,128)(2,1)S(1)}, u32[]{:S(2)}, u32[]{:S(2)}) collective-permute-start(bf16[16,64,128]{2,1,0:T(8,128)(2,1)S(1)} %collective-permute-done.refs_1_), channel_id=1, source_target_pairs={{1,0},{0,1},{3,2},{2,3},{5,4},{4,5},{7,6},{6,7},{9,8},{8,9},{11,10... | collective-permute-start | bytes 786440 | tf_op jit(solution)/shard_map/ppermute | solution.py:63
  17.9 7.3 %copy-start.1 = (bf16[256,256]{1,0:T(8,128)(2,1)S(1)}, bf16[256,256]{1,0:T(8,128)(2,1)}, u32[]{:S(2)}) copy-start(bf16[256,256]{1,0:T(8,128)(2,1)} %constant.44.clone.refs_13_.refs_10_) | copy-start | bytes 393220
  17.9 7.3 %copy-start.2 = (bf16[256,256]{1,0:T(8,128)(2,1)S(1)}, bf16[256,256]{1,0:T(8,128)(2,1)}, u32[]{:S(2)}) copy-start(bf16[256,256]{1,0:T(8,128)(2,1)} %constant.45.clone.refs_14_.refs_11_) | copy-start | bytes 393220
  18.0 7.3 %copy-start.3 = (bf16[128,128]{1,0:T(8,128)(2,1)S(1)}, bf16[128,128]{1,0:T(8,128)(2,1)}, u32[]{:S(2)}) copy-start(bf16[128,128]{1,0:T(8,128)(2,1)} %constant.42.clone.refs_11_.refs_8_) | copy-start | bytes 98308
  18.0 7.3 %copy-start.4 = (bf16[128,128]{1,0:T(8,128)(2,1)S(1)}, bf16[128,128]{1,0:T(8,128)(2,1)}, u32[]{:S(2)}) copy-start(bf16[128,128]{1,0:T(8,128)(2,1)} %constant.43.clone.refs_12_.refs_9_) | copy-start | bytes 98308
  20.1 2.7 %collective-permute-start.5 = (bf16[16,64,128]{2,1,0:T(8,128)(2,1)S(1)}, bf16[16,64,128]{2,1,0:T(8,128)(2,1)S(1)}, u32[]{:S(2)}, u32[]{:S(2)}) collective-permute-start(bf16[16,64,128]{2,1,0:T(8,128)(2,1)S(1)} %collective-permute-done.2.refs_3_), channel_id=1, source_target_pairs={{1,0},{0,1},{3,2},{2,3},{5,4},{4,5},{7,6},{6,7},{9,8},{8,9},{11,10... | collective-permute-start | bytes 786440 | tf_op jit(solution)/shard_map/ppermute | solution.py:63
  21.7 1.5 %collective-permute-start.6 = (bf16[16,64,128]{2,1,0:T(8,128)(2,1)S(1)}, bf16[16,64,128]{2,1,0:T(8,128)(2,1)S(1)}, u32[]{:S(2)}, u32[]{:S(2)}) collective-permute-start(bf16[16,64,128]{2,1,0:T(8,128)(2,1)S(1)} %collective-permute-done.3.refs_5_), channel_id=1, source_target_pairs={{1,0},{0,1},{3,2},{2,3},{5,4},{4,5},{7,6},{6,7},{9,8},{8,9},{11,10... | collective-permute-start | bytes 786440 | tf_op jit(solution)/shard_map/ppermute | solution.py:63
  21.7 1.9 %collective-permute-start.7 = (bf16[16,64,128]{2,1,0:T(8,128)(2,1)S(1)}, bf16[16,64,128]{2,1,0:T(8,128)(2,1)S(1)}, u32[]{:S(2)}, u32[]{:S(2)}) collective-permute-start(bf16[16,64,128]{2,1,0:T(8,128)(2,1)S(1)} %collective-permute-done.4.refs_7_), channel_id=1, source_target_pairs={{1,0},{0,1},{3,2},{2,3},{5,4},{4,5},{7,6},{6,7},{9,8},{8,9},{11,10... | collective-permute-start | bytes 786440 | tf_op jit(solution)/shard_map/ppermute | solution.py:63
  32.4 18.2 %copy-start = (bf16[1,16,64,128]{3,2,1,0:T(8,128)(2,1)S(1)}, bf16[1,16,64,128]{3,2,1,0:T(8,128)(2,1)}, u32[]{:S(2)}) copy-start(bf16[1,16,64,128]{3,2,1,0:T(8,128)(2,1)} %param.10) | copy-start | bytes 786436
  50.6 16.6 %collective-permute-start.10 = (bf16[2,2,16,64,128]{4,3,2,1,0:T(8,128)(2,1)S(1)}, bf16[2,2,16,64,128]{4,3,2,1,0:T(8,128)(2,1)S(1)}, u32[]{:S(2)}, u32[]{:S(2)}) collective-permute-start(bf16[2,2,16,64,128]{4,3,2,1,0:T(8,128)(2,1)S(1)} %get-tuple-element.62), channel_id=1, source_target_pairs={{1,0},{0,1},{3,2},{2,3},{5,4},{4,5},{7,6},{6,7},{9,8},{8,9},{11,10... | collective-permute-start | bytes 3145736 | tf_op jit(solution)/shard_map/ppermute | solution.py:63
  50.7 8.4 %collective-permute-start.11 = (bf16[16,64,128]{2,1,0:T(8,128)(2,1)S(1)}, bf16[16,64,128]{2,1,0:T(8,128)(2,1)S(1)}, u32[]{:S(2)}, u32[]{:S(2)}) collective-permute-start(bf16[16,64,128]{2,1,0:T(8,128)(2,1)S(1)} %bitcast.41), channel_id=1, source_target_pairs={{20,0},{21,1},{22,2},{23,3},{16,4},{17,5},{18,6},{19,7},{28,8},{29... | collective-permute-start | bytes 786440 | tf_op jit(solution)/shard_map/ppermute | solution.py:63
  50.7 13.5 %collective-permute-start.12 = (bf16[16,64,128]{2,1,0:T(8,128)(2,1)S(1)}, bf16[16,64,128]{2,1,0:T(8,128)(2,1)S(1)}, u32[]{:S(2)}, u32[]{:S(2)}) collective-permute-start(bf16[16,64,128]{2,1,0:T(8,128)(2,1)S(1)} %bitcast.42), channel_id=1, source_target_pairs={{22,0},{23,1},{20,2},{21,3},{18,4},{19,5},{16,6},{17,7},{30,8},{31... | collective-permute-start | bytes 786440 | tf_op jit(solution)/shard_map/ppermute | solution.py:63
  64.2 3.4 %collective-permute-start.13 = (bf16[16,64,128]{2,1,0:T(8,128)(2,1)S(1)}, bf16[16,64,128]{2,1,0:T(8,128)(2,1)S(1)}, u32[]{:S(2)}, u32[]{:S(2)}) collective-permute-start(bf16[16,64,128]{2,1,0:T(8,128)(2,1)S(1)} %collective-permute-done.11.refs_1_), channel_id=1, source_target_pairs={{1,0},{0,1},{3,2},{2,3},{5,4},{4,5},{7,6},{6,7},{9,8},{8,9},{11,10... | collective-permute-start | bytes 786440 | tf_op jit(solution)/shard_map/ppermute | solution.py:63
  65.5 2.2 %collective-permute-start.14 = (bf16[16,64,128]{2,1,0:T(8,128)(2,1)S(1)}, bf16[16,64,128]{2,1,0:T(8,128)(2,1)S(1)}, u32[]{:S(2)}, u32[]{:S(2)}) collective-permute-start(bf16[16,64,128]{2,1,0:T(8,128)(2,1)S(1)} %collective-permute-done.12.refs_3_), channel_id=1, source_target_pairs={{1,0},{0,1},{3,2},{2,3},{5,4},{4,5},{7,6},{6,7},{9,8},{8,9},{11,10... | collective-permute-start | bytes 786440 | tf_op jit(solution)/shard_map/ppermute | solution.py:63
  65.5 10.3 %collective-permute-start.17 = (bf16[16,64,128]{2,1,0:T(8,128)(2,1)S(1)}, bf16[16,64,128]{2,1,0:T(8,128)(2,1)S(1)}, u32[]{:S(2)}, u32[]{:S(2)}) collective-permute-start(bf16[16,64,128]{2,1,0:T(8,128)(2,1)S(1)} %bitcast.43), channel_id=1, source_target_pairs={{2,0},{3,1},{0,2},{1,3},{6,4},{7,5},{4,6},{5,7},{10,8},{11,9},{8,1... | collective-permute-start | bytes 786440 | tf_op jit(solution)/shard_map/ppermute | solution.py:63
  74.9 2.0 %collective-permute-start.16 = (bf16[16,64,128]{2,1,0:T(8,128)(2,1)S(1)}, bf16[16,64,128]{2,1,0:T(8,128)(2,1)S(1)}, u32[]{:S(2)}, u32[]{:S(2)}) collective-permute-start(bf16[16,64,128]{2,1,0:T(8,128)(2,1)S(1)} %get-tuple-element.97), channel_id=1, source_target_pairs={{1,0},{0,1},{3,2},{2,3},{5,4},{4,5},{7,6},{6,7},{9,8},{8,9},{11,10... | collective-permute-start | bytes 786440 | tf_op jit(solution)/shard_map/ppermute | solution.py:63
  75.7 2.4 %collective-permute-start.15 = (bf16[16,64,128]{2,1,0:T(8,128)(2,1)S(1)}, bf16[16,64,128]{2,1,0:T(8,128)(2,1)S(1)}, u32[]{:S(2)}, u32[]{:S(2)}) collective-permute-start(bf16[16,64,128]{2,1,0:T(8,128)(2,1)S(1)} %get-tuple-element.98), channel_id=1, source_target_pairs={{1,0},{0,1},{3,2},{2,3},{5,4},{4,5},{7,6},{6,7},{9,8},{8,9},{11,10... | collective-permute-start | bytes 786440 | tf_op jit(solution)/shard_map/ppermute | solution.py:63
  75.8 2.5 %collective-permute-start.18 = (bf16[16,64,128]{2,1,0:T(8,128)(2,1)S(1)}, bf16[16,64,128]{2,1,0:T(8,128)(2,1)S(1)}, u32[]{:S(2)}, u32[]{:S(2)}) collective-permute-start(bf16[16,64,128]{2,1,0:T(8,128)(2,1)S(1)} %bitcast.44), channel_id=1, source_target_pairs={{1,0},{0,1},{3,2},{2,3},{5,4},{4,5},{7,6},{6,7},{9,8},{8,9},{11,10... | collective-permute-start | bytes 786440 | tf_op jit(solution)/shard_map/ppermute | solution.py:63
  76.2 2.1 %collective-permute-start.19 = (bf16[16,64,128]{2,1,0:T(8,128)(2,1)S(1)}, bf16[16,64,128]{2,1,0:T(8,128)(2,1)S(1)}, u32[]{:S(2)}, u32[]{:S(2)}) collective-permute-start(bf16[16,64,128]{2,1,0:T(8,128)(2,1)S(1)} %collective-permute-done.17.refs_3_), channel_id=1, source_target_pairs={{1,0},{0,1},{3,2},{2,3},{5,4},{4,5},{7,6},{6,7},{9,8},{8,9},{11,10... | collective-permute-start | bytes 786440 | tf_op jit(solution)/shard_map/ppermute | solution.py:63
  76.3 12.3 %collective-permute-start.25 = (bf16[16,64,128]{2,1,0:T(8,128)(2,1)S(1)}, bf16[16,64,128]{2,1,0:T(8,128)(2,1)S(1)}, u32[]{:S(2)}, u32[]{:S(2)}) collective-permute-start(bf16[16,64,128]{2,1,0:T(8,128)(2,1)S(1)} %get-tuple-element.85), channel_id=1, source_target_pairs={{18,0},{19,1},{16,2},{17,3},{22,4},{23,5},{20,6},{21,7},{26,8},{27... | collective-permute-start | bytes 786440 | tf_op jit(solution)/shard_map/ppermute | solution.py:63
  76.9 12.9 %collective-permute-start.24 = (bf16[16,64,128]{2,1,0:T(8,128)(2,1)S(1)}, bf16[16,64,128]{2,1,0:T(8,128)(2,1)S(1)}, u32[]{:S(2)}, u32[]{:S(2)}) collective-permute-start(bf16[16,64,128]{2,1,0:T(8,128)(2,1)S(1)} %get-tuple-element.84), channel_id=1, source_target_pairs={{16,0},{17,1},{18,2},{19,3},{20,4},{21,5},{22,6},{23,7},{24,8},{25... | collective-permute-start | bytes 786440 | tf_op jit(solution)/shard_map/ppermute | solution.py:63
  85.5 5.7 %collective-permute-start.20 = (bf16[16,64,128]{2,1,0:T(8,128)(2,1)S(1)}, bf16[16,64,128]{2,1,0:T(8,128)(2,1)S(1)}, u32[]{:S(2)}, u32[]{:S(2)}) collective-permute-start(bf16[16,64,128]{2,1,0:T(8,128)(2,1)S(1)} %get-tuple-element.93), channel_id=1, source_target_pairs={{1,0},{0,1},{3,2},{2,3},{5,4},{4,5},{7,6},{6,7},{9,8},{8,9},{11,10... | collective-permute-start | bytes 786440 | tf_op jit(solution)/shard_map/ppermute | solution.py:63
  86.5 8.7 %collective-permute-start.23 = (bf16[16,64,128]{2,1,0:T(8,128)(2,1)S(1)}, bf16[16,64,128]{2,1,0:T(8,128)(2,1)S(1)}, u32[]{:S(2)}, u32[]{:S(2)}) collective-permute-start(bf16[16,64,128]{2,1,0:T(8,128)(2,1)S(1)} %get-tuple-element.83), channel_id=1, source_target_pairs={{6,0},{7,1},{4,2},{5,3},{2,4},{3,5},{0,6},{1,7},{14,8},{15,9},{12,... | collective-permute-start | bytes 786440 | tf_op jit(solution)/shard_map/ppermute | solution.py:63
  87.1 13.4 %collective-permute-start.22 = (bf16[16,64,128]{2,1,0:T(8,128)(2,1)S(1)}, bf16[16,64,128]{2,1,0:T(8,128)(2,1)S(1)}, u32[]{:S(2)}, u32[]{:S(2)}) collective-permute-start(bf16[16,64,128]{2,1,0:T(8,128)(2,1)S(1)} %get-tuple-element.82), channel_id=1, source_target_pairs={{4,0},{5,1},{6,2},{7,3},{0,4},{1,5},{2,6},{3,7},{12,8},{13,9},{14,... | collective-permute-start | bytes 786440 | tf_op jit(solution)/shard_map/ppermute | solution.py:63
  88.6 17.5 %collective-permute-start.27 = (bf16[16,64,128]{2,1,0:T(8,128)(2,1)S(1)}, bf16[16,64,128]{2,1,0:T(8,128)(2,1)S(1)}, u32[]{:S(2)}, u32[]{:S(2)}) collective-permute-start(bf16[16,64,128]{2,1,0:T(8,128)(2,1)S(1)} %get-tuple-element.87), channel_id=1, source_target_pairs={{22,0},{23,1},{20,2},{21,3},{18,4},{19,5},{16,6},{17,7},{30,8},{31... | collective-permute-start | bytes 786440 | tf_op jit(solution)/shard_map/ppermute | solution.py:63
  89.8 21.6 %collective-permute-start.26 = (bf16[16,64,128]{2,1,0:T(8,128)(2,1)S(1)}, bf16[16,64,128]{2,1,0:T(8,128)(2,1)S(1)}, u32[]{:S(2)}, u32[]{:S(2)}) collective-permute-start(bf16[16,64,128]{2,1,0:T(8,128)(2,1)S(1)} %get-tuple-element.86), channel_id=1, source_target_pairs={{20,0},{21,1},{22,2},{23,3},{16,4},{17,5},{18,6},{19,7},{28,8},{29... | collective-permute-start | bytes 786440 | tf_op jit(solution)/shard_map/ppermute | solution.py:63
  91.3 20.1 %collective-permute-start.21 = (bf16[16,64,128]{2,1,0:T(8,128)(2,1)S(1)}, bf16[16,64,128]{2,1,0:T(8,128)(2,1)S(1)}, u32[]{:S(2)}, u32[]{:S(2)}) collective-permute-start(bf16[16,64,128]{2,1,0:T(8,128)(2,1)S(1)} %get-tuple-element.94), channel_id=1, source_target_pairs={{1,0},{0,1},{3,2},{2,3},{5,4},{4,5},{7,6},{6,7},{9,8},{8,9},{11,10... | collective-permute-start | bytes 786440 | tf_op jit(solution)/shard_map/ppermute | solution.py:63
  95.2 16.5 %collective-permute-start.28 = (bf16[16,64,128]{2,1,0:T(8,128)(2,1)S(1)}, bf16[16,64,128]{2,1,0:T(8,128)(2,1)S(1)}, u32[]{:S(2)}, u32[]{:S(2)}) collective-permute-start(bf16[16,64,128]{2,1,0:T(8,128)(2,1)S(1)} %fusion.3), channel_id=1, source_target_pairs={{2,0},{3,1},{0,2},{1,3},{6,4},{7,5},{4,6},{5,7},{10,8},{11,9},{8,1... | collective-permute-start | bytes 786440 | tf_op jit(solution)/shard_map/ppermute | solution.py:63

commit v6 on v5

--- a/solution.py
+++ b/solution.py
@@ -38,19 +38,19 @@
 
 def first_source(zh, y, x, zl, c):
     return {
-        (0, 0): (zh, y, x, 0, 1),
-        (0, 1): (zh ^ 1, y, x, 1, 0),
-        (1, 0): (zh, outer(y), x, 1, 1),
-        (1, 1): (zh ^ 1, y, outer(x), 0, 0),
+        (0, 0): (zh, y, outer(x), 0, 0),
+        (0, 1): (zh ^ 1, outer(y), outer(x), 1, 0),
+        (1, 0): (zh, y, x, 1, 1),
+        (1, 1): (zh ^ 1, outer(y), x, 0, 1),
     }[zl, c]
 
 
 def second_source(zh, y, x, zl, c):
     return {
-        (0, 0): (zh, outer(y), outer(x), 0, 1),
-        (0, 1): (zh ^ 1, outer(y), outer(x), 1, 0),
-        (1, 0): (zh, y, outer(x), 1, 1),
-        (1, 1): (zh ^ 1, outer(y), x, 0, 0),
+        (0, 0): (zh, outer(y), outer(x), 0, 0),
+        (0, 1): (zh ^ 1, y, outer(x), 1, 0),
+        (1, 0): (zh, outer(y), x, 1, 1),
+        (1, 1): (zh ^ 1, y, x, 0, 1),
     }[zl, c]
 
 
@@ -208,15 +208,13 @@
         for j in range(quarter):
             s_ref[pl.ds(plane + j, lanes, stride=pitch), :] = along_y[:, j * lanes : (j + 1) * lanes]
 
-    def forward(step, carry):
+    arrive(0)
+    forward_z(0)
+    for step in range(3):
         arrive(step + 1)
+    for step in range(3):
         forward_y(step)
         forward_z(step + 1)
-        return carry
-
-    arrive(0)
-    forward_z(0)
-    lax.fori_loop(0, 3, forward, 0)
     forward_y(3)
     k_copy.wait()
 
@@ -297,10 +295,16 @@
         return carry
 
     inverse_y(0)
-    lax.fori_loop(0, 3, inverse, 0)
+    if stage == "last":
+        lax.fori_loop(0, 3, inverse, 0)
+    else:
+        for step in range(3):
+            inverse_z(step)
+            inverse_y(step + 1)
     inverse_z(3)
-    for copy in put(3, 1):
-        copy.start()
+    for step in range(3 if stage == "last" else 0, 4):
+        for copy in put(step, step % 2):
+            copy.start()
     for step in range(4):
         for copy in put(step, step % 2):
             copy.wait()

time: 113 us -> 108 us (0.956)
  Pallas kernels: 28.9 us -> 25.6 us
  waiting for transfers between devices: 44.3 us -> 42.1 us
    pallas_call x4, Pallas kernels: 28.9 us -> 25.6 us  [exchange_part(): pl.pallas_call(functools.partial(pair_kernel, two_targets, stage), out_sh...]
    ppermute x29, waiting for transfers between devices: 44.3 us -> 42.1 us  [receive(): return lax.ppermute(value, axes, pairs)]
  transfers between devices with their start and end apart: 29 -> 29, of which waited for: 13 -> 13; matrix products, arithmetic and copies ran while one was open for 6% -> 6% of each run, Pallas kernels for 19% -> 17%
where the time goes in v6:
time: 108 us
  waiting for transfers between devices  42.1 us (39%)
  starting transfers between devices  31.6 us (29%)
  Pallas kernels  25.6 us (24%)
  other arithmetic  6.29 us (6%)
  local copies, waits for them, and re-layouts  1.54 us (1%)
    ppermute x29, waiting for transfers between devices, receive(): return lax.ppermute(value, axes, pairs)  42.1 us
    ppermute x29, starting transfers between devices, receive(): return lax.ppermute(value, axes, pairs)  31.6 us
    pallas_call x4, Pallas kernels, exchange_part(): pl.pallas_call(functools.partial(pair_kernel, two_targets, stage), out_sh...  25.6 us
  transfers between devices with their start and end apart: 29, of which 13 were waited for; matrix products, arithmetic and copies ran while one was open for 6% of the time, Pallas kernels for 17%

profile of v6, /device:TPU:1, one launch (start us, length us, event | category | flops | bytes accessed | tf_op | source)
XLA Modules:
  0.0 108.0 jit_solution(10274310222836751988)
XLA Ops:
  0.0 2.0 %collective-permute-start = (bf16[16,64,128]{2,1,0:T(8,128)(2,1)}, bf16[16,64,128]{2,1,0:T(8,128)(2,1)S(1)}, u32[]{:S(2)}, u32[]{:S(2)}) collective-permute-start(bf16[16,64,128]{2,1,0:T(8,128)(2,1)} %bitcast.37), channel_id=1, source_target_pairs={{4,0},{5,1},{6,2},{7,3},{0,4},{1,5},{2,6},{3,7},{12,8},{13,9},{14,... | collective-permute-start | bytes 786440 | tf_op jit(solution)/shard_map/ppermute | solution.py:63
  2.0 1.6 %collective-permute-start.2 = (bf16[16,64,128]{2,1,0:T(8,128)(2,1)}, bf16[16,64,128]{2,1,0:T(8,128)(2,1)S(1)}, u32[]{:S(2)}, u32[]{:S(2)}) collective-permute-start(bf16[16,64,128]{2,1,0:T(8,128)(2,1)} %bitcast.38), channel_id=1, source_target_pairs={{6,0},{7,1},{4,2},{5,3},{2,4},{3,5},{0,6},{1,7},{14,8},{15,9},{12,... | collective-permute-start | bytes 786440 | tf_op jit(solution)/shard_map/ppermute | solution.py:63
  3.6 1.3 %collective-permute-start.3 = (bf16[16,64,128]{2,1,0:T(8,128)(2,1)}, bf16[16,64,128]{2,1,0:T(8,128)(2,1)S(1)}, u32[]{:S(2)}, u32[]{:S(2)}) collective-permute-start(bf16[16,64,128]{2,1,0:T(8,128)(2,1)} %bitcast.39), channel_id=1, source_target_pairs={{16,0},{17,1},{18,2},{19,3},{20,4},{21,5},{22,6},{23,7},{24,8},{25... | collective-permute-start | bytes 786440 | tf_op jit(solution)/shard_map/ppermute | solution.py:63
  4.9 0.0 collective-permute-start.4
  4.9 5.9 %collective-permute-start.8 = (bf16[64,64,128]{2,1,0:T(8,128)(2,1)}, bf16[64,64,128]{2,1,0:T(8,128)(2,1)S(1)}, u32[]{:S(2)}, u32[]{:S(2)}) collective-permute-start(bf16[64,64,128]{2,1,0:T(8,128)(2,1)} %bitcast.46), channel_id=1, source_target_pairs={{12,0},{126,1},{3,2},{113,3},{8,4},{122,5},{7,6},{117,7},{4,8},{11... | collective-permute-start | bytes 3145736 | tf_op jit(solution)/shard_map/ppermute | solution.py:63
  10.9 0.8 select_reduce_fusion
  11.7 0.7 dynamic-slice_bitcast_fusion
  12.4 0.2 fusion.6
  12.6 0.6 fusion.10
  13.2 1.2 %compare_select_fusion.1 = f32[128]{0:T(128)S(1)} fusion(f32[]{:T(128)} %bitcast.5, f32[]{:T(128)} %bitcast.4), kind=kLoop, calls=%fused_computation.26 | loop fusion | flops 256 | bytes 520 | tf_op jit(solution)/shard_map/jit(_where)/select_n | solution.py:110
  15.0 0.1 add.130
  15.1 0.1 broadcast_add_fusion
  15.2 0.1 collective-permute-start.9
  15.3 0.0 collective-permute-done.3.refs_5_
  15.3 1.3 %collective-permute-start.1 = (bf16[16,64,128]{2,1,0:T(8,128)(2,1)S(1)}, bf16[16,64,128]{2,1,0:T(8,128)(2,1)S(1)}, u32[]{:S(2)}, u32[]{:S(2)}) collective-permute-start(bf16[16,64,128]{2,1,0:T(8,128)(2,1)S(1)} %collective-permute-done.refs_1_), channel_id=1, source_target_pairs={{1,0},{0,1},{3,2},{2,3},{5,4},{4,5},{7,6},{6,7},{9,8},{8,9},{11,10... | collective-permute-start | bytes 786440 | tf_op jit(solution)/shard_map/ppermute | solution.py:63
  16.6 2.1 %fusion = (f32[64,64,128]{2,1,0:T(8,128)S(1)}, f32[64,64,128]{2,1,0:T(8,128)S(1)}, f32[64,64,128]{2,1,0:T(8,128)S(1)}) fusion(f32[128]{0:T(128)S(1)} %compare_select_fusion.1, f32[]{:T(128)} %bitcast.2, f32[128]{0:T(128)S(1)} %add.130, f32[64,64]{1,0:T(8,128)S(1)} %broadcast_add_fusion, f32[]{:T(128)} %bitcast.5, f32[]{:T(128)} %bitcast.4), kind=kLoop, calls=%fused_computation.2 | loop fusion | flops 3145728 | bytes 6308876 | tf_op jit(solution)/shard_map/mul | solution.py:111
  18.7 0.5 collective-permute-done.4.refs_7_
  19.2 0.0 collective-permute-done.2.refs_3_
  19.2 2.5 %collective-permute-start.5 = (bf16[16,64,128]{2,1,0:T(8,128)(2,1)S(1)}, bf16[16,64,128]{2,1,0:T(8,128)(2,1)S(1)}, u32[]{:S(2)}, u32[]{:S(2)}) collective-permute-start(bf16[16,64,128]{2,1,0:T(8,128)(2,1)S(1)} %collective-permute-done.2.refs_3_), channel_id=1, source_target_pairs={{1,0},{0,1},{3,2},{2,3},{5,4},{4,5},{7,6},{6,7},{9,8},{8,9},{11,10... | collective-permute-start | bytes 786440 | tf_op jit(solution)/shard_map/ppermute | solution.py:63
  21.7 0.0 collective-permute-start.6
  21.7 0.0 collective-permute-done.1.refs_2_
  21.7 0.5 collective-permute-start.7
  22.2 0.6 collective-permute-done.5.refs_4_
  22.8 0.4 collective-permute-done.6.refs_6_
  23.2 0.4 collective-permute-done.7.refs_8_
  23.6 10.6 %collective-permute-done.8.refs_9_.refs_5_ = bf16[64,64,128]{2,1,0:T(8,128)(2,1)S(1)} collective-permute-done((bf16[64,64,128]{2,1,0:T(8,128)(2,1)}, bf16[64,64,128]{2,1,0:T(8,128)(2,1)S(1)}, u32[]{:S(2)}, u32[]{:S(2)}) %collective-permute-start.8) | collective-permute-done | bytes 1048608 | tf_op jit(solution)/shard_map/ppermute | solution.py:63
  34.2 6.2 %shard_map.100 = (bf16[2,2,16,64,128]{4,3,2,1,0:T(8,128)(2,1)S(1)}, bf16[2,2,16,64,128]{4,3,2,1,0:T(8,128)(2,1)S(1)}) custom-call(s32[1]{0:T(128)} %bitcast.refs_0_, bf16[16,64,128]{2,1,0:T(8,128)(2,1)S(1)} %collective-permute-done.refs_1_, bf16[16,64,128]{2,1,0:T(8,128)(2,1)S(1)} %collective-permute-done.1.refs_2_, ...), custom_call_target="tpu_custom_call" | custom-call | flops 5000000000 | bytes 25165824 | tf_op jit(solution)/shard_map/pallas_call | solution.py:320
  40.4 0.0 copy-start
  40.4 7.2 %shard_map.101 = (bf16[2,2,16,64,128]{4,3,2,1,0:T(8,128)(2,1)S(1)}, bf16[2,2,16,64,128]{4,3,2,1,0:T(8,128)(2,1)S(1)}) custom-call(s32[1]{0:T(128)} %bitcast.refs_0_, bf16[16,64,128]{2,1,0:T(8,128)(2,1)S(1)} %collective-permute-done.refs_1_, bf16[16,64,128]{2,1,0:T(8,128)(2,1)S(1)} %collective-permute-done.1.refs_2_, ...), custom_call_target="tpu_custom_call" | custom-call | flops 5000000000 | bytes 25165824 | tf_op jit(solution)/shard_map/pallas_call | solution.py:320
  47.7 0.3 collective-permute-start.10
  47.9 0.9 collective-permute-start.11
  48.8 0.0 collective-permute-start.12
  48.8 7.6 %collective-permute-done.11.refs_1_ = bf16[16,64,128]{2,1,0:T(8,128)(2,1)S(1)} collective-permute-done((bf16[16,64,128]{2,1,0:T(8,128)(2,1)S(1)}, bf16[16,64,128]{2,1,0:T(8,128)(2,1)S(1)}, u32[]{:S(2)}, u32[]{:S(2)}) %collective-permute-start.11) | collective-permute-done | bytes 262176 | tf_op jit(solution)/shard_map/ppermute | solution.py:63
  56.4 3.3 %collective-permute-done.12.refs_3_ = bf16[16,64,128]{2,1,0:T(8,128)(2,1)S(1)} collective-permute-done((bf16[16,64,128]{2,1,0:T(8,128)(2,1)S(1)}, bf16[16,64,128]{2,1,0:T(8,128)(2,1)S(1)}, u32[]{:S(2)}, u32[]{:S(2)}) %collective-permute-start.12) | collective-permute-done | bytes 262176 | tf_op jit(solution)/shard_map/ppermute | solution.py:63
  59.7 1.3 %collective-permute-start.13 = (bf16[16,64,128]{2,1,0:T(8,128)(2,1)S(1)}, bf16[16,64,128]{2,1,0:T(8,128)(2,1)S(1)}, u32[]{:S(2)}, u32[]{:S(2)}) collective-permute-start(bf16[16,64,128]{2,1,0:T(8,128)(2,1)S(1)} %collective-permute-done.11.refs_1_), channel_id=1, source_target_pairs={{1,0},{0,1},{3,2},{2,3},{5,4},{4,5},{7,6},{6,7},{9,8},{8,9},{11,10... | collective-permute-start | bytes 786440 | tf_op jit(solution)/shard_map/ppermute | solution.py:63
  60.9 0.0 collective-permute-start.14
  60.9 3.5 %collective-permute-start.17 = (bf16[16,64,128]{2,1,0:T(8,128)(2,1)S(1)}, bf16[16,64,128]{2,1,0:T(8,128)(2,1)S(1)}, u32[]{:S(2)}, u32[]{:S(2)}) collective-permute-start(bf16[16,64,128]{2,1,0:T(8,128)(2,1)S(1)} %bitcast.43), channel_id=1, source_target_pairs={{2,0},{3,1},{0,2},{1,3},{6,4},{7,5},{4,6},{5,7},{10,8},{11,9},{8,1... | collective-permute-start | bytes 786440 | tf_op jit(solution)/shard_map/ppermute | solution.py:63
  64.4 0.4 add_convert_fusion
  64.9 0.1 slice_bitcast_fusion
  65.0 6.1 %shard_map.102 = (bf16[1,2,16,64,128]{4,3,2,1,0:T(8,128)(2,1)S(1)}, bf16[1,2,16,64,128]{4,3,2,1,0:T(8,128)(2,1)S(1)}) custom-call(s32[1]{0:T(128)} %bitcast.refs_0_, bf16[16,64,128]{2,1,0:T(8,128)(2,1)S(1)} %collective-permute-done.11.refs_1_, bf16[16,64,128]{2,1,0:T(8,128)(2,1)S(1)} %collective-permute-done.13.refs_2_, ...), custom_call_target="tpu_custom_call" | custom-call | flops 5000000000 | bytes 25165824 | tf_op jit(solution)/shard_map/pallas_call | solution.py:320
  71.1 0.9 collective-permute-start.16
  72.0 0.1 collective-permute-start.15
  72.1 0.4 collective-permute-start.18
  72.5 0.1 collective-permute-start.19
  72.6 0.4 collective-permute-start.25
  73.0 0.2 collective-permute-done.16
  73.2 1.2 %collective-permute-start.24 = (bf16[16,64,128]{2,1,0:T(8,128)(2,1)S(1)}, bf16[16,64,128]{2,1,0:T(8,128)(2,1)S(1)}, u32[]{:S(2)}, u32[]{:S(2)}) collective-permute-start(bf16[16,64,128]{2,1,0:T(8,128)(2,1)S(1)} %get-tuple-element.84), channel_id=1, source_target_pairs={{16,0},{17,1},{18,2},{19,3},{20,4},{21,5},{22,6},{23,7},{24,8},{25... | collective-permute-start | bytes 786440 | tf_op jit(solution)/shard_map/ppermute | solution.py:63
  74.4 0.2 fusion.4
  74.6 6.1 %shard_map.103 = (bf16[1,2,16,64,128]{4,3,2,1,0:T(8,128)(2,1)S(1)}, bf16[1,2,16,64,128]{4,3,2,1,0:T(8,128)(2,1)S(1)}) custom-call(s32[1]{0:T(128)} %bitcast.refs_0_, bf16[16,64,128]{2,1,0:T(8,128)(2,1)S(1)} %bitcast.45, bf16[16,64,128]{2,1,0:T(8,128)(2,1)S(1)} %collective-permute-done.18.refs_2_, bf16[16,64,128]{2,1,0:T(8,128)(2,1)S(1)} %collective-permute-done.17.refs_3_, ...), custom_call_target="tpu_custom_call" | custom-call | flops 5000000000 | bytes 25165824 | tf_op jit(solution)/shard_map/pallas_call | solution.py:320
  80.8 1.1 %collective-permute-start.20 = (bf16[16,64,128]{2,1,0:T(8,128)(2,1)S(1)}, bf16[16,64,128]{2,1,0:T(8,128)(2,1)S(1)}, u32[]{:S(2)}, u32[]{:S(2)}) collective-permute-start(bf16[16,64,128]{2,1,0:T(8,128)(2,1)S(1)} %get-tuple-element.93), channel_id=1, source_target_pairs={{1,0},{0,1},{3,2},{2,3},{5,4},{4,5},{7,6},{6,7},{9,8},{8,9},{11,10... | collective-permute-start | bytes 786440 | tf_op jit(solution)/shard_map/ppermute | solution.py:63
  81.9 1.7 %collective-permute-start.23 = (bf16[16,64,128]{2,1,0:T(8,128)(2,1)S(1)}, bf16[16,64,128]{2,1,0:T(8,128)(2,1)S(1)}, u32[]{:S(2)}, u32[]{:S(2)}) collective-permute-start(bf16[16,64,128]{2,1,0:T(8,128)(2,1)S(1)} %get-tuple-element.83), channel_id=1, source_target_pairs={{6,0},{7,1},{4,2},{5,3},{2,4},{3,5},{0,6},{1,7},{14,8},{15,9},{12,... | collective-permute-start | bytes 786440 | tf_op jit(solution)/shard_map/ppermute | solution.py:63
  83.6 0.3 collective-permute-start.22
  83.9 1.2 %collective-permute-start.27 = (bf16[16,64,128]{2,1,0:T(8,128)(2,1)S(1)}, bf16[16,64,128]{2,1,0:T(8,128)(2,1)S(1)}, u32[]{:S(2)}, u32[]{:S(2)}) collective-permute-start(bf16[16,64,128]{2,1,0:T(8,128)(2,1)S(1)} %get-tuple-element.87), channel_id=1, source_target_pairs={{22,0},{23,1},{20,2},{21,3},{18,4},{19,5},{16,6},{17,7},{30,8},{31... | collective-permute-start | bytes 786440 | tf_op jit(solution)/shard_map/ppermute | solution.py:63
  85.1 0.9 collective-permute-done.24
  86.0 0.8 collective-permute-start.26
  86.8 1.6 %collective-permute-start.21 = (bf16[16,64,128]{2,1,0:T(8,128)(2,1)S(1)}, bf16[16,64,128]{2,1,0:T(8,128)(2,1)S(1)}, u32[]{:S(2)}, u32[]{:S(2)}) collective-permute-start(bf16[16,64,128]{2,1,0:T(8,128)(2,1)S(1)} %get-tuple-element.94), channel_id=1, source_target_pairs={{1,0},{0,1},{3,2},{2,3},{5,4},{4,5},{7,6},{6,7},{9,8},{8,9},{11,10... | collective-permute-start | bytes 786440 | tf_op jit(solution)/shard_map/ppermute | solution.py:63
  88.4 0.1 fusion.3
  88.5 2.1 %collective-permute-done.23 = bf16[16,64,128]{2,1,0:T(8,128)(2,1)S(1)} collective-permute-done((bf16[16,64,128]{2,1,0:T(8,128)(2,1)S(1)}, bf16[16,64,128]{2,1,0:T(8,128)(2,1)S(1)}, u32[]{:S(2)}, u32[]{:S(2)}) %collective-permute-start.23) | collective-permute-done | bytes 262176 | tf_op jit(solution)/shard_map/ppermute | solution.py:63
  90.6 0.8 collective-permute-start.28
  91.4 4.4 %collective-permute-done.22 = bf16[16,64,128]{2,1,0:T(8,128)(2,1)S(1)} collective-permute-done((bf16[16,64,128]{2,1,0:T(8,128)(2,1)S(1)}, bf16[16,64,128]{2,1,0:T(8,128)(2,1)S(1)}, u32[]{:S(2)}, u32[]{:S(2)}) %collective-permute-start.22) | collective-permute-done | bytes 262176 | tf_op jit(solution)/shard_map/ppermute | solution.py:63
  95.8 5.7 %collective-permute-done.27 = bf16[16,64,128]{2,1,0:T(8,128)(2,1)S(1)} collective-permute-done((bf16[16,64,128]{2,1,0:T(8,128)(2,1)S(1)}, bf16[16,64,128]{2,1,0:T(8,128)(2,1)S(1)}, u32[]{:S(2)}, u32[]{:S(2)}) %collective-permute-start.27) | collective-permute-done | bytes 262176 | tf_op jit(solution)/shard_map/ppermute | solution.py:63
  101.5 5.3 %collective-permute-done.26 = bf16[16,64,128]{2,1,0:T(8,128)(2,1)S(1)} collective-permute-done((bf16[16,64,128]{2,1,0:T(8,128)(2,1)S(1)}, bf16[16,64,128]{2,1,0:T(8,128)(2,1)S(1)}, u32[]{:S(2)}, u32[]{:S(2)}) %collective-permute-start.26) | collective-permute-done | bytes 262176 | tf_op jit(solution)/shard_map/ppermute | solution.py:63
  106.8 0.3 convert_add_fusion.3
  107.2 0.9 negate_bitcast_fusion
  (27 shorter events, 0.2 us)
Async XLA Ops:
  0.0 15.2 %collective-permute-start = (bf16[16,64,128]{2,1,0:T(8,128)(2,1)}, bf16[16,64,128]{2,1,0:T(8,128)(2,1)S(1)}, u32[]{:S(2)}, u32[]{:S(2)}) collective-permute-start(bf16[16,64,128]{2,1,0:T(8,128)(2,1)} %bitcast.37), channel_id=1, source_target_pairs={{4,0},{5,1},{6,2},{7,3},{0,4},{1,5},{2,6},{3,7},{12,8},{13,9},{14,... | collective-permute-start | bytes 786440 | tf_op jit(solution)/shard_map/ppermute | solution.py:63
  2.0 17.2 %collective-permute-start.2 = (bf16[16,64,128]{2,1,0:T(8,128)(2,1)}, bf16[16,64,128]{2,1,0:T(8,128)(2,1)S(1)}, u32[]{:S(2)}, u32[]{:S(2)}) collective-permute-start(bf16[16,64,128]{2,1,0:T(8,128)(2,1)} %bitcast.38), channel_id=1, source_target_pairs={{6,0},{7,1},{4,2},{5,3},{2,4},{3,5},{0,6},{1,7},{14,8},{15,9},{12,... | collective-permute-start | bytes 786440 | tf_op jit(solution)/shard_map/ppermute | solution.py:63
  3.6 11.6 %collective-permute-start.3 = (bf16[16,64,128]{2,1,0:T(8,128)(2,1)}, bf16[16,64,128]{2,1,0:T(8,128)(2,1)S(1)}, u32[]{:S(2)}, u32[]{:S(2)}) collective-permute-start(bf16[16,64,128]{2,1,0:T(8,128)(2,1)} %bitcast.39), channel_id=1, source_target_pairs={{16,0},{17,1},{18,2},{19,3},{20,4},{21,5},{22,6},{23,7},{24,8},{25... | collective-permute-start | bytes 786440 | tf_op jit(solution)/shard_map/ppermute | solution.py:63
  4.9 14.3 %collective-permute-start.4 = (bf16[16,64,128]{2,1,0:T(8,128)(2,1)}, bf16[16,64,128]{2,1,0:T(8,128)(2,1)S(1)}, u32[]{:S(2)}, u32[]{:S(2)}) collective-permute-start(bf16[16,64,128]{2,1,0:T(8,128)(2,1)} %bitcast.40), channel_id=1, source_target_pairs={{18,0},{19,1},{16,2},{17,3},{22,4},{23,5},{20,6},{21,7},{26,8},{27... | collective-permute-start | bytes 786440 | tf_op jit(solution)/shard_map/ppermute | solution.py:63
  4.9 29.3 %collective-permute-start.8 = (bf16[64,64,128]{2,1,0:T(8,128)(2,1)}, bf16[64,64,128]{2,1,0:T(8,128)(2,1)S(1)}, u32[]{:S(2)}, u32[]{:S(2)}) collective-permute-start(bf16[64,64,128]{2,1,0:T(8,128)(2,1)} %bitcast.46), channel_id=1, source_target_pairs={{12,0},{126,1},{3,2},{113,3},{8,4},{122,5},{7,6},{117,7},{4,8},{11... | collective-permute-start | bytes 3145736 | tf_op jit(solution)/shard_map/ppermute | solution.py:63
  15.2 25.2 %collective-permute-start.9 = (bf16[64,64,128]{2,1,0:T(8,128)(2,1)}, bf16[64,64,128]{2,1,0:T(8,128)(2,1)S(1)}, u32[]{:S(2)}, u32[]{:S(2)}) collective-permute-start(bf16[64,64,128]{2,1,0:T(8,128)(2,1)} %bitcast.47), channel_id=1, source_target_pairs={{60,0},{78,1},{51,2},{65,3},{56,4},{74,5},{55,6},{69,7},{52,8},{70... | collective-permute-start | bytes 3145736 | tf_op jit(solution)/shard_map/ppermute | solution.py:63
  15.3 6.4 %collective-permute-start.1 = (bf16[16,64,128]{2,1,0:T(8,128)(2,1)S(1)}, bf16[16,64,128]{2,1,0:T(8,128)(2,1)S(1)}, u32[]{:S(2)}, u32[]{:S(2)}) collective-permute-start(bf16[16,64,128]{2,1,0:T(8,128)(2,1)S(1)} %collective-permute-done.refs_1_), channel_id=1, source_target_pairs={{1,0},{0,1},{3,2},{2,3},{5,4},{4,5},{7,6},{6,7},{9,8},{8,9},{11,10... | collective-permute-start | bytes 786440 | tf_op jit(solution)/shard_map/ppermute | solution.py:63
  16.5 17.7 %copy-start.1 = (bf16[256,256]{1,0:T(8,128)(2,1)S(1)}, bf16[256,256]{1,0:T(8,128)(2,1)}, u32[]{:S(2)}) copy-start(bf16[256,256]{1,0:T(8,128)(2,1)} %constant.44.clone.refs_13_.refs_10_) | copy-start | bytes 393220
  16.5 17.7 %copy-start.2 = (bf16[256,256]{1,0:T(8,128)(2,1)S(1)}, bf16[256,256]{1,0:T(8,128)(2,1)}, u32[]{:S(2)}) copy-start(bf16[256,256]{1,0:T(8,128)(2,1)} %constant.45.clone.refs_14_.refs_11_) | copy-start | bytes 393220
  16.5 17.7 %copy-start.3 = (bf16[128,128]{1,0:T(8,128)(2,1)S(1)}, bf16[128,128]{1,0:T(8,128)(2,1)}, u32[]{:S(2)}) copy-start(bf16[128,128]{1,0:T(8,128)(2,1)} %constant.42.clone.refs_11_.refs_8_) | copy-start | bytes 98308
  16.5 17.7 %copy-start.4 = (bf16[128,128]{1,0:T(8,128)(2,1)S(1)}, bf16[128,128]{1,0:T(8,128)(2,1)}, u32[]{:S(2)}) copy-start(bf16[128,128]{1,0:T(8,128)(2,1)} %constant.43.clone.refs_12_.refs_9_) | copy-start | bytes 98308
  19.2 3.6 %collective-permute-start.5 = (bf16[16,64,128]{2,1,0:T(8,128)(2,1)S(1)}, bf16[16,64,128]{2,1,0:T(8,128)(2,1)S(1)}, u32[]{:S(2)}, u32[]{:S(2)}) collective-permute-start(bf16[16,64,128]{2,1,0:T(8,128)(2,1)S(1)} %collective-permute-done.2.refs_3_), channel_id=1, source_target_pairs={{1,0},{0,1},{3,2},{2,3},{5,4},{4,5},{7,6},{6,7},{9,8},{8,9},{11,10... | collective-permute-start | bytes 786440 | tf_op jit(solution)/shard_map/ppermute | solution.py:63
  21.7 1.5 %collective-permute-start.6 = (bf16[16,64,128]{2,1,0:T(8,128)(2,1)S(1)}, bf16[16,64,128]{2,1,0:T(8,128)(2,1)S(1)}, u32[]{:S(2)}, u32[]{:S(2)}) collective-permute-start(bf16[16,64,128]{2,1,0:T(8,128)(2,1)S(1)} %collective-permute-done.3.refs_5_), channel_id=1, source_target_pairs={{1,0},{0,1},{3,2},{2,3},{5,4},{4,5},{7,6},{6,7},{9,8},{8,9},{11,10... | collective-permute-start | bytes 786440 | tf_op jit(solution)/shard_map/ppermute | solution.py:63
  21.7 1.9 %collective-permute-start.7 = (bf16[16,64,128]{2,1,0:T(8,128)(2,1)S(1)}, bf16[16,64,128]{2,1,0:T(8,128)(2,1)S(1)}, u32[]{:S(2)}, u32[]{:S(2)}) collective-permute-start(bf16[16,64,128]{2,1,0:T(8,128)(2,1)S(1)} %collective-permute-done.4.refs_7_), channel_id=1, source_target_pairs={{1,0},{0,1},{3,2},{2,3},{5,4},{4,5},{7,6},{6,7},{9,8},{8,9},{11,10... | collective-permute-start | bytes 786440 | tf_op jit(solution)/shard_map/ppermute | solution.py:63
  40.4 7.5 %copy-start = (bf16[1,16,64,128]{3,2,1,0:T(8,128)(2,1)S(1)}, bf16[1,16,64,128]{3,2,1,0:T(8,128)(2,1)}, u32[]{:S(2)}) copy-start(bf16[1,16,64,128]{3,2,1,0:T(8,128)(2,1)} %param.10) | copy-start | bytes 786436
  47.7 16.8 %collective-permute-start.10 = (bf16[2,2,16,64,128]{4,3,2,1,0:T(8,128)(2,1)S(1)}, bf16[2,2,16,64,128]{4,3,2,1,0:T(8,128)(2,1)S(1)}, u32[]{:S(2)}, u32[]{:S(2)}) collective-permute-start(bf16[2,2,16,64,128]{4,3,2,1,0:T(8,128)(2,1)S(1)} %get-tuple-element.62), channel_id=1, source_target_pairs={{1,0},{0,1},{3,2},{2,3},{5,4},{4,5},{7,6},{6,7},{9,8},{8,9},{11,10... | collective-permute-start | bytes 3145736 | tf_op jit(solution)/shard_map/ppermute | solution.py:63
  47.9 8.4 %collective-permute-start.11 = (bf16[16,64,128]{2,1,0:T(8,128)(2,1)S(1)}, bf16[16,64,128]{2,1,0:T(8,128)(2,1)S(1)}, u32[]{:S(2)}, u32[]{:S(2)}) collective-permute-start(bf16[16,64,128]{2,1,0:T(8,128)(2,1)S(1)} %bitcast.41), channel_id=1, source_target_pairs={{20,0},{21,1},{22,2},{23,3},{16,4},{17,5},{18,6},{19,7},{28,8},{29... | collective-permute-start | bytes 786440 | tf_op jit(solution)/shard_map/ppermute | solution.py:63
  48.8 10.9 %collective-permute-start.12 = (bf16[16,64,128]{2,1,0:T(8,128)(2,1)S(1)}, bf16[16,64,128]{2,1,0:T(8,128)(2,1)S(1)}, u32[]{:S(2)}, u32[]{:S(2)}) collective-permute-start(bf16[16,64,128]{2,1,0:T(8,128)(2,1)S(1)} %bitcast.42), channel_id=1, source_target_pairs={{22,0},{23,1},{20,2},{21,3},{18,4},{19,5},{16,6},{17,7},{30,8},{31... | collective-permute-start | bytes 786440 | tf_op jit(solution)/shard_map/ppermute | solution.py:63
  59.7 5.3 %collective-permute-start.13 = (bf16[16,64,128]{2,1,0:T(8,128)(2,1)S(1)}, bf16[16,64,128]{2,1,0:T(8,128)(2,1)S(1)}, u32[]{:S(2)}, u32[]{:S(2)}) collective-permute-start(bf16[16,64,128]{2,1,0:T(8,128)(2,1)S(1)} %collective-permute-done.11.refs_1_), channel_id=1, source_target_pairs={{1,0},{0,1},{3,2},{2,3},{5,4},{4,5},{7,6},{6,7},{9,8},{8,9},{11,10... | collective-permute-start | bytes 786440 | tf_op jit(solution)/shard_map/ppermute | solution.py:63
  60.9 4.0 %collective-permute-start.14 = (bf16[16,64,128]{2,1,0:T(8,128)(2,1)S(1)}, bf16[16,64,128]{2,1,0:T(8,128)(2,1)S(1)}, u32[]{:S(2)}, u32[]{:S(2)}) collective-permute-start(bf16[16,64,128]{2,1,0:T(8,128)(2,1)S(1)} %collective-permute-done.12.refs_3_), channel_id=1, source_target_pairs={{1,0},{0,1},{3,2},{2,3},{5,4},{4,5},{7,6},{6,7},{9,8},{8,9},{11,10... | collective-permute-start | bytes 786440 | tf_op jit(solution)/shard_map/ppermute | solution.py:63
  60.9 11.2 %collective-permute-start.17 = (bf16[16,64,128]{2,1,0:T(8,128)(2,1)S(1)}, bf16[16,64,128]{2,1,0:T(8,128)(2,1)S(1)}, u32[]{:S(2)}, u32[]{:S(2)}) collective-permute-start(bf16[16,64,128]{2,1,0:T(8,128)(2,1)S(1)} %bitcast.43), channel_id=1, source_target_pairs={{2,0},{3,1},{0,2},{1,3},{6,4},{7,5},{4,6},{5,7},{10,8},{11,9},{8,1... | collective-permute-start | bytes 786440 | tf_op jit(solution)/shard_map/ppermute | solution.py:63
  71.1 2.0 %collective-permute-start.16 = (bf16[16,64,128]{2,1,0:T(8,128)(2,1)S(1)}, bf16[16,64,128]{2,1,0:T(8,128)(2,1)S(1)}, u32[]{:S(2)}, u32[]{:S(2)}) collective-permute-start(bf16[16,64,128]{2,1,0:T(8,128)(2,1)S(1)} %get-tuple-element.97), channel_id=1, source_target_pairs={{1,0},{0,1},{3,2},{2,3},{5,4},{4,5},{7,6},{6,7},{9,8},{8,9},{11,10... | collective-permute-start | bytes 786440 | tf_op jit(solution)/shard_map/ppermute | solution.py:63
  72.0 2.4 %collective-permute-start.15 = (bf16[16,64,128]{2,1,0:T(8,128)(2,1)S(1)}, bf16[16,64,128]{2,1,0:T(8,128)(2,1)S(1)}, u32[]{:S(2)}, u32[]{:S(2)}) collective-permute-start(bf16[16,64,128]{2,1,0:T(8,128)(2,1)S(1)} %get-tuple-element.98), channel_id=1, source_target_pairs={{1,0},{0,1},{3,2},{2,3},{5,4},{4,5},{7,6},{6,7},{9,8},{8,9},{11,10... | collective-permute-start | bytes 786440 | tf_op jit(solution)/shard_map/ppermute | solution.py:63
  72.1 2.5 %collective-permute-start.18 = (bf16[16,64,128]{2,1,0:T(8,128)(2,1)S(1)}, bf16[16,64,128]{2,1,0:T(8,128)(2,1)S(1)}, u32[]{:S(2)}, u32[]{:S(2)}) collective-permute-start(bf16[16,64,128]{2,1,0:T(8,128)(2,1)S(1)} %bitcast.44), channel_id=1, source_target_pairs={{1,0},{0,1},{3,2},{2,3},{5,4},{4,5},{7,6},{6,7},{9,8},{8,9},{11,10... | collective-permute-start | bytes 786440 | tf_op jit(solution)/shard_map/ppermute | solution.py:63
  72.5 2.1 %collective-permute-start.19 = (bf16[16,64,128]{2,1,0:T(8,128)(2,1)S(1)}, bf16[16,64,128]{2,1,0:T(8,128)(2,1)S(1)}, u32[]{:S(2)}, u32[]{:S(2)}) collective-permute-start(bf16[16,64,128]{2,1,0:T(8,128)(2,1)S(1)} %collective-permute-done.17.refs_3_), channel_id=1, source_target_pairs={{1,0},{0,1},{3,2},{2,3},{5,4},{4,5},{7,6},{6,7},{9,8},{8,9},{11,10... | collective-permute-start | bytes 786440 | tf_op jit(solution)/shard_map/ppermute | solution.py:63
  72.6 11.3 %collective-permute-start.25 = (bf16[16,64,128]{2,1,0:T(8,128)(2,1)S(1)}, bf16[16,64,128]{2,1,0:T(8,128)(2,1)S(1)}, u32[]{:S(2)}, u32[]{:S(2)}) collective-permute-start(bf16[16,64,128]{2,1,0:T(8,128)(2,1)S(1)} %get-tuple-element.85), channel_id=1, source_target_pairs={{18,0},{19,1},{16,2},{17,3},{22,4},{23,5},{20,6},{21,7},{26,8},{27... | collective-permute-start | bytes 786440 | tf_op jit(solution)/shard_map/ppermute | solution.py:63
  73.2 12.8 %collective-permute-start.24 = (bf16[16,64,128]{2,1,0:T(8,128)(2,1)S(1)}, bf16[16,64,128]{2,1,0:T(8,128)(2,1)S(1)}, u32[]{:S(2)}, u32[]{:S(2)}) collective-permute-start(bf16[16,64,128]{2,1,0:T(8,128)(2,1)S(1)} %get-tuple-element.84), channel_id=1, source_target_pairs={{16,0},{17,1},{18,2},{19,3},{20,4},{21,5},{22,6},{23,7},{24,8},{25... | collective-permute-start | bytes 786440 | tf_op jit(solution)/shard_map/ppermute | solution.py:63
  80.8 6.0 %collective-permute-start.20 = (bf16[16,64,128]{2,1,0:T(8,128)(2,1)S(1)}, bf16[16,64,128]{2,1,0:T(8,128)(2,1)S(1)}, u32[]{:S(2)}, u32[]{:S(2)}) collective-permute-start(bf16[16,64,128]{2,1,0:T(8,128)(2,1)S(1)} %get-tuple-element.93), channel_id=1, source_target_pairs={{1,0},{0,1},{3,2},{2,3},{5,4},{4,5},{7,6},{6,7},{9,8},{8,9},{11,10... | collective-permute-start | bytes 786440 | tf_op jit(solution)/shard_map/ppermute | solution.py:63
  81.9 8.7 %collective-permute-start.23 = (bf16[16,64,128]{2,1,0:T(8,128)(2,1)S(1)}, bf16[16,64,128]{2,1,0:T(8,128)(2,1)S(1)}, u32[]{:S(2)}, u32[]{:S(2)}) collective-permute-start(bf16[16,64,128]{2,1,0:T(8,128)(2,1)S(1)} %get-tuple-element.83), channel_id=1, source_target_pairs={{6,0},{7,1},{4,2},{5,3},{2,4},{3,5},{0,6},{1,7},{14,8},{15,9},{12,... | collective-permute-start | bytes 786440 | tf_op jit(solution)/shard_map/ppermute | solution.py:63
  83.6 12.2 %collective-permute-start.22 = (bf16[16,64,128]{2,1,0:T(8,128)(2,1)S(1)}, bf16[16,64,128]{2,1,0:T(8,128)(2,1)S(1)}, u32[]{:S(2)}, u32[]{:S(2)}) collective-permute-start(bf16[16,64,128]{2,1,0:T(8,128)(2,1)S(1)} %get-tuple-element.82), channel_id=1, source_target_pairs={{4,0},{5,1},{6,2},{7,3},{0,4},{1,5},{2,6},{3,7},{12,8},{13,9},{14,... | collective-permute-start | bytes 786440 | tf_op jit(solution)/shard_map/ppermute | solution.py:63
  83.9 17.7 %collective-permute-start.27 = (bf16[16,64,128]{2,1,0:T(8,128)(2,1)S(1)}, bf16[16,64,128]{2,1,0:T(8,128)(2,1)S(1)}, u32[]{:S(2)}, u32[]{:S(2)}) collective-permute-start(bf16[16,64,128]{2,1,0:T(8,128)(2,1)S(1)} %get-tuple-element.87), channel_id=1, source_target_pairs={{22,0},{23,1},{20,2},{21,3},{18,4},{19,5},{16,6},{17,7},{30,8},{31... | collective-permute-start | bytes 786440 | tf_op jit(solution)/shard_map/ppermute | solution.py:63
  86.0 20.8 %collective-permute-start.26 = (bf16[16,64,128]{2,1,0:T(8,128)(2,1)S(1)}, bf16[16,64,128]{2,1,0:T(8,128)(2,1)S(1)}, u32[]{:S(2)}, u32[]{:S(2)}) collective-permute-start(bf16[16,64,128]{2,1,0:T(8,128)(2,1)S(1)} %get-tuple-element.86), channel_id=1, source_target_pairs={{20,0},{21,1},{22,2},{23,3},{16,4},{17,5},{18,6},{19,7},{28,8},{29... | collective-permute-start | bytes 786440 | tf_op jit(solution)/shard_map/ppermute | solution.py:63
  86.8 20.0 %collective-permute-start.21 = (bf16[16,64,128]{2,1,0:T(8,128)(2,1)S(1)}, bf16[16,64,128]{2,1,0:T(8,128)(2,1)S(1)}, u32[]{:S(2)}, u32[]{:S(2)}) collective-permute-start(bf16[16,64,128]{2,1,0:T(8,128)(2,1)S(1)} %get-tuple-element.94), channel_id=1, source_target_pairs={{1,0},{0,1},{3,2},{2,3},{5,4},{4,5},{7,6},{6,7},{9,8},{8,9},{11,10... | collective-permute-start | bytes 786440 | tf_op jit(solution)/shard_map/ppermute | solution.py:63
  90.6 16.6 %collective-permute-start.28 = (bf16[16,64,128]{2,1,0:T(8,128)(2,1)S(1)}, bf16[16,64,128]{2,1,0:T(8,128)(2,1)S(1)}, u32[]{:S(2)}, u32[]{:S(2)}) collective-permute-start(bf16[16,64,128]{2,1,0:T(8,128)(2,1)S(1)} %fusion.3), channel_id=1, source_target_pairs={{2,0},{3,1},{0,2},{1,3},{6,4},{7,5},{4,6},{5,7},{10,8},{11,9},{8,1... | collective-permute-start | bytes 786440 | tf_op jit(solution)/shard_map/ppermute | solution.py:63

commit v7 on v6

--- a/solution.py
+++ b/solution.py
@@ -39,18 +39,18 @@
 def first_source(zh, y, x, zl, c):
     return {
         (0, 0): (zh, y, outer(x), 0, 0),
-        (0, 1): (zh ^ 1, outer(y), outer(x), 1, 0),
+        (0, 1): (zh ^ 1, outer(y), x, 1, 0),
         (1, 0): (zh, y, x, 1, 1),
-        (1, 1): (zh ^ 1, outer(y), x, 0, 1),
+        (1, 1): (zh ^ 1, outer(y), outer(x), 0, 1),
     }[zl, c]
 
 
 def second_source(zh, y, x, zl, c):
     return {
         (0, 0): (zh, outer(y), outer(x), 0, 0),
-        (0, 1): (zh ^ 1, y, outer(x), 1, 0),
+        (0, 1): (zh ^ 1, y, x, 1, 0),
         (1, 0): (zh, outer(y), x, 1, 1),
-        (1, 1): (zh ^ 1, y, x, 0, 1),
+        (1, 1): (zh ^ 1, y, outer(x), 0, 1),
     }[zl, c]
 
 
@@ -362,7 +362,6 @@
             source = offset_source(dy, dx, dz, 0)
             half.append(own if (dy, dx) == (0, 0) else receive(sent, source))
         halves.append(half)
-    second = receive(partner, second_source)
     matrices = section_matrices()
     device = lax.axis_index("tgt") * 4 + lax.axis_index("grp")
     slots = lax.dynamic_slice_in_dim(jnp.asarray(slot_table()), device, 1)[0]
@@ -394,18 +393,17 @@
     coulombs = [
         coulomb_kernel(screening, (weights[a], weights[b])) for a, b in ((0, 0), (1, 1), (0, 1))
     ]
-    *coulombs, halves[0][1], halves[1][1] = lax.optimization_barrier(
-        (*coulombs, halves[0][1], halves[1][1])
-    )
+    coulombs[2], late = lax.optimization_barrier((coulombs[2], partner))
+    second = receive(late, second_source)
     two = pieces(0) + pieces(1)
     place, *earlier = call(
         place, two + [first], coulombs[0], matrices, two_targets=True, stage="first"
     )
     mark = place
-    _, sent = lax.optimization_barrier((mark, own))
-    halves[3][1] = receive(sent, offset_source(0, 0, 1, 0))
     place, kept, given = call(place, two + [second], coulombs[1], matrices, True, "last", earlier)
     crossed = receive(given, sibling)
+    _, sent = lax.optimization_barrier((place, own))
+    halves[3][1] = receive(sent, offset_source(0, 0, 1, 0))
     summed = (kept.astype(f32) + crossed.astype(f32)).astype(bf16)
     sums = [[summed[n, dz] for dz in range(2)] for n in range(2)]
     place, *flat = lax.optimization_barrier((place, *sums[0], *sums[1]))

time: 108 us -> 130 us (1.20)
  starting transfers between devices: 31.6 us -> 43.6 us
  waiting for transfers between devices: 42.1 us -> 51.3 us
    ppermute x29, starting transfers between devices: 31.6 us -> 43.6 us  [receive(): return lax.ppermute(value, axes, pairs)]
    ppermute x29, waiting for transfers between devices: 42.1 us -> 51.3 us  [receive(): return lax.ppermute(value, axes, pairs)]
  transfers between devices with their start and end apart: 29 -> 29, of which waited for: 13 -> 14; matrix products, arithmetic and copies ran while one was open for 6% -> 6% of each run, Pallas kernels for 17% -> 14%
where the time goes in v7:
time: 130 us; the launch traced here: 129 us
  waiting for transfers between devices  51.3 us (39%)
  starting transfers between devices  43.6 us (34%)
  Pallas kernels  25.6 us (20%)
  other arithmetic  6.46 us (5%)
  local copies, waits for them, and re-layouts  1.58 us (1%)
    ppermute x29, waiting for transfers between devices, receive(): return lax.ppermute(value, axes, pairs)  51.3 us
    ppermute x29, starting transfers between devices, receive(): return lax.ppermute(value, axes, pairs)  43.6 us
    pallas_call x4, Pallas kernels, exchange_part(): pl.pallas_call(functools.partial(pair_kernel, two_targets, stage), out_sh...  25.6 us
  transfers between devices with their start and end apart: 29, of which 14 were waited for; matrix products, arithmetic and copies ran while one was open for 6% of the time, Pallas kernels for 14%

profile of v7, /device:TPU:1, one launch (start us, length us, event | category | flops | bytes accessed | tf_op | source)
XLA Modules:
  0.0 129.5 jit_solution(8040539390093671040)
XLA Ops:
  0.0 2.1 %collective-permute-start.4 = (bf16[16,64,128]{2,1,0:T(8,128)(2,1)}, bf16[16,64,128]{2,1,0:T(8,128)(2,1)S(1)}, u32[]{:S(2)}, u32[]{:S(2)}) collective-permute-start(bf16[16,64,128]{2,1,0:T(8,128)(2,1)} %bitcast.37), channel_id=1, source_target_pairs={{16,0},{17,1},{18,2},{19,3},{20,4},{21,5},{22,6},{23,7},{24,8},{25... | collective-permute-start | bytes 786440 | tf_op jit(solution)/shard_map/ppermute | solution.py:63
  2.1 1.5 %collective-permute-start.5 = (bf16[16,64,128]{2,1,0:T(8,128)(2,1)}, bf16[16,64,128]{2,1,0:T(8,128)(2,1)S(1)}, u32[]{:S(2)}, u32[]{:S(2)}) collective-permute-start(bf16[16,64,128]{2,1,0:T(8,128)(2,1)} %bitcast.38), channel_id=1, source_target_pairs={{18,0},{19,1},{16,2},{17,3},{22,4},{23,5},{20,6},{21,7},{26,8},{27... | collective-permute-start | bytes 786440 | tf_op jit(solution)/shard_map/ppermute | solution.py:63
  3.6 6.9 %collective-permute-start.8 = (bf16[64,64,128]{2,1,0:T(8,128)(2,1)}, bf16[64,64,128]{2,1,0:T(8,128)(2,1)S(1)}, u32[]{:S(2)}, u32[]{:S(2)}) collective-permute-start(bf16[64,64,128]{2,1,0:T(8,128)(2,1)} %bitcast.46), channel_id=1, source_target_pairs={{12,0},{114,1},{3,2},{125,3},{8,4},{118,5},{7,6},{121,7},{4,8},{12... | collective-permute-start | bytes 3145736 | tf_op jit(solution)/shard_map/ppermute | solution.py:63
  10.5 0.7 dynamic-slice_bitcast_fusion
  11.2 0.8 select_reduce_fusion
  12.1 0.2 fusion.6
  12.3 0.6 fusion.10
  12.9 0.1 broadcast_add_fusion
  12.9 0.1 add.130
  13.7 1.2 compare_select_fusion.1
  14.9 0.0 copy-start.5
  14.9 0.0 copy-start
  15.0 0.0 copy-start.1
  15.0 0.0 copy-start.2
  15.0 0.0 copy-start.3
  15.0 0.0 copy-start.4
  15.0 2.2 %fusion = (f32[64,64,128]{2,1,0:T(8,128)S(1)}, f32[64,64,128]{2,1,0:T(8,128)S(1)}, f32[64,64,128]{2,1,0:T(8,128)S(1)}) fusion(f32[]{:T(128)} %bitcast.6, f32[]{:T(128)} %bitcast.3, f32[128]{0:T(128)S(1)} %add.130, f32[64,64]{1,0:T(8,128)S(1)} %broadcast_add_fusion, f32[128]{0:T(128)S(1)} %compare_select_fusion.1, f32[]{:T(128)} %bitcast.5), kind=kLoop, calls=%fused_computation.2 | loop fusion | flops 3145728 | bytes 6308876 | tf_op jit(solution)/shard_map/mul | solution.py:111
  17.2 0.1 collective-permute-start.9
  17.3 0.1 collective-permute-start
  17.4 0.0 collective-permute-done.4.refs_5_
  17.4 0.1 collective-permute-start.2
  17.5 1.0 collective-permute-start.6
  18.5 6.8 %collective-permute-done.refs_1_ = bf16[16,64,128]{2,1,0:T(8,128)(2,1)S(1)} collective-permute-done((bf16[16,64,128]{2,1,0:T(8,128)(2,1)S(1)}, bf16[16,64,128]{2,1,0:T(8,128)(2,1)S(1)}, u32[]{:S(2)}, u32[]{:S(2)}) %collective-permute-start) | collective-permute-done | bytes 262176 | tf_op jit(solution)/shard_map/ppermute | solution.py:63
  25.4 1.2 collective-permute-start.7
  26.5 2.2 %collective-permute-done.2.refs_3_ = bf16[16,64,128]{2,1,0:T(8,128)(2,1)S(1)} collective-permute-done((bf16[16,64,128]{2,1,0:T(8,128)(2,1)S(1)}, bf16[16,64,128]{2,1,0:T(8,128)(2,1)S(1)}, u32[]{:S(2)}, u32[]{:S(2)}) %collective-permute-start.2) | collective-permute-done | bytes 262176 | tf_op jit(solution)/shard_map/ppermute | solution.py:63
  28.8 1.4 %collective-permute-start.1 = (bf16[16,64,128]{2,1,0:T(8,128)(2,1)S(1)}, bf16[16,64,128]{2,1,0:T(8,128)(2,1)S(1)}, u32[]{:S(2)}, u32[]{:S(2)}) collective-permute-start(bf16[16,64,128]{2,1,0:T(8,128)(2,1)S(1)} %collective-permute-done.refs_1_), channel_id=1, source_target_pairs={{1,0},{0,1},{3,2},{2,3},{5,4},{4,5},{7,6},{6,7},{9,8},{8,9},{11,10... | collective-permute-start | bytes 786440 | tf_op jit(solution)/shard_map/ppermute | solution.py:63
  30.1 0.0 collective-permute-start.3
  30.2 1.1 collective-permute-done.1.refs_2_
  31.3 0.4 collective-permute-done.3.refs_4_
  31.7 2.1 %collective-permute-done.8.refs_9_.refs_5_ = bf16[64,64,128]{2,1,0:T(8,128)(2,1)S(1)} collective-permute-done((bf16[64,64,128]{2,1,0:T(8,128)(2,1)}, bf16[64,64,128]{2,1,0:T(8,128)(2,1)S(1)}, u32[]{:S(2)}, u32[]{:S(2)}) %collective-permute-start.8) | collective-permute-done | bytes 1048608 | tf_op jit(solution)/shard_map/ppermute | solution.py:63
  33.8 6.2 %shard_map.100 = (bf16[2,2,16,64,128]{4,3,2,1,0:T(8,128)(2,1)S(1)}, bf16[2,2,16,64,128]{4,3,2,1,0:T(8,128)(2,1)S(1)}) custom-call(s32[1]{0:T(128)} %bitcast.refs_0_, bf16[16,64,128]{2,1,0:T(8,128)(2,1)S(1)} %collective-permute-done.refs_1_, bf16[16,64,128]{2,1,0:T(8,128)(2,1)S(1)} %collective-permute-done.1.refs_2_, ...), custom_call_target="tpu_custom_call" | custom-call | flops 5000000000 | bytes 25165824 | tf_op jit(solution)/shard_map/pallas_call | solution.py:320
  40.0 13.4 %collective-permute-done.9.refs_9_.refs_6_ = bf16[64,64,128]{2,1,0:T(8,128)(2,1)S(1)} collective-permute-done((bf16[64,64,128]{2,1,0:T(8,128)(2,1)S(1)}, bf16[64,64,128]{2,1,0:T(8,128)(2,1)S(1)}, u32[]{:S(2)}, u32[]{:S(2)}) %collective-permute-start.9) | collective-permute-done | bytes 1048608 | tf_op jit(solution)/shard_map/ppermute | solution.py:63
  53.5 7.2 %shard_map.101 = (bf16[2,2,16,64,128]{4,3,2,1,0:T(8,128)(2,1)S(1)}, bf16[2,2,16,64,128]{4,3,2,1,0:T(8,128)(2,1)S(1)}) custom-call(s32[1]{0:T(128)} %bitcast.refs_0_, bf16[16,64,128]{2,1,0:T(8,128)(2,1)S(1)} %collective-permute-done.refs_1_, bf16[16,64,128]{2,1,0:T(8,128)(2,1)S(1)} %collective-permute-done.1.refs_2_, ...), custom_call_target="tpu_custom_call" | custom-call | flops 5000000000 | bytes 25165824 | tf_op jit(solution)/shard_map/pallas_call | solution.py:320
  60.7 4.0 %collective-permute-start.10 = (bf16[2,2,16,64,128]{4,3,2,1,0:T(8,128)(2,1)S(1)}, bf16[2,2,16,64,128]{4,3,2,1,0:T(8,128)(2,1)S(1)}, u32[]{:S(2)}, u32[]{:S(2)}) collective-permute-start(bf16[2,2,16,64,128]{4,3,2,1,0:T(8,128)(2,1)S(1)} %get-tuple-element.56), channel_id=1, source_target_pairs={{1,0},{0,1},{3,2},{2,3},{5,4},{4,5},{7,6},{6,7},{9,8},{8,9},{11,10... | collective-permute-start | bytes 3145736 | tf_op jit(solution)/shard_map/ppermute | solution.py:63
  64.7 3.5 %collective-permute-start.17 = (bf16[16,64,128]{2,1,0:T(8,128)(2,1)S(1)}, bf16[16,64,128]{2,1,0:T(8,128)(2,1)S(1)}, u32[]{:S(2)}, u32[]{:S(2)}) collective-permute-start(bf16[16,64,128]{2,1,0:T(8,128)(2,1)S(1)} %bitcast.43), channel_id=1, source_target_pairs={{2,0},{3,1},{0,2},{1,3},{6,4},{7,5},{4,6},{5,7},{10,8},{11,9},{8,1... | collective-permute-start | bytes 786440 | tf_op jit(solution)/shard_map/ppermute | solution.py:63
  68.2 5.1 %collective-permute-done.11.refs_1_ = bf16[16,64,128]{2,1,0:T(8,128)(2,1)S(1)} collective-permute-done((bf16[16,64,128]{2,1,0:T(8,128)(2,1)S(1)}, bf16[16,64,128]{2,1,0:T(8,128)(2,1)S(1)}, u32[]{:S(2)}, u32[]{:S(2)}) %collective-permute-start.11) | collective-permute-done | bytes 262176 | tf_op jit(solution)/shard_map/ppermute | solution.py:63
  73.3 2.8 %collective-permute-done.12.refs_3_ = bf16[16,64,128]{2,1,0:T(8,128)(2,1)S(1)} collective-permute-done((bf16[16,64,128]{2,1,0:T(8,128)(2,1)S(1)}, bf16[16,64,128]{2,1,0:T(8,128)(2,1)S(1)}, u32[]{:S(2)}, u32[]{:S(2)}) %collective-permute-start.12) | collective-permute-done | bytes 262176 | tf_op jit(solution)/shard_map/ppermute | solution.py:63
  76.1 0.9 collective-permute-start.13
  77.0 0.0 collective-permute-start.14
  77.0 0.4 add_convert_fusion
  77.4 0.1 slice_bitcast_fusion
  77.5 0.6 collective-permute-done.13.refs_2_
  78.2 0.4 collective-permute-done.14.refs_4_
  78.5 6.1 %shard_map.102 = (bf16[1,2,16,64,128]{4,3,2,1,0:T(8,128)(2,1)S(1)}, bf16[1,2,16,64,128]{4,3,2,1,0:T(8,128)(2,1)S(1)}) custom-call(s32[1]{0:T(128)} %bitcast.refs_0_, bf16[16,64,128]{2,1,0:T(8,128)(2,1)S(1)} %collective-permute-done.11.refs_1_, bf16[16,64,128]{2,1,0:T(8,128)(2,1)S(1)} %collective-permute-done.13.refs_2_, ...), custom_call_target="tpu_custom_call" | custom-call | flops 5000000000 | bytes 25165824 | tf_op jit(solution)/shard_map/pallas_call | solution.py:320
  84.7 0.5 collective-permute-start.15
  85.1 0.1 collective-permute-start.16
  85.3 0.4 collective-permute-start.18
  85.7 0.1 collective-permute-start.19
  85.8 0.7 collective-permute-start.22
  86.6 4.6 %collective-permute-start.23 = (bf16[16,64,128]{2,1,0:T(8,128)(2,1)S(1)}, bf16[16,64,128]{2,1,0:T(8,128)(2,1)S(1)}, u32[]{:S(2)}, u32[]{:S(2)}) collective-permute-start(bf16[16,64,128]{2,1,0:T(8,128)(2,1)S(1)} %get-tuple-element.77), channel_id=1, source_target_pairs={{6,0},{7,1},{4,2},{5,3},{2,4},{3,5},{0,6},{1,7},{14,8},{15,9},{12,... | collective-permute-start | bytes 786440 | tf_op jit(solution)/shard_map/ppermute | solution.py:63
  91.2 0.2 fusion.4
  91.4 6.1 %shard_map.103 = (bf16[1,2,16,64,128]{4,3,2,1,0:T(8,128)(2,1)S(1)}, bf16[1,2,16,64,128]{4,3,2,1,0:T(8,128)(2,1)S(1)}) custom-call(s32[1]{0:T(128)} %bitcast.refs_0_, bf16[16,64,128]{2,1,0:T(8,128)(2,1)S(1)} %bitcast.45, bf16[16,64,128]{2,1,0:T(8,128)(2,1)S(1)} %collective-permute-done.18.refs_2_, bf16[16,64,128]{2,1,0:T(8,128)(2,1)S(1)} %collective-permute-done.17.refs_3_, ...), custom_call_target="tpu_custom_call" | custom-call | flops 5000000000 | bytes 25165824 | tf_op jit(solution)/shard_map/pallas_call | solution.py:320
  97.5 1.0 collective-permute-start.20
  98.5 0.8 collective-permute-start.25
  99.4 0.7 collective-permute-start.21
  100.1 2.7 %collective-permute-done.23 = bf16[16,64,128]{2,1,0:T(8,128)(2,1)S(1)} collective-permute-done((bf16[16,64,128]{2,1,0:T(8,128)(2,1)S(1)}, bf16[16,64,128]{2,1,0:T(8,128)(2,1)S(1)}, u32[]{:S(2)}, u32[]{:S(2)}) %collective-permute-start.23) | collective-permute-done | bytes 262176 | tf_op jit(solution)/shard_map/ppermute | solution.py:63
  102.8 1.1 collective-permute-start.27
  104.0 0.1 fusion.3
  104.0 2.3 %collective-permute-done.24 = bf16[16,64,128]{2,1,0:T(8,128)(2,1)S(1)} collective-permute-done((bf16[16,64,128]{2,1,0:T(8,128)(2,1)S(1)}, bf16[16,64,128]{2,1,0:T(8,128)(2,1)S(1)}, u32[]{:S(2)}, u32[]{:S(2)}) %collective-permute-start.24) | collective-permute-done | bytes 262176 | tf_op jit(solution)/shard_map/ppermute | solution.py:63
  106.3 10.8 %collective-permute-start.28 = (bf16[16,64,128]{2,1,0:T(8,128)(2,1)S(1)}, bf16[16,64,128]{2,1,0:T(8,128)(2,1)S(1)}, u32[]{:S(2)}, u32[]{:S(2)}) collective-permute-start(bf16[16,64,128]{2,1,0:T(8,128)(2,1)S(1)} %fusion.3), channel_id=1, source_target_pairs={{2,0},{3,1},{0,2},{1,3},{6,4},{7,5},{4,6},{5,7},{10,8},{11,9},{8,1... | collective-permute-start | bytes 786440 | tf_op jit(solution)/shard_map/ppermute | solution.py:63
  117.1 5.4 %collective-permute-done.25 = bf16[16,64,128]{2,1,0:T(8,128)(2,1)S(1)} collective-permute-done((bf16[16,64,128]{2,1,0:T(8,128)(2,1)S(1)}, bf16[16,64,128]{2,1,0:T(8,128)(2,1)S(1)}, u32[]{:S(2)}, u32[]{:S(2)}) %collective-permute-start.25) | collective-permute-done | bytes 262176 | tf_op jit(solution)/shard_map/ppermute | solution.py:63
  122.5 0.3 convert_add_fusion.3
  122.8 5.8 %collective-permute-done.28 = bf16[16,64,128]{2,1,0:T(8,128)(2,1)S(1)} collective-permute-done((bf16[16,64,128]{2,1,0:T(8,128)(2,1)S(1)}, bf16[16,64,128]{2,1,0:T(8,128)(2,1)S(1)}, u32[]{:S(2)}, u32[]{:S(2)}) %collective-permute-start.28) | collective-permute-done | bytes 262176 | tf_op jit(solution)/shard_map/ppermute | solution.py:63
  128.6 0.9 negate_bitcast_fusion
  (29 shorter events, 0.2 us)
Async XLA Ops:
  0.0 17.4 %collective-permute-start.4 = (bf16[16,64,128]{2,1,0:T(8,128)(2,1)}, bf16[16,64,128]{2,1,0:T(8,128)(2,1)S(1)}, u32[]{:S(2)}, u32[]{:S(2)}) collective-permute-start(bf16[16,64,128]{2,1,0:T(8,128)(2,1)} %bitcast.37), channel_id=1, source_target_pairs={{16,0},{17,1},{18,2},{19,3},{20,4},{21,5},{22,6},{23,7},{24,8},{25... | collective-permute-start | bytes 786440 | tf_op jit(solution)/shard_map/ppermute | solution.py:63
  2.1 15.4 %collective-permute-start.5 = (bf16[16,64,128]{2,1,0:T(8,128)(2,1)}, bf16[16,64,128]{2,1,0:T(8,128)(2,1)S(1)}, u32[]{:S(2)}, u32[]{:S(2)}) collective-permute-start(bf16[16,64,128]{2,1,0:T(8,128)(2,1)} %bitcast.38), channel_id=1, source_target_pairs={{18,0},{19,1},{16,2},{17,3},{22,4},{23,5},{20,6},{21,7},{26,8},{27... | collective-permute-start | bytes 786440 | tf_op jit(solution)/shard_map/ppermute | solution.py:63
  3.6 30.2 %collective-permute-start.8 = (bf16[64,64,128]{2,1,0:T(8,128)(2,1)}, bf16[64,64,128]{2,1,0:T(8,128)(2,1)S(1)}, u32[]{:S(2)}, u32[]{:S(2)}) collective-permute-start(bf16[64,64,128]{2,1,0:T(8,128)(2,1)} %bitcast.46), channel_id=1, source_target_pairs={{12,0},{114,1},{3,2},{125,3},{8,4},{118,5},{7,6},{121,7},{4,8},{12... | collective-permute-start | bytes 3145736 | tf_op jit(solution)/shard_map/ppermute | solution.py:63
  14.9 2.3 %copy-start.5 = (bf16[1,64,64,128]{3,2,1,0:T(8,128)(2,1)S(1)}, bf16[1,64,64,128]{3,2,1,0:T(8,128)(2,1)}, u32[]{:S(2)}) copy-start(bf16[1,64,64,128]{3,2,1,0:T(8,128)(2,1)} %param.11) | copy-start | bytes 3145732
  14.9 2.4 %copy-start = (bf16[1,16,64,128]{3,2,1,0:T(8,128)(2,1)S(1)}, bf16[1,16,64,128]{3,2,1,0:T(8,128)(2,1)}, u32[]{:S(2)}) copy-start(bf16[1,16,64,128]{3,2,1,0:T(8,128)(2,1)} %param.10) | copy-start | bytes 786436
  15.0 18.9 %copy-start.1 = (bf16[256,256]{1,0:T(8,128)(2,1)S(1)}, bf16[256,256]{1,0:T(8,128)(2,1)}, u32[]{:S(2)}) copy-start(bf16[256,256]{1,0:T(8,128)(2,1)} %constant.44.clone.refs_13_.refs_10_) | copy-start | bytes 393220
  15.0 18.9 %copy-start.2 = (bf16[256,256]{1,0:T(8,128)(2,1)S(1)}, bf16[256,256]{1,0:T(8,128)(2,1)}, u32[]{:S(2)}) copy-start(bf16[256,256]{1,0:T(8,128)(2,1)} %constant.45.clone.refs_14_.refs_11_) | copy-start | bytes 393220
  15.0 18.8 %copy-start.3 = (bf16[128,128]{1,0:T(8,128)(2,1)S(1)}, bf16[128,128]{1,0:T(8,128)(2,1)}, u32[]{:S(2)}) copy-start(bf16[128,128]{1,0:T(8,128)(2,1)} %constant.42.clone.refs_11_.refs_8_) | copy-start | bytes 98308
  15.0 18.8 %copy-start.4 = (bf16[128,128]{1,0:T(8,128)(2,1)S(1)}, bf16[128,128]{1,0:T(8,128)(2,1)}, u32[]{:S(2)}) copy-start(bf16[128,128]{1,0:T(8,128)(2,1)} %constant.43.clone.refs_12_.refs_9_) | copy-start | bytes 98308
  17.2 36.2 %collective-permute-start.9 = (bf16[64,64,128]{2,1,0:T(8,128)(2,1)S(1)}, bf16[64,64,128]{2,1,0:T(8,128)(2,1)S(1)}, u32[]{:S(2)}, u32[]{:S(2)}) collective-permute-start(bf16[64,64,128]{2,1,0:T(8,128)(2,1)S(1)} %bitcast.47), channel_id=1, source_target_pairs={{60,0},{66,1},{51,2},{77,3},{56,4},{70,5},{55,6},{73,7},{52,8},{74... | collective-permute-start | bytes 3145736 | tf_op jit(solution)/shard_map/ppermute | solution.py:63
  17.3 8.0 %collective-permute-start = (bf16[16,64,128]{2,1,0:T(8,128)(2,1)S(1)}, bf16[16,64,128]{2,1,0:T(8,128)(2,1)S(1)}, u32[]{:S(2)}, u32[]{:S(2)}) collective-permute-start(bf16[16,64,128]{2,1,0:T(8,128)(2,1)S(1)} %bitcast.39), channel_id=1, source_target_pairs={{4,0},{5,1},{6,2},{7,3},{0,4},{1,5},{2,6},{3,7},{12,8},{13,9},{14,... | collective-permute-start | bytes 786440 | tf_op jit(solution)/shard_map/ppermute | solution.py:63
  17.4 11.3 %collective-permute-start.2 = (bf16[16,64,128]{2,1,0:T(8,128)(2,1)S(1)}, bf16[16,64,128]{2,1,0:T(8,128)(2,1)S(1)}, u32[]{:S(2)}, u32[]{:S(2)}) collective-permute-start(bf16[16,64,128]{2,1,0:T(8,128)(2,1)S(1)} %bitcast.40), channel_id=1, source_target_pairs={{6,0},{7,1},{4,2},{5,3},{2,4},{3,5},{0,6},{1,7},{14,8},{15,9},{12,... | collective-permute-start | bytes 786440 | tf_op jit(solution)/shard_map/ppermute | solution.py:63
  17.5 12.6 %collective-permute-start.6 = (bf16[16,64,128]{2,1,0:T(8,128)(2,1)S(1)}, bf16[16,64,128]{2,1,0:T(8,128)(2,1)S(1)}, u32[]{:S(2)}, u32[]{:S(2)}) collective-permute-start(bf16[16,64,128]{2,1,0:T(8,128)(2,1)S(1)} %collective-permute-done.4.refs_5_), channel_id=1, source_target_pairs={{1,0},{0,1},{3,2},{2,3},{5,4},{4,5},{7,6},{6,7},{9,8},{8,9},{11,10... | collective-permute-start | bytes 786440 | tf_op jit(solution)/shard_map/ppermute | solution.py:63
  25.4 4.8 %collective-permute-start.7 = (bf16[16,64,128]{2,1,0:T(8,128)(2,1)S(1)}, bf16[16,64,128]{2,1,0:T(8,128)(2,1)S(1)}, u32[]{:S(2)}, u32[]{:S(2)}) collective-permute-start(bf16[16,64,128]{2,1,0:T(8,128)(2,1)S(1)} %collective-permute-done.5.refs_7_), channel_id=1, source_target_pairs={{1,0},{0,1},{3,2},{2,3},{5,4},{4,5},{7,6},{6,7},{9,8},{8,9},{11,10... | collective-permute-start | bytes 786440 | tf_op jit(solution)/shard_map/ppermute | solution.py:63
  28.8 2.5 %collective-permute-start.1 = (bf16[16,64,128]{2,1,0:T(8,128)(2,1)S(1)}, bf16[16,64,128]{2,1,0:T(8,128)(2,1)S(1)}, u32[]{:S(2)}, u32[]{:S(2)}) collective-permute-start(bf16[16,64,128]{2,1,0:T(8,128)(2,1)S(1)} %collective-permute-done.refs_1_), channel_id=1, source_target_pairs={{1,0},{0,1},{3,2},{2,3},{5,4},{4,5},{7,6},{6,7},{9,8},{8,9},{11,10... | collective-permute-start | bytes 786440 | tf_op jit(solution)/shard_map/ppermute | solution.py:63
  30.1 1.5 %collective-permute-start.3 = (bf16[16,64,128]{2,1,0:T(8,128)(2,1)S(1)}, bf16[16,64,128]{2,1,0:T(8,128)(2,1)S(1)}, u32[]{:S(2)}, u32[]{:S(2)}) collective-permute-start(bf16[16,64,128]{2,1,0:T(8,128)(2,1)S(1)} %collective-permute-done.2.refs_3_), channel_id=1, source_target_pairs={{1,0},{0,1},{3,2},{2,3},{5,4},{4,5},{7,6},{6,7},{9,8},{8,9},{11,10... | collective-permute-start | bytes 786440 | tf_op jit(solution)/shard_map/ppermute | solution.py:63
  60.7 16.3 %collective-permute-start.10 = (bf16[2,2,16,64,128]{4,3,2,1,0:T(8,128)(2,1)S(1)}, bf16[2,2,16,64,128]{4,3,2,1,0:T(8,128)(2,1)S(1)}, u32[]{:S(2)}, u32[]{:S(2)}) collective-permute-start(bf16[2,2,16,64,128]{4,3,2,1,0:T(8,128)(2,1)S(1)} %get-tuple-element.56), channel_id=1, source_target_pairs={{1,0},{0,1},{3,2},{2,3},{5,4},{4,5},{7,6},{6,7},{9,8},{8,9},{11,10... | collective-permute-start | bytes 3145736 | tf_op jit(solution)/shard_map/ppermute | solution.py:63
  64.6 8.7 %collective-permute-start.11 = (bf16[16,64,128]{2,1,0:T(8,128)(2,1)S(1)}, bf16[16,64,128]{2,1,0:T(8,128)(2,1)S(1)}, u32[]{:S(2)}, u32[]{:S(2)}) collective-permute-start(bf16[16,64,128]{2,1,0:T(8,128)(2,1)S(1)} %bitcast.41), channel_id=1, source_target_pairs={{20,0},{21,1},{22,2},{23,3},{16,4},{17,5},{18,6},{19,7},{28,8},{29... | collective-permute-start | bytes 786440 | tf_op jit(solution)/shard_map/ppermute | solution.py:63
  64.6 11.5 %collective-permute-start.12 = (bf16[16,64,128]{2,1,0:T(8,128)(2,1)S(1)}, bf16[16,64,128]{2,1,0:T(8,128)(2,1)S(1)}, u32[]{:S(2)}, u32[]{:S(2)}) collective-permute-start(bf16[16,64,128]{2,1,0:T(8,128)(2,1)S(1)} %bitcast.42), channel_id=1, source_target_pairs={{22,0},{23,1},{20,2},{21,3},{18,4},{19,5},{16,6},{17,7},{30,8},{31... | collective-permute-start | bytes 786440 | tf_op jit(solution)/shard_map/ppermute | solution.py:63
  64.7 20.6 %collective-permute-start.17 = (bf16[16,64,128]{2,1,0:T(8,128)(2,1)S(1)}, bf16[16,64,128]{2,1,0:T(8,128)(2,1)S(1)}, u32[]{:S(2)}, u32[]{:S(2)}) collective-permute-start(bf16[16,64,128]{2,1,0:T(8,128)(2,1)S(1)} %bitcast.43), channel_id=1, source_target_pairs={{2,0},{3,1},{0,2},{1,3},{6,4},{7,5},{4,6},{5,7},{10,8},{11,9},{8,1... | collective-permute-start | bytes 786440 | tf_op jit(solution)/shard_map/ppermute | solution.py:63
  76.1 2.0 %collective-permute-start.13 = (bf16[16,64,128]{2,1,0:T(8,128)(2,1)S(1)}, bf16[16,64,128]{2,1,0:T(8,128)(2,1)S(1)}, u32[]{:S(2)}, u32[]{:S(2)}) collective-permute-start(bf16[16,64,128]{2,1,0:T(8,128)(2,1)S(1)} %collective-permute-done.11.refs_1_), channel_id=1, source_target_pairs={{1,0},{0,1},{3,2},{2,3},{5,4},{4,5},{7,6},{6,7},{9,8},{8,9},{11,10... | collective-permute-start | bytes 786440 | tf_op jit(solution)/shard_map/ppermute | solution.py:63
  77.0 1.5 %collective-permute-start.14 = (bf16[16,64,128]{2,1,0:T(8,128)(2,1)S(1)}, bf16[16,64,128]{2,1,0:T(8,128)(2,1)S(1)}, u32[]{:S(2)}, u32[]{:S(2)}) collective-permute-start(bf16[16,64,128]{2,1,0:T(8,128)(2,1)S(1)} %collective-permute-done.12.refs_3_), channel_id=1, source_target_pairs={{1,0},{0,1},{3,2},{2,3},{5,4},{4,5},{7,6},{6,7},{9,8},{8,9},{11,10... | collective-permute-start | bytes 786440 | tf_op jit(solution)/shard_map/ppermute | solution.py:63
  84.7 1.9 %collective-permute-start.15 = (bf16[16,64,128]{2,1,0:T(8,128)(2,1)S(1)}, bf16[16,64,128]{2,1,0:T(8,128)(2,1)S(1)}, u32[]{:S(2)}, u32[]{:S(2)}) collective-permute-start(bf16[16,64,128]{2,1,0:T(8,128)(2,1)S(1)} %get-tuple-element.92), channel_id=1, source_target_pairs={{1,0},{0,1},{3,2},{2,3},{5,4},{4,5},{7,6},{6,7},{9,8},{8,9},{11,10... | collective-permute-start | bytes 786440 | tf_op jit(solution)/shard_map/ppermute | solution.py:63
  85.1 6.0 %collective-permute-start.16 = (bf16[16,64,128]{2,1,0:T(8,128)(2,1)S(1)}, bf16[16,64,128]{2,1,0:T(8,128)(2,1)S(1)}, u32[]{:S(2)}, u32[]{:S(2)}) collective-permute-start(bf16[16,64,128]{2,1,0:T(8,128)(2,1)S(1)} %get-tuple-element.91), channel_id=1, source_target_pairs={{1,0},{0,1},{3,2},{2,3},{5,4},{4,5},{7,6},{6,7},{9,8},{8,9},{11,10... | collective-permute-start | bytes 786440 | tf_op jit(solution)/shard_map/ppermute | solution.py:63
  85.3 6.1 %collective-permute-start.18 = (bf16[16,64,128]{2,1,0:T(8,128)(2,1)S(1)}, bf16[16,64,128]{2,1,0:T(8,128)(2,1)S(1)}, u32[]{:S(2)}, u32[]{:S(2)}) collective-permute-start(bf16[16,64,128]{2,1,0:T(8,128)(2,1)S(1)} %bitcast.44), channel_id=1, source_target_pairs={{1,0},{0,1},{3,2},{2,3},{5,4},{4,5},{7,6},{6,7},{9,8},{8,9},{11,10... | collective-permute-start | bytes 786440 | tf_op jit(solution)/shard_map/ppermute | solution.py:63
  85.7 5.7 %collective-permute-start.19 = (bf16[16,64,128]{2,1,0:T(8,128)(2,1)S(1)}, bf16[16,64,128]{2,1,0:T(8,128)(2,1)S(1)}, u32[]{:S(2)}, u32[]{:S(2)}) collective-permute-start(bf16[16,64,128]{2,1,0:T(8,128)(2,1)S(1)} %collective-permute-done.17.refs_3_), channel_id=1, source_target_pairs={{1,0},{0,1},{3,2},{2,3},{5,4},{4,5},{7,6},{6,7},{9,8},{8,9},{11,10... | collective-permute-start | bytes 786440 | tf_op jit(solution)/shard_map/ppermute | solution.py:63
  85.8 13.6 %collective-permute-start.22 = (bf16[16,64,128]{2,1,0:T(8,128)(2,1)S(1)}, bf16[16,64,128]{2,1,0:T(8,128)(2,1)S(1)}, u32[]{:S(2)}, u32[]{:S(2)}) collective-permute-start(bf16[16,64,128]{2,1,0:T(8,128)(2,1)S(1)} %get-tuple-element.76), channel_id=1, source_target_pairs={{4,0},{5,1},{6,2},{7,3},{0,4},{1,5},{2,6},{3,7},{12,8},{13,9},{14,... | collective-permute-start | bytes 786440 | tf_op jit(solution)/shard_map/ppermute | solution.py:63
  86.6 16.3 %collective-permute-start.23 = (bf16[16,64,128]{2,1,0:T(8,128)(2,1)S(1)}, bf16[16,64,128]{2,1,0:T(8,128)(2,1)S(1)}, u32[]{:S(2)}, u32[]{:S(2)}) collective-permute-start(bf16[16,64,128]{2,1,0:T(8,128)(2,1)S(1)} %get-tuple-element.77), channel_id=1, source_target_pairs={{6,0},{7,1},{4,2},{5,3},{2,4},{3,5},{0,6},{1,7},{14,8},{15,9},{12,... | collective-permute-start | bytes 786440 | tf_op jit(solution)/shard_map/ppermute | solution.py:63
  97.5 5.3 %collective-permute-start.20 = (bf16[16,64,128]{2,1,0:T(8,128)(2,1)S(1)}, bf16[16,64,128]{2,1,0:T(8,128)(2,1)S(1)}, u32[]{:S(2)}, u32[]{:S(2)}) collective-permute-start(bf16[16,64,128]{2,1,0:T(8,128)(2,1)S(1)} %get-tuple-element.87), channel_id=1, source_target_pairs={{1,0},{0,1},{3,2},{2,3},{5,4},{4,5},{7,6},{6,7},{9,8},{8,9},{11,10... | collective-permute-start | bytes 786440 | tf_op jit(solution)/shard_map/ppermute | solution.py:63
  98.5 7.8 %collective-permute-start.24 = (bf16[16,64,128]{2,1,0:T(8,128)(2,1)S(1)}, bf16[16,64,128]{2,1,0:T(8,128)(2,1)S(1)}, u32[]{:S(2)}, u32[]{:S(2)}) collective-permute-start(bf16[16,64,128]{2,1,0:T(8,128)(2,1)S(1)} %get-tuple-element.78), channel_id=1, source_target_pairs={{16,0},{17,1},{18,2},{19,3},{20,4},{21,5},{22,6},{23,7},{24,8},{25... | collective-permute-start | bytes 786440 | tf_op jit(solution)/shard_map/ppermute | solution.py:63
  98.5 23.9 %collective-permute-start.25 = (bf16[16,64,128]{2,1,0:T(8,128)(2,1)S(1)}, bf16[16,64,128]{2,1,0:T(8,128)(2,1)S(1)}, u32[]{:S(2)}, u32[]{:S(2)}) collective-permute-start(bf16[16,64,128]{2,1,0:T(8,128)(2,1)S(1)} %get-tuple-element.79), channel_id=1, source_target_pairs={{18,0},{19,1},{16,2},{17,3},{22,4},{23,5},{20,6},{21,7},{26,8},{27... | collective-permute-start | bytes 786440 | tf_op jit(solution)/shard_map/ppermute | solution.py:63
  99.4 23.1 %collective-permute-start.21 = (bf16[16,64,128]{2,1,0:T(8,128)(2,1)S(1)}, bf16[16,64,128]{2,1,0:T(8,128)(2,1)S(1)}, u32[]{:S(2)}, u32[]{:S(2)}) collective-permute-start(bf16[16,64,128]{2,1,0:T(8,128)(2,1)S(1)} %get-tuple-element.88), channel_id=1, source_target_pairs={{1,0},{0,1},{3,2},{2,3},{5,4},{4,5},{7,6},{6,7},{9,8},{8,9},{11,10... | collective-permute-start | bytes 786440 | tf_op jit(solution)/shard_map/ppermute | solution.py:63
  102.8 19.7 %collective-permute-start.26 = (bf16[16,64,128]{2,1,0:T(8,128)(2,1)S(1)}, bf16[16,64,128]{2,1,0:T(8,128)(2,1)S(1)}, u32[]{:S(2)}, u32[]{:S(2)}) collective-permute-start(bf16[16,64,128]{2,1,0:T(8,128)(2,1)S(1)} %get-tuple-element.80), channel_id=1, source_target_pairs={{20,0},{21,1},{22,2},{23,3},{16,4},{17,5},{18,6},{19,7},{28,8},{29... | collective-permute-start | bytes 786440 | tf_op jit(solution)/shard_map/ppermute | solution.py:63
  102.8 19.7 %collective-permute-start.27 = (bf16[16,64,128]{2,1,0:T(8,128)(2,1)S(1)}, bf16[16,64,128]{2,1,0:T(8,128)(2,1)S(1)}, u32[]{:S(2)}, u32[]{:S(2)}) collective-permute-start(bf16[16,64,128]{2,1,0:T(8,128)(2,1)S(1)} %get-tuple-element.81), channel_id=1, source_target_pairs={{22,0},{23,1},{20,2},{21,3},{18,4},{19,5},{16,6},{17,7},{30,8},{31... | collective-permute-start | bytes 786440 | tf_op jit(solution)/shard_map/ppermute | solution.py:63
  106.3 22.3 %collective-permute-start.28 = (bf16[16,64,128]{2,1,0:T(8,128)(2,1)S(1)}, bf16[16,64,128]{2,1,0:T(8,128)(2,1)S(1)}, u32[]{:S(2)}, u32[]{:S(2)}) collective-permute-start(bf16[16,64,128]{2,1,0:T(8,128)(2,1)S(1)} %fusion.3), channel_id=1, source_target_pairs={{2,0},{3,1},{0,2},{1,3},{6,4},{7,5},{4,6},{5,7},{10,8},{11,9},{8,1... | collective-permute-start | bytes 786440 | tf_op jit(solution)/shard_map/ppermute | solution.py:63

commit v8 on v6

--- a/solution.py
+++ b/solution.py
@@ -360,9 +360,8 @@
         half = []
         for dz in range(2):
             source = offset_source(dy, dx, dz, 0)
-            half.append(own if (dy, dx) == (0, 0) else receive(sent, source))
+            half.append(own if (dy, dx, dz) == (0, 0, 0) else receive(sent, source))
         halves.append(half)
-    second = receive(partner, second_source)
     matrices = section_matrices()
     device = lax.axis_index("tgt") * 4 + lax.axis_index("grp")
     slots = lax.dynamic_slice_in_dim(jnp.asarray(slot_table()), device, 1)[0]
@@ -394,16 +393,13 @@
     coulombs = [
         coulomb_kernel(screening, (weights[a], weights[b])) for a, b in ((0, 0), (1, 1), (0, 1))
     ]
-    *coulombs, halves[0][1], halves[1][1] = lax.optimization_barrier(
-        (*coulombs, halves[0][1], halves[1][1])
-    )
+    coulombs[2], late = lax.optimization_barrier((coulombs[2], partner))
+    second = receive(late, second_source)
     two = pieces(0) + pieces(1)
     place, *earlier = call(
         place, two + [first], coulombs[0], matrices, two_targets=True, stage="first"
     )
     mark = place
-    _, sent = lax.optimization_barrier((mark, own))
-    halves[3][1] = receive(sent, offset_source(0, 0, 1, 0))
     place, kept, given = call(place, two + [second], coulombs[1], matrices, True, "last", earlier)
     crossed = receive(given, sibling)
     summed = (kept.astype(f32) + crossed.astype(f32)).astype(bf16)

time: 108 us -> 113 us (1.046)
  starting transfers between devices: 31.6 us -> 45.2 us
  waiting for transfers between devices: 42.1 us -> 33.1 us
    ppermute x29, starting transfers between devices: 31.6 us -> 45.2 us  [receive(): return lax.ppermute(value, axes, pairs)]
    ppermute x29, waiting for transfers between devices: 42.1 us -> 33.1 us  [receive(): return lax.ppermute(value, axes, pairs)]
  transfers between devices with their start and end apart: 29 -> 29, of which waited for: 13 -> 12; matrix products, arithmetic and copies ran while one was open for 6% -> 6% of each run, Pallas kernels for 17% -> 16%
where the time goes in v8:
time: 113 us
  starting transfers between devices  45.2 us (40%)
  waiting for transfers between devices  33.1 us (29%)
  Pallas kernels  25.6 us (23%)
  other arithmetic  6.46 us (6%)
  local copies, waits for them, and re-layouts  1.58 us (1%)
    ppermute x29, starting transfers between devices, receive(): return lax.ppermute(value, axes, pairs)  45.2 us
    ppermute x29, waiting for transfers between devices, receive(): return lax.ppermute(value, axes, pairs)  33.1 us
    pallas_call x4, Pallas kernels, exchange_part(): pl.pallas_call(functools.partial(pair_kernel, two_targets, stage), out_sh...  25.6 us
  transfers between devices with their start and end apart: 29, of which 12 were waited for; matrix products, arithmetic and copies ran while one was open for 6% of the time, Pallas kernels for 16%

profile of v8, /device:TPU:1, one launch (start us, length us, event | category | flops | bytes accessed | tf_op | source)
XLA Modules:
  0.0 112.8 jit_solution(5578168046815243528)
XLA Ops:
  0.0 2.1 %collective-permute-start.4 = (bf16[16,64,128]{2,1,0:T(8,128)(2,1)}, bf16[16,64,128]{2,1,0:T(8,128)(2,1)S(1)}, u32[]{:S(2)}, u32[]{:S(2)}) collective-permute-start(bf16[16,64,128]{2,1,0:T(8,128)(2,1)} %bitcast.37), channel_id=1, source_target_pairs={{16,0},{17,1},{18,2},{19,3},{20,4},{21,5},{22,6},{23,7},{24,8},{25... | collective-permute-start | bytes 786440 | tf_op jit(solution)/shard_map/ppermute | solution.py:63
  2.1 1.5 %collective-permute-start.5 = (bf16[16,64,128]{2,1,0:T(8,128)(2,1)}, bf16[16,64,128]{2,1,0:T(8,128)(2,1)S(1)}, u32[]{:S(2)}, u32[]{:S(2)}) collective-permute-start(bf16[16,64,128]{2,1,0:T(8,128)(2,1)} %bitcast.38), channel_id=1, source_target_pairs={{18,0},{19,1},{16,2},{17,3},{22,4},{23,5},{20,6},{21,7},{26,8},{27... | collective-permute-start | bytes 786440 | tf_op jit(solution)/shard_map/ppermute | solution.py:63
  3.6 4.7 %collective-permute-start.8 = (bf16[64,64,128]{2,1,0:T(8,128)(2,1)}, bf16[64,64,128]{2,1,0:T(8,128)(2,1)S(1)}, u32[]{:S(2)}, u32[]{:S(2)}) collective-permute-start(bf16[64,64,128]{2,1,0:T(8,128)(2,1)} %bitcast.46), channel_id=1, source_target_pairs={{12,0},{126,1},{3,2},{113,3},{8,4},{122,5},{7,6},{117,7},{4,8},{11... | collective-permute-start | bytes 3145736 | tf_op jit(solution)/shard_map/ppermute | solution.py:63
  8.3 0.7 dynamic-slice_bitcast_fusion
  9.0 0.8 select_reduce_fusion
  9.9 0.2 fusion.6
  10.1 0.6 fusion.10
  10.7 0.1 broadcast_add_fusion
  10.7 0.1 add.130
  11.5 1.2 %compare_select_fusion.1 = f32[128]{0:T(128)S(1)} fusion(f32[]{:T(128)} %bitcast.6, f32[]{:T(128)} %bitcast.5), kind=kLoop, calls=%fused_computation.26 | loop fusion | flops 256 | bytes 520 | tf_op jit(solution)/shard_map/jit(_where)/select_n | solution.py:110
  12.7 0.0 copy-start.5
  12.8 0.0 copy-start
  12.8 0.0 copy-start.1
  12.8 0.0 copy-start.2
  12.8 0.0 copy-start.3
  12.8 0.0 copy-start.4
  12.8 2.2 %fusion = (f32[64,64,128]{2,1,0:T(8,128)S(1)}, f32[64,64,128]{2,1,0:T(8,128)S(1)}, f32[64,64,128]{2,1,0:T(8,128)S(1)}) fusion(f32[]{:T(128)} %bitcast.6, f32[]{:T(128)} %bitcast.3, f32[128]{0:T(128)S(1)} %add.130, f32[64,64]{1,0:T(8,128)S(1)} %broadcast_add_fusion, f32[128]{0:T(128)S(1)} %compare_select_fusion.1, f32[]{:T(128)} %bitcast.5), kind=kLoop, calls=%fused_computation.2 | loop fusion | flops 3145728 | bytes 6308876 | tf_op jit(solution)/shard_map/mul | solution.py:111
  15.0 0.1 collective-permute-start.9
  15.1 1.3 %collective-permute-start = (bf16[16,64,128]{2,1,0:T(8,128)(2,1)S(1)}, bf16[16,64,128]{2,1,0:T(8,128)(2,1)S(1)}, u32[]{:S(2)}, u32[]{:S(2)}) collective-permute-start(bf16[16,64,128]{2,1,0:T(8,128)(2,1)S(1)} %bitcast.39), channel_id=1, source_target_pairs={{4,0},{5,1},{6,2},{7,3},{0,4},{1,5},{2,6},{3,7},{12,8},{13,9},{14,... | collective-permute-start | bytes 786440 | tf_op jit(solution)/shard_map/ppermute | solution.py:63
  16.4 0.0 collective-permute-done.4.refs_5_
  16.4 3.0 %collective-permute-start.2 = (bf16[16,64,128]{2,1,0:T(8,128)(2,1)S(1)}, bf16[16,64,128]{2,1,0:T(8,128)(2,1)S(1)}, u32[]{:S(2)}, u32[]{:S(2)}) collective-permute-start(bf16[16,64,128]{2,1,0:T(8,128)(2,1)S(1)} %bitcast.40), channel_id=1, source_target_pairs={{6,0},{7,1},{4,2},{5,3},{2,4},{3,5},{0,6},{1,7},{14,8},{15,9},{12,... | collective-permute-start | bytes 786440 | tf_op jit(solution)/shard_map/ppermute | solution.py:63
  19.5 0.8 collective-permute-start.6
  20.3 0.9 collective-permute-done.refs_1_
  21.2 5.4 %collective-permute-start.7 = (bf16[16,64,128]{2,1,0:T(8,128)(2,1)S(1)}, bf16[16,64,128]{2,1,0:T(8,128)(2,1)S(1)}, u32[]{:S(2)}, u32[]{:S(2)}) collective-permute-start(bf16[16,64,128]{2,1,0:T(8,128)(2,1)S(1)} %collective-permute-done.5.refs_7_), channel_id=1, source_target_pairs={{1,0},{0,1},{3,2},{2,3},{5,4},{4,5},{7,6},{6,7},{9,8},{8,9},{11,10... | collective-permute-start | bytes 786440 | tf_op jit(solution)/shard_map/ppermute | solution.py:63
  26.5 4.7 %collective-permute-done.2.refs_3_ = bf16[16,64,128]{2,1,0:T(8,128)(2,1)S(1)} collective-permute-done((bf16[16,64,128]{2,1,0:T(8,128)(2,1)S(1)}, bf16[16,64,128]{2,1,0:T(8,128)(2,1)S(1)}, u32[]{:S(2)}, u32[]{:S(2)}) %collective-permute-start.2) | collective-permute-done | bytes 262176 | tf_op jit(solution)/shard_map/ppermute | solution.py:63
  31.2 1.1 %collective-permute-start.1 = (bf16[16,64,128]{2,1,0:T(8,128)(2,1)S(1)}, bf16[16,64,128]{2,1,0:T(8,128)(2,1)S(1)}, u32[]{:S(2)}, u32[]{:S(2)}) collective-permute-start(bf16[16,64,128]{2,1,0:T(8,128)(2,1)S(1)} %collective-permute-done.refs_1_), channel_id=1, source_target_pairs={{1,0},{0,1},{3,2},{2,3},{5,4},{4,5},{7,6},{6,7},{9,8},{8,9},{11,10... | collective-permute-start | bytes 786440 | tf_op jit(solution)/shard_map/ppermute | solution.py:63
  32.3 0.0 collective-permute-start.3
  32.4 1.1 %collective-permute-done.1.refs_2_ = bf16[16,64,128]{2,1,0:T(8,128)(2,1)S(1)} collective-permute-done((bf16[16,64,128]{2,1,0:T(8,128)(2,1)S(1)}, bf16[16,64,128]{2,1,0:T(8,128)(2,1)S(1)}, u32[]{:S(2)}, u32[]{:S(2)}) %collective-permute-start.1) | collective-permute-done | bytes 262176 | tf_op jit(solution)/shard_map/ppermute | solution.py:63
  33.5 0.4 collective-permute-done.3.refs_4_
  33.9 6.2 %shard_map.100 = (bf16[2,2,16,64,128]{4,3,2,1,0:T(8,128)(2,1)S(1)}, bf16[2,2,16,64,128]{4,3,2,1,0:T(8,128)(2,1)S(1)}) custom-call(s32[1]{0:T(128)} %bitcast.refs_0_, bf16[16,64,128]{2,1,0:T(8,128)(2,1)S(1)} %collective-permute-done.refs_1_, bf16[16,64,128]{2,1,0:T(8,128)(2,1)S(1)} %collective-permute-done.1.refs_2_, ...), custom_call_target="tpu_custom_call" | custom-call | flops 5000000000 | bytes 25165824 | tf_op jit(solution)/shard_map/pallas_call | solution.py:320
  40.1 7.2 %shard_map.101 = (bf16[2,2,16,64,128]{4,3,2,1,0:T(8,128)(2,1)S(1)}, bf16[2,2,16,64,128]{4,3,2,1,0:T(8,128)(2,1)S(1)}) custom-call(s32[1]{0:T(128)} %bitcast.refs_0_, bf16[16,64,128]{2,1,0:T(8,128)(2,1)S(1)} %collective-permute-done.refs_1_, bf16[16,64,128]{2,1,0:T(8,128)(2,1)S(1)} %collective-permute-done.1.refs_2_, ...), custom_call_target="tpu_custom_call" | custom-call | flops 5000000000 | bytes 25165824 | tf_op jit(solution)/shard_map/pallas_call | solution.py:320
  47.3 0.6 collective-permute-start.10
  48.0 0.5 collective-permute-start.12
  48.4 3.1 %collective-permute-start.17 = (bf16[16,64,128]{2,1,0:T(8,128)(2,1)S(1)}, bf16[16,64,128]{2,1,0:T(8,128)(2,1)S(1)}, u32[]{:S(2)}, u32[]{:S(2)}) collective-permute-start(bf16[16,64,128]{2,1,0:T(8,128)(2,1)S(1)} %bitcast.43), channel_id=1, source_target_pairs={{2,0},{3,1},{0,2},{1,3},{6,4},{7,5},{4,6},{5,7},{10,8},{11,9},{8,1... | collective-permute-start | bytes 786440 | tf_op jit(solution)/shard_map/ppermute | solution.py:63
  51.5 5.1 %collective-permute-done.11.refs_1_ = bf16[16,64,128]{2,1,0:T(8,128)(2,1)S(1)} collective-permute-done((bf16[16,64,128]{2,1,0:T(8,128)(2,1)S(1)}, bf16[16,64,128]{2,1,0:T(8,128)(2,1)S(1)}, u32[]{:S(2)}, u32[]{:S(2)}) %collective-permute-start.11) | collective-permute-done | bytes 262176 | tf_op jit(solution)/shard_map/ppermute | solution.py:63
  56.6 3.7 %collective-permute-done.12.refs_3_ = bf16[16,64,128]{2,1,0:T(8,128)(2,1)S(1)} collective-permute-done((bf16[16,64,128]{2,1,0:T(8,128)(2,1)S(1)}, bf16[16,64,128]{2,1,0:T(8,128)(2,1)S(1)}, u32[]{:S(2)}, u32[]{:S(2)}) %collective-permute-start.12) | collective-permute-done | bytes 262176 | tf_op jit(solution)/shard_map/ppermute | solution.py:63
  60.3 1.1 collective-permute-start.13
  61.4 0.0 collective-permute-start.14
  61.4 0.4 add_convert_fusion
  61.9 0.1 slice_bitcast_fusion
  61.9 0.6 collective-permute-done.13.refs_2_
  62.6 0.4 collective-permute-done.14.refs_4_
  63.0 6.1 %shard_map.102 = (bf16[1,2,16,64,128]{4,3,2,1,0:T(8,128)(2,1)S(1)}, bf16[1,2,16,64,128]{4,3,2,1,0:T(8,128)(2,1)S(1)}) custom-call(s32[1]{0:T(128)} %bitcast.refs_0_, bf16[16,64,128]{2,1,0:T(8,128)(2,1)S(1)} %collective-permute-done.11.refs_1_, bf16[16,64,128]{2,1,0:T(8,128)(2,1)S(1)} %collective-permute-done.13.refs_2_, ...), custom_call_target="tpu_custom_call" | custom-call | flops 5000000000 | bytes 25165824 | tf_op jit(solution)/shard_map/pallas_call | solution.py:320
  69.1 0.5 collective-permute-start.15
  69.6 0.1 collective-permute-start.16
  69.7 0.4 collective-permute-start.18
  70.1 0.1 collective-permute-start.19
  70.2 1.2 %collective-permute-start.22 = (bf16[16,64,128]{2,1,0:T(8,128)(2,1)S(1)}, bf16[16,64,128]{2,1,0:T(8,128)(2,1)S(1)}, u32[]{:S(2)}, u32[]{:S(2)}) collective-permute-start(bf16[16,64,128]{2,1,0:T(8,128)(2,1)S(1)} %get-tuple-element.74), channel_id=1, source_target_pairs={{4,0},{5,1},{6,2},{7,3},{0,4},{1,5},{2,6},{3,7},{12,8},{13,9},{14,... | collective-permute-start | bytes 786440 | tf_op jit(solution)/shard_map/ppermute | solution.py:63
  71.4 3.0 %collective-permute-start.23 = (bf16[16,64,128]{2,1,0:T(8,128)(2,1)S(1)}, bf16[16,64,128]{2,1,0:T(8,128)(2,1)S(1)}, u32[]{:S(2)}, u32[]{:S(2)}) collective-permute-start(bf16[16,64,128]{2,1,0:T(8,128)(2,1)S(1)} %get-tuple-element.75), channel_id=1, source_target_pairs={{6,0},{7,1},{4,2},{5,3},{2,4},{3,5},{0,6},{1,7},{14,8},{15,9},{12,... | collective-permute-start | bytes 786440 | tf_op jit(solution)/shard_map/ppermute | solution.py:63
  74.5 0.2 fusion.4
  74.7 6.1 %shard_map.103 = (bf16[1,2,16,64,128]{4,3,2,1,0:T(8,128)(2,1)S(1)}, bf16[1,2,16,64,128]{4,3,2,1,0:T(8,128)(2,1)S(1)}) custom-call(s32[1]{0:T(128)} %bitcast.refs_0_, bf16[16,64,128]{2,1,0:T(8,128)(2,1)S(1)} %bitcast.45, bf16[16,64,128]{2,1,0:T(8,128)(2,1)S(1)} %collective-permute-done.18.refs_2_, bf16[16,64,128]{2,1,0:T(8,128)(2,1)S(1)} %collective-permute-done.17.refs_3_, ...), custom_call_target="tpu_custom_call" | custom-call | flops 5000000000 | bytes 25165824 | tf_op jit(solution)/shard_map/pallas_call | solution.py:320
  80.9 1.0 collective-permute-start.20
  81.9 0.1 collective-permute-start.24
  82.0 0.7 collective-permute-start.25
  82.7 0.7 collective-permute-start.21
  83.4 2.7 %collective-permute-done.23 = bf16[16,64,128]{2,1,0:T(8,128)(2,1)S(1)} collective-permute-done((bf16[16,64,128]{2,1,0:T(8,128)(2,1)S(1)}, bf16[16,64,128]{2,1,0:T(8,128)(2,1)S(1)}, u32[]{:S(2)}, u32[]{:S(2)}) %collective-permute-start.23) | collective-permute-done | bytes 262176 | tf_op jit(solution)/shard_map/ppermute | solution.py:63
  86.1 1.1 collective-permute-start.27
  87.3 0.1 fusion.3
  87.4 2.3 %collective-permute-done.24 = bf16[16,64,128]{2,1,0:T(8,128)(2,1)S(1)} collective-permute-done((bf16[16,64,128]{2,1,0:T(8,128)(2,1)S(1)}, bf16[16,64,128]{2,1,0:T(8,128)(2,1)S(1)}, u32[]{:S(2)}, u32[]{:S(2)}) %collective-permute-start.24) | collective-permute-done | bytes 262176 | tf_op jit(solution)/shard_map/ppermute | solution.py:63
  89.6 10.8 %collective-permute-start.28 = (bf16[16,64,128]{2,1,0:T(8,128)(2,1)S(1)}, bf16[16,64,128]{2,1,0:T(8,128)(2,1)S(1)}, u32[]{:S(2)}, u32[]{:S(2)}) collective-permute-start(bf16[16,64,128]{2,1,0:T(8,128)(2,1)S(1)} %fusion.3), channel_id=1, source_target_pairs={{2,0},{3,1},{0,2},{1,3},{6,4},{7,5},{4,6},{5,7},{10,8},{11,9},{8,1... | collective-permute-start | bytes 786440 | tf_op jit(solution)/shard_map/ppermute | solution.py:63
  100.4 5.4 %collective-permute-done.25 = bf16[16,64,128]{2,1,0:T(8,128)(2,1)S(1)} collective-permute-done((bf16[16,64,128]{2,1,0:T(8,128)(2,1)S(1)}, bf16[16,64,128]{2,1,0:T(8,128)(2,1)S(1)}, u32[]{:S(2)}, u32[]{:S(2)}) %collective-permute-start.25) | collective-permute-done | bytes 262176 | tf_op jit(solution)/shard_map/ppermute | solution.py:63
  105.8 0.3 convert_add_fusion.3
  106.2 5.8 %collective-permute-done.28 = bf16[16,64,128]{2,1,0:T(8,128)(2,1)S(1)} collective-permute-done((bf16[16,64,128]{2,1,0:T(8,128)(2,1)S(1)}, bf16[16,64,128]{2,1,0:T(8,128)(2,1)S(1)}, u32[]{:S(2)}, u32[]{:S(2)}) %collective-permute-start.28) | collective-permute-done | bytes 262176 | tf_op jit(solution)/shard_map/ppermute | solution.py:63
  111.9 0.9 negate_bitcast_fusion
  (29 shorter events, 0.2 us)
Async XLA Ops:
  0.0 16.4 %collective-permute-start.4 = (bf16[16,64,128]{2,1,0:T(8,128)(2,1)}, bf16[16,64,128]{2,1,0:T(8,128)(2,1)S(1)}, u32[]{:S(2)}, u32[]{:S(2)}) collective-permute-start(bf16[16,64,128]{2,1,0:T(8,128)(2,1)} %bitcast.37), channel_id=1, source_target_pairs={{16,0},{17,1},{18,2},{19,3},{20,4},{21,5},{22,6},{23,7},{24,8},{25... | collective-permute-start | bytes 786440 | tf_op jit(solution)/shard_map/ppermute | solution.py:63
  2.1 17.4 %collective-permute-start.5 = (bf16[16,64,128]{2,1,0:T(8,128)(2,1)}, bf16[16,64,128]{2,1,0:T(8,128)(2,1)S(1)}, u32[]{:S(2)}, u32[]{:S(2)}) collective-permute-start(bf16[16,64,128]{2,1,0:T(8,128)(2,1)} %bitcast.38), channel_id=1, source_target_pairs={{18,0},{19,1},{16,2},{17,3},{22,4},{23,5},{20,6},{21,7},{26,8},{27... | collective-permute-start | bytes 786440 | tf_op jit(solution)/shard_map/ppermute | solution.py:63
  3.6 30.2 %collective-permute-start.8 = (bf16[64,64,128]{2,1,0:T(8,128)(2,1)}, bf16[64,64,128]{2,1,0:T(8,128)(2,1)S(1)}, u32[]{:S(2)}, u32[]{:S(2)}) collective-permute-start(bf16[64,64,128]{2,1,0:T(8,128)(2,1)} %bitcast.46), channel_id=1, source_target_pairs={{12,0},{126,1},{3,2},{113,3},{8,4},{122,5},{7,6},{117,7},{4,8},{11... | collective-permute-start | bytes 3145736 | tf_op jit(solution)/shard_map/ppermute | solution.py:63
  12.7 2.3 %copy-start.5 = (bf16[1,64,64,128]{3,2,1,0:T(8,128)(2,1)S(1)}, bf16[1,64,64,128]{3,2,1,0:T(8,128)(2,1)}, u32[]{:S(2)}) copy-start(bf16[1,64,64,128]{3,2,1,0:T(8,128)(2,1)} %param.11) | copy-start | bytes 3145732
  12.8 2.4 %copy-start = (bf16[1,16,64,128]{3,2,1,0:T(8,128)(2,1)S(1)}, bf16[1,16,64,128]{3,2,1,0:T(8,128)(2,1)}, u32[]{:S(2)}) copy-start(bf16[1,16,64,128]{3,2,1,0:T(8,128)(2,1)} %param.10) | copy-start | bytes 786436
  12.8 21.1 %copy-start.1 = (bf16[256,256]{1,0:T(8,128)(2,1)S(1)}, bf16[256,256]{1,0:T(8,128)(2,1)}, u32[]{:S(2)}) copy-start(bf16[256,256]{1,0:T(8,128)(2,1)} %constant.44.clone.refs_13_.refs_10_) | copy-start | bytes 393220
  12.8 21.1 %copy-start.2 = (bf16[256,256]{1,0:T(8,128)(2,1)S(1)}, bf16[256,256]{1,0:T(8,128)(2,1)}, u32[]{:S(2)}) copy-start(bf16[256,256]{1,0:T(8,128)(2,1)} %constant.45.clone.refs_14_.refs_11_) | copy-start | bytes 393220
  12.8 21.1 %copy-start.3 = (bf16[128,128]{1,0:T(8,128)(2,1)S(1)}, bf16[128,128]{1,0:T(8,128)(2,1)}, u32[]{:S(2)}) copy-start(bf16[128,128]{1,0:T(8,128)(2,1)} %constant.42.clone.refs_11_.refs_8_) | copy-start | bytes 98308
  12.8 21.1 %copy-start.4 = (bf16[128,128]{1,0:T(8,128)(2,1)S(1)}, bf16[128,128]{1,0:T(8,128)(2,1)}, u32[]{:S(2)}) copy-start(bf16[128,128]{1,0:T(8,128)(2,1)} %constant.43.clone.refs_12_.refs_9_) | copy-start | bytes 98308
  15.0 25.1 %collective-permute-start.9 = (bf16[64,64,128]{2,1,0:T(8,128)(2,1)S(1)}, bf16[64,64,128]{2,1,0:T(8,128)(2,1)S(1)}, u32[]{:S(2)}, u32[]{:S(2)}) collective-permute-start(bf16[64,64,128]{2,1,0:T(8,128)(2,1)S(1)} %bitcast.47), channel_id=1, source_target_pairs={{60,0},{78,1},{51,2},{65,3},{56,4},{74,5},{55,6},{69,7},{52,8},{70... | collective-permute-start | bytes 3145736 | tf_op jit(solution)/shard_map/ppermute | solution.py:63
  15.1 6.0 %collective-permute-start = (bf16[16,64,128]{2,1,0:T(8,128)(2,1)S(1)}, bf16[16,64,128]{2,1,0:T(8,128)(2,1)S(1)}, u32[]{:S(2)}, u32[]{:S(2)}) collective-permute-start(bf16[16,64,128]{2,1,0:T(8,128)(2,1)S(1)} %bitcast.39), channel_id=1, source_target_pairs={{4,0},{5,1},{6,2},{7,3},{0,4},{1,5},{2,6},{3,7},{12,8},{13,9},{14,... | collective-permute-start | bytes 786440 | tf_op jit(solution)/shard_map/ppermute | solution.py:63
  16.4 14.8 %collective-permute-start.2 = (bf16[16,64,128]{2,1,0:T(8,128)(2,1)S(1)}, bf16[16,64,128]{2,1,0:T(8,128)(2,1)S(1)}, u32[]{:S(2)}, u32[]{:S(2)}) collective-permute-start(bf16[16,64,128]{2,1,0:T(8,128)(2,1)S(1)} %bitcast.40), channel_id=1, source_target_pairs={{6,0},{7,1},{4,2},{5,3},{2,4},{3,5},{0,6},{1,7},{14,8},{15,9},{12,... | collective-permute-start | bytes 786440 | tf_op jit(solution)/shard_map/ppermute | solution.py:63
  19.5 12.9 %collective-permute-start.6 = (bf16[16,64,128]{2,1,0:T(8,128)(2,1)S(1)}, bf16[16,64,128]{2,1,0:T(8,128)(2,1)S(1)}, u32[]{:S(2)}, u32[]{:S(2)}) collective-permute-start(bf16[16,64,128]{2,1,0:T(8,128)(2,1)S(1)} %collective-permute-done.4.refs_5_), channel_id=1, source_target_pairs={{1,0},{0,1},{3,2},{2,3},{5,4},{4,5},{7,6},{6,7},{9,8},{8,9},{11,10... | collective-permute-start | bytes 786440 | tf_op jit(solution)/shard_map/ppermute | solution.py:63
  21.2 11.2 %collective-permute-start.7 = (bf16[16,64,128]{2,1,0:T(8,128)(2,1)S(1)}, bf16[16,64,128]{2,1,0:T(8,128)(2,1)S(1)}, u32[]{:S(2)}, u32[]{:S(2)}) collective-permute-start(bf16[16,64,128]{2,1,0:T(8,128)(2,1)S(1)} %collective-permute-done.5.refs_7_), channel_id=1, source_target_pairs={{1,0},{0,1},{3,2},{2,3},{5,4},{4,5},{7,6},{6,7},{9,8},{8,9},{11,10... | collective-permute-start | bytes 786440 | tf_op jit(solution)/shard_map/ppermute | solution.py:63
  31.2 2.3 %collective-permute-start.1 = (bf16[16,64,128]{2,1,0:T(8,128)(2,1)S(1)}, bf16[16,64,128]{2,1,0:T(8,128)(2,1)S(1)}, u32[]{:S(2)}, u32[]{:S(2)}) collective-permute-start(bf16[16,64,128]{2,1,0:T(8,128)(2,1)S(1)} %collective-permute-done.refs_1_), channel_id=1, source_target_pairs={{1,0},{0,1},{3,2},{2,3},{5,4},{4,5},{7,6},{6,7},{9,8},{8,9},{11,10... | collective-permute-start | bytes 786440 | tf_op jit(solution)/shard_map/ppermute | solution.py:63
  32.3 1.5 %collective-permute-start.3 = (bf16[16,64,128]{2,1,0:T(8,128)(2,1)S(1)}, bf16[16,64,128]{2,1,0:T(8,128)(2,1)S(1)}, u32[]{:S(2)}, u32[]{:S(2)}) collective-permute-start(bf16[16,64,128]{2,1,0:T(8,128)(2,1)S(1)} %collective-permute-done.2.refs_3_), channel_id=1, source_target_pairs={{1,0},{0,1},{3,2},{2,3},{5,4},{4,5},{7,6},{6,7},{9,8},{8,9},{11,10... | collective-permute-start | bytes 786440 | tf_op jit(solution)/shard_map/ppermute | solution.py:63
  47.3 14.1 %collective-permute-start.10 = (bf16[2,2,16,64,128]{4,3,2,1,0:T(8,128)(2,1)S(1)}, bf16[2,2,16,64,128]{4,3,2,1,0:T(8,128)(2,1)S(1)}, u32[]{:S(2)}, u32[]{:S(2)}) collective-permute-start(bf16[2,2,16,64,128]{4,3,2,1,0:T(8,128)(2,1)S(1)} %get-tuple-element.55), channel_id=1, source_target_pairs={{1,0},{0,1},{3,2},{2,3},{5,4},{4,5},{7,6},{6,7},{9,8},{8,9},{11,10... | collective-permute-start | bytes 3145736 | tf_op jit(solution)/shard_map/ppermute | solution.py:63
  48.0 8.6 %collective-permute-start.11 = (bf16[16,64,128]{2,1,0:T(8,128)(2,1)S(1)}, bf16[16,64,128]{2,1,0:T(8,128)(2,1)S(1)}, u32[]{:S(2)}, u32[]{:S(2)}) collective-permute-start(bf16[16,64,128]{2,1,0:T(8,128)(2,1)S(1)} %bitcast.41), channel_id=1, source_target_pairs={{20,0},{21,1},{22,2},{23,3},{16,4},{17,5},{18,6},{19,7},{28,8},{29... | collective-permute-start | bytes 786440 | tf_op jit(solution)/shard_map/ppermute | solution.py:63
  48.0 12.3 %collective-permute-start.12 = (bf16[16,64,128]{2,1,0:T(8,128)(2,1)S(1)}, bf16[16,64,128]{2,1,0:T(8,128)(2,1)S(1)}, u32[]{:S(2)}, u32[]{:S(2)}) collective-permute-start(bf16[16,64,128]{2,1,0:T(8,128)(2,1)S(1)} %bitcast.42), channel_id=1, source_target_pairs={{22,0},{23,1},{20,2},{21,3},{18,4},{19,5},{16,6},{17,7},{30,8},{31... | collective-permute-start | bytes 786440 | tf_op jit(solution)/shard_map/ppermute | solution.py:63
  48.4 21.3 %collective-permute-start.17 = (bf16[16,64,128]{2,1,0:T(8,128)(2,1)S(1)}, bf16[16,64,128]{2,1,0:T(8,128)(2,1)S(1)}, u32[]{:S(2)}, u32[]{:S(2)}) collective-permute-start(bf16[16,64,128]{2,1,0:T(8,128)(2,1)S(1)} %bitcast.43), channel_id=1, source_target_pairs={{2,0},{3,1},{0,2},{1,3},{6,4},{7,5},{4,6},{5,7},{10,8},{11,9},{8,1... | collective-permute-start | bytes 786440 | tf_op jit(solution)/shard_map/ppermute | solution.py:63
  60.3 2.3 %collective-permute-start.13 = (bf16[16,64,128]{2,1,0:T(8,128)(2,1)S(1)}, bf16[16,64,128]{2,1,0:T(8,128)(2,1)S(1)}, u32[]{:S(2)}, u32[]{:S(2)}) collective-permute-start(bf16[16,64,128]{2,1,0:T(8,128)(2,1)S(1)} %collective-permute-done.11.refs_1_), channel_id=1, source_target_pairs={{1,0},{0,1},{3,2},{2,3},{5,4},{4,5},{7,6},{6,7},{9,8},{8,9},{11,10... | collective-permute-start | bytes 786440 | tf_op jit(solution)/shard_map/ppermute | solution.py:63
  61.4 1.5 %collective-permute-start.14 = (bf16[16,64,128]{2,1,0:T(8,128)(2,1)S(1)}, bf16[16,64,128]{2,1,0:T(8,128)(2,1)S(1)}, u32[]{:S(2)}, u32[]{:S(2)}) collective-permute-start(bf16[16,64,128]{2,1,0:T(8,128)(2,1)S(1)} %collective-permute-done.12.refs_3_), channel_id=1, source_target_pairs={{1,0},{0,1},{3,2},{2,3},{5,4},{4,5},{7,6},{6,7},{9,8},{8,9},{11,10... | collective-permute-start | bytes 786440 | tf_op jit(solution)/shard_map/ppermute | solution.py:63
  69.1 2.3 %collective-permute-start.15 = (bf16[16,64,128]{2,1,0:T(8,128)(2,1)S(1)}, bf16[16,64,128]{2,1,0:T(8,128)(2,1)S(1)}, u32[]{:S(2)}, u32[]{:S(2)}) collective-permute-start(bf16[16,64,128]{2,1,0:T(8,128)(2,1)S(1)} %get-tuple-element.90), channel_id=1, source_target_pairs={{1,0},{0,1},{3,2},{2,3},{5,4},{4,5},{7,6},{6,7},{9,8},{8,9},{11,10... | collective-permute-start | bytes 786440 | tf_op jit(solution)/shard_map/ppermute | solution.py:63
  69.6 4.9 %collective-permute-start.16 = (bf16[16,64,128]{2,1,0:T(8,128)(2,1)S(1)}, bf16[16,64,128]{2,1,0:T(8,128)(2,1)S(1)}, u32[]{:S(2)}, u32[]{:S(2)}) collective-permute-start(bf16[16,64,128]{2,1,0:T(8,128)(2,1)S(1)} %get-tuple-element.89), channel_id=1, source_target_pairs={{1,0},{0,1},{3,2},{2,3},{5,4},{4,5},{7,6},{6,7},{9,8},{8,9},{11,10... | collective-permute-start | bytes 786440 | tf_op jit(solution)/shard_map/ppermute | solution.py:63
  69.7 5.0 %collective-permute-start.18 = (bf16[16,64,128]{2,1,0:T(8,128)(2,1)S(1)}, bf16[16,64,128]{2,1,0:T(8,128)(2,1)S(1)}, u32[]{:S(2)}, u32[]{:S(2)}) collective-permute-start(bf16[16,64,128]{2,1,0:T(8,128)(2,1)S(1)} %bitcast.44), channel_id=1, source_target_pairs={{1,0},{0,1},{3,2},{2,3},{5,4},{4,5},{7,6},{6,7},{9,8},{8,9},{11,10... | collective-permute-start | bytes 786440 | tf_op jit(solution)/shard_map/ppermute | solution.py:63
  70.1 4.6 %collective-permute-start.19 = (bf16[16,64,128]{2,1,0:T(8,128)(2,1)S(1)}, bf16[16,64,128]{2,1,0:T(8,128)(2,1)S(1)}, u32[]{:S(2)}, u32[]{:S(2)}) collective-permute-start(bf16[16,64,128]{2,1,0:T(8,128)(2,1)S(1)} %collective-permute-done.17.refs_3_), channel_id=1, source_target_pairs={{1,0},{0,1},{3,2},{2,3},{5,4},{4,5},{7,6},{6,7},{9,8},{8,9},{11,10... | collective-permute-start | bytes 786440 | tf_op jit(solution)/shard_map/ppermute | solution.py:63
  70.2 12.5 %collective-permute-start.22 = (bf16[16,64,128]{2,1,0:T(8,128)(2,1)S(1)}, bf16[16,64,128]{2,1,0:T(8,128)(2,1)S(1)}, u32[]{:S(2)}, u32[]{:S(2)}) collective-permute-start(bf16[16,64,128]{2,1,0:T(8,128)(2,1)S(1)} %get-tuple-element.74), channel_id=1, source_target_pairs={{4,0},{5,1},{6,2},{7,3},{0,4},{1,5},{2,6},{3,7},{12,8},{13,9},{14,... | collective-permute-start | bytes 786440 | tf_op jit(solution)/shard_map/ppermute | solution.py:63
  71.4 14.7 %collective-permute-start.23 = (bf16[16,64,128]{2,1,0:T(8,128)(2,1)S(1)}, bf16[16,64,128]{2,1,0:T(8,128)(2,1)S(1)}, u32[]{:S(2)}, u32[]{:S(2)}) collective-permute-start(bf16[16,64,128]{2,1,0:T(8,128)(2,1)S(1)} %get-tuple-element.75), channel_id=1, source_target_pairs={{6,0},{7,1},{4,2},{5,3},{2,4},{3,5},{0,6},{1,7},{14,8},{15,9},{12,... | collective-permute-start | bytes 786440 | tf_op jit(solution)/shard_map/ppermute | solution.py:63
  80.9 5.3 %collective-permute-start.20 = (bf16[16,64,128]{2,1,0:T(8,128)(2,1)S(1)}, bf16[16,64,128]{2,1,0:T(8,128)(2,1)S(1)}, u32[]{:S(2)}, u32[]{:S(2)}) collective-permute-start(bf16[16,64,128]{2,1,0:T(8,128)(2,1)S(1)} %get-tuple-element.85), channel_id=1, source_target_pairs={{1,0},{0,1},{3,2},{2,3},{5,4},{4,5},{7,6},{6,7},{9,8},{8,9},{11,10... | collective-permute-start | bytes 786440 | tf_op jit(solution)/shard_map/ppermute | solution.py:63
  81.9 7.8 %collective-permute-start.24 = (bf16[16,64,128]{2,1,0:T(8,128)(2,1)S(1)}, bf16[16,64,128]{2,1,0:T(8,128)(2,1)S(1)}, u32[]{:S(2)}, u32[]{:S(2)}) collective-permute-start(bf16[16,64,128]{2,1,0:T(8,128)(2,1)S(1)} %get-tuple-element.76), channel_id=1, source_target_pairs={{16,0},{17,1},{18,2},{19,3},{20,4},{21,5},{22,6},{23,7},{24,8},{25... | collective-permute-start | bytes 786440 | tf_op jit(solution)/shard_map/ppermute | solution.py:63
  82.0 23.8 %collective-permute-start.25 = (bf16[16,64,128]{2,1,0:T(8,128)(2,1)S(1)}, bf16[16,64,128]{2,1,0:T(8,128)(2,1)S(1)}, u32[]{:S(2)}, u32[]{:S(2)}) collective-permute-start(bf16[16,64,128]{2,1,0:T(8,128)(2,1)S(1)} %get-tuple-element.77), channel_id=1, source_target_pairs={{18,0},{19,1},{16,2},{17,3},{22,4},{23,5},{20,6},{21,7},{26,8},{27... | collective-permute-start | bytes 786440 | tf_op jit(solution)/shard_map/ppermute | solution.py:63
  82.7 23.1 %collective-permute-start.21 = (bf16[16,64,128]{2,1,0:T(8,128)(2,1)S(1)}, bf16[16,64,128]{2,1,0:T(8,128)(2,1)S(1)}, u32[]{:S(2)}, u32[]{:S(2)}) collective-permute-start(bf16[16,64,128]{2,1,0:T(8,128)(2,1)S(1)} %get-tuple-element.86), channel_id=1, source_target_pairs={{1,0},{0,1},{3,2},{2,3},{5,4},{4,5},{7,6},{6,7},{9,8},{8,9},{11,10... | collective-permute-start | bytes 786440 | tf_op jit(solution)/shard_map/ppermute | solution.py:63
  86.1 19.7 %collective-permute-start.26 = (bf16[16,64,128]{2,1,0:T(8,128)(2,1)S(1)}, bf16[16,64,128]{2,1,0:T(8,128)(2,1)S(1)}, u32[]{:S(2)}, u32[]{:S(2)}) collective-permute-start(bf16[16,64,128]{2,1,0:T(8,128)(2,1)S(1)} %get-tuple-element.78), channel_id=1, source_target_pairs={{20,0},{21,1},{22,2},{23,3},{16,4},{17,5},{18,6},{19,7},{28,8},{29... | collective-permute-start | bytes 786440 | tf_op jit(solution)/shard_map/ppermute | solution.py:63
  86.1 19.7 %collective-permute-start.27 = (bf16[16,64,128]{2,1,0:T(8,128)(2,1)S(1)}, bf16[16,64,128]{2,1,0:T(8,128)(2,1)S(1)}, u32[]{:S(2)}, u32[]{:S(2)}) collective-permute-start(bf16[16,64,128]{2,1,0:T(8,128)(2,1)S(1)} %get-tuple-element.79), channel_id=1, source_target_pairs={{22,0},{23,1},{20,2},{21,3},{18,4},{19,5},{16,6},{17,7},{30,8},{31... | collective-permute-start | bytes 786440 | tf_op jit(solution)/shard_map/ppermute | solution.py:63
  89.6 22.3 %collective-permute-start.28 = (bf16[16,64,128]{2,1,0:T(8,128)(2,1)S(1)}, bf16[16,64,128]{2,1,0:T(8,128)(2,1)S(1)}, u32[]{:S(2)}, u32[]{:S(2)}) collective-permute-start(bf16[16,64,128]{2,1,0:T(8,128)(2,1)S(1)} %fusion.3), channel_id=1, source_target_pairs={{2,0},{3,1},{0,2},{1,3},{6,4},{7,5},{4,6},{5,7},{10,8},{11,9},{8,1... | collective-permute-start | bytes 786440 | tf_op jit(solution)/shard_map/ppermute | solution.py:63

commit v9 on v6

--- a/solution.py
+++ b/solution.py
@@ -38,19 +38,19 @@
 
 def first_source(zh, y, x, zl, c):
     return {
-        (0, 0): (zh, y, outer(x), 0, 0),
-        (0, 1): (zh ^ 1, outer(y), outer(x), 1, 0),
-        (1, 0): (zh, y, x, 1, 1),
-        (1, 1): (zh ^ 1, outer(y), x, 0, 1),
+        (0, 0): (zh, y, x, 0, 1),
+        (0, 1): (zh ^ 1, y, x, 1, 0),
+        (1, 0): (zh, outer(y), x, 1, 1),
+        (1, 1): (zh ^ 1, y, outer(x), 0, 0),
     }[zl, c]
 
 
 def second_source(zh, y, x, zl, c):
     return {
-        (0, 0): (zh, outer(y), outer(x), 0, 0),
-        (0, 1): (zh ^ 1, y, outer(x), 1, 0),
-        (1, 0): (zh, outer(y), x, 1, 1),
-        (1, 1): (zh ^ 1, y, x, 0, 1),
+        (0, 0): (zh, outer(y), outer(x), 0, 1),
+        (0, 1): (zh ^ 1, outer(y), outer(x), 1, 0),
+        (1, 0): (zh, y, outer(x), 1, 1),
+        (1, 1): (zh ^ 1, outer(y), x, 0, 0),
     }[zl, c]
 
 
@@ -238,7 +238,7 @@
                 ]
         return carry
 
-    lax.fori_loop(0, 4, middle, 0)
+    lax.fori_loop(0, 4, middle, 0, unroll=2)
     for copy in e_copies:
         copy.wait()
 

time: 108 us -> 110 us (1.019)
  waiting for transfers between devices: 42.1 us -> 46.4 us
  starting transfers between devices: 31.6 us -> 29.7 us
  Pallas kernels: 25.6 us -> 24.4 us
    ppermute x29, waiting for transfers between devices: 42.1 us -> 46.4 us  [receive(): return lax.ppermute(value, axes, pairs)]
    ppermute x29, starting transfers between devices: 31.6 us -> 29.7 us  [receive(): return lax.ppermute(value, axes, pairs)]
    pallas_call x4, Pallas kernels: 25.6 us -> 24.4 us  [exchange_part(): pl.pallas_call(functools.partial(pair_kernel, two_targets, stage), out_sh...]
  transfers between devices with their start and end apart: 29 -> 29, of which waited for: 13 -> 13; matrix products, arithmetic and copies ran while one was open for 6% -> 6% of each run, Pallas kernels for 17% -> 16%
where the time goes in v9:
time: 110 us; the launch traced here: 109 us
  waiting for transfers between devices  46.4 us (42%)
  starting transfers between devices  29.7 us (27%)
  Pallas kernels  24.4 us (22%)
  other arithmetic  6.3 us (6%)
  local copies, waits for them, and re-layouts  1.55 us (1%)
    ppermute x29, waiting for transfers between devices, receive(): return lax.ppermute(value, axes, pairs)  46.4 us
    ppermute x29, starting transfers between devices, receive(): return lax.ppermute(value, axes, pairs)  29.7 us
    pallas_call x4, Pallas kernels, exchange_part(): pl.pallas_call(functools.partial(pair_kernel, two_targets, stage), out_sh...  24.4 us
  transfers between devices with their start and end apart: 29, of which 13 were waited for; matrix products, arithmetic and copies ran while one was open for 6% of the time, Pallas kernels for 16%

profile of v9, /device:TPU:1, one launch (start us, length us, event | category | flops | bytes accessed | tf_op | source)
XLA Modules:
  0.0 109.3 jit_solution(17755624918188458749)
XLA Ops:
  0.0 2.0 %collective-permute-start = (bf16[16,64,128]{2,1,0:T(8,128)(2,1)}, bf16[16,64,128]{2,1,0:T(8,128)(2,1)S(1)}, u32[]{:S(2)}, u32[]{:S(2)}) collective-permute-start(bf16[16,64,128]{2,1,0:T(8,128)(2,1)} %bitcast.37), channel_id=1, source_target_pairs={{4,0},{5,1},{6,2},{7,3},{0,4},{1,5},{2,6},{3,7},{12,8},{13,9},{14,... | collective-permute-start | bytes 786440 | tf_op jit(solution)/shard_map/ppermute | solution.py:63
  2.0 1.6 %collective-permute-start.2 = (bf16[16,64,128]{2,1,0:T(8,128)(2,1)}, bf16[16,64,128]{2,1,0:T(8,128)(2,1)S(1)}, u32[]{:S(2)}, u32[]{:S(2)}) collective-permute-start(bf16[16,64,128]{2,1,0:T(8,128)(2,1)} %bitcast.38), channel_id=1, source_target_pairs={{6,0},{7,1},{4,2},{5,3},{2,4},{3,5},{0,6},{1,7},{14,8},{15,9},{12,... | collective-permute-start | bytes 786440 | tf_op jit(solution)/shard_map/ppermute | solution.py:63
  3.6 1.3 %collective-permute-start.3 = (bf16[16,64,128]{2,1,0:T(8,128)(2,1)}, bf16[16,64,128]{2,1,0:T(8,128)(2,1)S(1)}, u32[]{:S(2)}, u32[]{:S(2)}) collective-permute-start(bf16[16,64,128]{2,1,0:T(8,128)(2,1)} %bitcast.39), channel_id=1, source_target_pairs={{16,0},{17,1},{18,2},{19,3},{20,4},{21,5},{22,6},{23,7},{24,8},{25... | collective-permute-start | bytes 786440 | tf_op jit(solution)/shard_map/ppermute | solution.py:63
  4.9 0.0 collective-permute-start.4
  4.9 1.5 %collective-permute-start.8 = (bf16[64,64,128]{2,1,0:T(8,128)(2,1)}, bf16[64,64,128]{2,1,0:T(8,128)(2,1)S(1)}, u32[]{:S(2)}, u32[]{:S(2)}) collective-permute-start(bf16[64,64,128]{2,1,0:T(8,128)(2,1)} %bitcast.46), channel_id=1, source_target_pairs={{1,0},{66,1},{51,2},{76,3},{5,4},{70,5},{55,6},{72,7},{9,8},{74,9}... | collective-permute-start | bytes 3145736 | tf_op jit(solution)/shard_map/ppermute | solution.py:63
  6.5 0.8 select_reduce_fusion
  7.3 0.7 dynamic-slice_bitcast_fusion
  8.0 0.2 fusion.6
  8.2 0.6 fusion.10
  8.8 1.2 %compare_select_fusion.1 = f32[128]{0:T(128)S(1)} fusion(f32[]{:T(128)} %bitcast.5, f32[]{:T(128)} %bitcast.4), kind=kLoop, calls=%fused_computation.26 | loop fusion | flops 256 | bytes 520 | tf_op jit(solution)/shard_map/jit(_where)/select_n | solution.py:110
  10.6 0.1 add.130
  10.7 0.1 broadcast_add_fusion
  10.8 7.1 %collective-permute-start.9 = (bf16[64,64,128]{2,1,0:T(8,128)(2,1)}, bf16[64,64,128]{2,1,0:T(8,128)(2,1)S(1)}, u32[]{:S(2)}, u32[]{:S(2)}) collective-permute-start(bf16[64,64,128]{2,1,0:T(8,128)(2,1)} %bitcast.47), channel_id=1, source_target_pairs={{61,0},{126,1},{15,2},{112,3},{57,4},{122,5},{11,6},{116,7},{53,8}... | collective-permute-start | bytes 3145736 | tf_op jit(solution)/shard_map/ppermute | solution.py:63
  17.9 0.0 collective-permute-done.3.refs_5_
  17.9 0.0 copy-start.2
  18.0 0.0 copy-start.3
  18.0 0.0 copy-start.4
  18.0 2.1 %fusion = (f32[64,64,128]{2,1,0:T(8,128)S(1)}, f32[64,64,128]{2,1,0:T(8,128)S(1)}, f32[64,64,128]{2,1,0:T(8,128)S(1)}) fusion(f32[128]{0:T(128)S(1)} %compare_select_fusion.1, f32[]{:T(128)} %bitcast.2, f32[128]{0:T(128)S(1)} %add.130, f32[64,64]{1,0:T(8,128)S(1)} %broadcast_add_fusion, f32[]{:T(128)} %bitcast.5, f32[]{:T(128)} %bitcast.4), kind=kLoop, calls=%fused_computation.2 | loop fusion | flops 3145728 | bytes 6308876 | tf_op jit(solution)/shard_map/mul | solution.py:111
  20.1 1.6 %collective-permute-start.5 = (bf16[16,64,128]{2,1,0:T(8,128)(2,1)S(1)}, bf16[16,64,128]{2,1,0:T(8,128)(2,1)S(1)}, u32[]{:S(2)}, u32[]{:S(2)}) collective-permute-start(bf16[16,64,128]{2,1,0:T(8,128)(2,1)S(1)} %collective-permute-done.2.refs_3_), channel_id=1, source_target_pairs={{1,0},{0,1},{3,2},{2,3},{5,4},{4,5},{7,6},{6,7},{9,8},{8,9},{11,10... | collective-permute-start | bytes 786440 | tf_op jit(solution)/shard_map/ppermute | solution.py:63
  21.7 0.0 collective-permute-start.6
  21.7 0.5 collective-permute-start.7
  22.2 0.6 collective-permute-done.5.refs_4_
  22.8 0.4 collective-permute-done.6.refs_6_
  23.2 0.4 collective-permute-done.7.refs_8_
  23.6 1.6 %collective-permute-done.8.refs_9_.refs_5_ = bf16[64,64,128]{2,1,0:T(8,128)(2,1)S(1)} collective-permute-done((bf16[64,64,128]{2,1,0:T(8,128)(2,1)}, bf16[64,64,128]{2,1,0:T(8,128)(2,1)S(1)}, u32[]{:S(2)}, u32[]{:S(2)}) %collective-permute-start.8) | collective-permute-done | bytes 1048608 | tf_op jit(solution)/shard_map/ppermute | solution.py:63
  25.2 5.9 %shard_map.100 = (bf16[2,2,16,64,128]{4,3,2,1,0:T(8,128)(2,1)S(1)}, bf16[2,2,16,64,128]{4,3,2,1,0:T(8,128)(2,1)S(1)}) custom-call(s32[1]{0:T(128)} %bitcast.refs_0_, bf16[16,64,128]{2,1,0:T(8,128)(2,1)S(1)} %collective-permute-done.refs_1_, bf16[16,64,128]{2,1,0:T(8,128)(2,1)S(1)} %collective-permute-done.1.refs_2_, ...), custom_call_target="tpu_custom_call" | custom-call | flops 5000000000 | bytes 25165824 | tf_op jit(solution)/shard_map/pallas_call | solution.py:320
  31.1 0.0 copy-start
  31.1 11.9 %collective-permute-done.9.refs_9_.refs_6_ = bf16[64,64,128]{2,1,0:T(8,128)(2,1)S(1)} collective-permute-done((bf16[64,64,128]{2,1,0:T(8,128)(2,1)}, bf16[64,64,128]{2,1,0:T(8,128)(2,1)S(1)}, u32[]{:S(2)}, u32[]{:S(2)}) %collective-permute-start.9) | collective-permute-done | bytes 1048608 | tf_op jit(solution)/shard_map/ppermute | solution.py:63
  43.0 6.9 %shard_map.101 = (bf16[2,2,16,64,128]{4,3,2,1,0:T(8,128)(2,1)S(1)}, bf16[2,2,16,64,128]{4,3,2,1,0:T(8,128)(2,1)S(1)}) custom-call(s32[1]{0:T(128)} %bitcast.refs_0_, bf16[16,64,128]{2,1,0:T(8,128)(2,1)S(1)} %collective-permute-done.refs_1_, bf16[16,64,128]{2,1,0:T(8,128)(2,1)S(1)} %collective-permute-done.1.refs_2_, ...), custom_call_target="tpu_custom_call" | custom-call | flops 5000000000 | bytes 25165824 | tf_op jit(solution)/shard_map/pallas_call | solution.py:320
  49.9 0.1 collective-permute-start.10
  50.0 0.1 collective-permute-start.11
  50.1 1.9 %collective-permute-start.12 = (bf16[16,64,128]{2,1,0:T(8,128)(2,1)S(1)}, bf16[16,64,128]{2,1,0:T(8,128)(2,1)S(1)}, u32[]{:S(2)}, u32[]{:S(2)}) collective-permute-start(bf16[16,64,128]{2,1,0:T(8,128)(2,1)S(1)} %bitcast.42), channel_id=1, source_target_pairs={{22,0},{23,1},{20,2},{21,3},{18,4},{19,5},{16,6},{17,7},{30,8},{31... | collective-permute-start | bytes 786440 | tf_op jit(solution)/shard_map/ppermute | solution.py:63
  52.0 6.4 %collective-permute-done.11.refs_1_ = bf16[16,64,128]{2,1,0:T(8,128)(2,1)S(1)} collective-permute-done((bf16[16,64,128]{2,1,0:T(8,128)(2,1)S(1)}, bf16[16,64,128]{2,1,0:T(8,128)(2,1)S(1)}, u32[]{:S(2)}, u32[]{:S(2)}) %collective-permute-start.11) | collective-permute-done | bytes 262176 | tf_op jit(solution)/shard_map/ppermute | solution.py:63
  58.4 5.2 %collective-permute-done.12.refs_3_ = bf16[16,64,128]{2,1,0:T(8,128)(2,1)S(1)} collective-permute-done((bf16[16,64,128]{2,1,0:T(8,128)(2,1)S(1)}, bf16[16,64,128]{2,1,0:T(8,128)(2,1)S(1)}, u32[]{:S(2)}, u32[]{:S(2)}) %collective-permute-start.12) | collective-permute-done | bytes 262176 | tf_op jit(solution)/shard_map/ppermute | solution.py:63
  63.6 1.3 %collective-permute-start.13 = (bf16[16,64,128]{2,1,0:T(8,128)(2,1)S(1)}, bf16[16,64,128]{2,1,0:T(8,128)(2,1)S(1)}, u32[]{:S(2)}, u32[]{:S(2)}) collective-permute-start(bf16[16,64,128]{2,1,0:T(8,128)(2,1)S(1)} %collective-permute-done.11.refs_1_), channel_id=1, source_target_pairs={{1,0},{0,1},{3,2},{2,3},{5,4},{4,5},{7,6},{6,7},{9,8},{8,9},{11,10... | collective-permute-start | bytes 786440 | tf_op jit(solution)/shard_map/ppermute | solution.py:63
  64.9 0.0 collective-permute-start.14
  64.9 1.6 %collective-permute-start.17 = (bf16[16,64,128]{2,1,0:T(8,128)(2,1)S(1)}, bf16[16,64,128]{2,1,0:T(8,128)(2,1)S(1)}, u32[]{:S(2)}, u32[]{:S(2)}) collective-permute-start(bf16[16,64,128]{2,1,0:T(8,128)(2,1)S(1)} %bitcast.43), channel_id=1, source_target_pairs={{2,0},{3,1},{0,2},{1,3},{6,4},{7,5},{4,6},{5,7},{10,8},{11,9},{8,1... | collective-permute-start | bytes 786440 | tf_op jit(solution)/shard_map/ppermute | solution.py:63
  66.5 0.4 add_convert_fusion
  66.9 0.1 slice_bitcast_fusion
  67.0 5.8 %shard_map.102 = (bf16[1,2,16,64,128]{4,3,2,1,0:T(8,128)(2,1)S(1)}, bf16[1,2,16,64,128]{4,3,2,1,0:T(8,128)(2,1)S(1)}) custom-call(s32[1]{0:T(128)} %bitcast.refs_0_, bf16[16,64,128]{2,1,0:T(8,128)(2,1)S(1)} %collective-permute-done.11.refs_1_, bf16[16,64,128]{2,1,0:T(8,128)(2,1)S(1)} %collective-permute-done.13.refs_2_, ...), custom_call_target="tpu_custom_call" | custom-call | flops 5000000000 | bytes 25165824 | tf_op jit(solution)/shard_map/pallas_call | solution.py:320
  72.9 0.9 collective-permute-start.16
  73.8 0.1 collective-permute-start.15
  73.9 0.4 collective-permute-start.18
  74.3 0.1 collective-permute-start.19
  74.4 0.4 collective-permute-start.25
  74.8 0.1 collective-permute-done.16
  74.9 1.5 %collective-permute-start.24 = (bf16[16,64,128]{2,1,0:T(8,128)(2,1)S(1)}, bf16[16,64,128]{2,1,0:T(8,128)(2,1)S(1)}, u32[]{:S(2)}, u32[]{:S(2)}) collective-permute-start(bf16[16,64,128]{2,1,0:T(8,128)(2,1)S(1)} %get-tuple-element.84), channel_id=1, source_target_pairs={{16,0},{17,1},{18,2},{19,3},{20,4},{21,5},{22,6},{23,7},{24,8},{25... | collective-permute-start | bytes 786440 | tf_op jit(solution)/shard_map/ppermute | solution.py:63
  76.4 0.2 fusion.4
  76.6 5.8 %shard_map.103 = (bf16[1,2,16,64,128]{4,3,2,1,0:T(8,128)(2,1)S(1)}, bf16[1,2,16,64,128]{4,3,2,1,0:T(8,128)(2,1)S(1)}) custom-call(s32[1]{0:T(128)} %bitcast.refs_0_, bf16[16,64,128]{2,1,0:T(8,128)(2,1)S(1)} %bitcast.45, bf16[16,64,128]{2,1,0:T(8,128)(2,1)S(1)} %collective-permute-done.18.refs_2_, bf16[16,64,128]{2,1,0:T(8,128)(2,1)S(1)} %collective-permute-done.17.refs_3_, ...), custom_call_target="tpu_custom_call" | custom-call | flops 5000000000 | bytes 25165824 | tf_op jit(solution)/shard_map/pallas_call | solution.py:320
  82.5 1.1 %collective-permute-start.20 = (bf16[16,64,128]{2,1,0:T(8,128)(2,1)S(1)}, bf16[16,64,128]{2,1,0:T(8,128)(2,1)S(1)}, u32[]{:S(2)}, u32[]{:S(2)}) collective-permute-start(bf16[16,64,128]{2,1,0:T(8,128)(2,1)S(1)} %get-tuple-element.93), channel_id=1, source_target_pairs={{1,0},{0,1},{3,2},{2,3},{5,4},{4,5},{7,6},{6,7},{9,8},{8,9},{11,10... | collective-permute-start | bytes 786440 | tf_op jit(solution)/shard_map/ppermute | solution.py:63
  83.6 0.3 collective-permute-start.23
  83.9 1.5 %collective-permute-start.22 = (bf16[16,64,128]{2,1,0:T(8,128)(2,1)S(1)}, bf16[16,64,128]{2,1,0:T(8,128)(2,1)S(1)}, u32[]{:S(2)}, u32[]{:S(2)}) collective-permute-start(bf16[16,64,128]{2,1,0:T(8,128)(2,1)S(1)} %get-tuple-element.82), channel_id=1, source_target_pairs={{4,0},{5,1},{6,2},{7,3},{0,4},{1,5},{2,6},{3,7},{12,8},{13,9},{14,... | collective-permute-start | bytes 786440 | tf_op jit(solution)/shard_map/ppermute | solution.py:63
  85.4 0.7 collective-permute-start.27
  86.0 1.9 %collective-permute-done.24 = bf16[16,64,128]{2,1,0:T(8,128)(2,1)S(1)} collective-permute-done((bf16[16,64,128]{2,1,0:T(8,128)(2,1)S(1)}, bf16[16,64,128]{2,1,0:T(8,128)(2,1)S(1)}, u32[]{:S(2)}, u32[]{:S(2)}) %collective-permute-start.24) | collective-permute-done | bytes 262176 | tf_op jit(solution)/shard_map/ppermute | solution.py:63
  87.9 0.5 collective-permute-start.26
  88.4 1.2 %collective-permute-start.21 = (bf16[16,64,128]{2,1,0:T(8,128)(2,1)S(1)}, bf16[16,64,128]{2,1,0:T(8,128)(2,1)S(1)}, u32[]{:S(2)}, u32[]{:S(2)}) collective-permute-start(bf16[16,64,128]{2,1,0:T(8,128)(2,1)S(1)} %get-tuple-element.94), channel_id=1, source_target_pairs={{1,0},{0,1},{3,2},{2,3},{5,4},{4,5},{7,6},{6,7},{9,8},{8,9},{11,10... | collective-permute-start | bytes 786440 | tf_op jit(solution)/shard_map/ppermute | solution.py:63
  89.6 0.1 fusion.3
  89.7 2.6 %collective-permute-done.23 = bf16[16,64,128]{2,1,0:T(8,128)(2,1)S(1)} collective-permute-done((bf16[16,64,128]{2,1,0:T(8,128)(2,1)S(1)}, bf16[16,64,128]{2,1,0:T(8,128)(2,1)S(1)}, u32[]{:S(2)}, u32[]{:S(2)}) %collective-permute-start.23) | collective-permute-done | bytes 262176 | tf_op jit(solution)/shard_map/ppermute | solution.py:63
  92.3 0.5 collective-permute-start.28
  92.9 4.4 %collective-permute-done.22 = bf16[16,64,128]{2,1,0:T(8,128)(2,1)S(1)} collective-permute-done((bf16[16,64,128]{2,1,0:T(8,128)(2,1)S(1)}, bf16[16,64,128]{2,1,0:T(8,128)(2,1)S(1)}, u32[]{:S(2)}, u32[]{:S(2)}) %collective-permute-start.22) | collective-permute-done | bytes 262176 | tf_op jit(solution)/shard_map/ppermute | solution.py:63
  97.3 5.8 %collective-permute-done.27 = bf16[16,64,128]{2,1,0:T(8,128)(2,1)S(1)} collective-permute-done((bf16[16,64,128]{2,1,0:T(8,128)(2,1)S(1)}, bf16[16,64,128]{2,1,0:T(8,128)(2,1)S(1)}, u32[]{:S(2)}, u32[]{:S(2)}) %collective-permute-start.27) | collective-permute-done | bytes 262176 | tf_op jit(solution)/shard_map/ppermute | solution.py:63
  103.1 5.0 %collective-permute-done.26 = bf16[16,64,128]{2,1,0:T(8,128)(2,1)S(1)} collective-permute-done((bf16[16,64,128]{2,1,0:T(8,128)(2,1)S(1)}, bf16[16,64,128]{2,1,0:T(8,128)(2,1)S(1)}, u32[]{:S(2)}, u32[]{:S(2)}) %collective-permute-start.26) | collective-permute-done | bytes 262176 | tf_op jit(solution)/shard_map/ppermute | solution.py:63
  108.1 0.3 convert_add_fusion.3
  108.5 0.9 negate_bitcast_fusion
  (27 shorter events, 0.2 us)
Async XLA Ops:
  0.0 10.8 %collective-permute-start = (bf16[16,64,128]{2,1,0:T(8,128)(2,1)}, bf16[16,64,128]{2,1,0:T(8,128)(2,1)S(1)}, u32[]{:S(2)}, u32[]{:S(2)}) collective-permute-start(bf16[16,64,128]{2,1,0:T(8,128)(2,1)} %bitcast.37), channel_id=1, source_target_pairs={{4,0},{5,1},{6,2},{7,3},{0,4},{1,5},{2,6},{3,7},{12,8},{13,9},{14,... | collective-permute-start | bytes 786440 | tf_op jit(solution)/shard_map/ppermute | solution.py:63
  2.0 18.1 %collective-permute-start.2 = (bf16[16,64,128]{2,1,0:T(8,128)(2,1)}, bf16[16,64,128]{2,1,0:T(8,128)(2,1)S(1)}, u32[]{:S(2)}, u32[]{:S(2)}) collective-permute-start(bf16[16,64,128]{2,1,0:T(8,128)(2,1)} %bitcast.38), channel_id=1, source_target_pairs={{6,0},{7,1},{4,2},{5,3},{2,4},{3,5},{0,6},{1,7},{14,8},{15,9},{12,... | collective-permute-start | bytes 786440 | tf_op jit(solution)/shard_map/ppermute | solution.py:63
  3.6 14.3 %collective-permute-start.3 = (bf16[16,64,128]{2,1,0:T(8,128)(2,1)}, bf16[16,64,128]{2,1,0:T(8,128)(2,1)S(1)}, u32[]{:S(2)}, u32[]{:S(2)}) collective-permute-start(bf16[16,64,128]{2,1,0:T(8,128)(2,1)} %bitcast.39), channel_id=1, source_target_pairs={{16,0},{17,1},{18,2},{19,3},{20,4},{21,5},{22,6},{23,7},{24,8},{25... | collective-permute-start | bytes 786440 | tf_op jit(solution)/shard_map/ppermute | solution.py:63
  4.9 15.2 %collective-permute-start.4 = (bf16[16,64,128]{2,1,0:T(8,128)(2,1)}, bf16[16,64,128]{2,1,0:T(8,128)(2,1)S(1)}, u32[]{:S(2)}, u32[]{:S(2)}) collective-permute-start(bf16[16,64,128]{2,1,0:T(8,128)(2,1)} %bitcast.40), channel_id=1, source_target_pairs={{18,0},{19,1},{16,2},{17,3},{22,4},{23,5},{20,6},{21,7},{26,8},{27... | collective-permute-start | bytes 786440 | tf_op jit(solution)/shard_map/ppermute | solution.py:63
  4.9 20.3 %collective-permute-start.8 = (bf16[64,64,128]{2,1,0:T(8,128)(2,1)}, bf16[64,64,128]{2,1,0:T(8,128)(2,1)S(1)}, u32[]{:S(2)}, u32[]{:S(2)}) collective-permute-start(bf16[64,64,128]{2,1,0:T(8,128)(2,1)} %bitcast.46), channel_id=1, source_target_pairs={{1,0},{66,1},{51,2},{76,3},{5,4},{70,5},{55,6},{72,7},{9,8},{74,9}... | collective-permute-start | bytes 3145736 | tf_op jit(solution)/shard_map/ppermute | solution.py:63
  10.8 32.2 %collective-permute-start.9 = (bf16[64,64,128]{2,1,0:T(8,128)(2,1)}, bf16[64,64,128]{2,1,0:T(8,128)(2,1)S(1)}, u32[]{:S(2)}, u32[]{:S(2)}) collective-permute-start(bf16[64,64,128]{2,1,0:T(8,128)(2,1)} %bitcast.47), channel_id=1, source_target_pairs={{61,0},{126,1},{15,2},{112,3},{57,4},{122,5},{11,6},{116,7},{53,8}... | collective-permute-start | bytes 3145736 | tf_op jit(solution)/shard_map/ppermute | solution.py:63
  17.9 3.8 %collective-permute-start.1 = (bf16[16,64,128]{2,1,0:T(8,128)(2,1)S(1)}, bf16[16,64,128]{2,1,0:T(8,128)(2,1)S(1)}, u32[]{:S(2)}, u32[]{:S(2)}) collective-permute-start(bf16[16,64,128]{2,1,0:T(8,128)(2,1)S(1)} %collective-permute-done.refs_1_), channel_id=1, source_target_pairs={{1,0},{0,1},{3,2},{2,3},{5,4},{4,5},{7,6},{6,7},{9,8},{8,9},{11,10... | collective-permute-start | bytes 786440 | tf_op jit(solution)/shard_map/ppermute | solution.py:63
  17.9 7.3 %copy-start.1 = (bf16[256,256]{1,0:T(8,128)(2,1)S(1)}, bf16[256,256]{1,0:T(8,128)(2,1)}, u32[]{:S(2)}) copy-start(bf16[256,256]{1,0:T(8,128)(2,1)} %constant.44.clone.refs_13_.refs_10_) | copy-start | bytes 393220
  17.9 7.3 %copy-start.2 = (bf16[256,256]{1,0:T(8,128)(2,1)S(1)}, bf16[256,256]{1,0:T(8,128)(2,1)}, u32[]{:S(2)}) copy-start(bf16[256,256]{1,0:T(8,128)(2,1)} %constant.45.clone.refs_14_.refs_11_) | copy-start | bytes 393220
  18.0 7.3 %copy-start.3 = (bf16[128,128]{1,0:T(8,128)(2,1)S(1)}, bf16[128,128]{1,0:T(8,128)(2,1)}, u32[]{:S(2)}) copy-start(bf16[128,128]{1,0:T(8,128)(2,1)} %constant.42.clone.refs_11_.refs_8_) | copy-start | bytes 98308
  18.0 7.3 %copy-start.4 = (bf16[128,128]{1,0:T(8,128)(2,1)S(1)}, bf16[128,128]{1,0:T(8,128)(2,1)}, u32[]{:S(2)}) copy-start(bf16[128,128]{1,0:T(8,128)(2,1)} %constant.43.clone.refs_12_.refs_9_) | copy-start | bytes 98308
  20.1 2.7 %collective-permute-start.5 = (bf16[16,64,128]{2,1,0:T(8,128)(2,1)S(1)}, bf16[16,64,128]{2,1,0:T(8,128)(2,1)S(1)}, u32[]{:S(2)}, u32[]{:S(2)}) collective-permute-start(bf16[16,64,128]{2,1,0:T(8,128)(2,1)S(1)} %collective-permute-done.2.refs_3_), channel_id=1, source_target_pairs={{1,0},{0,1},{3,2},{2,3},{5,4},{4,5},{7,6},{6,7},{9,8},{8,9},{11,10... | collective-permute-start | bytes 786440 | tf_op jit(solution)/shard_map/ppermute | solution.py:63
  21.7 1.5 %collective-permute-start.6 = (bf16[16,64,128]{2,1,0:T(8,128)(2,1)S(1)}, bf16[16,64,128]{2,1,0:T(8,128)(2,1)S(1)}, u32[]{:S(2)}, u32[]{:S(2)}) collective-permute-start(bf16[16,64,128]{2,1,0:T(8,128)(2,1)S(1)} %collective-permute-done.3.refs_5_), channel_id=1, source_target_pairs={{1,0},{0,1},{3,2},{2,3},{5,4},{4,5},{7,6},{6,7},{9,8},{8,9},{11,10... | collective-permute-start | bytes 786440 | tf_op jit(solution)/shard_map/ppermute | solution.py:63
  21.7 1.9 %collective-permute-start.7 = (bf16[16,64,128]{2,1,0:T(8,128)(2,1)S(1)}, bf16[16,64,128]{2,1,0:T(8,128)(2,1)S(1)}, u32[]{:S(2)}, u32[]{:S(2)}) collective-permute-start(bf16[16,64,128]{2,1,0:T(8,128)(2,1)S(1)} %collective-permute-done.4.refs_7_), channel_id=1, source_target_pairs={{1,0},{0,1},{3,2},{2,3},{5,4},{4,5},{7,6},{6,7},{9,8},{8,9},{11,10... | collective-permute-start | bytes 786440 | tf_op jit(solution)/shard_map/ppermute | solution.py:63
  31.1 18.9 %copy-start = (bf16[1,16,64,128]{3,2,1,0:T(8,128)(2,1)S(1)}, bf16[1,16,64,128]{3,2,1,0:T(8,128)(2,1)}, u32[]{:S(2)}) copy-start(bf16[1,16,64,128]{3,2,1,0:T(8,128)(2,1)} %param.10) | copy-start | bytes 786436
  49.9 16.6 %collective-permute-start.10 = (bf16[2,2,16,64,128]{4,3,2,1,0:T(8,128)(2,1)S(1)}, bf16[2,2,16,64,128]{4,3,2,1,0:T(8,128)(2,1)S(1)}, u32[]{:S(2)}, u32[]{:S(2)}) collective-permute-start(bf16[2,2,16,64,128]{4,3,2,1,0:T(8,128)(2,1)S(1)} %get-tuple-element.62), channel_id=1, source_target_pairs={{1,0},{0,1},{3,2},{2,3},{5,4},{4,5},{7,6},{6,7},{9,8},{8,9},{11,10... | collective-permute-start | bytes 3145736 | tf_op jit(solution)/shard_map/ppermute | solution.py:63
  50.0 8.4 %collective-permute-start.11 = (bf16[16,64,128]{2,1,0:T(8,128)(2,1)S(1)}, bf16[16,64,128]{2,1,0:T(8,128)(2,1)S(1)}, u32[]{:S(2)}, u32[]{:S(2)}) collective-permute-start(bf16[16,64,128]{2,1,0:T(8,128)(2,1)S(1)} %bitcast.41), channel_id=1, source_target_pairs={{20,0},{21,1},{22,2},{23,3},{16,4},{17,5},{18,6},{19,7},{28,8},{29... | collective-permute-start | bytes 786440 | tf_op jit(solution)/shard_map/ppermute | solution.py:63
  50.1 13.5 %collective-permute-start.12 = (bf16[16,64,128]{2,1,0:T(8,128)(2,1)S(1)}, bf16[16,64,128]{2,1,0:T(8,128)(2,1)S(1)}, u32[]{:S(2)}, u32[]{:S(2)}) collective-permute-start(bf16[16,64,128]{2,1,0:T(8,128)(2,1)S(1)} %bitcast.42), channel_id=1, source_target_pairs={{22,0},{23,1},{20,2},{21,3},{18,4},{19,5},{16,6},{17,7},{30,8},{31... | collective-permute-start | bytes 786440 | tf_op jit(solution)/shard_map/ppermute | solution.py:63
  63.6 3.4 %collective-permute-start.13 = (bf16[16,64,128]{2,1,0:T(8,128)(2,1)S(1)}, bf16[16,64,128]{2,1,0:T(8,128)(2,1)S(1)}, u32[]{:S(2)}, u32[]{:S(2)}) collective-permute-start(bf16[16,64,128]{2,1,0:T(8,128)(2,1)S(1)} %collective-permute-done.11.refs_1_), channel_id=1, source_target_pairs={{1,0},{0,1},{3,2},{2,3},{5,4},{4,5},{7,6},{6,7},{9,8},{8,9},{11,10... | collective-permute-start | bytes 786440 | tf_op jit(solution)/shard_map/ppermute | solution.py:63
  64.9 2.2 %collective-permute-start.14 = (bf16[16,64,128]{2,1,0:T(8,128)(2,1)S(1)}, bf16[16,64,128]{2,1,0:T(8,128)(2,1)S(1)}, u32[]{:S(2)}, u32[]{:S(2)}) collective-permute-start(bf16[16,64,128]{2,1,0:T(8,128)(2,1)S(1)} %collective-permute-done.12.refs_3_), channel_id=1, source_target_pairs={{1,0},{0,1},{3,2},{2,3},{5,4},{4,5},{7,6},{6,7},{9,8},{8,9},{11,10... | collective-permute-start | bytes 786440 | tf_op jit(solution)/shard_map/ppermute | solution.py:63
  64.9 9.0 %collective-permute-start.17 = (bf16[16,64,128]{2,1,0:T(8,128)(2,1)S(1)}, bf16[16,64,128]{2,1,0:T(8,128)(2,1)S(1)}, u32[]{:S(2)}, u32[]{:S(2)}) collective-permute-start(bf16[16,64,128]{2,1,0:T(8,128)(2,1)S(1)} %bitcast.43), channel_id=1, source_target_pairs={{2,0},{3,1},{0,2},{1,3},{6,4},{7,5},{4,6},{5,7},{10,8},{11,9},{8,1... | collective-permute-start | bytes 786440 | tf_op jit(solution)/shard_map/ppermute | solution.py:63
  72.9 2.0 %collective-permute-start.16 = (bf16[16,64,128]{2,1,0:T(8,128)(2,1)S(1)}, bf16[16,64,128]{2,1,0:T(8,128)(2,1)S(1)}, u32[]{:S(2)}, u32[]{:S(2)}) collective-permute-start(bf16[16,64,128]{2,1,0:T(8,128)(2,1)S(1)} %get-tuple-element.97), channel_id=1, source_target_pairs={{1,0},{0,1},{3,2},{2,3},{5,4},{4,5},{7,6},{6,7},{9,8},{8,9},{11,10... | collective-permute-start | bytes 786440 | tf_op jit(solution)/shard_map/ppermute | solution.py:63
  73.8 2.6 %collective-permute-start.15 = (bf16[16,64,128]{2,1,0:T(8,128)(2,1)S(1)}, bf16[16,64,128]{2,1,0:T(8,128)(2,1)S(1)}, u32[]{:S(2)}, u32[]{:S(2)}) collective-permute-start(bf16[16,64,128]{2,1,0:T(8,128)(2,1)S(1)} %get-tuple-element.98), channel_id=1, source_target_pairs={{1,0},{0,1},{3,2},{2,3},{5,4},{4,5},{7,6},{6,7},{9,8},{8,9},{11,10... | collective-permute-start | bytes 786440 | tf_op jit(solution)/shard_map/ppermute | solution.py:63
  73.9 2.7 %collective-permute-start.18 = (bf16[16,64,128]{2,1,0:T(8,128)(2,1)S(1)}, bf16[16,64,128]{2,1,0:T(8,128)(2,1)S(1)}, u32[]{:S(2)}, u32[]{:S(2)}) collective-permute-start(bf16[16,64,128]{2,1,0:T(8,128)(2,1)S(1)} %bitcast.44), channel_id=1, source_target_pairs={{1,0},{0,1},{3,2},{2,3},{5,4},{4,5},{7,6},{6,7},{9,8},{8,9},{11,10... | collective-permute-start | bytes 786440 | tf_op jit(solution)/shard_map/ppermute | solution.py:63
  74.3 2.3 %collective-permute-start.19 = (bf16[16,64,128]{2,1,0:T(8,128)(2,1)S(1)}, bf16[16,64,128]{2,1,0:T(8,128)(2,1)S(1)}, u32[]{:S(2)}, u32[]{:S(2)}) collective-permute-start(bf16[16,64,128]{2,1,0:T(8,128)(2,1)S(1)} %collective-permute-done.17.refs_3_), channel_id=1, source_target_pairs={{1,0},{0,1},{3,2},{2,3},{5,4},{4,5},{7,6},{6,7},{9,8},{8,9},{11,10... | collective-permute-start | bytes 786440 | tf_op jit(solution)/shard_map/ppermute | solution.py:63
  74.4 11.0 %collective-permute-start.25 = (bf16[16,64,128]{2,1,0:T(8,128)(2,1)S(1)}, bf16[16,64,128]{2,1,0:T(8,128)(2,1)S(1)}, u32[]{:S(2)}, u32[]{:S(2)}) collective-permute-start(bf16[16,64,128]{2,1,0:T(8,128)(2,1)S(1)} %get-tuple-element.85), channel_id=1, source_target_pairs={{18,0},{19,1},{16,2},{17,3},{22,4},{23,5},{20,6},{21,7},{26,8},{27... | collective-permute-start | bytes 786440 | tf_op jit(solution)/shard_map/ppermute | solution.py:63
  74.9 13.0 %collective-permute-start.24 = (bf16[16,64,128]{2,1,0:T(8,128)(2,1)S(1)}, bf16[16,64,128]{2,1,0:T(8,128)(2,1)S(1)}, u32[]{:S(2)}, u32[]{:S(2)}) collective-permute-start(bf16[16,64,128]{2,1,0:T(8,128)(2,1)S(1)} %get-tuple-element.84), channel_id=1, source_target_pairs={{16,0},{17,1},{18,2},{19,3},{20,4},{21,5},{22,6},{23,7},{24,8},{25... | collective-permute-start | bytes 786440 | tf_op jit(solution)/shard_map/ppermute | solution.py:63
  82.5 5.9 %collective-permute-start.20 = (bf16[16,64,128]{2,1,0:T(8,128)(2,1)S(1)}, bf16[16,64,128]{2,1,0:T(8,128)(2,1)S(1)}, u32[]{:S(2)}, u32[]{:S(2)}) collective-permute-start(bf16[16,64,128]{2,1,0:T(8,128)(2,1)S(1)} %get-tuple-element.93), channel_id=1, source_target_pairs={{1,0},{0,1},{3,2},{2,3},{5,4},{4,5},{7,6},{6,7},{9,8},{8,9},{11,10... | collective-permute-start | bytes 786440 | tf_op jit(solution)/shard_map/ppermute | solution.py:63
  83.6 8.7 %collective-permute-start.23 = (bf16[16,64,128]{2,1,0:T(8,128)(2,1)S(1)}, bf16[16,64,128]{2,1,0:T(8,128)(2,1)S(1)}, u32[]{:S(2)}, u32[]{:S(2)}) collective-permute-start(bf16[16,64,128]{2,1,0:T(8,128)(2,1)S(1)} %get-tuple-element.83), channel_id=1, source_target_pairs={{6,0},{7,1},{4,2},{5,3},{2,4},{3,5},{0,6},{1,7},{14,8},{15,9},{12,... | collective-permute-start | bytes 786440 | tf_op jit(solution)/shard_map/ppermute | solution.py:63
  83.9 13.4 %collective-permute-start.22 = (bf16[16,64,128]{2,1,0:T(8,128)(2,1)S(1)}, bf16[16,64,128]{2,1,0:T(8,128)(2,1)S(1)}, u32[]{:S(2)}, u32[]{:S(2)}) collective-permute-start(bf16[16,64,128]{2,1,0:T(8,128)(2,1)S(1)} %get-tuple-element.82), channel_id=1, source_target_pairs={{4,0},{5,1},{6,2},{7,3},{0,4},{1,5},{2,6},{3,7},{12,8},{13,9},{14,... | collective-permute-start | bytes 786440 | tf_op jit(solution)/shard_map/ppermute | solution.py:63
  85.4 17.8 %collective-permute-start.27 = (bf16[16,64,128]{2,1,0:T(8,128)(2,1)S(1)}, bf16[16,64,128]{2,1,0:T(8,128)(2,1)S(1)}, u32[]{:S(2)}, u32[]{:S(2)}) collective-permute-start(bf16[16,64,128]{2,1,0:T(8,128)(2,1)S(1)} %get-tuple-element.87), channel_id=1, source_target_pairs={{22,0},{23,1},{20,2},{21,3},{18,4},{19,5},{16,6},{17,7},{30,8},{31... | collective-permute-start | bytes 786440 | tf_op jit(solution)/shard_map/ppermute | solution.py:63
  87.9 20.2 %collective-permute-start.26 = (bf16[16,64,128]{2,1,0:T(8,128)(2,1)S(1)}, bf16[16,64,128]{2,1,0:T(8,128)(2,1)S(1)}, u32[]{:S(2)}, u32[]{:S(2)}) collective-permute-start(bf16[16,64,128]{2,1,0:T(8,128)(2,1)S(1)} %get-tuple-element.86), channel_id=1, source_target_pairs={{20,0},{21,1},{22,2},{23,3},{16,4},{17,5},{18,6},{19,7},{28,8},{29... | collective-permute-start | bytes 786440 | tf_op jit(solution)/shard_map/ppermute | solution.py:63
  88.4 19.7 %collective-permute-start.21 = (bf16[16,64,128]{2,1,0:T(8,128)(2,1)S(1)}, bf16[16,64,128]{2,1,0:T(8,128)(2,1)S(1)}, u32[]{:S(2)}, u32[]{:S(2)}) collective-permute-start(bf16[16,64,128]{2,1,0:T(8,128)(2,1)S(1)} %get-tuple-element.94), channel_id=1, source_target_pairs={{1,0},{0,1},{3,2},{2,3},{5,4},{4,5},{7,6},{6,7},{9,8},{8,9},{11,10... | collective-permute-start | bytes 786440 | tf_op jit(solution)/shard_map/ppermute | solution.py:63
  92.3 16.1 %collective-permute-start.28 = (bf16[16,64,128]{2,1,0:T(8,128)(2,1)S(1)}, bf16[16,64,128]{2,1,0:T(8,128)(2,1)S(1)}, u32[]{:S(2)}, u32[]{:S(2)}) collective-permute-start(bf16[16,64,128]{2,1,0:T(8,128)(2,1)S(1)} %fusion.3), channel_id=1, source_target_pairs={{2,0},{3,1},{0,2},{1,3},{6,4},{7,5},{4,6},{5,7},{10,8},{11,9},{8,1... | collective-permute-start | bytes 786440 | tf_op jit(solution)/shard_map/ppermute | solution.py:63
